TPU v7x, 32 devices: a whole 2x2x4 slice. The times are simulated.
32 devices in a mesh: node: 16 (over z, y, x), rep: 2 (over core).
Axes of the slice: x: 2, y: 2, z: 4, core: 2. Of those that a mesh axis runs over, the one named last changes fastest.
Arguments:
- features: bfloat16 [4096, 512], P(('rep', 'node')), parts along dimension 0, may hold values from -24 to 24
- upstream: bfloat16 [4096, 512], P(('rep', 'node')), parts along dimension 0, may hold values from -36 to 36
- weight_one: bfloat16 [512, 512], replicated, may hold values from -0.25 to 0.25
- weight_two: bfloat16 [512, 512], replicated, may hold values from -0.25 to 0.25
- neighbours: int32 [4096, 32], P(('rep', 'node')), parts along dimension 0, may hold values from 0 to 2047, as said below
- edge_weight: int32 [4096, 32], P(('rep', 'node')), parts along dimension 0, may hold values from 1 to 8
- fetch_block: int32 [512, 2], P('rep'), parts along dimension 0, may hold values from 0 to 15, as said below
- fetch_count: int32 [512], P('rep'), parts along dimension 0, may hold values from 0 to 2, as said below
Outputs:
- d_features: bfloat16 [4096, 512], P(('rep', 'node')), parts along dimension 0
- grad_one: bfloat16 [1024, 512], P('rep'), parts along dimension 0
- grad_two: bfloat16 [1024, 512], P('rep'), parts along dimension 0
There are 2 independent parts, one for each index of `rep`. A program takes and returns all parts, laid end to end along the dimension named above; an argument that names none is the same for every part. Nothing has to cross between parts.
Inputs may be any that keep to these rules, and one draw needn't show every extreme that they name: `neighbours`: no node names itself. `fetch_block`: the 2 blocks listed for one pair of devices are distinct. `fetch_count`: zero where p = d; every device has 2 live blocks from some other device.
All inputs are finite; a program needn't handle non-finite values.
Results may differ from a plain program's by a relative error of at most 0.013.
Values may be sent and summed in bfloat16 or wider, within the bound.
No kernel may reach another device: no remote copies, remote signals or barrier semaphores. Data moves between devices by JAX's collectives and lax.ppermute only.
A program may use at most 64 MiB of HBM per device.

v0:
```python
import math

import jax
import jax.numpy as jnp
from jax import lax
from jax.sharding import PartitionSpec as P

D = 512
ROWS = 128
HALO = 32
BLK = 8
CAP = 2


SELF_WEIGHT = 8.0


def with_halo(block, sides, width):
    for axis, dim in sides:
        count = lax.axis_size(axis)
        forward = [(i, i + 1) for i in range(count - 1)]
        backward = [(target, source) for source, target in forward]
        low = lax.ppermute(
            lax.slice_in_dim(block, block.shape[dim] - width, None, axis=dim), axis, forward
        )
        high = lax.ppermute(lax.slice_in_dim(block, 0, width, axis=dim), axis, backward)
        block = jnp.concatenate([low, block, high], axis=dim)
    return block


def gelu_tanh(values):
    return jax.nn.gelu(values, approximate=True)


def edge_tables(neighbours, edge_weight, fetch_block, fetch_count, peer_count, device):
    first_row = device * ROWS
    local_rows = jnp.arange(ROWS, dtype=jnp.int32)
    owner_dev = neighbours // ROWS
    in_band = (neighbours >= first_row - HALO) & (neighbours < first_row + ROWS + HALO)
    my_table = lax.dynamic_slice_in_dim(fetch_block, device * peer_count, peer_count, 0)
    my_counts = lax.dynamic_slice_in_dim(fetch_count, device * peer_count, peer_count, 0)
    target = neighbours % ROWS // BLK
    listed = jnp.take(my_table, owner_dev, axis=0)
    live_slot = (
        jnp.arange(CAP, dtype=jnp.int32)[None, None, :] < jnp.take(my_counts, owner_dev)[..., None]
    )
    matched = (listed == target[..., None]) & live_slot
    found_slot = jnp.any(matched, axis=-1)
    slot_index = jnp.argmax(matched, axis=-1)
    weight = edge_weight.astype(jnp.float32)
    band_weight = jnp.where(in_band, weight, 0.0)
    far_use = jnp.logical_not(in_band) & found_slot
    far_weight = jnp.where(far_use, weight, 0.0)
    band_col = jnp.where(in_band, neighbours - first_row + HALO, 0)
    far_col = jnp.where(far_use, (owner_dev * CAP + slot_index) * BLK + neighbours % BLK, 0)
    row_index = jnp.broadcast_to(local_rows[:, None], neighbours.shape)
    band_matrix = (
        jnp.zeros((ROWS, ROWS + 2 * HALO), jnp.float32).at[row_index, band_col].add(band_weight)
    )
    band_matrix = band_matrix.at[local_rows, local_rows + HALO].add(SELF_WEIGHT)
    far_matrix = (
        jnp.zeros((ROWS, peer_count * CAP * BLK), jnp.float32)
        .at[row_index, far_col]
        .add(far_weight)
    )
    row_total = SELF_WEIGHT + jnp.sum(band_weight + far_weight, axis=1)
    asked_blocks = jnp.take(
        fetch_block, jnp.arange(peer_count, dtype=jnp.int32) * peer_count + device, axis=0
    )
    return (
        band_matrix.astype(jnp.bfloat16),
        far_matrix.astype(jnp.bfloat16),
        row_total,
        asked_blocks,
    )


def aggregate(values, band_matrix, far_matrix, row_total, asked_blocks):
    extended = with_halo(values, (("node", 0),), HALO)
    outgoing = values.reshape(ROWS // BLK, BLK, D)[asked_blocks]
    incoming = lax.all_to_all(outgoing, "node", split_axis=0, concat_axis=0, tiled=True)
    sums = jnp.dot(band_matrix, extended, preferred_element_type=jnp.float32)
    sums = sums + jnp.dot(far_matrix, incoming.reshape(-1, D), preferred_element_type=jnp.float32)
    return (sums / row_total[:, None]).astype(jnp.bfloat16)


def adjoint(cotangent, band_matrix, far_matrix, asked_blocks, peer_count):
    back_band = lax.dot_general(
        band_matrix, cotangent, (((0,), (0,)), ((), ())), preferred_element_type=jnp.float32
    )
    own_rows = back_band[HALO : HALO + ROWS]
    rim_terms = jnp.concatenate([back_band[:HALO], back_band[HALO + ROWS :]], axis=0)
    rim_back = with_halo(rim_terms.astype(jnp.bfloat16), (("node", 0),), HALO).astype(
        rim_terms.dtype
    )
    own_rows = own_rows.at[:HALO].add(rim_back[:HALO])
    own_rows = own_rows.at[ROWS - HALO :].add(rim_back[3 * HALO :])
    back_far = lax.dot_general(
        far_matrix, cotangent, (((0,), (0,)), ((), ())), preferred_element_type=jnp.float32
    )
    back_far = back_far.reshape(peer_count, CAP, BLK, D)
    returned = lax.all_to_all(
        back_far.astype(jnp.bfloat16), "node", split_axis=0, concat_axis=0, tiled=True
    ).astype(back_far.dtype)
    own_rows = own_rows.reshape(ROWS // BLK, BLK, D).at[asked_blocks].add(returned)
    return own_rows.reshape(ROWS, D)


def contract_rows(left, right):
    return lax.dot_general(
        left, right, (((0,), (0,)), ((), ())), preferred_element_type=jnp.float32
    )


def sum_weight_grad(partial_grad):
    return lax.psum(partial_grad, "node")


def shards(
    features, upstream, weight_one, weight_two, neighbours, edge_weight, fetch_block, fetch_count
):
    peer_count = lax.axis_size("node")
    device = lax.axis_index("node")
    band_matrix, far_matrix, row_total, asked_blocks = edge_tables(
        neighbours, edge_weight, fetch_block, fetch_count, peer_count, device
    )
    grad_scale = 1.0 / math.sqrt(ROWS * peer_count)
    agg_one = aggregate(features, band_matrix, far_matrix, row_total, asked_blocks)
    pre_one = jnp.dot(agg_one, weight_one, preferred_element_type=jnp.float32)
    hidden_f, gelu_back = jax.vjp(gelu_tanh, pre_one)
    hidden = hidden_f.astype(jnp.bfloat16)
    agg_two = aggregate(hidden, band_matrix, far_matrix, row_total, asked_blocks)
    part_two = contract_rows(agg_two, upstream)
    summed_two = sum_weight_grad(part_two)
    q_two = lax.dot_general(
        upstream, weight_two, (((1,), (1,)), ((), ())), preferred_element_type=jnp.float32
    )
    q_two = (q_two / row_total[:, None]).astype(jnp.bfloat16)
    back_hidden = adjoint(q_two, band_matrix, far_matrix, asked_blocks, peer_count)
    d_pre = gelu_back(back_hidden)[0].astype(jnp.bfloat16)
    part_one = contract_rows(agg_one, d_pre)
    summed_one = sum_weight_grad(part_one)
    q_one = lax.dot_general(
        d_pre, weight_one, (((1,), (1,)), ((), ())), preferred_element_type=jnp.float32
    )
    q_one = (q_one / row_total[:, None]).astype(jnp.bfloat16)
    d_features = adjoint(q_one, band_matrix, far_matrix, asked_blocks, peer_count)
    grad_one = (summed_one * grad_scale).astype(jnp.bfloat16)
    grad_two = (summed_two * grad_scale).astype(jnp.bfloat16)
    return (d_features.astype(jnp.bfloat16), grad_one, grad_two)


def solution(mesh):
    placed = (
        P(("rep", "node"), None),
        P(("rep", "node"), None),
        P(),
        P(),
        P(("rep", "node"), None),
        P(("rep", "node"), None),
        P("rep", None),
        P("rep"),
    )
    return jax.shard_map(
        shards,
        mesh=mesh,
        in_specs=placed,
        out_specs=(P(("rep", "node"), None), P("rep", None), P("rep", None)),
        check_vma=False,
    )
```

profile of v0, /device:TPU:0, one launch (start us, length us, event | category | flops | bytes accessed | tf_op | source)
XLA Modules:
  0.0 309.5 jit_solution(4038717599790663979)
XLA Ops:
  8.6 5.4 %collective-permute-start.2 = (bf16[32,512]{1,0:T(8,128)(2,1)}, bf16[32,512]{1,0:T(8,128)(2,1)}, u32[]{:S(2)}, u32[]{:S(2)}) collective-permute-start(bf16[32,512]{1,0:T(8,128)(2,1)} %get-tuple-element.74), channel_id=1, source_target_pairs={{0,2},{2,4},{4,6},{6,8},{8,10},{10,12},{12,14},{14,16},{16,18},{18... | collective-permute-start | bytes 98312 | tf_op jit(solution)/shard_map/ppermute | solution.py:23
  17.1 2.2 gather_fusion.2
  19.3 8.0 %all-to-all-start.1 = ((bf16[16,2,8,512]{3,2,1,0:T(8,128)(2,1)}), bf16[16,2,8,512]{3,2,1,0:T(8,128)(2,1)S(1)}, u32[]{:S(2)}, u32[]{:S(2)}) async-start(bf16[16,2,8,512]{3,2,1,0:T(8,128)(2,1)} %bitcast.29), calls=%async_computation.1 | async-start | bytes 524288 | tf_op jit(solution)/shard_map/all_to_all | solution.py:81
  31.9 10.1 %select_select_fusion = s32[128,32]{0,1:T(8,128)S(1)} fusion(s32[128,32]{0,1:T(8,128)S(1)} %get-tuple-element.65, s32[]{:T(128)} %bitcast.5, s32[]{:T(128)} %bitcast.6, s32[]{:T(128)} %bitcast.7, s32[]{:T(128)} %bitcast.8, s32[]{:T(128)} %bitcast.9, s32[]{:T(128)} %bitcast.10, s32[]{:T(128)} %bitcast.11, s32[]{:T(128)} %bitcast.12, s32[]{:T(128)} %bitcast.13, ...), kind=kLoop, calls=%fused_computation.100 | loop fusion | flops 139264 | bytes 32832 | tf_op jit(solution)/shard_map/jit(_take)/select_n | solution.py:45
  42.1 10.8 %gather_fusion = s32[4096,2]{1,0:T(8,128)S(1)} fusion(s32[16,2]{1,0:T(8,128)S(1)} %constant_dynamic-slice_fusion, s32[4096]{0:T(1024)S(1)} %broadcast_clamp_fusion), kind=kCustom, calls=%fused_computation | custom fusion | bytes 81920 | tf_op jit(solution)/shard_map/jit(_take)/gather | solution.py:43
  52.8 6.2 %fusion.57 = (pred[128,32]{1,0:T(8,128)(4,1)}, pred[128,32,2]{2,1,0:T(8,128)(4,1)S(1)}) fusion(s32[128,32]{1,0:T(8,128)S(1)} %copy.64, s32[128,32]{1,0:T(8,128)S(1)} %copy.63, s32[128,32,2]{2,1,0:T(8,128)S(1)} %bitcast.88, pred[128,32]{1,0:T(8,128)(4,1)} %copy.60), kind=kLoop, calls=%fused_computation.136 | loop fusion | flops 36864 | bytes 81920 | tf_op jit(solution)/shard_map/reduce_or | solution.py:48
  60.9 5.1 %iota_reduce_fusion = (pred[128,32]{1,0:T(8,128)(4,1)}, s32[128,32]{1,0:T(8,128)S(1)}) fusion(pred[128,32,2]{2,1,0:T(8,128)(4,1)S(1)} %get-tuple-element.63), kind=kLoop, calls=%fused_computation.9 | loop fusion | flops 28672 | bytes 28672 | tf_op jit(solution)/shard_map/edge_tables/reduce | solution.py:49
  68.6 21.9 %scatter_custom_fusion.3 = f32[24576]{0:T(1024)S(1)} fusion(s32[4096]{0:T(1024)S(1)} %reshape.324, f32[4096]{0:T(1024)S(1)} %reshape.326, f32[]{:T(128)} %constant.212.clone.1), kind=kCustom, calls=%fused_computation.67 | custom fusion | flops 4096 | bytes 98308
  90.6 7.1 %scatter_fusion = f32[128,192]{0,1:T(8,128)S(1)} fusion(f32[128,192]{0,1:T(8,128)S(1)} %bitcast.89, s32[128]{0:T(128)S(1)} %fusion.52, f32[128]{0:T(128)S(1)} %broadcast.327), kind=kCustom, calls=%fused_computation.4 | custom fusion | flops 128 | bytes 2560 | tf_op jit(solution)/shard_map/scatter-add | solution.py:60
  98.3 3.8 %collective-permute-start = (bf16[32,512]{1,0:T(8,128)(2,1)S(1)}, bf16[32,512]{1,0:T(8,128)(2,1)S(1)}, u32[]{:S(2)}, u32[]{:S(2)}) collective-permute-start(bf16[32,512]{1,0:T(8,128)(2,1)S(1)} %get-tuple-element.70), channel_id=1, source_target_pairs={{0,2},{2,4},{4,6},{6,8},{8,10},{10,12},{12,14},{14,16},{16,18},{18... | collective-permute-start | bytes 98312 | tf_op jit(solution)/shard_map/ppermute | solution.py:23
  103.8 28.8 %scatter_custom_fusion.4 = f32[32768]{0:T(1024)S(1)} fusion(s32[4096]{0:T(1024)S(1)} %reshape.330, f32[4096]{0:T(1024)S(1)} %reshape.332, f32[]{:T(128)} %constant.212.clone.1), kind=kCustom, calls=%fused_computation.65 | custom fusion | flops 4096 | bytes 131076
  133.7 7.7 %all-to-all-start = ((bf16[16,2,8,512]{3,2,1,0:T(8,128)(2,1)}), bf16[16,2,8,512]{3,2,1,0:T(8,128)(2,1)S(1)}, u32[]{:S(2)}, u32[]{:S(2)}) async-start(bf16[16,2,8,512]{3,2,1,0:T(8,128)(2,1)} %bitcast.25), calls=%async_computation | async-start | bytes 524288 | tf_op jit(solution)/shard_map/all_to_all | solution.py:102
  142.8 7.0 %all-to-all-done = bf16[16,2,8,512]{3,2,1,0:T(8,128)(2,1)S(1)} async-done(((bf16[16,2,8,512]{3,2,1,0:T(8,128)(2,1)}), bf16[16,2,8,512]{3,2,1,0:T(8,128)(2,1)S(1)}, u32[]{:S(2)}, u32[]{:S(2)}) %all-to-all-start) | async-done | bytes 262176 | tf_op jit(solution)/shard_map/all_to_all | solution.py:102
  149.9 1.9 scatter_fusion.1
  153.2 3.5 %all-to-all-start.3 = ((bf16[16,2,8,512]{3,2,1,0:T(8,128)(2,1)}), bf16[16,2,8,512]{3,2,1,0:T(8,128)(2,1)S(1)}, u32[]{:S(2)}, u32[]{:S(2)}) async-start(bf16[16,2,8,512]{3,2,1,0:T(8,128)(2,1)} %bitcast.36), calls=%async_computation.3 | async-start | bytes 524288 | tf_op jit(solution)/shard_map/all_to_all | solution.py:81
  156.8 3.8 %collective-permute-start.6 = (bf16[32,512]{1,0:T(8,128)(2,1)S(1)}, bf16[32,512]{1,0:T(8,128)(2,1)S(1)}, u32[]{:S(2)}, u32[]{:S(2)}) collective-permute-start(bf16[32,512]{1,0:T(8,128)(2,1)S(1)} %get-tuple-element.72), channel_id=1, source_target_pairs={{0,2},{2,4},{4,6},{6,8},{8,10},{10,12},{12,14},{14,16},{16,18},{18... | collective-permute-start | bytes 98312 | tf_op jit(solution)/shard_map/ppermute | solution.py:23
  163.3 2.0 all-to-all-done.3
  169.3 7.3 %all-to-all-start.2 = ((bf16[16,2,8,512]{3,2,1,0:T(8,128)(2,1)}), bf16[16,2,8,512]{3,2,1,0:T(8,128)(2,1)S(1)}, u32[]{:S(2)}, u32[]{:S(2)}) async-start(bf16[16,2,8,512]{3,2,1,0:T(8,128)(2,1)} %bitcast.32), calls=%async_computation.2 | async-start | bytes 524288 | tf_op jit(solution)/shard_map/all_to_all | solution.py:102
  176.8 3.8 %collective-permute-start.4 = (bf16[32,512]{1,0:T(8,128)(2,1)S(1)}, bf16[32,512]{1,0:T(8,128)(2,1)S(1)}, u32[]{:S(2)}, u32[]{:S(2)}) collective-permute-start(bf16[32,512]{1,0:T(8,128)(2,1)S(1)} %get-tuple-element.68), channel_id=1, source_target_pairs={{0,2},{2,4},{4,6},{6,8},{8,10},{10,12},{12,14},{14,16},{16,18},{18... | collective-permute-start | bytes 98312 | tf_op jit(solution)/shard_map/ppermute | solution.py:23
  182.7 4.0 %collective-permute-done.5 = bf16[32,512]{1,0:T(8,128)(2,1)S(1)} collective-permute-done((bf16[32,512]{1,0:T(8,128)(2,1)S(1)}, bf16[32,512]{1,0:T(8,128)(2,1)S(1)}, u32[]{:S(2)}, u32[]{:S(2)}) %collective-permute-start.5) | collective-permute-done | bytes 32800 | tf_op jit(solution)/shard_map/ppermute | solution.py:26
  186.7 2.6 all-to-all-done.2
  189.4 1.9 scatter_fusion.2
  191.9 107.6 %all-reduce.3.cloned.1.call-done = (f32[512,512]{1,0:T(8,128)}, f32[512,512]{1,0:T(8,128)}) async-done(((f32[512,512]{1,0:T(8,128)}, f32[512,512]{1,0:T(8,128)}), (f32[512,512]{1,0:T(8,128)}, f32[512,512]{1,0:T(8,128)})) %all-reduce.3.cloned.1.call-update) | async-done | bytes 2097168 | tf_op jit(solution)/shard_map/psum | solution.py:116
  299.5 2.2 multiply_convert_fusion.1
  (99 shorter events, 30.2 us)
Async XLA Ops:
  7.2 135.4 %copy-start = (bf16[512,512]{1,0:T(8,128)(2,1)S(1)}, bf16[512,512]{1,0:T(8,128)(2,1)}, u32[]{:S(2)}) copy-start(bf16[512,512]{1,0:T(8,128)(2,1)} %param.18) | copy-start | bytes 1572868
  8.6 132.9 %collective-permute-start.2 = (bf16[32,512]{1,0:T(8,128)(2,1)}, bf16[32,512]{1,0:T(8,128)(2,1)}, u32[]{:S(2)}, u32[]{:S(2)}) collective-permute-start(bf16[32,512]{1,0:T(8,128)(2,1)} %get-tuple-element.74), channel_id=1, source_target_pairs={{0,2},{2,4},{4,6},{6,8},{8,10},{10,12},{12,14},{14,16},{16,18},{18... | collective-permute-start | bytes 98312 | tf_op jit(solution)/shard_map/ppermute | solution.py:23
  14.1 127.5 %collective-permute-start.3 = (bf16[32,512]{1,0:T(8,128)(2,1)}, bf16[32,512]{1,0:T(8,128)(2,1)}, u32[]{:S(2)}, u32[]{:S(2)}) collective-permute-start(bf16[32,512]{1,0:T(8,128)(2,1)} %get-tuple-element.75), channel_id=1, source_target_pairs={{2,0},{4,2},{6,4},{8,6},{10,8},{12,10},{14,12},{16,14},{18,16},{20... | collective-permute-start | bytes 98312 | tf_op jit(solution)/shard_map/ppermute | solution.py:26
  17.1 10.2 %copy-start.4 = (s32[1024]{0:T(1024)}, s32[1024]{0:T(1024)S(1)}, u32[]{:S(2)}) copy-start(s32[1024]{0:T(1024)S(1)} %pad_clamp_fusion) | copy-start | bytes 12292
  19.3 114.4 %all-to-all-start.1 = ((bf16[16,2,8,512]{3,2,1,0:T(8,128)(2,1)}), bf16[16,2,8,512]{3,2,1,0:T(8,128)(2,1)S(1)}, u32[]{:S(2)}, u32[]{:S(2)}) async-start(bf16[16,2,8,512]{3,2,1,0:T(8,128)(2,1)} %bitcast.29), calls=%async_computation.1 | async-start | bytes 524288 | tf_op jit(solution)/shard_map/all_to_all | solution.py:81
  59.0 38.7 %copy-start.3 = (bf16[128,512]{1,0:T(8,128)(2,1)S(1)}, bf16[128,512]{1,0:T(8,128)(2,1)}, u32[]{:S(2)}) copy-start(bf16[128,512]{1,0:T(8,128)(2,1)} %param.17) | copy-start | bytes 393220
  59.1 38.7 %copy-start.6 = (bf16[512,512]{1,0:T(8,128)(2,1)S(1)}, bf16[512,512]{1,0:T(8,128)(2,1)}, u32[]{:S(2)}) copy-start(bf16[512,512]{1,0:T(8,128)(2,1)} %param.19) | copy-start | bytes 1572868
  98.1 43.5 %copy-start.2 = (bf16[128,512]{1,0:T(8,128)(2,1)S(1)}, bf16[128,512]{1,0:T(8,128)(2,1)}, u32[]{:S(2)}) copy-start(bf16[128,512]{1,0:T(8,128)(2,1)} %param.16) | copy-start | bytes 393220
  98.3 35.3 %collective-permute-start = (bf16[32,512]{1,0:T(8,128)(2,1)S(1)}, bf16[32,512]{1,0:T(8,128)(2,1)S(1)}, u32[]{:S(2)}, u32[]{:S(2)}) collective-permute-start(bf16[32,512]{1,0:T(8,128)(2,1)S(1)} %get-tuple-element.70), channel_id=1, source_target_pairs={{0,2},{2,4},{4,6},{6,8},{8,10},{10,12},{12,14},{14,16},{16,18},{18... | collective-permute-start | bytes 98312 | tf_op jit(solution)/shard_map/ppermute | solution.py:23
  102.1 31.5 %collective-permute-start.1 = (bf16[32,512]{1,0:T(8,128)(2,1)S(1)}, bf16[32,512]{1,0:T(8,128)(2,1)S(1)}, u32[]{:S(2)}, u32[]{:S(2)}) collective-permute-start(bf16[32,512]{1,0:T(8,128)(2,1)S(1)} %get-tuple-element.71), channel_id=1, source_target_pairs={{2,0},{4,2},{6,4},{8,6},{10,8},{12,10},{14,12},{16,14},{18,16},{20... | collective-permute-start | bytes 98312 | tf_op jit(solution)/shard_map/ppermute | solution.py:26
  133.7 16.2 %all-to-all-start = ((bf16[16,2,8,512]{3,2,1,0:T(8,128)(2,1)}), bf16[16,2,8,512]{3,2,1,0:T(8,128)(2,1)S(1)}, u32[]{:S(2)}, u32[]{:S(2)}) async-start(bf16[16,2,8,512]{3,2,1,0:T(8,128)(2,1)} %bitcast.25), calls=%async_computation | async-start | bytes 524288 | tf_op jit(solution)/shard_map/all_to_all | solution.py:102
  142.5 9.4 %copy-start.5 = (s32[1024]{0:T(1024)S(1)}, s32[1024]{0:T(1024)}, u32[]{:S(2)}) copy-start(s32[1024]{0:T(1024)} %copy-done.4) | copy-start | bytes 12292
  153.2 12.0 %all-to-all-start.3 = ((bf16[16,2,8,512]{3,2,1,0:T(8,128)(2,1)}), bf16[16,2,8,512]{3,2,1,0:T(8,128)(2,1)S(1)}, u32[]{:S(2)}, u32[]{:S(2)}) async-start(bf16[16,2,8,512]{3,2,1,0:T(8,128)(2,1)} %bitcast.36), calls=%async_computation.3 | async-start | bytes 524288 | tf_op jit(solution)/shard_map/all_to_all | solution.py:81
  156.8 142.7 %all-reduce.3.cloned.1.call-start = ((), (), s32[]{:S(2)}) async-start(), calls=%async_computation.4 | async-start | bytes 4194304 | tf_op jit(solution)/shard_map/psum | solution.py:116
  156.8 8.6 %collective-permute-start.6 = (bf16[32,512]{1,0:T(8,128)(2,1)S(1)}, bf16[32,512]{1,0:T(8,128)(2,1)S(1)}, u32[]{:S(2)}, u32[]{:S(2)}) collective-permute-start(bf16[32,512]{1,0:T(8,128)(2,1)S(1)} %get-tuple-element.72), channel_id=1, source_target_pairs={{0,2},{2,4},{4,6},{6,8},{8,10},{10,12},{12,14},{14,16},{16,18},{18... | collective-permute-start | bytes 98312 | tf_op jit(solution)/shard_map/ppermute | solution.py:23
  160.7 5.8 %collective-permute-start.7 = (bf16[32,512]{1,0:T(8,128)(2,1)S(1)}, bf16[32,512]{1,0:T(8,128)(2,1)S(1)}, u32[]{:S(2)}, u32[]{:S(2)}) collective-permute-start(bf16[32,512]{1,0:T(8,128)(2,1)S(1)} %get-tuple-element.73), channel_id=1, source_target_pairs={{2,0},{4,2},{6,4},{8,6},{10,8},{12,10},{14,12},{16,14},{18,16},{20... | collective-permute-start | bytes 98312 | tf_op jit(solution)/shard_map/ppermute | solution.py:26
  169.3 20.0 %all-to-all-start.2 = ((bf16[16,2,8,512]{3,2,1,0:T(8,128)(2,1)}), bf16[16,2,8,512]{3,2,1,0:T(8,128)(2,1)S(1)}, u32[]{:S(2)}, u32[]{:S(2)}) async-start(bf16[16,2,8,512]{3,2,1,0:T(8,128)(2,1)} %bitcast.32), calls=%async_computation.2 | async-start | bytes 524288 | tf_op jit(solution)/shard_map/all_to_all | solution.py:102
  176.8 5.9 %collective-permute-start.4 = (bf16[32,512]{1,0:T(8,128)(2,1)S(1)}, bf16[32,512]{1,0:T(8,128)(2,1)S(1)}, u32[]{:S(2)}, u32[]{:S(2)}) collective-permute-start(bf16[32,512]{1,0:T(8,128)(2,1)S(1)} %get-tuple-element.68), channel_id=1, source_target_pairs={{0,2},{2,4},{4,6},{6,8},{8,10},{10,12},{12,14},{14,16},{16,18},{18... | collective-permute-start | bytes 98312 | tf_op jit(solution)/shard_map/ppermute | solution.py:23
  180.7 6.0 %collective-permute-start.5 = (bf16[32,512]{1,0:T(8,128)(2,1)S(1)}, bf16[32,512]{1,0:T(8,128)(2,1)S(1)}, u32[]{:S(2)}, u32[]{:S(2)}) collective-permute-start(bf16[32,512]{1,0:T(8,128)(2,1)S(1)} %get-tuple-element.69), channel_id=1, source_target_pairs={{2,0},{4,2},{6,4},{8,6},{10,8},{12,10},{14,12},{16,14},{18,16},{20... | collective-permute-start | bytes 98312 | tf_op jit(solution)/shard_map/ppermute | solution.py:26
  299.5 2.2 copy-start.1
Sparse Core Ops, SparseCore 0:
  168.1 131.3 all-reduce.2
where the time goes:
time: 311 us; the launch traced here: 309 us
  waiting for transfers between devices  125 us (40%)
  other arithmetic  92.5 us (30%)
  starting transfers between devices  48.6 us (16%)
  local copies, waits for them, and re-layouts  21.6 us (7%)
  between operations  14.6 us (5%)
  matrix products  7.28 us (2%)
    psum x1, waiting for transfers between devices, sum_weight_grad(): return lax.psum(partial_grad, 'node')  108 us
    unnamed x5, other arithmetic  52.4 us
    ppermute x4, starting transfers between devices, with_halo(): lax.ppermute(lax.slice_in_dim(block, block.shape[dim] - width, None, axis...  16.9 us
    all_to_all x2, starting transfers between devices, adjoint(): lax.all_to_all(back_far.astype(jnp.bfloat16), 'node', split_axis=0, conca...  15 us
    all_to_all x2, starting transfers between devices, aggregate(): lax.all_to_all(outgoing, 'node', split_axis=0, concat_axis=0, tiled=True)  11.5 us
    gather x1, local copies, waits for them, and re-layouts, edge_tables(): listed = jnp.take(my_table, owner_dev, axis=0)  10.8 us
    select_n x1, other arithmetic, edge_tables(): jnp.take(my_counts, owner_dev)[..., None]  10.1 us
    all_to_all x2, waiting for transfers between devices, adjoint(): lax.all_to_all(back_far.astype(jnp.bfloat16), 'node', split_axis=0, conca...  9.64 us
  transfers between devices with their start and end apart: 13, of which 7 were waited for; matrix products, arithmetic and copies ran while one was open for 36% of the time, Pallas kernels for 0%

commit v1 on v0

v1 whole, which is shorter than its diff:
```python
import functools
import math

import jax
import jax.numpy as jnp
from jax import lax
from jax.experimental import pallas as pl
from jax.experimental.pallas import tpu as pltpu
from jax.sharding import PartitionSpec as P

D = 512
K = 32
ROWS = 128
HALO = 32
BLK = 8
CAP = 2
SELF_WEIGHT = 8.0
SLOT = CAP * BLK
HALO_COL = ROWS
FAR_COL = 2 * ROWS
PLANE = 4

F32 = jnp.float32
BF16 = jnp.bfloat16
VMEM_LIMIT = 48 * 1024 * 1024


def nn(left, right):
    return jnp.dot(left, right, preferred_element_type=F32)


def nt(left, right):
    return lax.dot_general(left, right, (((1,), (1,)), ((), ())), preferred_element_type=F32)


def tn(left, right):
    return lax.dot_general(left, right, (((0,), (0,)), ((), ())), preferred_element_type=F32)


def iota(shape, dim):
    return lax.broadcasted_iota(jnp.int32, shape, dim)


def call(kernel, out_shape, scratch=()):
    return pl.pallas_call(
        kernel,
        out_shape=out_shape,
        scratch_shapes=list(scratch),
        compiler_params=pltpu.CompilerParams(vmem_limit_bytes=VMEM_LIMIT),
    )


def struct(shape, dtype):
    return jax.ShapeDtypeStruct(shape, dtype)


def prepare_kernel(
    count, nbr_ref, wgt_ref, tab_ref, cnt_ref, feat_ref, up_ref,
    mat_ref, own_ref, send_ref, fwd_ref, bwd_ref, rows_scr, at_scr,
):
    device = lax.axis_index("node")
    first = device * ROWS
    far = count * SLOT
    pairs = count * count
    rows_scr[...] = jnp.zeros_like(rows_scr)
    rows_scr[0:CAP, :] = tab_ref[...].astype(F32)
    rows_scr[CAP : CAP + 1, :] = cnt_ref[...].astype(F32)
    step = min(pairs, 256)
    listed = jnp.zeros((far, 8), F32)
    asked = jnp.zeros((far, 8), F32)
    peer_wide = iota((far, step), 0) // SLOT
    for at in range(0, pairs, step):
        pair = iota((far, step), 1) + at
        rows = rows_scr[:, at : at + step].astype(BF16)
        mine = jnp.where(pair == device * count + peer_wide, 1.0, 0.0).astype(BF16)
        theirs = jnp.where(pair == peer_wide * count + device, 1.0, 0.0).astype(BF16)
        listed = listed + nt(mine, rows)
        asked = asked + nt(theirs, rows)
    listed = listed.astype(jnp.int32)
    asked = asked.astype(jnp.int32)
    col = iota((far, 1), 0)
    slot = col // BLK % CAP
    inner = col % BLK
    block = jnp.where(slot == 0, listed[:, 0:1], listed[:, 1:2])
    node = col // SLOT * ROWS + block * BLK + inner
    in_band = (node >= first - HALO) & (node < first + ROWS + HALO)
    far_node = jnp.where((slot < listed[:, 2:3]) & jnp.logical_not(in_band), node, -1)
    asked_row = jnp.where(slot == 0, asked[:, 0:1], asked[:, 1:2]) * BLK + inner

    weight = wgt_ref[...].astype(F32)
    neighbour = nbr_ref[...]

    def counted(nodes, total):
        for k in range(K):
            total = total + jnp.where(neighbour[k : k + 1, :] == nodes, weight[k : k + 1, :], 0.0)
        return total

    square = (ROWS, ROWS)
    row = iota(square, 0)
    at_scr[0:ROWS, :] = counted(first + row, jnp.where(row == iota(square, 1), SELF_WEIGHT, 0.0))
    rim = iota((2 * HALO, ROWS), 0)
    rim_node = first + jnp.where(rim < HALO, rim - HALO, rim - HALO + ROWS)
    at_scr[HALO_COL : HALO_COL + 2 * HALO, :] = counted(rim_node, jnp.zeros((2 * HALO, ROWS), F32))
    at_scr[HALO_COL + 2 * HALO : FAR_COL, :] = jnp.zeros((FAR_COL - HALO_COL - 2 * HALO, ROWS), F32)
    for at in range(0, far, ROWS):
        nodes = jnp.broadcast_to(far_node[at : at + ROWS], square)
        at_scr[FAR_COL + at : FAR_COL + at + ROWS, :] = counted(nodes, jnp.zeros(square, F32))

    adj_mat = at_scr[...]
    matrix = adj_mat.T
    adj_mat = adj_mat.astype(BF16)
    total = jnp.sum(matrix, axis=1, keepdims=True)
    mat_ref[:, 0 : FAR_COL + far] = matrix.astype(BF16)
    pick = jnp.where(asked_row == iota((far, ROWS), 1), 1.0, 0.0)
    mat_ref[:, FAR_COL + far :] = pick.T.astype(BF16)

    scaled = (up_ref[...].astype(F32) / total).astype(BF16)
    features = feat_ref[...]
    own_ref[...] = nn(adj_mat[0:ROWS], scaled)
    rims = nn(adj_mat[HALO_COL : HALO_COL + 2 * HALO], scaled).astype(BF16)
    fwd_ref[0:HALO, :] = features[ROWS - HALO : ROWS]
    fwd_ref[HALO : 2 * HALO, :] = rims[HALO : 2 * HALO]
    bwd_ref[0:HALO, :] = features[0:HALO]
    bwd_ref[HALO : 2 * HALO, :] = rims[0:HALO]
    rows_out = nn(pick.astype(BF16), features).astype(BF16)
    send_ref[:, 0:SLOT, :] = rows_out.reshape(count, SLOT, D)
    terms = nn(adj_mat[FAR_COL:], scaled).astype(BF16)
    send_ref[:, SLOT : 2 * SLOT, :] = terms.reshape(count, SLOT, D)


def row_total(mat_ref, far):
    return jnp.sum(mat_ref[:, 0 : FAR_COL + far].astype(F32), axis=1, keepdims=True)


def layer_kernel(
    count, mat_ref, feat_ref, own_ref, recv_ref, left_ref, right_ref, w_one_ref, w_two_ref,
    *refs,
):
    plane, piece = PLANE, 2 * D // count
    groups = count // plane
    part_refs = refs[:plane]
    d_pre_ref, rim_scr, u_scr, hidden_scr, agg_scr = refs[plane:]
    device = lax.axis_index("node")
    group, place = device // plane, device % plane
    far = count * SLOT
    total = row_total(mat_ref, far)
    rim_scr[0:HALO, :] = left_ref[0:HALO, :]
    rim_scr[HALO : 2 * HALO, :] = right_ref[0:HALO, :]
    rim_scr[2 * HALO :, :] = jnp.zeros((ROWS - 2 * HALO, D), BF16)
    sums = nn(mat_ref[:, 0:ROWS], feat_ref[...])
    sums = sums + nn(mat_ref[:, HALO_COL:FAR_COL], rim_scr[...])
    sums = sums + nn(
        mat_ref[:, FAR_COL : FAR_COL + far], recv_ref[:, 0:SLOT, :].reshape(far, D)
    )
    agg = (sums / total).astype(BF16)
    agg_scr[...] = agg
    u_scr[...] = own_ref[...] + nn(
        mat_ref[:, FAR_COL + far :], recv_ref[:, SLOT : 2 * SLOT, :].reshape(far, D)
    )
    u_scr[0:HALO, :] += left_ref[HALO : 2 * HALO, :].astype(F32)
    u_scr[ROWS - HALO : ROWS, :] += right_ref[HALO : 2 * HALO, :].astype(F32)
    u = u_scr[...].astype(BF16)
    back = nt(u, w_two_ref[...])
    pre = nn(agg, w_one_ref[...])
    square = pre * pre
    bend = jnp.tanh(0.7978845608 * pre * (1.0 + 0.044715 * square))
    hidden_scr[...] = (0.5 * pre * (1.0 + bend)).astype(BF16)
    slope = 0.5 * (1.0 + bend) + 0.5 * pre * (1.0 - bend * bend) * (
        0.7978845608 * (1.0 + 3.0 * 0.044715 * square)
    )
    d_pre = (back * slope).astype(BF16)
    d_pre_ref[...] = d_pre
    wide = D // plane
    for v in range(plane):
        cols = pl.ds(pl.multiple_of((place ^ v) * wide, wide), wide)
        for half, (left, right) in enumerate(((hidden_scr, u), (agg_scr, d_pre))):
            part = tn(left[:, cols], right).astype(part_refs[v].dtype)
            for j in range(groups // 2):
                to = lax.rem(half * (groups // 2) + j + groups - group, groups)
                part_refs[v][pl.ds(pl.multiple_of(to * piece, piece), piece), :] = part[
                    j * piece : (j + 1) * piece
                ]


def back_kernel(count, mat_ref, d_pre_ref, w_one_ref, own_ref, send_ref, fwd_ref, bwd_ref):
    far = count * SLOT
    q = (nt(d_pre_ref[...], w_one_ref[...]) / row_total(mat_ref, far)).astype(BF16)
    own_ref[...] = tn(mat_ref[:, 0:ROWS], q)
    rims = tn(mat_ref[:, HALO_COL:FAR_COL], q).astype(BF16)
    bwd_ref[...] = rims[0:HALO]
    fwd_ref[...] = rims[HALO : 2 * HALO]
    terms = tn(mat_ref[:, FAR_COL : FAR_COL + far], q).astype(BF16)
    send_ref[...] = terms.reshape(count, SLOT, D)


def features_kernel(count, mat_ref, own_ref, recv_ref, left_ref, right_ref, out_ref, sum_scr):
    far = count * SLOT
    sum_scr[...] = own_ref[...] + nn(mat_ref[:, FAR_COL + far :], recv_ref[...].reshape(far, D))
    sum_scr[0:HALO, :] += left_ref[...].astype(F32)
    sum_scr[ROWS - HALO : ROWS, :] += right_ref[...].astype(F32)
    out_ref[...] = sum_scr[...].astype(BF16)


def plane_sum_kernel(piece, *refs):
    part_refs, out_refs = refs[:PLANE], refs[PLANE:]
    for k, out in enumerate(out_refs):
        rows = slice(k * piece, (k + 1) * piece)
        total = part_refs[0][rows, :].astype(F32)
        for ref in part_refs[1:]:
            total = total + ref[rows, :].astype(F32)
        out[...] = total.astype(out.dtype)


def group_sum_kernel(scale, *refs):
    total = refs[0][...]
    for ref in refs[1:-1]:
        total = total + ref[...].astype(F32)
    refs[-1][...] = (total * scale).astype(BF16)


def gather_kernel(count, *refs):
    piece, groups, wide = 2 * D // count, count // PLANE, D // PLANE
    device = lax.axis_index("node")
    group, place = device // PLANE, device % PLANE
    outs = refs[PLANE:]
    per = groups // 2
    for v in range(PLANE):
        row = (place ^ v) * wide
        for half in range(2):
            for j in range(per):
                at = lax.rem(group + 2 * groups - (half * per + j), groups)
                rows = refs[v][pl.ds(pl.multiple_of(at * piece, piece), piece), :]
                outs[half][pl.ds(pl.multiple_of(row + j * piece, piece), piece), :] = rows


def shards(
    features, upstream, weight_one, weight_two, neighbours, edge_weight, fetch_block, fetch_count
):
    count = lax.axis_size("node")
    groups = count // PLANE
    piece = 2 * D // count
    far = count * SLOT
    chain = FAR_COL + far
    up = [(i, i + 1) for i in range(count - 1)]
    down = [(i + 1, i) for i in range(count - 1)]

    def in_plane(value, v):
        return lax.ppermute(value, "node", [(i, i ^ v) for i in range(count)])

    def across(value, k):
        return lax.ppermute(
            value, "node", [(i, (i + k * PLANE) % count) for i in range(count)]
        )

    matrix, own, send, to_right, to_left = call(
        functools.partial(prepare_kernel, count),
        (
            struct((ROWS, chain + far), BF16),
            struct((ROWS, D), F32),
            struct((count, 2 * SLOT, D), BF16),
            struct((2 * HALO, D), BF16),
            struct((2 * HALO, D), BF16),
        ),
        (pltpu.VMEM((8, count * count), F32), pltpu.VMEM((chain, ROWS), F32)),
    )(
        neighbours.T, edge_weight.T, fetch_block.T, fetch_count.reshape(1, -1), features, upstream
    )
    from_left = lax.ppermute(to_right, "node", up)
    from_right = lax.ppermute(to_left, "node", down)
    received = lax.all_to_all(send, "node", split_axis=0, concat_axis=0, tiled=True)

    *parts, d_pre = call(
        functools.partial(layer_kernel, count),
        (
            struct((2 * D // PLANE, D), F32),
            *[struct((2 * D // PLANE, D), BF16)] * (PLANE - 1),
            struct((ROWS, D), BF16),
        ),
        (
            pltpu.VMEM((ROWS, D), BF16),
            pltpu.VMEM((ROWS, D), F32),
            pltpu.VMEM((ROWS, D), BF16),
            pltpu.VMEM((ROWS, D), BF16),
        ),
    )(matrix, features, own, received, from_left, from_right, weight_one, weight_two)
    plane_parts = [parts[0]] + [in_plane(parts[v], v) for v in range(1, PLANE)]

    own, send, to_right, to_left = call(
        functools.partial(back_kernel, count),
        (
            struct((ROWS, D), F32),
            struct((count, SLOT, D), BF16),
            struct((HALO, D), BF16),
            struct((HALO, D), BF16),
        ),
    )(matrix, d_pre, weight_one)
    from_left = lax.ppermute(to_right, "node", up)
    from_right = lax.ppermute(to_left, "node", down)
    received = lax.all_to_all(send, "node", split_axis=0, concat_axis=0, tiled=True)
    d_features = call(
        functools.partial(features_kernel, count),
        struct((ROWS, D), BF16),
        (pltpu.VMEM((ROWS, D), F32),),
    )(matrix, own, received, from_left, from_right)

    sums = call(
        functools.partial(plane_sum_kernel, piece),
        (struct((piece, D), F32), *[struct((piece, D), BF16)] * (groups - 1)),
    )(*plane_parts)
    shared = [sums[0]] + [across(sums[k], k) for k in range(1, groups)]
    total = call(
        functools.partial(group_sum_kernel, 1.0 / math.sqrt(ROWS * count)),
        struct((piece, D), BF16),
    )(*shared)
    chunk = jnp.concatenate([total] + [across(total, k) for k in range(1, groups)], axis=0)
    chunks = [chunk] + [in_plane(chunk, v) for v in range(1, PLANE)]
    grad_two, grad_one = call(
        functools.partial(gather_kernel, count),
        (struct((D, D), BF16), struct((D, D), BF16)),
    )(*chunks)
    return d_features, grad_one, grad_two


def solution(mesh):
    placed = (
        P(("rep", "node"), None),
        P(("rep", "node"), None),
        P(),
        P(),
        P(("rep", "node"), None),
        P(("rep", "node"), None),
        P("rep", None),
        P("rep"),
    )
    return jax.shard_map(
        shards,
        mesh=mesh,
        in_specs=placed,
        out_specs=(P(("rep", "node"), None), P("rep", None), P("rep", None)),
        check_vma=False,
    )
```

time: 311 us -> 86.1 us (0.28)
  other arithmetic: 92.5 us -> 0.02 us
  waiting for transfers between devices: 125 us -> 33 us
  local copies, waits for them, and re-layouts: 21.6 us -> 3.93 us
  between operations: 14.6 us -> 0.77 us
  starting transfers between devices: 48.6 us -> 40.9 us
  matrix products: 7.28 us -> 0 us
  Pallas kernels: 0 us -> 6.86 us
    psum x1 -> x0, waiting for transfers between devices: 108 us -> none  [sum_weight_grad(): return lax.psum(partial_grad, 'node')]
    unnamed x5 -> x0, other arithmetic: 52.4 us -> none
    ppermute x8 -> x16, waiting for transfers between devices: 5.67 us -> 28.5 us  [the longest x6 8.83 us: in_plane(): return lax.ppermute(value, 'node', [(i, i ^ v) for i in range(count)])]
    gather x6 -> x0, local copies, waits for them, and re-layouts: 15.6 us -> none  [the longest x1 10.8 us: edge_tables(): listed = jnp.take(my_table, owner_dev, axis=0)]
    all_to_all x4 -> x2, starting transfers between devices: 26.6 us -> 12 us  [shards(): lax.all_to_all(send, 'node', split_axis=0, concat_axis=0, tiled=True)]
    scatter-add x7 -> x0, other arithmetic: 10.9 us -> none  [the longest x1 7.11 us: edge_tables(): band_matrix = band_matrix.at[local_rows, local_rows + HALO].add(SELF_WEIGHT)]
    select_n x3 -> x0, other arithmetic: 10.1 us -> none  [the longest x1 10.1 us: edge_tables(): jnp.take(my_counts, owner_dev)[..., None]]
    dot_general x12 -> x0, matrix products: 7.28 us -> none  [the longest x2 2.8 us: contract_rows(): lax.dot_general(left, right, (((0,), (0,)), ((), ())), preferred_element_...]
  transfers between devices with their start and end apart: 13 -> 18, of which waited for: 7 -> 10; matrix products, arithmetic and copies ran while one was open for 36% -> 0% of each run, Pallas kernels for 0% -> 3%
where the time goes in v1:
time: 86.1 us; the launch traced here: 85.5 us
  starting transfers between devices  40.9 us (48%)
  waiting for transfers between devices  33 us (38%)
  Pallas kernels  6.86 us (8%)
  local copies, waits for them, and re-layouts  3.93 us (5%)
    ppermute x6, starting transfers between devices, across(): lax.ppermute(value, 'node', [(i, (i + k * PLANE) % count) for i in range(...  12.1 us
    all_to_all x2, starting transfers between devices, shards(): lax.all_to_all(send, 'node', split_axis=0, concat_axis=0, tiled=True)  12 us
    ppermute x6, waiting for transfers between devices, in_plane(): return lax.ppermute(value, 'node', [(i, i ^ v) for i in range(count)])  8.83 us
    ppermute x6, waiting for transfers between devices, across(): lax.ppermute(value, 'node', [(i, (i + k * PLANE) % count) for i in range(...  7.82 us
    ppermute x2, starting transfers between devices, shards(): from_left = lax.ppermute(to_right, 'node', up)  7.18 us
    ppermute x6, starting transfers between devices, in_plane(): return lax.ppermute(value, 'node', [(i, i ^ v) for i in range(count)])  7.11 us
    ppermute x2, waiting for transfers between devices, shards(): from_left = lax.ppermute(to_right, 'node', up)  5.93 us
    ppermute x2, waiting for transfers between devices, shards(): from_right = lax.ppermute(to_left, 'node', down)  5.9 us
  transfers between devices with their start and end apart: 18, of which 10 were waited for; matrix products, arithmetic and copies ran while one was open for 0% of the time, Pallas kernels for 3%

profile of v1, /device:TPU:0, one launch (start us, length us, event | category | flops | bytes accessed | tf_op | source)
XLA Modules:
  0.0 85.5 jit_solution(11198635542711572505)
XLA Ops:
  4.6 2.3 %shard_map.103 = (bf16[128,768]{1,0:T(8,128)(2,1)S(1)}, f32[128,512]{1,0:T(8,128)S(1)}, bf16[16,32,512]{2,1,0:T(8,128)(2,1)}, bf16[64,512]{1,0:T(8,128)(2,1)S(1)}, bf16[64,512]{1,0:T(8,128)(2,1)S(1)}) custom-call(s32[32,128]{1,0:T(8,128)S(1)} %bitcast.4, s32[32,128]{1,0:T(8,128)S(1)} %bitcast.5, s32[2,256]{1,0:T(2,128)S(1)} %bitcast.6, ...), custom_call_target="tpu_custom_call" | custom-call | tf_op jit(solution)/shard_map/pallas_call | solution.py:255
  6.9 8.4 %all-to-all-start = ((bf16[16,32,512]{2,1,0:T(8,128)(2,1)}), bf16[16,32,512]{2,1,0:T(8,128)(2,1)S(1)}, u32[]{:S(2)}, u32[]{:S(2)}) async-start(bf16[16,32,512]{2,1,0:T(8,128)(2,1)} %get-tuple-element.25), calls=%async_computation | async-start | bytes 1048576 | tf_op jit(solution)/shard_map/all_to_all | solution.py:270
  15.4 3.8 %collective-permute-start = (bf16[64,512]{1,0:T(8,128)(2,1)S(1)}, bf16[64,512]{1,0:T(8,128)(2,1)S(1)}, u32[]{:S(2)}, u32[]{:S(2)}) collective-permute-start(bf16[64,512]{1,0:T(8,128)(2,1)S(1)} %get-tuple-element.26), channel_id=1, source_target_pairs={{0,2},{2,4},{4,6},{6,8},{8,10},{10,12},{12,14},{14,16},{16,18},{18... | collective-permute-start | bytes 196616 | tf_op jit(solution)/shard_map/ppermute | solution.py:268
  19.2 1.3 %collective-permute-start.1 = (bf16[64,512]{1,0:T(8,128)(2,1)S(1)}, bf16[64,512]{1,0:T(8,128)(2,1)S(1)}, u32[]{:S(2)}, u32[]{:S(2)}) collective-permute-start(bf16[64,512]{1,0:T(8,128)(2,1)S(1)} %get-tuple-element.27), channel_id=1, source_target_pairs={{2,0},{4,2},{6,4},{8,6},{10,8},{12,10},{14,12},{16,14},{18,16},{20... | collective-permute-start | bytes 196616 | tf_op jit(solution)/shard_map/ppermute | solution.py:269
  21.1 4.9 %collective-permute-done.1.right_ref = bf16[64,512]{1,0:T(8,128)(2,1)S(1)} collective-permute-done((bf16[64,512]{1,0:T(8,128)(2,1)S(1)}, bf16[64,512]{1,0:T(8,128)(2,1)S(1)}, u32[]{:S(2)}, u32[]{:S(2)}) %collective-permute-start.1) | collective-permute-done | bytes 65568 | tf_op jit(solution)/shard_map/ppermute | solution.py:269
  26.0 4.5 %all-to-all-done.recv_ref = bf16[16,32,512]{2,1,0:T(8,128)(2,1)S(1)} async-done(((bf16[16,32,512]{2,1,0:T(8,128)(2,1)}), bf16[16,32,512]{2,1,0:T(8,128)(2,1)S(1)}, u32[]{:S(2)}, u32[]{:S(2)}) %all-to-all-start) | async-done | bytes 524320 | tf_op jit(solution)/shard_map/all_to_all | solution.py:270
  30.5 1.2 %shard_map.104 = (f32[256,512]{1,0:T(8,128)S(1)}, bf16[256,512]{1,0:T(8,128)(2,1)S(1)}, bf16[256,512]{1,0:T(8,128)(2,1)S(1)}, bf16[256,512]{1,0:T(8,128)(2,1)S(1)}, bf16[128,512]{1,0:T(8,128)(2,1)S(1)}) custom-call(bf16[128,768]{1,0:T(8,128)(2,1)S(1)} %get-tuple-element.23.mat_ref, bf16[128,512]{1,0:T(8,128)(2,1)S(1)} %copy-done.2, ...), custom_call_target="tpu_custom_call" | custom-call | tf_op jit(solution)/shard_map/pallas_call | solution.py:272
  32.3 1.3 %collective-permute-start.5 = (bf16[256,512]{1,0:T(8,128)(2,1)S(1)}, bf16[256,512]{1,0:T(8,128)(2,1)S(1)}, u32[]{:S(2)}, u32[]{:S(2)}) collective-permute-start(bf16[256,512]{1,0:T(8,128)(2,1)S(1)} %get-tuple-element.35), channel_id=1, source_target_pairs={{0,4},{2,6},{4,0},{6,2},{8,12},{10,14},{12,8},{14,10},{16,20},{18,... | collective-permute-start | bytes 786440 | tf_op jit(solution)/shard_map/ppermute | solution.py:248
  33.6 1.7 %collective-permute-start.6 = (bf16[256,512]{1,0:T(8,128)(2,1)S(1)}, bf16[256,512]{1,0:T(8,128)(2,1)S(1)}, u32[]{:S(2)}, u32[]{:S(2)}) collective-permute-start(bf16[256,512]{1,0:T(8,128)(2,1)S(1)} %get-tuple-element.36), channel_id=1, source_target_pairs={{0,6},{2,4},{4,2},{6,0},{8,14},{10,12},{12,10},{14,8},{16,22},{18,... | collective-permute-start | bytes 786440 | tf_op jit(solution)/shard_map/ppermute | solution.py:248
  35.3 4.3 %collective-permute-done.4.refs_1_ = bf16[256,512]{1,0:T(8,128)(2,1)S(1)} collective-permute-done((bf16[256,512]{1,0:T(8,128)(2,1)S(1)}, bf16[256,512]{1,0:T(8,128)(2,1)S(1)}, u32[]{:S(2)}, u32[]{:S(2)}) %collective-permute-start.4) | collective-permute-done | bytes 262176 | tf_op jit(solution)/shard_map/ppermute | solution.py:248
  39.5 2.8 %collective-permute-done.5.refs_2_ = bf16[256,512]{1,0:T(8,128)(2,1)S(1)} collective-permute-done((bf16[256,512]{1,0:T(8,128)(2,1)S(1)}, bf16[256,512]{1,0:T(8,128)(2,1)S(1)}, u32[]{:S(2)}, u32[]{:S(2)}) %collective-permute-start.5) | collective-permute-done | bytes 262176 | tf_op jit(solution)/shard_map/ppermute | solution.py:248
  42.3 1.8 %collective-permute-done.6.refs_3_ = bf16[256,512]{1,0:T(8,128)(2,1)S(1)} collective-permute-done((bf16[256,512]{1,0:T(8,128)(2,1)S(1)}, bf16[256,512]{1,0:T(8,128)(2,1)S(1)}, u32[]{:S(2)}, u32[]{:S(2)}) %collective-permute-start.6) | collective-permute-done | bytes 262176 | tf_op jit(solution)/shard_map/ppermute | solution.py:248
  44.2 2.5 %collective-permute-start.7 = (bf16[64,512]{1,0:T(8,128)(2,1)S(1)}, bf16[64,512]{1,0:T(8,128)(2,1)S(1)}, u32[]{:S(2)}, u32[]{:S(2)}) collective-permute-start(bf16[64,512]{1,0:T(8,128)(2,1)S(1)} %get-tuple-element.38), channel_id=1, source_target_pairs={{0,8},{2,10},{4,12},{6,14},{8,16},{10,18},{12,20},{14,22},{16,24},... | collective-permute-start | bytes 196616 | tf_op jit(solution)/shard_map/ppermute | solution.py:251
  46.7 1.9 %collective-permute-start.8 = (bf16[64,512]{1,0:T(8,128)(2,1)S(1)}, bf16[64,512]{1,0:T(8,128)(2,1)S(1)}, u32[]{:S(2)}, u32[]{:S(2)}) collective-permute-start(bf16[64,512]{1,0:T(8,128)(2,1)S(1)} %get-tuple-element.39), channel_id=1, source_target_pairs={{0,16},{2,18},{4,20},{6,22},{8,24},{10,26},{12,28},{14,30},{16,0},... | collective-permute-start | bytes 196616 | tf_op jit(solution)/shard_map/ppermute | solution.py:251
  48.6 2.8 %collective-permute-start.9 = (bf16[64,512]{1,0:T(8,128)(2,1)S(1)}, bf16[64,512]{1,0:T(8,128)(2,1)S(1)}, u32[]{:S(2)}, u32[]{:S(2)}) collective-permute-start(bf16[64,512]{1,0:T(8,128)(2,1)S(1)} %get-tuple-element.40), channel_id=1, source_target_pairs={{0,24},{2,26},{4,28},{6,30},{8,0},{10,2},{12,4},{14,6},{16,8},{18,... | collective-permute-start | bytes 196616 | tf_op jit(solution)/shard_map/ppermute | solution.py:251
  51.4 1.3 %shard_map.105 = (f32[128,512]{1,0:T(8,128)S(1)}, bf16[16,16,512]{2,1,0:T(8,128)(2,1)}, bf16[32,512]{1,0:T(8,128)(2,1)S(1)}, bf16[32,512]{1,0:T(8,128)(2,1)S(1)}) custom-call(bf16[128,768]{1,0:T(8,128)(2,1)S(1)} %get-tuple-element.23.mat_ref, bf16[128,512]{1,0:T(8,128)(2,1)S(1)} %get-tuple-element.28.d_pre_ref, bf16[512,512]{1,0:T(8,128)(2,1)S(1)} %copy-done), custom_call_target="tpu_custom_call" | custom-call | tf_op jit(solution)/shard_map/pallas_call | solution.py:288
  52.7 3.5 %all-to-all-start.1 = ((bf16[16,16,512]{2,1,0:T(8,128)(2,1)}), bf16[16,16,512]{2,1,0:T(8,128)(2,1)S(1)}, u32[]{:S(2)}, u32[]{:S(2)}) async-start(bf16[16,16,512]{2,1,0:T(8,128)(2,1)} %get-tuple-element.30), calls=%async_computation.1 | async-start | bytes 524288 | tf_op jit(solution)/shard_map/all_to_all | solution.py:299
  56.3 3.7 %collective-permute-start.12 = (bf16[64,512]{1,0:T(8,128)(2,1)S(1)}, bf16[64,512]{1,0:T(8,128)(2,1)S(1)}, u32[]{:S(2)}, u32[]{:S(2)}) collective-permute-start(bf16[64,512]{1,0:T(8,128)(2,1)S(1)} %shard_map.108), channel_id=1, source_target_pairs={{0,24},{2,26},{4,28},{6,30},{8,0},{10,2},{12,4},{14,6},{16,8},{18,... | collective-permute-start | bytes 196616 | tf_op jit(solution)/shard_map/ppermute | solution.py:251
  61.1 1.2 %collective-permute-done.12 = bf16[64,512]{1,0:T(8,128)(2,1)S(1)} collective-permute-done((bf16[64,512]{1,0:T(8,128)(2,1)S(1)}, bf16[64,512]{1,0:T(8,128)(2,1)S(1)}, u32[]{:S(2)}, u32[]{:S(2)}) %collective-permute-start.12) | collective-permute-done | bytes 65568 | tf_op jit(solution)/shard_map/ppermute | solution.py:251
  62.4 6.6 %collective-permute-done.11 = bf16[64,512]{1,0:T(8,128)(2,1)S(1)} collective-permute-done((bf16[64,512]{1,0:T(8,128)(2,1)S(1)}, bf16[64,512]{1,0:T(8,128)(2,1)S(1)}, u32[]{:S(2)}, u32[]{:S(2)}) %collective-permute-start.11) | collective-permute-done | bytes 65568 | tf_op jit(solution)/shard_map/ppermute | solution.py:251
  69.0 2.4 %collective-permute-start.15 = (bf16[256,512]{1,0:T(8,128)(2,1)S(1)}, bf16[256,512]{1,0:T(8,128)(2,1)S(1)}, u32[]{:S(2)}, u32[]{:S(2)}) collective-permute-start(bf16[256,512]{1,0:T(8,128)(2,1)S(1)} %pad_maximum_fusion.refs_0_), channel_id=1, source_target_pairs={{0,6},{2,4},{4,2},{6,0},{8,14},{10,12},{12,10},{14,8},{16,22},{18,... | collective-permute-start | bytes 786440 | tf_op jit(solution)/shard_map/ppermute | solution.py:248
  72.5 3.4 %collective-permute-start.2 = (bf16[32,512]{1,0:T(8,128)(2,1)S(1)}, bf16[32,512]{1,0:T(8,128)(2,1)S(1)}, u32[]{:S(2)}, u32[]{:S(2)}) collective-permute-start(bf16[32,512]{1,0:T(8,128)(2,1)S(1)} %get-tuple-element.31), channel_id=1, source_target_pairs={{0,2},{2,4},{4,6},{6,8},{8,10},{10,12},{12,14},{14,16},{16,18},{18... | collective-permute-start | bytes 98312 | tf_op jit(solution)/shard_map/ppermute | solution.py:297
  75.9 1.3 %collective-permute-start.3 = (bf16[32,512]{1,0:T(8,128)(2,1)S(1)}, bf16[32,512]{1,0:T(8,128)(2,1)S(1)}, u32[]{:S(2)}, u32[]{:S(2)}) collective-permute-start(bf16[32,512]{1,0:T(8,128)(2,1)S(1)} %get-tuple-element.32), channel_id=1, source_target_pairs={{2,0},{4,2},{6,4},{8,6},{10,8},{12,10},{14,12},{16,14},{18,16},{20... | collective-permute-start | bytes 98312 | tf_op jit(solution)/shard_map/ppermute | solution.py:298
  77.2 5.3 %collective-permute-done.2.left_ref = bf16[32,512]{1,0:T(8,128)(2,1)S(1)} collective-permute-done((bf16[32,512]{1,0:T(8,128)(2,1)S(1)}, bf16[32,512]{1,0:T(8,128)(2,1)S(1)}, u32[]{:S(2)}, u32[]{:S(2)}) %collective-permute-start.2) | collective-permute-done | bytes 32800 | tf_op jit(solution)/shard_map/ppermute | solution.py:297
  (38 shorter events, 10.5 us)
Async XLA Ops:
  1.3 0.9 %copy-start.1 = (bf16[128,512]{1,0:T(8,128)(2,1)S(1)}, bf16[128,512]{1,0:T(8,128)(2,1)}, u32[]{:S(2)}) copy-start(bf16[128,512]{1,0:T(8,128)(2,1)} %feat_ref.3) | copy-start | bytes 393220
  2.2 0.9 %copy-start.4 = (bf16[128,512]{1,0:T(8,128)(2,1)S(1)}, bf16[128,512]{1,0:T(8,128)(2,1)}, u32[]{:S(2)}) copy-start(bf16[128,512]{1,0:T(8,128)(2,1)} %up_ref.1) | copy-start | bytes 393220
  3.1 0.7 copy-start.5
  4.6 25.9 %copy-start.3 = (bf16[512,512]{1,0:T(8,128)(2,1)S(1)}, bf16[512,512]{1,0:T(8,128)(2,1)}, u32[]{:S(2)}) copy-start(bf16[512,512]{1,0:T(8,128)(2,1)} %w_two_ref.1) | copy-start | bytes 1572868
  6.9 23.6 %copy-start = (bf16[512,512]{1,0:T(8,128)(2,1)S(1)}, bf16[512,512]{1,0:T(8,128)(2,1)}, u32[]{:S(2)}) copy-start(bf16[512,512]{1,0:T(8,128)(2,1)} %w_one_ref.3) | copy-start | bytes 1572868
  6.9 23.6 %copy-start.2 = (bf16[128,512]{1,0:T(8,128)(2,1)S(1)}, bf16[128,512]{1,0:T(8,128)(2,1)}, u32[]{:S(2)}) copy-start(bf16[128,512]{1,0:T(8,128)(2,1)} %feat_ref.3) | copy-start | bytes 393220
  6.9 23.6 %all-to-all-start = ((bf16[16,32,512]{2,1,0:T(8,128)(2,1)}), bf16[16,32,512]{2,1,0:T(8,128)(2,1)S(1)}, u32[]{:S(2)}, u32[]{:S(2)}) async-start(bf16[16,32,512]{2,1,0:T(8,128)(2,1)} %get-tuple-element.25), calls=%async_computation | async-start | bytes 1048576 | tf_op jit(solution)/shard_map/all_to_all | solution.py:270
  15.4 5.7 %collective-permute-start = (bf16[64,512]{1,0:T(8,128)(2,1)S(1)}, bf16[64,512]{1,0:T(8,128)(2,1)S(1)}, u32[]{:S(2)}, u32[]{:S(2)}) collective-permute-start(bf16[64,512]{1,0:T(8,128)(2,1)S(1)} %get-tuple-element.26), channel_id=1, source_target_pairs={{0,2},{2,4},{4,6},{6,8},{8,10},{10,12},{12,14},{14,16},{16,18},{18... | collective-permute-start | bytes 196616 | tf_op jit(solution)/shard_map/ppermute | solution.py:268
  19.2 6.8 %collective-permute-start.1 = (bf16[64,512]{1,0:T(8,128)(2,1)S(1)}, bf16[64,512]{1,0:T(8,128)(2,1)S(1)}, u32[]{:S(2)}, u32[]{:S(2)}) collective-permute-start(bf16[64,512]{1,0:T(8,128)(2,1)S(1)} %get-tuple-element.27), channel_id=1, source_target_pairs={{2,0},{4,2},{6,4},{8,6},{10,8},{12,10},{14,12},{16,14},{18,16},{20... | collective-permute-start | bytes 196616 | tf_op jit(solution)/shard_map/ppermute | solution.py:269
  31.7 7.8 %collective-permute-start.4 = (bf16[256,512]{1,0:T(8,128)(2,1)S(1)}, bf16[256,512]{1,0:T(8,128)(2,1)S(1)}, u32[]{:S(2)}, u32[]{:S(2)}) collective-permute-start(bf16[256,512]{1,0:T(8,128)(2,1)S(1)} %get-tuple-element.34), channel_id=1, source_target_pairs={{0,2},{2,0},{4,6},{6,4},{8,10},{10,8},{12,14},{14,12},{16,18},{18,... | collective-permute-start | bytes 786440 | tf_op jit(solution)/shard_map/ppermute | solution.py:248
  32.3 10.0 %collective-permute-start.5 = (bf16[256,512]{1,0:T(8,128)(2,1)S(1)}, bf16[256,512]{1,0:T(8,128)(2,1)S(1)}, u32[]{:S(2)}, u32[]{:S(2)}) collective-permute-start(bf16[256,512]{1,0:T(8,128)(2,1)S(1)} %get-tuple-element.35), channel_id=1, source_target_pairs={{0,4},{2,6},{4,0},{6,2},{8,12},{10,14},{12,8},{14,10},{16,20},{18,... | collective-permute-start | bytes 786440 | tf_op jit(solution)/shard_map/ppermute | solution.py:248
  33.6 10.5 %collective-permute-start.6 = (bf16[256,512]{1,0:T(8,128)(2,1)S(1)}, bf16[256,512]{1,0:T(8,128)(2,1)S(1)}, u32[]{:S(2)}, u32[]{:S(2)}) collective-permute-start(bf16[256,512]{1,0:T(8,128)(2,1)S(1)} %get-tuple-element.36), channel_id=1, source_target_pairs={{0,6},{2,4},{4,2},{6,0},{8,14},{10,12},{12,10},{14,8},{16,22},{18,... | collective-permute-start | bytes 786440 | tf_op jit(solution)/shard_map/ppermute | solution.py:248
  44.2 12.0 %collective-permute-start.7 = (bf16[64,512]{1,0:T(8,128)(2,1)S(1)}, bf16[64,512]{1,0:T(8,128)(2,1)S(1)}, u32[]{:S(2)}, u32[]{:S(2)}) collective-permute-start(bf16[64,512]{1,0:T(8,128)(2,1)S(1)} %get-tuple-element.38), channel_id=1, source_target_pairs={{0,8},{2,10},{4,12},{6,14},{8,16},{10,18},{12,20},{14,22},{16,24},... | collective-permute-start | bytes 196616 | tf_op jit(solution)/shard_map/ppermute | solution.py:251
  46.7 9.6 %collective-permute-start.8 = (bf16[64,512]{1,0:T(8,128)(2,1)S(1)}, bf16[64,512]{1,0:T(8,128)(2,1)S(1)}, u32[]{:S(2)}, u32[]{:S(2)}) collective-permute-start(bf16[64,512]{1,0:T(8,128)(2,1)S(1)} %get-tuple-element.39), channel_id=1, source_target_pairs={{0,16},{2,18},{4,20},{6,22},{8,24},{10,26},{12,28},{14,30},{16,0},... | collective-permute-start | bytes 196616 | tf_op jit(solution)/shard_map/ppermute | solution.py:251
  48.6 7.7 %collective-permute-start.9 = (bf16[64,512]{1,0:T(8,128)(2,1)S(1)}, bf16[64,512]{1,0:T(8,128)(2,1)S(1)}, u32[]{:S(2)}, u32[]{:S(2)}) collective-permute-start(bf16[64,512]{1,0:T(8,128)(2,1)S(1)} %get-tuple-element.40), channel_id=1, source_target_pairs={{0,24},{2,26},{4,28},{6,30},{8,0},{10,2},{12,4},{14,6},{16,8},{18,... | collective-permute-start | bytes 196616 | tf_op jit(solution)/shard_map/ppermute | solution.py:251
  52.7 30.9 %all-to-all-start.1 = ((bf16[16,16,512]{2,1,0:T(8,128)(2,1)}), bf16[16,16,512]{2,1,0:T(8,128)(2,1)S(1)}, u32[]{:S(2)}, u32[]{:S(2)}) async-start(bf16[16,16,512]{2,1,0:T(8,128)(2,1)} %get-tuple-element.30), calls=%async_computation.1 | async-start | bytes 524288 | tf_op jit(solution)/shard_map/all_to_all | solution.py:299
  56.3 6.1 %collective-permute-start.12 = (bf16[64,512]{1,0:T(8,128)(2,1)S(1)}, bf16[64,512]{1,0:T(8,128)(2,1)S(1)}, u32[]{:S(2)}, u32[]{:S(2)}) collective-permute-start(bf16[64,512]{1,0:T(8,128)(2,1)S(1)} %shard_map.108), channel_id=1, source_target_pairs={{0,24},{2,26},{4,28},{6,30},{8,0},{10,2},{12,4},{14,6},{16,8},{18,... | collective-permute-start | bytes 196616 | tf_op jit(solution)/shard_map/ppermute | solution.py:251
  60.0 8.9 %collective-permute-start.11 = (bf16[64,512]{1,0:T(8,128)(2,1)S(1)}, bf16[64,512]{1,0:T(8,128)(2,1)S(1)}, u32[]{:S(2)}, u32[]{:S(2)}) collective-permute-start(bf16[64,512]{1,0:T(8,128)(2,1)S(1)} %shard_map.108), channel_id=1, source_target_pairs={{0,16},{2,18},{4,20},{6,22},{8,24},{10,26},{12,28},{14,30},{16,0},... | collective-permute-start | bytes 196616 | tf_op jit(solution)/shard_map/ppermute | solution.py:251
  60.0 8.9 %collective-permute-start.10 = (bf16[64,512]{1,0:T(8,128)(2,1)S(1)}, bf16[64,512]{1,0:T(8,128)(2,1)S(1)}, u32[]{:S(2)}, u32[]{:S(2)}) collective-permute-start(bf16[64,512]{1,0:T(8,128)(2,1)S(1)} %shard_map.108), channel_id=1, source_target_pairs={{0,8},{2,10},{4,12},{6,14},{8,16},{10,18},{12,20},{14,22},{16,24},... | collective-permute-start | bytes 196616 | tf_op jit(solution)/shard_map/ppermute | solution.py:251
  69.0 15.4 %collective-permute-start.15 = (bf16[256,512]{1,0:T(8,128)(2,1)S(1)}, bf16[256,512]{1,0:T(8,128)(2,1)S(1)}, u32[]{:S(2)}, u32[]{:S(2)}) collective-permute-start(bf16[256,512]{1,0:T(8,128)(2,1)S(1)} %pad_maximum_fusion.refs_0_), channel_id=1, source_target_pairs={{0,6},{2,4},{4,2},{6,0},{8,14},{10,12},{12,10},{14,8},{16,22},{18,... | collective-permute-start | bytes 786440 | tf_op jit(solution)/shard_map/ppermute | solution.py:248
  71.4 13.0 %collective-permute-start.14 = (bf16[256,512]{1,0:T(8,128)(2,1)S(1)}, bf16[256,512]{1,0:T(8,128)(2,1)S(1)}, u32[]{:S(2)}, u32[]{:S(2)}) collective-permute-start(bf16[256,512]{1,0:T(8,128)(2,1)S(1)} %pad_maximum_fusion.refs_0_), channel_id=1, source_target_pairs={{0,4},{2,6},{4,0},{6,2},{8,12},{10,14},{12,8},{14,10},{16,20},{18,... | collective-permute-start | bytes 786440 | tf_op jit(solution)/shard_map/ppermute | solution.py:248
  72.0 12.4 %collective-permute-start.13 = (bf16[256,512]{1,0:T(8,128)(2,1)S(1)}, bf16[256,512]{1,0:T(8,128)(2,1)S(1)}, u32[]{:S(2)}, u32[]{:S(2)}) collective-permute-start(bf16[256,512]{1,0:T(8,128)(2,1)S(1)} %pad_maximum_fusion.refs_0_), channel_id=1, source_target_pairs={{0,2},{2,0},{4,6},{6,4},{8,10},{10,8},{12,14},{14,12},{16,18},{18,... | collective-permute-start | bytes 786440 | tf_op jit(solution)/shard_map/ppermute | solution.py:248
  72.5 10.0 %collective-permute-start.2 = (bf16[32,512]{1,0:T(8,128)(2,1)S(1)}, bf16[32,512]{1,0:T(8,128)(2,1)S(1)}, u32[]{:S(2)}, u32[]{:S(2)}) collective-permute-start(bf16[32,512]{1,0:T(8,128)(2,1)S(1)} %get-tuple-element.31), channel_id=1, source_target_pairs={{0,2},{2,4},{4,6},{6,8},{8,10},{10,12},{12,14},{14,16},{16,18},{18... | collective-permute-start | bytes 98312 | tf_op jit(solution)/shard_map/ppermute | solution.py:297
  75.9 7.6 %collective-permute-start.3 = (bf16[32,512]{1,0:T(8,128)(2,1)S(1)}, bf16[32,512]{1,0:T(8,128)(2,1)S(1)}, u32[]{:S(2)}, u32[]{:S(2)}) collective-permute-start(bf16[32,512]{1,0:T(8,128)(2,1)S(1)} %get-tuple-element.32), channel_id=1, source_target_pairs={{2,0},{4,2},{6,4},{8,6},{10,8},{12,10},{14,12},{16,14},{18,16},{20... | collective-permute-start | bytes 98312 | tf_op jit(solution)/shard_map/ppermute | solution.py:298
  (3 other events, 2.1 us)

commit v2 on v1

--- a/solution.py
+++ b/solution.py
@@ -41,10 +41,11 @@
     return lax.broadcasted_iota(jnp.int32, shape, dim)
 
 
-def call(kernel, out_shape, scratch=()):
+def call(kernel, out_shape, scratch=(), **specs):
     return pl.pallas_call(
         kernel,
         out_shape=out_shape,
+        **specs,
         scratch_shapes=list(scratch),
         compiler_params=pltpu.CompilerParams(vmem_limit_bytes=VMEM_LIMIT),
     )
@@ -55,9 +56,21 @@
 
 
 def prepare_kernel(
-    count, nbr_ref, wgt_ref, tab_ref, cnt_ref, feat_ref, up_ref,
-    mat_ref, own_ref, send_ref, fwd_ref, bwd_ref, rows_scr, at_scr,
+    count, nbr_hbm, wgt_hbm, tab_hbm, cnt_hbm, feat_hbm, up_hbm,
+    mat_ref, own_ref, send_ref, fwd_ref, bwd_ref,
+    nbr_ref, wgt_ref, tab_ref, cnt_ref, feat_ref, up_ref, sems, rows_scr, at_scr,
 ):
+    inputs = (
+        (tab_hbm, tab_ref), (cnt_hbm, cnt_ref), (nbr_hbm, nbr_ref),
+        (wgt_hbm, wgt_ref), (up_hbm, up_ref), (feat_hbm, feat_ref),
+    )
+    copies = [
+        pltpu.make_async_copy(src, dst, sems.at[i]) for i, (src, dst) in enumerate(inputs)
+    ]
+    for copy in copies:
+        copy.start()
+    copies[0].wait()
+    copies[1].wait()
     device = lax.axis_index("node")
     first = device * ROWS
     far = count * SLOT
@@ -87,6 +100,8 @@
     far_node = jnp.where((slot < listed[:, 2:3]) & jnp.logical_not(in_band), node, -1)
     asked_row = jnp.where(slot == 0, asked[:, 0:1], asked[:, 1:2]) * BLK + inner
 
+    copies[2].wait()
+    copies[3].wait()
     weight = wgt_ref[...].astype(F32)
     neighbour = nbr_ref[...]
 
@@ -114,7 +129,9 @@
     pick = jnp.where(asked_row == iota((far, ROWS), 1), 1.0, 0.0)
     mat_ref[:, FAR_COL + far :] = pick.T.astype(BF16)
 
+    copies[4].wait()
     scaled = (up_ref[...].astype(F32) / total).astype(BF16)
+    copies[5].wait()
     features = feat_ref[...]
     own_ref[...] = nn(adj_mat[0:ROWS], scaled)
     rims = nn(adj_mat[HALO_COL : HALO_COL + 2 * HALO], scaled).astype(BF16)
@@ -182,22 +199,67 @@
                 ]
 
 
-def back_kernel(count, mat_ref, d_pre_ref, w_one_ref, own_ref, send_ref, fwd_ref, bwd_ref):
+def back_kernel(count, mat_ref, d_pre_ref, w_one_ref, own_ref, *refs):
+    groups = count // PLANE
+    across_refs, (left_ref, right_ref, block_scr) = refs[:groups], refs[groups:]
+    device = lax.axis_index("node")
+    group, place = device // PLANE, device % PLANE
     far = count * SLOT
     q = (nt(d_pre_ref[...], w_one_ref[...]) / row_total(mat_ref, far)).astype(BF16)
     own_ref[...] = tn(mat_ref[:, 0:ROWS], q)
     rims = tn(mat_ref[:, HALO_COL:FAR_COL], q).astype(BF16)
-    bwd_ref[...] = rims[0:HALO]
-    fwd_ref[...] = rims[HALO : 2 * HALO]
-    terms = tn(mat_ref[:, FAR_COL : FAR_COL + far], q).astype(BF16)
-    send_ref[...] = terms.reshape(count, SLOT, D)
-
-
-def features_kernel(count, mat_ref, own_ref, recv_ref, left_ref, right_ref, out_ref, sum_scr):
+    left_ref[...] = rims[0:HALO]
+    right_ref[...] = rims[HALO : 2 * HALO]
+    terms = tn(mat_ref[:, FAR_COL : FAR_COL + far], q).astype(BF16).reshape(count, SLOT, D)
+    for peer in range(count):
+        k = lax.rem(peer // PLANE + groups - group, groups)
+        block_scr[k * PLANE + ((peer % PLANE) ^ place)] = terms[peer]
+    size = PLANE * SLOT
+    for k, ref in enumerate(across_refs):
+        ref[0:size, :] = block_scr[k * PLANE : (k + 1) * PLANE].reshape(size, D)
+        if k == 1:
+            ref[size:, :] = rims[HALO : 2 * HALO]
+        if k == groups - 1:
+            ref[size:, :] = rims[0:HALO]
+
+
+def turn_kernel(count, *refs):
+    groups = count // PLANE
+    across_refs, (left_ref, right_ref), plane_refs = (
+        refs[:groups], refs[groups : groups + 2], refs[groups + 2 :],
+    )
+    place = lax.axis_index("node") % PLANE
+    size = groups * SLOT
+    for v, ref in enumerate(plane_refs):
+        for k in range(groups):
+            ref[k * SLOT : (k + 1) * SLOT, :] = across_refs[k][v * SLOT : (v + 1) * SLOT, :]
+    left, right = left_ref[...], right_ref[...]
+    from_below = across_refs[1][PLANE * SLOT :, :]
+    from_above = across_refs[groups - 1][PLANE * SLOT :, :]
+    plane_refs[1][size:, :] = jnp.where(place % 2 == 0, right, left)
+    plane_refs[3][size:, :] = jnp.where(
+        place == 0,
+        from_above,
+        jnp.where(place == 1, right, jnp.where(place == 2, left, from_below)),
+    )
+
+
+def features_kernel(count, mat_ref, own_ref, *refs):
+    plane_refs, (out_ref, sum_scr, block_scr) = refs[:PLANE], refs[PLANE:]
+    groups = count // PLANE
+    device = lax.axis_index("node")
+    group, place = device // PLANE, device % PLANE
     far = count * SLOT
-    sum_scr[...] = own_ref[...] + nn(mat_ref[:, FAR_COL + far :], recv_ref[...].reshape(far, D))
-    sum_scr[0:HALO, :] += left_ref[...].astype(F32)
-    sum_scr[ROWS - HALO : ROWS, :] += right_ref[...].astype(F32)
+    size = groups * SLOT
+    for v, ref in enumerate(plane_refs):
+        for k in range(groups):
+            peer = lax.rem(group + groups - k, groups) * PLANE + (place ^ v)
+            block_scr[peer] = ref[k * SLOT : (k + 1) * SLOT, :]
+    sum_scr[...] = own_ref[...] + nn(mat_ref[:, FAR_COL + far :], block_scr[...].reshape(far, D))
+    one, three = plane_refs[1][size:, :].astype(F32), plane_refs[3][size:, :].astype(F32)
+    even = place % 2 == 0
+    sum_scr[0:HALO, :] += jnp.where(even, three, one)
+    sum_scr[ROWS - HALO : ROWS, :] += jnp.where(even, one, three)
     out_ref[...] = sum_scr[...].astype(BF16)
 
 
@@ -261,7 +323,18 @@
             struct((2 * HALO, D), BF16),
             struct((2 * HALO, D), BF16),
         ),
-        (pltpu.VMEM((8, count * count), F32), pltpu.VMEM((chain, ROWS), F32)),
+        (
+            pltpu.VMEM((K, ROWS), jnp.int32),
+            pltpu.VMEM((K, ROWS), jnp.int32),
+            pltpu.VMEM((CAP, count * count), jnp.int32),
+            pltpu.VMEM((1, count * count), jnp.int32),
+            pltpu.VMEM((ROWS, D), BF16),
+            pltpu.VMEM((ROWS, D), BF16),
+            pltpu.SemaphoreType.DMA((6,)),
+            pltpu.VMEM((8, count * count), F32),
+            pltpu.VMEM((chain, ROWS), F32),
+        ),
+        in_specs=[pl.BlockSpec(memory_space=pl.ANY)] * 6,
     )(
         neighbours.T, edge_weight.T, fetch_block.T, fetch_count.reshape(1, -1), features, upstream
     )
@@ -285,33 +358,42 @@
     )(matrix, features, own, received, from_left, from_right, weight_one, weight_two)
     plane_parts = [parts[0]] + [in_plane(parts[v], v) for v in range(1, PLANE)]
 
-    own, send, to_right, to_left = call(
+    across_rows = [PLANE * SLOT + HALO * (k in (1, groups - 1)) for k in range(groups)]
+    plane_rows = [groups * SLOT + HALO * (v in (1, 3)) for v in range(PLANE)]
+    own, *blocks, to_left, to_right = call(
         functools.partial(back_kernel, count),
         (
             struct((ROWS, D), F32),
-            struct((count, SLOT, D), BF16),
+            *[struct((rows, D), BF16) for rows in across_rows],
             struct((HALO, D), BF16),
             struct((HALO, D), BF16),
         ),
+        (pltpu.VMEM((count, SLOT, D), BF16),),
     )(matrix, d_pre, weight_one)
-    from_left = lax.ppermute(to_right, "node", up)
-    from_right = lax.ppermute(to_left, "node", down)
-    received = lax.all_to_all(send, "node", split_axis=0, concat_axis=0, tiled=True)
-    d_features = call(
-        functools.partial(features_kernel, count),
-        struct((ROWS, D), BF16),
-        (pltpu.VMEM((ROWS, D), F32),),
-    )(matrix, own, received, from_left, from_right)
+    blocks = [blocks[0]] + [across(blocks[k], k) for k in range(1, groups)]
+    plane_parts, blocks = lax.optimization_barrier((plane_parts, blocks))
 
     sums = call(
         functools.partial(plane_sum_kernel, piece),
         (struct((piece, D), F32), *[struct((piece, D), BF16)] * (groups - 1)),
     )(*plane_parts)
+    blocks = call(
+        functools.partial(turn_kernel, count),
+        tuple(struct((rows, D), BF16) for rows in plane_rows),
+    )(*blocks, to_left, to_right)
+    sums, blocks = lax.optimization_barrier((sums, blocks))
     shared = [sums[0]] + [across(sums[k], k) for k in range(1, groups)]
+    blocks = [blocks[0]] + [in_plane(blocks[v], v) for v in range(1, PLANE)]
+    shared, blocks = lax.optimization_barrier((shared, blocks))
     total = call(
         functools.partial(group_sum_kernel, 1.0 / math.sqrt(ROWS * count)),
         struct((piece, D), BF16),
     )(*shared)
+    d_features = call(
+        functools.partial(features_kernel, count),
+        struct((ROWS, D), BF16),
+        (pltpu.VMEM((ROWS, D), F32), pltpu.VMEM((count, SLOT, D), BF16)),
+    )(matrix, own, *blocks)
     chunk = jnp.concatenate([total] + [across(total, k) for k in range(1, groups)], axis=0)
     chunks = [chunk] + [in_plane(chunk, v) for v in range(1, PLANE)]
     grad_two, grad_one = call(

time: 86.1 us -> 80.4 us (0.934)
  starting transfers between devices: 40.9 us -> 34.6 us
    ppermute x6 -> x9, waiting for transfers between devices: 7.82 us -> 15.5 us  [across(): lax.ppermute(value, 'node', [(i, (i + k * PLANE) % count) for i in range(...]
    ppermute x2 -> x1, waiting for transfers between devices: 5.93 us -> 0.58 us  [shards(): from_left = lax.ppermute(to_right, 'node', up)]
    all_to_all x2 -> x1, starting transfers between devices: 12 us -> 8.46 us  [shards(): lax.all_to_all(send, 'node', split_axis=0, concat_axis=0, tiled=True)]
    ppermute x2 -> x1, starting transfers between devices: 7.18 us -> 3.82 us  [shards(): from_left = lax.ppermute(to_right, 'node', up)]
    ppermute x6 -> x9, starting transfers between devices: 7.11 us -> 10.3 us  [in_plane(): return lax.ppermute(value, 'node', [(i, i ^ v) for i in range(count)])]
    ppermute x2 -> x1, starting transfers between devices: 2.58 us -> 1.29 us  [shards(): from_right = lax.ppermute(to_left, 'node', down)]
    ppermute x6 -> x9, starting transfers between devices: 12.1 us -> 10.8 us  [across(): lax.ppermute(value, 'node', [(i, (i + k * PLANE) % count) for i in range(...]
    ppermute x2 -> x1, waiting for transfers between devices: 5.9 us -> 4.9 us  [shards(): from_right = lax.ppermute(to_left, 'node', down)]
  transfers between devices with their start and end apart: 18 -> 21, of which waited for: 10 -> 15; matrix products, arithmetic and copies ran while one was open for 0% -> 0% of each run, Pallas kernels for 3% -> 2%
where the time goes in v2:
time: 80.4 us; the launch traced here: 80 us
  starting transfers between devices  34.6 us (43%)
  waiting for transfers between devices  33.6 us (42%)
  Pallas kernels  7.04 us (9%)
  local copies, waits for them, and re-layouts  3.94 us (5%)
    ppermute x9, waiting for transfers between devices, across(): lax.ppermute(value, 'node', [(i, (i + k * PLANE) % count) for i in range(...  15.5 us
    ppermute x9, starting transfers between devices, across(): lax.ppermute(value, 'node', [(i, (i + k * PLANE) % count) for i in range(...  10.8 us
    ppermute x9, starting transfers between devices, in_plane(): return lax.ppermute(value, 'node', [(i, i ^ v) for i in range(count)])  10.3 us
    all_to_all x1, starting transfers between devices, shards(): lax.all_to_all(send, 'node', split_axis=0, concat_axis=0, tiled=True)  8.46 us
    ppermute x9, waiting for transfers between devices, in_plane(): return lax.ppermute(value, 'node', [(i, i ^ v) for i in range(count)])  8.09 us
    ppermute x1, waiting for transfers between devices, shards(): from_right = lax.ppermute(to_left, 'node', down)  4.9 us
    all_to_all x1, waiting for transfers between devices, shards(): lax.all_to_all(send, 'node', split_axis=0, concat_axis=0, tiled=True)  4.53 us
    unnamed x18, local copies, waits for them, and re-layouts  3.94 us
  transfers between devices with their start and end apart: 21, of which 15 were waited for; matrix products, arithmetic and copies ran while one was open for 0% of the time, Pallas kernels for 2%

profile of v2, /device:TPU:0, one launch (start us, length us, event | category | flops | bytes accessed | tf_op | source)
XLA Modules:
  0.0 80.0 jit_solution(13649734766298437093)
XLA Ops:
  4.6 3.2 %shard_map.103 = (bf16[128,768]{1,0:T(8,128)(2,1)S(1)}, f32[128,512]{1,0:T(8,128)S(1)}, bf16[16,32,512]{2,1,0:T(8,128)(2,1)}, bf16[64,512]{1,0:T(8,128)(2,1)S(1)}, bf16[64,512]{1,0:T(8,128)(2,1)S(1)}) custom-call(s32[32,128]{1,0:T(8,128)S(1)} %bitcast.4, s32[32,128]{1,0:T(8,128)S(1)} %bitcast.5, s32[2,256]{1,0:T(2,128)S(1)} %bitcast.6, ...), custom_call_target="tpu_custom_call" | custom-call | tf_op jit(solution)/shard_map/pallas_call | solution.py:317
  7.8 8.5 %all-to-all-start = ((bf16[16,32,512]{2,1,0:T(8,128)(2,1)}), bf16[16,32,512]{2,1,0:T(8,128)(2,1)S(1)}, u32[]{:S(2)}, u32[]{:S(2)}) async-start(bf16[16,32,512]{2,1,0:T(8,128)(2,1)} %get-tuple-element.56), calls=%async_computation | async-start | bytes 1048576 | tf_op jit(solution)/shard_map/all_to_all | solution.py:343
  16.2 3.8 %collective-permute-start = (bf16[64,512]{1,0:T(8,128)(2,1)S(1)}, bf16[64,512]{1,0:T(8,128)(2,1)S(1)}, u32[]{:S(2)}, u32[]{:S(2)}) collective-permute-start(bf16[64,512]{1,0:T(8,128)(2,1)S(1)} %get-tuple-element.57), channel_id=1, source_target_pairs={{0,2},{2,4},{4,6},{6,8},{8,10},{10,12},{12,14},{14,16},{16,18},{18... | collective-permute-start | bytes 196616 | tf_op jit(solution)/shard_map/ppermute | solution.py:341
  20.1 1.3 %collective-permute-start.1 = (bf16[64,512]{1,0:T(8,128)(2,1)S(1)}, bf16[64,512]{1,0:T(8,128)(2,1)S(1)}, u32[]{:S(2)}, u32[]{:S(2)}) collective-permute-start(bf16[64,512]{1,0:T(8,128)(2,1)S(1)} %get-tuple-element.58), channel_id=1, source_target_pairs={{2,0},{4,2},{6,4},{8,6},{10,8},{12,10},{14,12},{16,14},{18,16},{20... | collective-permute-start | bytes 196616 | tf_op jit(solution)/shard_map/ppermute | solution.py:342
  21.9 4.9 %collective-permute-done.1.right_ref = bf16[64,512]{1,0:T(8,128)(2,1)S(1)} collective-permute-done((bf16[64,512]{1,0:T(8,128)(2,1)S(1)}, bf16[64,512]{1,0:T(8,128)(2,1)S(1)}, u32[]{:S(2)}, u32[]{:S(2)}) %collective-permute-start.1) | collective-permute-done | bytes 65568 | tf_op jit(solution)/shard_map/ppermute | solution.py:342
  26.8 4.5 %all-to-all-done.recv_ref = bf16[16,32,512]{2,1,0:T(8,128)(2,1)S(1)} async-done(((bf16[16,32,512]{2,1,0:T(8,128)(2,1)}), bf16[16,32,512]{2,1,0:T(8,128)(2,1)S(1)}, u32[]{:S(2)}, u32[]{:S(2)}) %all-to-all-start) | async-done | bytes 524320 | tf_op jit(solution)/shard_map/all_to_all | solution.py:343
  33.2 1.3 %collective-permute-start.3 = (bf16[256,512]{1,0:T(8,128)(2,1)S(1)}, bf16[256,512]{1,0:T(8,128)(2,1)S(1)}, u32[]{:S(2)}, u32[]{:S(2)}) collective-permute-start(bf16[256,512]{1,0:T(8,128)(2,1)S(1)} %get-tuple-element.63), channel_id=1, source_target_pairs={{0,4},{2,6},{4,0},{6,2},{8,12},{10,14},{12,8},{14,10},{16,20},{18,... | collective-permute-start | bytes 786440 | tf_op jit(solution)/shard_map/ppermute | solution.py:310
  34.5 1.7 %collective-permute-start.4 = (bf16[256,512]{1,0:T(8,128)(2,1)S(1)}, bf16[256,512]{1,0:T(8,128)(2,1)S(1)}, u32[]{:S(2)}, u32[]{:S(2)}) collective-permute-start(bf16[256,512]{1,0:T(8,128)(2,1)S(1)} %get-tuple-element.64), channel_id=1, source_target_pairs={{0,6},{2,4},{4,2},{6,0},{8,14},{10,12},{12,10},{14,8},{16,22},{18,... | collective-permute-start | bytes 786440 | tf_op jit(solution)/shard_map/ppermute | solution.py:310
  36.7 3.1 %collective-permute-start.6 = (bf16[64,512]{1,0:T(8,128)(2,1)S(1)}, bf16[64,512]{1,0:T(8,128)(2,1)S(1)}, u32[]{:S(2)}, u32[]{:S(2)}) collective-permute-start(bf16[64,512]{1,0:T(8,128)(2,1)S(1)} %get-tuple-element.67), channel_id=1, source_target_pairs={{0,16},{2,18},{4,20},{6,22},{8,24},{10,26},{12,28},{14,30},{16,0},... | collective-permute-start | bytes 196616 | tf_op jit(solution)/shard_map/ppermute | solution.py:313
  39.8 4.1 %collective-permute-done.6.refs_2_ = bf16[64,512]{1,0:T(8,128)(2,1)S(1)} collective-permute-done((bf16[64,512]{1,0:T(8,128)(2,1)S(1)}, bf16[64,512]{1,0:T(8,128)(2,1)S(1)}, u32[]{:S(2)}, u32[]{:S(2)}) %collective-permute-start.6) | collective-permute-done | bytes 65568 | tf_op jit(solution)/shard_map/ppermute | solution.py:313
  44.7 2.4 %collective-permute-done.5.refs_1_ = bf16[96,512]{1,0:T(8,128)(2,1)S(1)} collective-permute-done((bf16[96,512]{1,0:T(8,128)(2,1)S(1)}, bf16[96,512]{1,0:T(8,128)(2,1)S(1)}, u32[]{:S(2)}, u32[]{:S(2)}) %collective-permute-start.5) | collective-permute-done | bytes 98336 | tf_op jit(solution)/shard_map/ppermute | solution.py:313
  47.2 1.4 %collective-permute-done.7.refs_3_ = bf16[96,512]{1,0:T(8,128)(2,1)S(1)} collective-permute-done((bf16[96,512]{1,0:T(8,128)(2,1)S(1)}, bf16[96,512]{1,0:T(8,128)(2,1)S(1)}, u32[]{:S(2)}, u32[]{:S(2)}) %collective-permute-start.7) | collective-permute-done | bytes 98336 | tf_op jit(solution)/shard_map/ppermute | solution.py:313
  49.4 1.7 %collective-permute-start.13 = (bf16[96,512]{1,0:T(8,128)(2,1)S(1)}, bf16[96,512]{1,0:T(8,128)(2,1)S(1)}, u32[]{:S(2)}, u32[]{:S(2)}) collective-permute-start(bf16[96,512]{1,0:T(8,128)(2,1)S(1)} %get-tuple-element.94), channel_id=1, source_target_pairs={{0,6},{2,4},{4,2},{6,0},{8,14},{10,12},{12,10},{14,8},{16,22},{18,... | collective-permute-start | bytes 294920 | tf_op jit(solution)/shard_map/ppermute | solution.py:310
  51.1 2.6 %collective-permute-start.9 = (bf16[64,512]{1,0:T(8,128)(2,1)S(1)}, bf16[64,512]{1,0:T(8,128)(2,1)S(1)}, u32[]{:S(2)}, u32[]{:S(2)}) collective-permute-start(bf16[64,512]{1,0:T(8,128)(2,1)S(1)} %get-tuple-element.89), channel_id=1, source_target_pairs={{0,16},{2,18},{4,20},{6,22},{8,24},{10,26},{12,28},{14,30},{16,0},... | collective-permute-start | bytes 196616 | tf_op jit(solution)/shard_map/ppermute | solution.py:313
  53.7 1.5 %collective-permute-start.10 = (bf16[64,512]{1,0:T(8,128)(2,1)S(1)}, bf16[64,512]{1,0:T(8,128)(2,1)S(1)}, u32[]{:S(2)}, u32[]{:S(2)}) collective-permute-start(bf16[64,512]{1,0:T(8,128)(2,1)S(1)} %get-tuple-element.90), channel_id=1, source_target_pairs={{0,24},{2,26},{4,28},{6,30},{8,0},{10,2},{12,4},{14,6},{16,8},{18,... | collective-permute-start | bytes 196616 | tf_op jit(solution)/shard_map/ppermute | solution.py:313
  56.4 1.6 %collective-permute-done.10.refs_3_ = bf16[64,512]{1,0:T(8,128)(2,1)S(1)} collective-permute-done((bf16[64,512]{1,0:T(8,128)(2,1)S(1)}, bf16[64,512]{1,0:T(8,128)(2,1)S(1)}, u32[]{:S(2)}, u32[]{:S(2)}) %collective-permute-start.10) | collective-permute-done | bytes 65568 | tf_op jit(solution)/shard_map/ppermute | solution.py:313
  58.0 1.8 %collective-permute-done.12.refs_2_ = bf16[64,512]{1,0:T(8,128)(2,1)S(1)} collective-permute-done((bf16[64,512]{1,0:T(8,128)(2,1)S(1)}, bf16[64,512]{1,0:T(8,128)(2,1)S(1)}, u32[]{:S(2)}, u32[]{:S(2)}) %collective-permute-start.12) | collective-permute-done | bytes 65568 | tf_op jit(solution)/shard_map/ppermute | solution.py:310
  59.8 1.6 %collective-permute-start.16 = (bf16[64,512]{1,0:T(8,128)(2,1)S(1)}, bf16[64,512]{1,0:T(8,128)(2,1)S(1)}, u32[]{:S(2)}, u32[]{:S(2)}) collective-permute-start(bf16[64,512]{1,0:T(8,128)(2,1)S(1)} %shard_map.109), channel_id=1, source_target_pairs={{0,24},{2,26},{4,28},{6,30},{8,0},{10,2},{12,4},{14,6},{16,8},{18,... | collective-permute-start | bytes 196616 | tf_op jit(solution)/shard_map/ppermute | solution.py:313
  62.5 1.6 %collective-permute-done.16 = bf16[64,512]{1,0:T(8,128)(2,1)S(1)} collective-permute-done((bf16[64,512]{1,0:T(8,128)(2,1)S(1)}, bf16[64,512]{1,0:T(8,128)(2,1)S(1)}, u32[]{:S(2)}, u32[]{:S(2)}) %collective-permute-start.16) | collective-permute-done | bytes 65568 | tf_op jit(solution)/shard_map/ppermute | solution.py:313
  64.1 3.1 %collective-permute-done.15 = bf16[64,512]{1,0:T(8,128)(2,1)S(1)} collective-permute-done((bf16[64,512]{1,0:T(8,128)(2,1)S(1)}, bf16[64,512]{1,0:T(8,128)(2,1)S(1)}, u32[]{:S(2)}, u32[]{:S(2)}) %collective-permute-start.15) | collective-permute-done | bytes 65568 | tf_op jit(solution)/shard_map/ppermute | solution.py:313
  68.2 1.5 %collective-permute-start.19 = (bf16[256,512]{1,0:T(8,128)(2,1)S(1)}, bf16[256,512]{1,0:T(8,128)(2,1)S(1)}, u32[]{:S(2)}, u32[]{:S(2)}) collective-permute-start(bf16[256,512]{1,0:T(8,128)(2,1)S(1)} %pad_maximum_fusion.refs_0_), channel_id=1, source_target_pairs={{0,6},{2,4},{4,2},{6,0},{8,14},{10,12},{12,10},{14,8},{16,22},{18,... | collective-permute-start | bytes 786440 | tf_op jit(solution)/shard_map/ppermute | solution.py:310
  70.3 1.4 %collective-permute-start.17 = (bf16[256,512]{1,0:T(8,128)(2,1)S(1)}, bf16[256,512]{1,0:T(8,128)(2,1)S(1)}, u32[]{:S(2)}, u32[]{:S(2)}) collective-permute-start(bf16[256,512]{1,0:T(8,128)(2,1)S(1)} %pad_maximum_fusion.refs_0_), channel_id=1, source_target_pairs={{0,2},{2,0},{4,6},{6,4},{8,10},{10,8},{12,14},{14,12},{16,18},{18,... | collective-permute-start | bytes 786440 | tf_op jit(solution)/shard_map/ppermute | solution.py:310
  72.6 3.0 %collective-permute-done.19.refs_3_ = bf16[256,512]{1,0:T(8,128)(2,1)S(1)} collective-permute-done((bf16[256,512]{1,0:T(8,128)(2,1)S(1)}, bf16[256,512]{1,0:T(8,128)(2,1)S(1)}, u32[]{:S(2)}, u32[]{:S(2)}) %collective-permute-start.19) | collective-permute-done | bytes 262176 | tf_op jit(solution)/shard_map/ppermute | solution.py:310
  75.6 2.7 %collective-permute-done.18.refs_2_ = bf16[256,512]{1,0:T(8,128)(2,1)S(1)} collective-permute-done((bf16[256,512]{1,0:T(8,128)(2,1)S(1)}, bf16[256,512]{1,0:T(8,128)(2,1)S(1)}, u32[]{:S(2)}, u32[]{:S(2)}) %collective-permute-start.18) | collective-permute-done | bytes 262176 | tf_op jit(solution)/shard_map/ppermute | solution.py:310
  (45 shorter events, 15.1 us)
Async XLA Ops:
  4.6 26.8 %copy-start.3 = (bf16[512,512]{1,0:T(8,128)(2,1)S(1)}, bf16[512,512]{1,0:T(8,128)(2,1)}, u32[]{:S(2)}) copy-start(bf16[512,512]{1,0:T(8,128)(2,1)} %w_two_ref.1) | copy-start | bytes 1572868
  7.7 23.6 %copy-start = (bf16[512,512]{1,0:T(8,128)(2,1)S(1)}, bf16[512,512]{1,0:T(8,128)(2,1)}, u32[]{:S(2)}) copy-start(bf16[512,512]{1,0:T(8,128)(2,1)} %w_one_ref.3) | copy-start | bytes 1572868
  7.8 23.6 %copy-start.2 = (bf16[128,512]{1,0:T(8,128)(2,1)S(1)}, bf16[128,512]{1,0:T(8,128)(2,1)}, u32[]{:S(2)}) copy-start(bf16[128,512]{1,0:T(8,128)(2,1)} %feat_ref.1) | copy-start | bytes 393220
  7.8 23.6 %all-to-all-start = ((bf16[16,32,512]{2,1,0:T(8,128)(2,1)}), bf16[16,32,512]{2,1,0:T(8,128)(2,1)S(1)}, u32[]{:S(2)}, u32[]{:S(2)}) async-start(bf16[16,32,512]{2,1,0:T(8,128)(2,1)} %get-tuple-element.56), calls=%async_computation | async-start | bytes 1048576 | tf_op jit(solution)/shard_map/all_to_all | solution.py:343
  16.2 5.7 %collective-permute-start = (bf16[64,512]{1,0:T(8,128)(2,1)S(1)}, bf16[64,512]{1,0:T(8,128)(2,1)S(1)}, u32[]{:S(2)}, u32[]{:S(2)}) collective-permute-start(bf16[64,512]{1,0:T(8,128)(2,1)S(1)} %get-tuple-element.57), channel_id=1, source_target_pairs={{0,2},{2,4},{4,6},{6,8},{8,10},{10,12},{12,14},{14,16},{16,18},{18... | collective-permute-start | bytes 196616 | tf_op jit(solution)/shard_map/ppermute | solution.py:341
  20.1 6.8 %collective-permute-start.1 = (bf16[64,512]{1,0:T(8,128)(2,1)S(1)}, bf16[64,512]{1,0:T(8,128)(2,1)S(1)}, u32[]{:S(2)}, u32[]{:S(2)}) collective-permute-start(bf16[64,512]{1,0:T(8,128)(2,1)S(1)} %get-tuple-element.58), channel_id=1, source_target_pairs={{2,0},{4,2},{6,4},{8,6},{10,8},{12,10},{14,12},{16,14},{18,16},{20... | collective-permute-start | bytes 196616 | tf_op jit(solution)/shard_map/ppermute | solution.py:342
  32.6 16.0 %collective-permute-start.2 = (bf16[256,512]{1,0:T(8,128)(2,1)S(1)}, bf16[256,512]{1,0:T(8,128)(2,1)S(1)}, u32[]{:S(2)}, u32[]{:S(2)}) collective-permute-start(bf16[256,512]{1,0:T(8,128)(2,1)S(1)} %get-tuple-element.62), channel_id=1, source_target_pairs={{0,2},{2,0},{4,6},{6,4},{8,10},{10,8},{12,14},{14,12},{16,18},{18,... | collective-permute-start | bytes 786440 | tf_op jit(solution)/shard_map/ppermute | solution.py:310
  33.2 15.4 %collective-permute-start.3 = (bf16[256,512]{1,0:T(8,128)(2,1)S(1)}, bf16[256,512]{1,0:T(8,128)(2,1)S(1)}, u32[]{:S(2)}, u32[]{:S(2)}) collective-permute-start(bf16[256,512]{1,0:T(8,128)(2,1)S(1)} %get-tuple-element.63), channel_id=1, source_target_pairs={{0,4},{2,6},{4,0},{6,2},{8,12},{10,14},{12,8},{14,10},{16,20},{18,... | collective-permute-start | bytes 786440 | tf_op jit(solution)/shard_map/ppermute | solution.py:310
  34.5 14.1 %collective-permute-start.4 = (bf16[256,512]{1,0:T(8,128)(2,1)S(1)}, bf16[256,512]{1,0:T(8,128)(2,1)S(1)}, u32[]{:S(2)}, u32[]{:S(2)}) collective-permute-start(bf16[256,512]{1,0:T(8,128)(2,1)S(1)} %get-tuple-element.64), channel_id=1, source_target_pairs={{0,6},{2,4},{4,2},{6,0},{8,14},{10,12},{12,10},{14,8},{16,22},{18,... | collective-permute-start | bytes 786440 | tf_op jit(solution)/shard_map/ppermute | solution.py:310
  36.7 7.2 %collective-permute-start.6 = (bf16[64,512]{1,0:T(8,128)(2,1)S(1)}, bf16[64,512]{1,0:T(8,128)(2,1)S(1)}, u32[]{:S(2)}, u32[]{:S(2)}) collective-permute-start(bf16[64,512]{1,0:T(8,128)(2,1)S(1)} %get-tuple-element.67), channel_id=1, source_target_pairs={{0,16},{2,18},{4,20},{6,22},{8,24},{10,26},{12,28},{14,30},{16,0},... | collective-permute-start | bytes 196616 | tf_op jit(solution)/shard_map/ppermute | solution.py:313
  39.8 7.3 %collective-permute-start.5 = (bf16[96,512]{1,0:T(8,128)(2,1)S(1)}, bf16[96,512]{1,0:T(8,128)(2,1)S(1)}, u32[]{:S(2)}, u32[]{:S(2)}) collective-permute-start(bf16[96,512]{1,0:T(8,128)(2,1)S(1)} %get-tuple-element.66), channel_id=1, source_target_pairs={{0,8},{2,10},{4,12},{6,14},{8,16},{10,18},{12,20},{14,22},{16,24},... | collective-permute-start | bytes 294920 | tf_op jit(solution)/shard_map/ppermute | solution.py:313
  43.9 4.6 %collective-permute-start.7 = (bf16[96,512]{1,0:T(8,128)(2,1)S(1)}, bf16[96,512]{1,0:T(8,128)(2,1)S(1)}, u32[]{:S(2)}, u32[]{:S(2)}) collective-permute-start(bf16[96,512]{1,0:T(8,128)(2,1)S(1)} %get-tuple-element.68), channel_id=1, source_target_pairs={{0,24},{2,26},{4,28},{6,30},{8,0},{10,2},{12,4},{14,6},{16,8},{18,... | collective-permute-start | bytes 294920 | tf_op jit(solution)/shard_map/ppermute | solution.py:313
  48.7 6.7 %collective-permute-start.8 = (bf16[64,512]{1,0:T(8,128)(2,1)S(1)}, bf16[64,512]{1,0:T(8,128)(2,1)S(1)}, u32[]{:S(2)}, u32[]{:S(2)}) collective-permute-start(bf16[64,512]{1,0:T(8,128)(2,1)S(1)} %get-tuple-element.88), channel_id=1, source_target_pairs={{0,8},{2,10},{4,12},{6,14},{8,16},{10,18},{12,20},{14,22},{16,24},... | collective-permute-start | bytes 196616 | tf_op jit(solution)/shard_map/ppermute | solution.py:313
  48.8 10.9 %collective-permute-start.11 = (bf16[96,512]{1,0:T(8,128)(2,1)S(1)}, bf16[96,512]{1,0:T(8,128)(2,1)S(1)}, u32[]{:S(2)}, u32[]{:S(2)}) collective-permute-start(bf16[96,512]{1,0:T(8,128)(2,1)S(1)} %get-tuple-element.92), channel_id=1, source_target_pairs={{0,2},{2,0},{4,6},{6,4},{8,10},{10,8},{12,14},{14,12},{16,18},{18,... | collective-permute-start | bytes 294920 | tf_op jit(solution)/shard_map/ppermute | solution.py:310
  49.4 10.4 %collective-permute-start.13 = (bf16[96,512]{1,0:T(8,128)(2,1)S(1)}, bf16[96,512]{1,0:T(8,128)(2,1)S(1)}, u32[]{:S(2)}, u32[]{:S(2)}) collective-permute-start(bf16[96,512]{1,0:T(8,128)(2,1)S(1)} %get-tuple-element.94), channel_id=1, source_target_pairs={{0,6},{2,4},{4,2},{6,0},{8,14},{10,12},{12,10},{14,8},{16,22},{18,... | collective-permute-start | bytes 294920 | tf_op jit(solution)/shard_map/ppermute | solution.py:310
  51.1 5.3 %collective-permute-start.9 = (bf16[64,512]{1,0:T(8,128)(2,1)S(1)}, bf16[64,512]{1,0:T(8,128)(2,1)S(1)}, u32[]{:S(2)}, u32[]{:S(2)}) collective-permute-start(bf16[64,512]{1,0:T(8,128)(2,1)S(1)} %get-tuple-element.89), channel_id=1, source_target_pairs={{0,16},{2,18},{4,20},{6,22},{8,24},{10,26},{12,28},{14,30},{16,0},... | collective-permute-start | bytes 196616 | tf_op jit(solution)/shard_map/ppermute | solution.py:313
  53.7 4.3 %collective-permute-start.10 = (bf16[64,512]{1,0:T(8,128)(2,1)S(1)}, bf16[64,512]{1,0:T(8,128)(2,1)S(1)}, u32[]{:S(2)}, u32[]{:S(2)}) collective-permute-start(bf16[64,512]{1,0:T(8,128)(2,1)S(1)} %get-tuple-element.90), channel_id=1, source_target_pairs={{0,24},{2,26},{4,28},{6,30},{8,0},{10,2},{12,4},{14,6},{16,8},{18,... | collective-permute-start | bytes 196616 | tf_op jit(solution)/shard_map/ppermute | solution.py:313
  55.5 4.3 %collective-permute-start.12 = (bf16[64,512]{1,0:T(8,128)(2,1)S(1)}, bf16[64,512]{1,0:T(8,128)(2,1)S(1)}, u32[]{:S(2)}, u32[]{:S(2)}) collective-permute-start(bf16[64,512]{1,0:T(8,128)(2,1)S(1)} %get-tuple-element.93), channel_id=1, source_target_pairs={{0,4},{2,6},{4,0},{6,2},{8,12},{10,14},{12,8},{14,10},{16,20},{18,... | collective-permute-start | bytes 196616 | tf_op jit(solution)/shard_map/ppermute | solution.py:310
  59.8 4.3 %collective-permute-start.16 = (bf16[64,512]{1,0:T(8,128)(2,1)S(1)}, bf16[64,512]{1,0:T(8,128)(2,1)S(1)}, u32[]{:S(2)}, u32[]{:S(2)}) collective-permute-start(bf16[64,512]{1,0:T(8,128)(2,1)S(1)} %shard_map.109), channel_id=1, source_target_pairs={{0,24},{2,26},{4,28},{6,30},{8,0},{10,2},{12,4},{14,6},{16,8},{18,... | collective-permute-start | bytes 196616 | tf_op jit(solution)/shard_map/ppermute | solution.py:313
  61.3 5.8 %collective-permute-start.15 = (bf16[64,512]{1,0:T(8,128)(2,1)S(1)}, bf16[64,512]{1,0:T(8,128)(2,1)S(1)}, u32[]{:S(2)}, u32[]{:S(2)}) collective-permute-start(bf16[64,512]{1,0:T(8,128)(2,1)S(1)} %shard_map.109), channel_id=1, source_target_pairs={{0,16},{2,18},{4,20},{6,22},{8,24},{10,26},{12,28},{14,30},{16,0},... | collective-permute-start | bytes 196616 | tf_op jit(solution)/shard_map/ppermute | solution.py:313
  62.1 6.1 %collective-permute-start.14 = (bf16[64,512]{1,0:T(8,128)(2,1)S(1)}, bf16[64,512]{1,0:T(8,128)(2,1)S(1)}, u32[]{:S(2)}, u32[]{:S(2)}) collective-permute-start(bf16[64,512]{1,0:T(8,128)(2,1)S(1)} %shard_map.109), channel_id=1, source_target_pairs={{0,8},{2,10},{4,12},{6,14},{8,16},{10,18},{12,20},{14,22},{16,24},... | collective-permute-start | bytes 196616 | tf_op jit(solution)/shard_map/ppermute | solution.py:313
  68.2 7.4 %collective-permute-start.19 = (bf16[256,512]{1,0:T(8,128)(2,1)S(1)}, bf16[256,512]{1,0:T(8,128)(2,1)S(1)}, u32[]{:S(2)}, u32[]{:S(2)}) collective-permute-start(bf16[256,512]{1,0:T(8,128)(2,1)S(1)} %pad_maximum_fusion.refs_0_), channel_id=1, source_target_pairs={{0,6},{2,4},{4,2},{6,0},{8,14},{10,12},{12,10},{14,8},{16,22},{18,... | collective-permute-start | bytes 786440 | tf_op jit(solution)/shard_map/ppermute | solution.py:310
  69.7 8.6 %collective-permute-start.18 = (bf16[256,512]{1,0:T(8,128)(2,1)S(1)}, bf16[256,512]{1,0:T(8,128)(2,1)S(1)}, u32[]{:S(2)}, u32[]{:S(2)}) collective-permute-start(bf16[256,512]{1,0:T(8,128)(2,1)S(1)} %pad_maximum_fusion.refs_0_), channel_id=1, source_target_pairs={{0,4},{2,6},{4,0},{6,2},{8,12},{10,14},{12,8},{14,10},{16,20},{18,... | collective-permute-start | bytes 786440 | tf_op jit(solution)/shard_map/ppermute | solution.py:310
  70.3 8.6 %collective-permute-start.17 = (bf16[256,512]{1,0:T(8,128)(2,1)S(1)}, bf16[256,512]{1,0:T(8,128)(2,1)S(1)}, u32[]{:S(2)}, u32[]{:S(2)}) collective-permute-start(bf16[256,512]{1,0:T(8,128)(2,1)S(1)} %pad_maximum_fusion.refs_0_), channel_id=1, source_target_pairs={{0,2},{2,0},{4,6},{6,4},{8,10},{10,8},{12,14},{14,12},{16,18},{18,... | collective-permute-start | bytes 786440 | tf_op jit(solution)/shard_map/ppermute | solution.py:310
  (6 other events, 4.6 us)

commit v3 on v2

--- a/solution.py
+++ b/solution.py
@@ -199,67 +199,94 @@
                 ]
 
 
-def back_kernel(count, mat_ref, d_pre_ref, w_one_ref, own_ref, *refs):
-    groups = count // PLANE
-    across_refs, (left_ref, right_ref, block_scr) = refs[:groups], refs[groups:]
-    device = lax.axis_index("node")
-    group, place = device // PLANE, device % PLANE
+def hop_bits(count):
+    bits = [b for b in range(count.bit_length() - 1)]
+    return [bits[2], bits[0], bits[1]] + bits[3:]
+
+
+def hop_rows(count, bit):
+    return count // 2 * SLOT + HALO * (2 if bit == 0 else 1)
+
+
+def right_moves(device, bit):
+    if bit == 2:
+        return device % 4 == 3
+    return device % (1 << bit) == 0
+
+
+def pack_hop(count, bit, held_ref, left, right, out_ref):
+    device = lax.axis_index("node")
+    chosen = [r for r in range(count) if r >> bit & 1]
+    for at, r in enumerate(chosen):
+        out_ref[at * SLOT : (at + 1) * SLOT, :] = held_ref[r]
+    size = len(chosen) * SLOT
+    if bit == 0:
+        out_ref[size : size + HALO, :] = left
+        out_ref[size + HALO :, :] = right
+    else:
+        out_ref[size:, :] = jnp.where(right_moves(device, bit), right, left)
+
+
+def unpack_hop(count, bit, got_ref, held_ref, left, right):
+    device = lax.axis_index("node")
+    chosen = [r for r in range(count) if r >> bit & 1]
+    for at, r in enumerate(chosen):
+        held_ref[r] = got_ref[at * SLOT : (at + 1) * SLOT, :]
+    size = len(chosen) * SLOT
+    if bit == 0:
+        return got_ref[size : size + HALO, :], got_ref[size + HALO :, :]
+    got = got_ref[size:, :]
+    if bit == 2:
+        moves = device % 4 == 0
+    else:
+        moves = device % (1 << bit) == (1 << bit) - 1
+    return jnp.where(moves, got, left), jnp.where(right_moves(device, bit), got, right)
+
+
+def back_kernel(
+    count, bit, mat_ref, d_pre_ref, w_one_ref, own_ref, held_ref, left_ref, right_ref, out_ref
+):
+    device = lax.axis_index("node")
     far = count * SLOT
     q = (nt(d_pre_ref[...], w_one_ref[...]) / row_total(mat_ref, far)).astype(BF16)
-    own_ref[...] = tn(mat_ref[:, 0:ROWS], q)
     rims = tn(mat_ref[:, HALO_COL:FAR_COL], q).astype(BF16)
     left_ref[...] = rims[0:HALO]
     right_ref[...] = rims[HALO : 2 * HALO]
     terms = tn(mat_ref[:, FAR_COL : FAR_COL + far], q).astype(BF16).reshape(count, SLOT, D)
     for peer in range(count):
-        k = lax.rem(peer // PLANE + groups - group, groups)
-        block_scr[k * PLANE + ((peer % PLANE) ^ place)] = terms[peer]
-    size = PLANE * SLOT
-    for k, ref in enumerate(across_refs):
-        ref[0:size, :] = block_scr[k * PLANE : (k + 1) * PLANE].reshape(size, D)
-        if k == 1:
-            ref[size:, :] = rims[HALO : 2 * HALO]
-        if k == groups - 1:
-            ref[size:, :] = rims[0:HALO]
-
-
-def turn_kernel(count, *refs):
-    groups = count // PLANE
-    across_refs, (left_ref, right_ref), plane_refs = (
-        refs[:groups], refs[groups : groups + 2], refs[groups + 2 :],
-    )
-    place = lax.axis_index("node") % PLANE
-    size = groups * SLOT
-    for v, ref in enumerate(plane_refs):
-        for k in range(groups):
-            ref[k * SLOT : (k + 1) * SLOT, :] = across_refs[k][v * SLOT : (v + 1) * SLOT, :]
-    left, right = left_ref[...], right_ref[...]
-    from_below = across_refs[1][PLANE * SLOT :, :]
-    from_above = across_refs[groups - 1][PLANE * SLOT :, :]
-    plane_refs[1][size:, :] = jnp.where(place % 2 == 0, right, left)
-    plane_refs[3][size:, :] = jnp.where(
-        place == 0,
-        from_above,
-        jnp.where(place == 1, right, jnp.where(place == 2, left, from_below)),
-    )
-
-
-def features_kernel(count, mat_ref, own_ref, *refs):
-    plane_refs, (out_ref, sum_scr, block_scr) = refs[:PLANE], refs[PLANE:]
-    groups = count // PLANE
-    device = lax.axis_index("node")
-    group, place = device // PLANE, device % PLANE
+        held_ref[device ^ peer] = terms[peer]
+    pack_hop(count, bit, held_ref, rims[0:HALO], rims[HALO : 2 * HALO], out_ref)
+    own_ref[...] = tn(mat_ref[:, 0:ROWS], q)
+
+
+def hop_kernel(
+    count, last, bit, got_ref, was_ref, was_left_ref, was_right_ref,
+    held_ref, left_ref, right_ref, out_ref,
+):
+    held_ref[...] = was_ref[...]
+    left, right = unpack_hop(
+        count, last, got_ref, held_ref, was_left_ref[...], was_right_ref[...]
+    )
+    left_ref[...] = left
+    right_ref[...] = right
+    pack_hop(count, bit, held_ref, left, right, out_ref)
+
+
+def features_kernel(
+    count, last, mat_ref, own_ref, got_ref, was_ref, was_left_ref, was_right_ref,
+    out_ref, sum_scr, held_scr, block_scr,
+):
+    device = lax.axis_index("node")
     far = count * SLOT
-    size = groups * SLOT
-    for v, ref in enumerate(plane_refs):
-        for k in range(groups):
-            peer = lax.rem(group + groups - k, groups) * PLANE + (place ^ v)
-            block_scr[peer] = ref[k * SLOT : (k + 1) * SLOT, :]
+    held_scr[...] = was_ref[...]
+    left, right = unpack_hop(
+        count, last, got_ref, held_scr, was_left_ref[...], was_right_ref[...]
+    )
+    for r in range(count):
+        block_scr[device ^ r] = held_scr[r]
     sum_scr[...] = own_ref[...] + nn(mat_ref[:, FAR_COL + far :], block_scr[...].reshape(far, D))
-    one, three = plane_refs[1][size:, :].astype(F32), plane_refs[3][size:, :].astype(F32)
-    even = place % 2 == 0
-    sum_scr[0:HALO, :] += jnp.where(even, three, one)
-    sum_scr[ROWS - HALO : ROWS, :] += jnp.where(even, one, three)
+    sum_scr[0:HALO, :] += right.astype(F32)
+    sum_scr[ROWS - HALO : ROWS, :] += left.astype(F32)
     out_ref[...] = sum_scr[...].astype(BF16)
 
 
@@ -334,7 +361,7 @@
             pltpu.VMEM((8, count * count), F32),
             pltpu.VMEM((chain, ROWS), F32),
         ),
-        in_specs=[pl.BlockSpec(memory_space=pl.ANY)] * 6,
+        in_specs=[pl.BlockSpec(memory_space=pltpu.HBM)] * 6,
     )(
         neighbours.T, edge_weight.T, fetch_block.T, fetch_count.reshape(1, -1), features, upstream
     )
@@ -358,44 +385,67 @@
     )(matrix, features, own, received, from_left, from_right, weight_one, weight_two)
     plane_parts = [parts[0]] + [in_plane(parts[v], v) for v in range(1, PLANE)]
 
-    across_rows = [PLANE * SLOT + HALO * (k in (1, groups - 1)) for k in range(groups)]
-    plane_rows = [groups * SLOT + HALO * (v in (1, 3)) for v in range(PLANE)]
-    own, *blocks, to_left, to_right = call(
-        functools.partial(back_kernel, count),
-        (
-            struct((ROWS, D), F32),
-            *[struct((rows, D), BF16) for rows in across_rows],
-            struct((HALO, D), BF16),
-            struct((HALO, D), BF16),
-        ),
-        (pltpu.VMEM((count, SLOT, D), BF16),),
+    bits = hop_bits(count)
+    carried = (
+        struct((count, SLOT, D), BF16),
+        struct((HALO, D), BF16),
+        struct((HALO, D), BF16),
+    )
+
+    def message(bit):
+        return struct((hop_rows(count, bit), D), BF16)
+
+    def swap(value, bit):
+        return lax.ppermute(value, "node", [(i, i ^ (1 << bit)) for i in range(count)])
+
+    def next_hop(at, got, held):
+        *held, out = call(
+            functools.partial(hop_kernel, count, bits[at - 1], bits[at]),
+            (*carried, message(bits[at])),
+        )(got, *held)
+        return out, held
+
+    own, *held, out = call(
+        functools.partial(back_kernel, count, bits[0]),
+        (struct((ROWS, D), F32), *carried, message(bits[0])),
     )(matrix, d_pre, weight_one)
-    blocks = [blocks[0]] + [across(blocks[k], k) for k in range(1, groups)]
-    plane_parts, blocks = lax.optimization_barrier((plane_parts, blocks))
+    plane_parts, got = lax.optimization_barrier((plane_parts, swap(out, bits[0])))
 
     sums = call(
         functools.partial(plane_sum_kernel, piece),
         (struct((piece, D), F32), *[struct((piece, D), BF16)] * (groups - 1)),
     )(*plane_parts)
-    blocks = call(
-        functools.partial(turn_kernel, count),
-        tuple(struct((rows, D), BF16) for rows in plane_rows),
-    )(*blocks, to_left, to_right)
-    sums, blocks = lax.optimization_barrier((sums, blocks))
+    out, held = next_hop(1, got, held)
+    sums, out = lax.optimization_barrier((sums, out))
     shared = [sums[0]] + [across(sums[k], k) for k in range(1, groups)]
-    blocks = [blocks[0]] + [in_plane(blocks[v], v) for v in range(1, PLANE)]
-    shared, blocks = lax.optimization_barrier((shared, blocks))
+    shared, got = lax.optimization_barrier((shared, swap(out, bits[1])))
+
     total = call(
         functools.partial(group_sum_kernel, 1.0 / math.sqrt(ROWS * count)),
         struct((piece, D), BF16),
     )(*shared)
+    out, held = next_hop(2, got, held)
+    total, out = lax.optimization_barrier((total, out))
+    pieces = [total] + [across(total, k) for k in range(1, groups)]
+    pieces, got = lax.optimization_barrier((pieces, swap(out, bits[2])))
+
+    chunk = jnp.concatenate(pieces, axis=0)
+    out, held = next_hop(3, got, held)
+    chunk, out = lax.optimization_barrier((chunk, out))
+    chunks = [chunk] + [in_plane(chunk, v) for v in range(1, PLANE)]
+    got = swap(out, bits[3])
+    for at in range(4, len(bits)):
+        out, held = next_hop(at, got, held)
+        got = swap(out, bits[at])
     d_features = call(
-        functools.partial(features_kernel, count),
+        functools.partial(features_kernel, count, bits[-1]),
         struct((ROWS, D), BF16),
-        (pltpu.VMEM((ROWS, D), F32), pltpu.VMEM((count, SLOT, D), BF16)),
-    )(matrix, own, *blocks)
-    chunk = jnp.concatenate([total] + [across(total, k) for k in range(1, groups)], axis=0)
-    chunks = [chunk] + [in_plane(chunk, v) for v in range(1, PLANE)]
+        (
+            pltpu.VMEM((ROWS, D), F32),
+            pltpu.VMEM((count, SLOT, D), BF16),
+            pltpu.VMEM((count, SLOT, D), BF16),
+        ),
+    )(matrix, own, got, *held)
     grad_two, grad_one = call(
         functools.partial(gather_kernel, count),
         (struct((D, D), BF16), struct((D, D), BF16)),

time: 80.4 us -> 79.6 us (0.990)
  waiting for transfers between devices: 33.6 us -> 31.9 us
    ppermute x0 -> x4, waiting for transfers between devices: none -> 9.95 us  [swap(): lax.ppermute(value, 'node', [(i, i ^ 1 << bit) for i in range(count)])]
    ppermute x9 -> x6, waiting for transfers between devices: 15.5 us -> 7.54 us  [across(): lax.ppermute(value, 'node', [(i, (i + k * PLANE) % count) for i in range(...]
    ppermute x9 -> x6, waiting for transfers between devices: 8.09 us -> 4.4 us  [in_plane(): return lax.ppermute(value, 'node', [(i, i ^ v) for i in range(count)])]
    ppermute x9 -> x6, starting transfers between devices: 10.3 us -> 7.11 us  [in_plane(): return lax.ppermute(value, 'node', [(i, i ^ v) for i in range(count)])]
    ppermute x0 -> x4, starting transfers between devices: none -> 2.73 us  [swap(): lax.ppermute(value, 'node', [(i, i ^ 1 << bit) for i in range(count)])]
    ppermute x9 -> x6, starting transfers between devices: 10.8 us -> 12 us  [across(): lax.ppermute(value, 'node', [(i, (i + k * PLANE) % count) for i in range(...]
  transfers between devices with their start and end apart: 21 -> 19, of which waited for: 15 -> 12; matrix products, arithmetic and copies ran while one was open for 0% -> 0% of each run, Pallas kernels for 2% -> 2%
where the time goes in v3:
time: 79.6 us; the launch traced here: 79.2 us
  starting transfers between devices  35.4 us (44%)
  waiting for transfers between devices  31.9 us (40%)
  Pallas kernels  7.11 us (9%)
  local copies, waits for them, and re-layouts  3.94 us (5%)
    ppermute x6, starting transfers between devices, across(): lax.ppermute(value, 'node', [(i, (i + k * PLANE) % count) for i in range(...  12 us
    ppermute x4, waiting for transfers between devices, swap(): lax.ppermute(value, 'node', [(i, i ^ 1 << bit) for i in range(count)])  9.95 us
    all_to_all x1, starting transfers between devices, shards(): lax.all_to_all(send, 'node', split_axis=0, concat_axis=0, tiled=True)  8.46 us
    ppermute x6, waiting for transfers between devices, across(): lax.ppermute(value, 'node', [(i, (i + k * PLANE) % count) for i in range(...  7.54 us
    ppermute x6, starting transfers between devices, in_plane(): return lax.ppermute(value, 'node', [(i, i ^ v) for i in range(count)])  7.11 us
    ppermute x1, waiting for transfers between devices, shards(): from_right = lax.ppermute(to_left, 'node', down)  4.9 us
    all_to_all x1, waiting for transfers between devices, shards(): lax.all_to_all(send, 'node', split_axis=0, concat_axis=0, tiled=True)  4.53 us
    ppermute x6, waiting for transfers between devices, in_plane(): return lax.ppermute(value, 'node', [(i, i ^ v) for i in range(count)])  4.4 us
  transfers between devices with their start and end apart: 19, of which 12 were waited for; matrix products, arithmetic and copies ran while one was open for 0% of the time, Pallas kernels for 2%

profile of v3, /device:TPU:0, one launch (start us, length us, event | category | flops | bytes accessed | tf_op | source)
XLA Modules:
  0.0 79.2 jit_solution(14290261662424039672)
XLA Ops:
  4.6 3.2 %shard_map.103 = (bf16[128,768]{1,0:T(8,128)(2,1)S(1)}, f32[128,512]{1,0:T(8,128)S(1)}, bf16[16,32,512]{2,1,0:T(8,128)(2,1)}, bf16[64,512]{1,0:T(8,128)(2,1)S(1)}, bf16[64,512]{1,0:T(8,128)(2,1)S(1)}) custom-call(s32[32,128]{1,0:T(8,128)S(1)} %bitcast.4, s32[32,128]{1,0:T(8,128)S(1)} %bitcast.5, s32[2,256]{1,0:T(2,128)S(1)} %bitcast.6, ...), custom_call_target="tpu_custom_call" | custom-call | tf_op jit(solution)/shard_map/pallas_call | solution.py:344
  7.8 8.5 %all-to-all-start = ((bf16[16,32,512]{2,1,0:T(8,128)(2,1)}), bf16[16,32,512]{2,1,0:T(8,128)(2,1)S(1)}, u32[]{:S(2)}, u32[]{:S(2)}) async-start(bf16[16,32,512]{2,1,0:T(8,128)(2,1)} %get-tuple-element.62), calls=%async_computation | async-start | bytes 1048576 | tf_op jit(solution)/shard_map/all_to_all | solution.py:370
  16.2 3.8 %collective-permute-start = (bf16[64,512]{1,0:T(8,128)(2,1)S(1)}, bf16[64,512]{1,0:T(8,128)(2,1)S(1)}, u32[]{:S(2)}, u32[]{:S(2)}) collective-permute-start(bf16[64,512]{1,0:T(8,128)(2,1)S(1)} %get-tuple-element.63), channel_id=1, source_target_pairs={{0,2},{2,4},{4,6},{6,8},{8,10},{10,12},{12,14},{14,16},{16,18},{18... | collective-permute-start | bytes 196616 | tf_op jit(solution)/shard_map/ppermute | solution.py:368
  20.1 1.3 %collective-permute-start.1 = (bf16[64,512]{1,0:T(8,128)(2,1)S(1)}, bf16[64,512]{1,0:T(8,128)(2,1)S(1)}, u32[]{:S(2)}, u32[]{:S(2)}) collective-permute-start(bf16[64,512]{1,0:T(8,128)(2,1)S(1)} %get-tuple-element.64), channel_id=1, source_target_pairs={{2,0},{4,2},{6,4},{8,6},{10,8},{12,10},{14,12},{16,14},{18,16},{20... | collective-permute-start | bytes 196616 | tf_op jit(solution)/shard_map/ppermute | solution.py:369
  21.9 4.9 %collective-permute-done.1.right_ref = bf16[64,512]{1,0:T(8,128)(2,1)S(1)} collective-permute-done((bf16[64,512]{1,0:T(8,128)(2,1)S(1)}, bf16[64,512]{1,0:T(8,128)(2,1)S(1)}, u32[]{:S(2)}, u32[]{:S(2)}) %collective-permute-start.1) | collective-permute-done | bytes 65568 | tf_op jit(solution)/shard_map/ppermute | solution.py:369
  26.8 4.5 %all-to-all-done.recv_ref = bf16[16,32,512]{2,1,0:T(8,128)(2,1)S(1)} async-done(((bf16[16,32,512]{2,1,0:T(8,128)(2,1)}), bf16[16,32,512]{2,1,0:T(8,128)(2,1)S(1)}, u32[]{:S(2)}, u32[]{:S(2)}) %all-to-all-start) | async-done | bytes 524320 | tf_op jit(solution)/shard_map/all_to_all | solution.py:370
  31.4 1.2 %shard_map.104 = (f32[256,512]{1,0:T(8,128)S(1)}, bf16[256,512]{1,0:T(8,128)(2,1)S(1)}, bf16[256,512]{1,0:T(8,128)(2,1)S(1)}, bf16[256,512]{1,0:T(8,128)(2,1)S(1)}, bf16[128,512]{1,0:T(8,128)(2,1)S(1)}) custom-call(bf16[128,768]{1,0:T(8,128)(2,1)S(1)} %get-tuple-element.60.mat_ref, bf16[128,512]{1,0:T(8,128)(2,1)S(1)} %copy-done.2, ...), custom_call_target="tpu_custom_call" | custom-call | tf_op jit(solution)/shard_map/pallas_call | solution.py:372
  33.2 1.3 %collective-permute-start.3 = (bf16[256,512]{1,0:T(8,128)(2,1)S(1)}, bf16[256,512]{1,0:T(8,128)(2,1)S(1)}, u32[]{:S(2)}, u32[]{:S(2)}) collective-permute-start(bf16[256,512]{1,0:T(8,128)(2,1)S(1)} %get-tuple-element.69), channel_id=1, source_target_pairs={{0,4},{2,6},{4,0},{6,2},{8,12},{10,14},{12,8},{14,10},{16,20},{18,... | collective-permute-start | bytes 786440 | tf_op jit(solution)/shard_map/ppermute | solution.py:337
  34.5 1.7 %collective-permute-start.4 = (bf16[256,512]{1,0:T(8,128)(2,1)S(1)}, bf16[256,512]{1,0:T(8,128)(2,1)S(1)}, u32[]{:S(2)}, u32[]{:S(2)}) collective-permute-start(bf16[256,512]{1,0:T(8,128)(2,1)S(1)} %get-tuple-element.70), channel_id=1, source_target_pairs={{0,6},{2,4},{4,2},{6,0},{8,14},{10,12},{12,10},{14,8},{16,22},{18,... | collective-permute-start | bytes 786440 | tf_op jit(solution)/shard_map/ppermute | solution.py:337
  36.7 1.3 %collective-permute-start.5 = (bf16[160,512]{1,0:T(8,128)(2,1)S(1)}, bf16[160,512]{1,0:T(8,128)(2,1)S(1)}, u32[]{:S(2)}, u32[]{:S(2)}) collective-permute-start(bf16[160,512]{1,0:T(8,128)(2,1)S(1)} %get-tuple-element.71), channel_id=1, source_target_pairs={{0,8},{2,10},{4,12},{6,14},{8,0},{10,2},{12,4},{14,6},{16,24},{18,... | collective-permute-start | bytes 491528 | tf_op jit(solution)/shard_map/ppermute | solution.py:399
  38.0 4.1 %collective-permute-done.5.got_ref = bf16[160,512]{1,0:T(8,128)(2,1)S(1)} collective-permute-done((bf16[160,512]{1,0:T(8,128)(2,1)S(1)}, bf16[160,512]{1,0:T(8,128)(2,1)S(1)}, u32[]{:S(2)}, u32[]{:S(2)}) %collective-permute-start.5) | collective-permute-done | bytes 163872 | tf_op jit(solution)/shard_map/ppermute | solution.py:399
  42.1 1.1 %collective-permute-done.3.refs_2_ = bf16[256,512]{1,0:T(8,128)(2,1)S(1)} collective-permute-done((bf16[256,512]{1,0:T(8,128)(2,1)S(1)}, bf16[256,512]{1,0:T(8,128)(2,1)S(1)}, u32[]{:S(2)}, u32[]{:S(2)}) %collective-permute-start.3) | collective-permute-done | bytes 262176 | tf_op jit(solution)/shard_map/ppermute | solution.py:337
  43.2 3.3 %collective-permute-done.4.refs_3_ = bf16[256,512]{1,0:T(8,128)(2,1)S(1)} collective-permute-done((bf16[256,512]{1,0:T(8,128)(2,1)S(1)}, bf16[256,512]{1,0:T(8,128)(2,1)S(1)}, u32[]{:S(2)}, u32[]{:S(2)}) %collective-permute-start.4) | collective-permute-done | bytes 262176 | tf_op jit(solution)/shard_map/ppermute | solution.py:337
  46.7 3.5 %collective-permute-start.6 = (bf16[64,512]{1,0:T(8,128)(2,1)S(1)}, bf16[64,512]{1,0:T(8,128)(2,1)S(1)}, u32[]{:S(2)}, u32[]{:S(2)}) collective-permute-start(bf16[64,512]{1,0:T(8,128)(2,1)S(1)} %get-tuple-element.86), channel_id=1, source_target_pairs={{0,8},{2,10},{4,12},{6,14},{8,16},{10,18},{12,20},{14,22},{16,24},... | collective-permute-start | bytes 196616 | tf_op jit(solution)/shard_map/ppermute | solution.py:340
  51.1 2.9 %collective-permute-start.8 = (bf16[64,512]{1,0:T(8,128)(2,1)S(1)}, bf16[64,512]{1,0:T(8,128)(2,1)S(1)}, u32[]{:S(2)}, u32[]{:S(2)}) collective-permute-start(bf16[64,512]{1,0:T(8,128)(2,1)S(1)} %get-tuple-element.88), channel_id=1, source_target_pairs={{0,24},{2,26},{4,28},{6,30},{8,0},{10,2},{12,4},{14,6},{16,8},{18,... | collective-permute-start | bytes 196616 | tf_op jit(solution)/shard_map/ppermute | solution.py:340
  54.0 1.5 %collective-permute-done.7.refs_2_ = bf16[64,512]{1,0:T(8,128)(2,1)S(1)} collective-permute-done((bf16[64,512]{1,0:T(8,128)(2,1)S(1)}, bf16[64,512]{1,0:T(8,128)(2,1)S(1)}, u32[]{:S(2)}, u32[]{:S(2)}) %collective-permute-start.7) | collective-permute-done | bytes 65568 | tf_op jit(solution)/shard_map/ppermute | solution.py:340
  56.4 4.2 %collective-permute-start.12 = (bf16[64,512]{1,0:T(8,128)(2,1)S(1)}, bf16[64,512]{1,0:T(8,128)(2,1)S(1)}, u32[]{:S(2)}, u32[]{:S(2)}) collective-permute-start(bf16[64,512]{1,0:T(8,128)(2,1)S(1)} %shard_map.108), channel_id=1, source_target_pairs={{0,24},{2,26},{4,28},{6,30},{8,0},{10,2},{12,4},{14,6},{16,8},{18,... | collective-permute-start | bytes 196616 | tf_op jit(solution)/shard_map/ppermute | solution.py:340
  61.1 1.3 %collective-permute-done.12 = bf16[64,512]{1,0:T(8,128)(2,1)S(1)} collective-permute-done((bf16[64,512]{1,0:T(8,128)(2,1)S(1)}, bf16[64,512]{1,0:T(8,128)(2,1)S(1)}, u32[]{:S(2)}, u32[]{:S(2)}) %collective-permute-start.12) | collective-permute-done | bytes 65568 | tf_op jit(solution)/shard_map/ppermute | solution.py:340
  62.4 3.3 %collective-permute-done.11 = bf16[64,512]{1,0:T(8,128)(2,1)S(1)} collective-permute-done((bf16[64,512]{1,0:T(8,128)(2,1)S(1)}, bf16[64,512]{1,0:T(8,128)(2,1)S(1)}, u32[]{:S(2)}, u32[]{:S(2)}) %collective-permute-start.11) | collective-permute-done | bytes 65568 | tf_op jit(solution)/shard_map/ppermute | solution.py:340
  66.7 1.6 %collective-permute-start.17 = (bf16[256,512]{1,0:T(8,128)(2,1)S(1)}, bf16[256,512]{1,0:T(8,128)(2,1)S(1)}, u32[]{:S(2)}, u32[]{:S(2)}) collective-permute-start(bf16[256,512]{1,0:T(8,128)(2,1)S(1)} %pad_maximum_fusion.refs_0_), channel_id=1, source_target_pairs={{0,6},{2,4},{4,2},{6,0},{8,14},{10,12},{12,10},{14,8},{16,22},{18,... | collective-permute-start | bytes 786440 | tf_op jit(solution)/shard_map/ppermute | solution.py:337
  68.3 1.4 %collective-permute-start.16 = (bf16[256,512]{1,0:T(8,128)(2,1)S(1)}, bf16[256,512]{1,0:T(8,128)(2,1)S(1)}, u32[]{:S(2)}, u32[]{:S(2)}) collective-permute-start(bf16[256,512]{1,0:T(8,128)(2,1)S(1)} %pad_maximum_fusion.refs_0_), channel_id=1, source_target_pairs={{0,4},{2,6},{4,0},{6,2},{8,12},{10,14},{12,8},{14,10},{16,20},{18,... | collective-permute-start | bytes 786440 | tf_op jit(solution)/shard_map/ppermute | solution.py:337
  70.2 1.1 %collective-permute-start.14 = (bf16[160,512]{1,0:T(8,128)(2,1)S(1)}, bf16[160,512]{1,0:T(8,128)(2,1)S(1)}, u32[]{:S(2)}, u32[]{:S(2)}) collective-permute-start(bf16[160,512]{1,0:T(8,128)(2,1)S(1)} %get-tuple-element.110), channel_id=1, source_target_pairs={{0,16},{2,18},{4,20},{6,22},{8,24},{10,26},{12,28},{14,30},{16,0},... | collective-permute-start | bytes 491528 | tf_op jit(solution)/shard_map/ppermute | solution.py:399
  71.3 5.9 %collective-permute-done.14.got_ref = bf16[160,512]{1,0:T(8,128)(2,1)S(1)} collective-permute-done((bf16[160,512]{1,0:T(8,128)(2,1)S(1)}, bf16[160,512]{1,0:T(8,128)(2,1)S(1)}, u32[]{:S(2)}, u32[]{:S(2)}) %collective-permute-start.14) | collective-permute-done | bytes 163872 | tf_op jit(solution)/shard_map/ppermute | solution.py:399
  78.1 1.1 %shard_map.112 = (bf16[512,512]{1,0:T(8,128)(2,1)}, bf16[512,512]{1,0:T(8,128)(2,1)}) custom-call(bf16[256,512]{1,0:T(8,128)(2,1)S(1)} %pad_maximum_fusion.refs_0_, bf16[256,512]{1,0:T(8,128)(2,1)S(1)} %collective-permute-done.15.refs_1_, bf16[256,512]{1,0:T(8,128)(2,1)S(1)} %collective-permute-done.16.refs_2_, ...), custom_call_target="tpu_custom_call" | custom-call | tf_op jit(solution)/shard_map/pallas_call | solution.py:449
  (43 shorter events, 10.6 us)
Async XLA Ops:
  1.3 0.9 %copy-start.1 = (bf16[128,512]{1,0:T(8,128)(2,1)S(1)}, bf16[128,512]{1,0:T(8,128)(2,1)}, u32[]{:S(2)}) copy-start(bf16[128,512]{1,0:T(8,128)(2,1)} %feat_ref.1) | copy-start | bytes 393220
  2.2 0.9 %copy-start.4 = (bf16[128,512]{1,0:T(8,128)(2,1)S(1)}, bf16[128,512]{1,0:T(8,128)(2,1)}, u32[]{:S(2)}) copy-start(bf16[128,512]{1,0:T(8,128)(2,1)} %up_hbm.1) | copy-start | bytes 393220
  4.6 26.8 %copy-start.3 = (bf16[512,512]{1,0:T(8,128)(2,1)S(1)}, bf16[512,512]{1,0:T(8,128)(2,1)}, u32[]{:S(2)}) copy-start(bf16[512,512]{1,0:T(8,128)(2,1)} %w_two_ref.1) | copy-start | bytes 1572868
  7.7 23.6 %copy-start = (bf16[512,512]{1,0:T(8,128)(2,1)S(1)}, bf16[512,512]{1,0:T(8,128)(2,1)}, u32[]{:S(2)}) copy-start(bf16[512,512]{1,0:T(8,128)(2,1)} %w_one_ref.3) | copy-start | bytes 1572868
  7.8 23.6 %copy-start.2 = (bf16[128,512]{1,0:T(8,128)(2,1)S(1)}, bf16[128,512]{1,0:T(8,128)(2,1)}, u32[]{:S(2)}) copy-start(bf16[128,512]{1,0:T(8,128)(2,1)} %feat_ref.1) | copy-start | bytes 393220
  7.8 23.6 %all-to-all-start = ((bf16[16,32,512]{2,1,0:T(8,128)(2,1)}), bf16[16,32,512]{2,1,0:T(8,128)(2,1)S(1)}, u32[]{:S(2)}, u32[]{:S(2)}) async-start(bf16[16,32,512]{2,1,0:T(8,128)(2,1)} %get-tuple-element.62), calls=%async_computation | async-start | bytes 1048576 | tf_op jit(solution)/shard_map/all_to_all | solution.py:370
  16.2 5.7 %collective-permute-start = (bf16[64,512]{1,0:T(8,128)(2,1)S(1)}, bf16[64,512]{1,0:T(8,128)(2,1)S(1)}, u32[]{:S(2)}, u32[]{:S(2)}) collective-permute-start(bf16[64,512]{1,0:T(8,128)(2,1)S(1)} %get-tuple-element.63), channel_id=1, source_target_pairs={{0,2},{2,4},{4,6},{6,8},{8,10},{10,12},{12,14},{14,16},{16,18},{18... | collective-permute-start | bytes 196616 | tf_op jit(solution)/shard_map/ppermute | solution.py:368
  20.1 6.8 %collective-permute-start.1 = (bf16[64,512]{1,0:T(8,128)(2,1)S(1)}, bf16[64,512]{1,0:T(8,128)(2,1)S(1)}, u32[]{:S(2)}, u32[]{:S(2)}) collective-permute-start(bf16[64,512]{1,0:T(8,128)(2,1)S(1)} %get-tuple-element.64), channel_id=1, source_target_pairs={{2,0},{4,2},{6,4},{8,6},{10,8},{12,10},{14,12},{16,14},{18,16},{20... | collective-permute-start | bytes 196616 | tf_op jit(solution)/shard_map/ppermute | solution.py:369
  32.6 9.5 %collective-permute-start.2 = (bf16[256,512]{1,0:T(8,128)(2,1)S(1)}, bf16[256,512]{1,0:T(8,128)(2,1)S(1)}, u32[]{:S(2)}, u32[]{:S(2)}) collective-permute-start(bf16[256,512]{1,0:T(8,128)(2,1)S(1)} %get-tuple-element.68), channel_id=1, source_target_pairs={{0,2},{2,0},{4,6},{6,4},{8,10},{10,8},{12,14},{14,12},{16,18},{18,... | collective-permute-start | bytes 786440 | tf_op jit(solution)/shard_map/ppermute | solution.py:337
  33.2 10.0 %collective-permute-start.3 = (bf16[256,512]{1,0:T(8,128)(2,1)S(1)}, bf16[256,512]{1,0:T(8,128)(2,1)S(1)}, u32[]{:S(2)}, u32[]{:S(2)}) collective-permute-start(bf16[256,512]{1,0:T(8,128)(2,1)S(1)} %get-tuple-element.69), channel_id=1, source_target_pairs={{0,4},{2,6},{4,0},{6,2},{8,12},{10,14},{12,8},{14,10},{16,20},{18,... | collective-permute-start | bytes 786440 | tf_op jit(solution)/shard_map/ppermute | solution.py:337
  34.5 12.0 %collective-permute-start.4 = (bf16[256,512]{1,0:T(8,128)(2,1)S(1)}, bf16[256,512]{1,0:T(8,128)(2,1)S(1)}, u32[]{:S(2)}, u32[]{:S(2)}) collective-permute-start(bf16[256,512]{1,0:T(8,128)(2,1)S(1)} %get-tuple-element.70), channel_id=1, source_target_pairs={{0,6},{2,4},{4,2},{6,0},{8,14},{10,12},{12,10},{14,8},{16,22},{18,... | collective-permute-start | bytes 786440 | tf_op jit(solution)/shard_map/ppermute | solution.py:337
  36.7 5.4 %collective-permute-start.5 = (bf16[160,512]{1,0:T(8,128)(2,1)S(1)}, bf16[160,512]{1,0:T(8,128)(2,1)S(1)}, u32[]{:S(2)}, u32[]{:S(2)}) collective-permute-start(bf16[160,512]{1,0:T(8,128)(2,1)S(1)} %get-tuple-element.71), channel_id=1, source_target_pairs={{0,8},{2,10},{4,12},{6,14},{8,0},{10,2},{12,4},{14,6},{16,24},{18,... | collective-permute-start | bytes 491528 | tf_op jit(solution)/shard_map/ppermute | solution.py:399
  46.6 9.4 %collective-permute-start.9 = (bf16[192,512]{1,0:T(8,128)(2,1)S(1)}, bf16[192,512]{1,0:T(8,128)(2,1)S(1)}, u32[]{:S(2)}, u32[]{:S(2)}) collective-permute-start(bf16[192,512]{1,0:T(8,128)(2,1)S(1)} %get-tuple-element.89), channel_id=1, source_target_pairs={{0,2},{2,0},{4,6},{6,4},{8,10},{10,8},{12,14},{14,12},{16,18},{18,... | collective-permute-start | bytes 589832 | tf_op jit(solution)/shard_map/ppermute | solution.py:399
  46.7 7.3 %collective-permute-start.6 = (bf16[64,512]{1,0:T(8,128)(2,1)S(1)}, bf16[64,512]{1,0:T(8,128)(2,1)S(1)}, u32[]{:S(2)}, u32[]{:S(2)}) collective-permute-start(bf16[64,512]{1,0:T(8,128)(2,1)S(1)} %get-tuple-element.86), channel_id=1, source_target_pairs={{0,8},{2,10},{4,12},{6,14},{8,16},{10,18},{12,20},{14,22},{16,24},... | collective-permute-start | bytes 196616 | tf_op jit(solution)/shard_map/ppermute | solution.py:340
  50.2 5.3 %collective-permute-start.7 = (bf16[64,512]{1,0:T(8,128)(2,1)S(1)}, bf16[64,512]{1,0:T(8,128)(2,1)S(1)}, u32[]{:S(2)}, u32[]{:S(2)}) collective-permute-start(bf16[64,512]{1,0:T(8,128)(2,1)S(1)} %get-tuple-element.87), channel_id=1, source_target_pairs={{0,16},{2,18},{4,20},{6,22},{8,24},{10,26},{12,28},{14,30},{16,0},... | collective-permute-start | bytes 196616 | tf_op jit(solution)/shard_map/ppermute | solution.py:340
  51.1 5.0 %collective-permute-start.8 = (bf16[64,512]{1,0:T(8,128)(2,1)S(1)}, bf16[64,512]{1,0:T(8,128)(2,1)S(1)}, u32[]{:S(2)}, u32[]{:S(2)}) collective-permute-start(bf16[64,512]{1,0:T(8,128)(2,1)S(1)} %get-tuple-element.88), channel_id=1, source_target_pairs={{0,24},{2,26},{4,28},{6,30},{8,0},{10,2},{12,4},{14,6},{16,8},{18,... | collective-permute-start | bytes 196616 | tf_op jit(solution)/shard_map/ppermute | solution.py:340
  56.1 10.4 %collective-permute-start.13 = (bf16[160,512]{1,0:T(8,128)(2,1)S(1)}, bf16[160,512]{1,0:T(8,128)(2,1)S(1)}, u32[]{:S(2)}, u32[]{:S(2)}) collective-permute-start(bf16[160,512]{1,0:T(8,128)(2,1)S(1)} %get-tuple-element.100), channel_id=1, source_target_pairs={{0,4},{2,6},{4,0},{6,2},{8,12},{10,14},{12,8},{14,10},{16,20},{18,... | collective-permute-start | bytes 491528 | tf_op jit(solution)/shard_map/ppermute | solution.py:399
  56.4 6.1 %collective-permute-start.12 = (bf16[64,512]{1,0:T(8,128)(2,1)S(1)}, bf16[64,512]{1,0:T(8,128)(2,1)S(1)}, u32[]{:S(2)}, u32[]{:S(2)}) collective-permute-start(bf16[64,512]{1,0:T(8,128)(2,1)S(1)} %shard_map.108), channel_id=1, source_target_pairs={{0,24},{2,26},{4,28},{6,30},{8,0},{10,2},{12,4},{14,6},{16,8},{18,... | collective-permute-start | bytes 196616 | tf_op jit(solution)/shard_map/ppermute | solution.py:340
  60.5 5.2 %collective-permute-start.11 = (bf16[64,512]{1,0:T(8,128)(2,1)S(1)}, bf16[64,512]{1,0:T(8,128)(2,1)S(1)}, u32[]{:S(2)}, u32[]{:S(2)}) collective-permute-start(bf16[64,512]{1,0:T(8,128)(2,1)S(1)} %shard_map.108), channel_id=1, source_target_pairs={{0,16},{2,18},{4,20},{6,22},{8,24},{10,26},{12,28},{14,30},{16,0},... | collective-permute-start | bytes 196616 | tf_op jit(solution)/shard_map/ppermute | solution.py:340
  60.5 6.1 %collective-permute-start.10 = (bf16[64,512]{1,0:T(8,128)(2,1)S(1)}, bf16[64,512]{1,0:T(8,128)(2,1)S(1)}, u32[]{:S(2)}, u32[]{:S(2)}) collective-permute-start(bf16[64,512]{1,0:T(8,128)(2,1)S(1)} %shard_map.108), channel_id=1, source_target_pairs={{0,8},{2,10},{4,12},{6,14},{8,16},{10,18},{12,20},{14,22},{16,24},... | collective-permute-start | bytes 196616 | tf_op jit(solution)/shard_map/ppermute | solution.py:340
  66.7 11.4 %collective-permute-start.17 = (bf16[256,512]{1,0:T(8,128)(2,1)S(1)}, bf16[256,512]{1,0:T(8,128)(2,1)S(1)}, u32[]{:S(2)}, u32[]{:S(2)}) collective-permute-start(bf16[256,512]{1,0:T(8,128)(2,1)S(1)} %pad_maximum_fusion.refs_0_), channel_id=1, source_target_pairs={{0,6},{2,4},{4,2},{6,0},{8,14},{10,12},{12,10},{14,8},{16,22},{18,... | collective-permute-start | bytes 786440 | tf_op jit(solution)/shard_map/ppermute | solution.py:337
  68.3 9.8 %collective-permute-start.16 = (bf16[256,512]{1,0:T(8,128)(2,1)S(1)}, bf16[256,512]{1,0:T(8,128)(2,1)S(1)}, u32[]{:S(2)}, u32[]{:S(2)}) collective-permute-start(bf16[256,512]{1,0:T(8,128)(2,1)S(1)} %pad_maximum_fusion.refs_0_), channel_id=1, source_target_pairs={{0,4},{2,6},{4,0},{6,2},{8,12},{10,14},{12,8},{14,10},{16,20},{18,... | collective-permute-start | bytes 786440 | tf_op jit(solution)/shard_map/ppermute | solution.py:337
  69.6 8.5 %collective-permute-start.15 = (bf16[256,512]{1,0:T(8,128)(2,1)S(1)}, bf16[256,512]{1,0:T(8,128)(2,1)S(1)}, u32[]{:S(2)}, u32[]{:S(2)}) collective-permute-start(bf16[256,512]{1,0:T(8,128)(2,1)S(1)} %pad_maximum_fusion.refs_0_), channel_id=1, source_target_pairs={{0,2},{2,0},{4,6},{6,4},{8,10},{10,8},{12,14},{14,12},{16,18},{18,... | collective-permute-start | bytes 786440 | tf_op jit(solution)/shard_map/ppermute | solution.py:337
  70.2 7.0 %collective-permute-start.14 = (bf16[160,512]{1,0:T(8,128)(2,1)S(1)}, bf16[160,512]{1,0:T(8,128)(2,1)S(1)}, u32[]{:S(2)}, u32[]{:S(2)}) collective-permute-start(bf16[160,512]{1,0:T(8,128)(2,1)S(1)} %get-tuple-element.110), channel_id=1, source_target_pairs={{0,16},{2,18},{4,20},{6,22},{8,24},{10,26},{12,28},{14,30},{16,0},... | collective-permute-start | bytes 491528 | tf_op jit(solution)/shard_map/ppermute | solution.py:399
  (4 other events, 2.8 us)

commit v4 on v3

--- a/solution.py
+++ b/solution.py
@@ -363,7 +363,13 @@
         ),
         in_specs=[pl.BlockSpec(memory_space=pltpu.HBM)] * 6,
     )(
-        neighbours.T, edge_weight.T, fetch_block.T, fetch_count.reshape(1, -1), features, upstream
+        *(
+            pltpu.with_memory_space_constraint(value, pltpu.HBM)
+            for value in (
+                neighbours.T, edge_weight.T, fetch_block.T, fetch_count.reshape(1, -1),
+                features, upstream,
+            )
+        )
     )
     from_left = lax.ppermute(to_right, "node", up)
     from_right = lax.ppermute(to_left, "node", down)

time: 79.6 us -> 75.9 us (0.954)
  local copies, waits for them, and re-layouts: 3.94 us -> 0.02 us
    unnamed x18 -> x6, local copies, waits for them, and re-layouts: 3.94 us -> 0.02 us
where the time goes in v4:
time: 75.9 us; the launch traced here: 75.6 us
  starting transfers between devices  35.4 us (47%)
  waiting for transfers between devices  31.9 us (42%)
  Pallas kernels  7.49 us (10%)
  between operations  0.77 us (1%)
    ppermute x6, starting transfers between devices, across(): lax.ppermute(value, 'node', [(i, (i + k * PLANE) % count) for i in range(...  12 us
    ppermute x4, waiting for transfers between devices, swap(): lax.ppermute(value, 'node', [(i, i ^ 1 << bit) for i in range(count)])  9.95 us
    all_to_all x1, starting transfers between devices, shards(): lax.all_to_all(send, 'node', split_axis=0, concat_axis=0, tiled=True)  8.46 us
    ppermute x6, waiting for transfers between devices, across(): lax.ppermute(value, 'node', [(i, (i + k * PLANE) % count) for i in range(...  7.54 us
    ppermute x6, starting transfers between devices, in_plane(): return lax.ppermute(value, 'node', [(i, i ^ v) for i in range(count)])  7.11 us
    ppermute x1, waiting for transfers between devices, shards(): from_right = lax.ppermute(to_left, 'node', down)  4.9 us
    all_to_all x1, waiting for transfers between devices, shards(): lax.all_to_all(send, 'node', split_axis=0, concat_axis=0, tiled=True)  4.53 us
    ppermute x6, waiting for transfers between devices, in_plane(): return lax.ppermute(value, 'node', [(i, i ^ v) for i in range(count)])  4.42 us
  transfers between devices with their start and end apart: 19, of which 12 were waited for; matrix products, arithmetic and copies ran while one was open for 0% of the time, Pallas kernels for 2%

profile of v4, /device:TPU:0, one launch (start us, length us, event | category | flops | bytes accessed | tf_op | source)
XLA Modules:
  0.0 75.6 jit_solution(7114327549247835589)
XLA Ops:
  0.6 3.5 %shard_map.103 = (bf16[128,768]{1,0:T(8,128)(2,1)S(1)}, f32[128,512]{1,0:T(8,128)S(1)}, bf16[16,32,512]{2,1,0:T(8,128)(2,1)}, bf16[64,512]{1,0:T(8,128)(2,1)S(1)}, bf16[64,512]{1,0:T(8,128)(2,1)S(1)}) custom-call(s32[32,128]{1,0:T(8,128)} %bitcast.4, s32[32,128]{1,0:T(8,128)} %bitcast.5, s32[2,256]{1,0:T(2,128)} %bitcast.6, s32[1,256]{1,0:T(1,128)} %bitcast.7, ...), custom_call_target="tpu_custom_call" | custom-call | tf_op jit(solution)/shard_map/pallas_call | solution.py:344
  4.2 8.5 %all-to-all-start = ((bf16[16,32,512]{2,1,0:T(8,128)(2,1)}), bf16[16,32,512]{2,1,0:T(8,128)(2,1)S(1)}, u32[]{:S(2)}, u32[]{:S(2)}) async-start(bf16[16,32,512]{2,1,0:T(8,128)(2,1)} %get-tuple-element.62), calls=%async_computation | async-start | bytes 1048576 | tf_op jit(solution)/shard_map/all_to_all | solution.py:376
  12.7 3.8 %collective-permute-start = (bf16[64,512]{1,0:T(8,128)(2,1)S(1)}, bf16[64,512]{1,0:T(8,128)(2,1)S(1)}, u32[]{:S(2)}, u32[]{:S(2)}) collective-permute-start(bf16[64,512]{1,0:T(8,128)(2,1)S(1)} %get-tuple-element.63), channel_id=1, source_target_pairs={{0,2},{2,4},{4,6},{6,8},{8,10},{10,12},{12,14},{14,16},{16,18},{18... | collective-permute-start | bytes 196616 | tf_op jit(solution)/shard_map/ppermute | solution.py:374
  16.5 1.3 %collective-permute-start.1 = (bf16[64,512]{1,0:T(8,128)(2,1)S(1)}, bf16[64,512]{1,0:T(8,128)(2,1)S(1)}, u32[]{:S(2)}, u32[]{:S(2)}) collective-permute-start(bf16[64,512]{1,0:T(8,128)(2,1)S(1)} %get-tuple-element.64), channel_id=1, source_target_pairs={{2,0},{4,2},{6,4},{8,6},{10,8},{12,10},{14,12},{16,14},{18,16},{20... | collective-permute-start | bytes 196616 | tf_op jit(solution)/shard_map/ppermute | solution.py:375
  18.4 4.9 %collective-permute-done.1.right_ref = bf16[64,512]{1,0:T(8,128)(2,1)S(1)} collective-permute-done((bf16[64,512]{1,0:T(8,128)(2,1)S(1)}, bf16[64,512]{1,0:T(8,128)(2,1)S(1)}, u32[]{:S(2)}, u32[]{:S(2)}) %collective-permute-start.1) | collective-permute-done | bytes 65568 | tf_op jit(solution)/shard_map/ppermute | solution.py:375
  23.3 4.5 %all-to-all-done.recv_ref = bf16[16,32,512]{2,1,0:T(8,128)(2,1)S(1)} async-done(((bf16[16,32,512]{2,1,0:T(8,128)(2,1)}), bf16[16,32,512]{2,1,0:T(8,128)(2,1)S(1)}, u32[]{:S(2)}, u32[]{:S(2)}) %all-to-all-start) | async-done | bytes 524320 | tf_op jit(solution)/shard_map/all_to_all | solution.py:376
  27.8 1.2 %shard_map.104 = (f32[256,512]{1,0:T(8,128)S(1)}, bf16[256,512]{1,0:T(8,128)(2,1)S(1)}, bf16[256,512]{1,0:T(8,128)(2,1)S(1)}, bf16[256,512]{1,0:T(8,128)(2,1)S(1)}, bf16[128,512]{1,0:T(8,128)(2,1)S(1)}) custom-call(bf16[128,768]{1,0:T(8,128)(2,1)S(1)} %get-tuple-element.60.mat_ref, bf16[128,512]{1,0:T(8,128)(2,1)S(1)} %copy-done.1, ...), custom_call_target="tpu_custom_call" | custom-call | tf_op jit(solution)/shard_map/pallas_call | solution.py:378
  29.6 1.3 %collective-permute-start.3 = (bf16[256,512]{1,0:T(8,128)(2,1)S(1)}, bf16[256,512]{1,0:T(8,128)(2,1)S(1)}, u32[]{:S(2)}, u32[]{:S(2)}) collective-permute-start(bf16[256,512]{1,0:T(8,128)(2,1)S(1)} %get-tuple-element.69), channel_id=1, source_target_pairs={{0,4},{2,6},{4,0},{6,2},{8,12},{10,14},{12,8},{14,10},{16,20},{18,... | collective-permute-start | bytes 786440 | tf_op jit(solution)/shard_map/ppermute | solution.py:337
  30.9 1.7 %collective-permute-start.4 = (bf16[256,512]{1,0:T(8,128)(2,1)S(1)}, bf16[256,512]{1,0:T(8,128)(2,1)S(1)}, u32[]{:S(2)}, u32[]{:S(2)}) collective-permute-start(bf16[256,512]{1,0:T(8,128)(2,1)S(1)} %get-tuple-element.70), channel_id=1, source_target_pairs={{0,6},{2,4},{4,2},{6,0},{8,14},{10,12},{12,10},{14,8},{16,22},{18,... | collective-permute-start | bytes 786440 | tf_op jit(solution)/shard_map/ppermute | solution.py:337
  33.1 1.3 %collective-permute-start.5 = (bf16[160,512]{1,0:T(8,128)(2,1)S(1)}, bf16[160,512]{1,0:T(8,128)(2,1)S(1)}, u32[]{:S(2)}, u32[]{:S(2)}) collective-permute-start(bf16[160,512]{1,0:T(8,128)(2,1)S(1)} %get-tuple-element.71), channel_id=1, source_target_pairs={{0,8},{2,10},{4,12},{6,14},{8,0},{10,2},{12,4},{14,6},{16,24},{18,... | collective-permute-start | bytes 491528 | tf_op jit(solution)/shard_map/ppermute | solution.py:405
  34.5 4.1 %collective-permute-done.5.got_ref = bf16[160,512]{1,0:T(8,128)(2,1)S(1)} collective-permute-done((bf16[160,512]{1,0:T(8,128)(2,1)S(1)}, bf16[160,512]{1,0:T(8,128)(2,1)S(1)}, u32[]{:S(2)}, u32[]{:S(2)}) %collective-permute-start.5) | collective-permute-done | bytes 163872 | tf_op jit(solution)/shard_map/ppermute | solution.py:405
  38.5 1.1 %collective-permute-done.3.refs_2_ = bf16[256,512]{1,0:T(8,128)(2,1)S(1)} collective-permute-done((bf16[256,512]{1,0:T(8,128)(2,1)S(1)}, bf16[256,512]{1,0:T(8,128)(2,1)S(1)}, u32[]{:S(2)}, u32[]{:S(2)}) %collective-permute-start.3) | collective-permute-done | bytes 262176 | tf_op jit(solution)/shard_map/ppermute | solution.py:337
  39.6 3.3 %collective-permute-done.4.refs_3_ = bf16[256,512]{1,0:T(8,128)(2,1)S(1)} collective-permute-done((bf16[256,512]{1,0:T(8,128)(2,1)S(1)}, bf16[256,512]{1,0:T(8,128)(2,1)S(1)}, u32[]{:S(2)}, u32[]{:S(2)}) %collective-permute-start.4) | collective-permute-done | bytes 262176 | tf_op jit(solution)/shard_map/ppermute | solution.py:337
  43.2 3.5 %collective-permute-start.6 = (bf16[64,512]{1,0:T(8,128)(2,1)S(1)}, bf16[64,512]{1,0:T(8,128)(2,1)S(1)}, u32[]{:S(2)}, u32[]{:S(2)}) collective-permute-start(bf16[64,512]{1,0:T(8,128)(2,1)S(1)} %get-tuple-element.86), channel_id=1, source_target_pairs={{0,8},{2,10},{4,12},{6,14},{8,16},{10,18},{12,20},{14,22},{16,24},... | collective-permute-start | bytes 196616 | tf_op jit(solution)/shard_map/ppermute | solution.py:340
  47.5 2.9 %collective-permute-start.8 = (bf16[64,512]{1,0:T(8,128)(2,1)S(1)}, bf16[64,512]{1,0:T(8,128)(2,1)S(1)}, u32[]{:S(2)}, u32[]{:S(2)}) collective-permute-start(bf16[64,512]{1,0:T(8,128)(2,1)S(1)} %get-tuple-element.88), channel_id=1, source_target_pairs={{0,24},{2,26},{4,28},{6,30},{8,0},{10,2},{12,4},{14,6},{16,8},{18,... | collective-permute-start | bytes 196616 | tf_op jit(solution)/shard_map/ppermute | solution.py:340
  50.5 1.5 %collective-permute-done.7.refs_2_ = bf16[64,512]{1,0:T(8,128)(2,1)S(1)} collective-permute-done((bf16[64,512]{1,0:T(8,128)(2,1)S(1)}, bf16[64,512]{1,0:T(8,128)(2,1)S(1)}, u32[]{:S(2)}, u32[]{:S(2)}) %collective-permute-start.7) | collective-permute-done | bytes 65568 | tf_op jit(solution)/shard_map/ppermute | solution.py:340
  52.8 4.2 %collective-permute-start.12 = (bf16[64,512]{1,0:T(8,128)(2,1)S(1)}, bf16[64,512]{1,0:T(8,128)(2,1)S(1)}, u32[]{:S(2)}, u32[]{:S(2)}) collective-permute-start(bf16[64,512]{1,0:T(8,128)(2,1)S(1)} %shard_map.108), channel_id=1, source_target_pairs={{0,24},{2,26},{4,28},{6,30},{8,0},{10,2},{12,4},{14,6},{16,8},{18,... | collective-permute-start | bytes 196616 | tf_op jit(solution)/shard_map/ppermute | solution.py:340
  57.5 1.3 %collective-permute-done.12 = bf16[64,512]{1,0:T(8,128)(2,1)S(1)} collective-permute-done((bf16[64,512]{1,0:T(8,128)(2,1)S(1)}, bf16[64,512]{1,0:T(8,128)(2,1)S(1)}, u32[]{:S(2)}, u32[]{:S(2)}) %collective-permute-start.12) | collective-permute-done | bytes 65568 | tf_op jit(solution)/shard_map/ppermute | solution.py:340
  58.9 3.3 %collective-permute-done.11 = bf16[64,512]{1,0:T(8,128)(2,1)S(1)} collective-permute-done((bf16[64,512]{1,0:T(8,128)(2,1)S(1)}, bf16[64,512]{1,0:T(8,128)(2,1)S(1)}, u32[]{:S(2)}, u32[]{:S(2)}) %collective-permute-start.11) | collective-permute-done | bytes 65568 | tf_op jit(solution)/shard_map/ppermute | solution.py:340
  63.1 1.6 %collective-permute-start.17 = (bf16[256,512]{1,0:T(8,128)(2,1)S(1)}, bf16[256,512]{1,0:T(8,128)(2,1)S(1)}, u32[]{:S(2)}, u32[]{:S(2)}) collective-permute-start(bf16[256,512]{1,0:T(8,128)(2,1)S(1)} %pad_maximum_fusion.refs_0_), channel_id=1, source_target_pairs={{0,6},{2,4},{4,2},{6,0},{8,14},{10,12},{12,10},{14,8},{16,22},{18,... | collective-permute-start | bytes 786440 | tf_op jit(solution)/shard_map/ppermute | solution.py:337
  64.7 1.4 %collective-permute-start.16 = (bf16[256,512]{1,0:T(8,128)(2,1)S(1)}, bf16[256,512]{1,0:T(8,128)(2,1)S(1)}, u32[]{:S(2)}, u32[]{:S(2)}) collective-permute-start(bf16[256,512]{1,0:T(8,128)(2,1)S(1)} %pad_maximum_fusion.refs_0_), channel_id=1, source_target_pairs={{0,4},{2,6},{4,0},{6,2},{8,12},{10,14},{12,8},{14,10},{16,20},{18,... | collective-permute-start | bytes 786440 | tf_op jit(solution)/shard_map/ppermute | solution.py:337
  66.7 1.1 %collective-permute-start.14 = (bf16[160,512]{1,0:T(8,128)(2,1)S(1)}, bf16[160,512]{1,0:T(8,128)(2,1)S(1)}, u32[]{:S(2)}, u32[]{:S(2)}) collective-permute-start(bf16[160,512]{1,0:T(8,128)(2,1)S(1)} %get-tuple-element.110), channel_id=1, source_target_pairs={{0,16},{2,18},{4,20},{6,22},{8,24},{10,26},{12,28},{14,30},{16,0},... | collective-permute-start | bytes 491528 | tf_op jit(solution)/shard_map/ppermute | solution.py:405
  67.8 5.9 %collective-permute-done.14.got_ref = bf16[160,512]{1,0:T(8,128)(2,1)S(1)} collective-permute-done((bf16[160,512]{1,0:T(8,128)(2,1)S(1)}, bf16[160,512]{1,0:T(8,128)(2,1)S(1)}, u32[]{:S(2)}, u32[]{:S(2)}) %collective-permute-start.14) | collective-permute-done | bytes 163872 | tf_op jit(solution)/shard_map/ppermute | solution.py:405
  74.6 1.1 %shard_map.112 = (bf16[512,512]{1,0:T(8,128)(2,1)}, bf16[512,512]{1,0:T(8,128)(2,1)}) custom-call(bf16[256,512]{1,0:T(8,128)(2,1)S(1)} %pad_maximum_fusion.refs_0_, bf16[256,512]{1,0:T(8,128)(2,1)S(1)} %collective-permute-done.15.refs_1_, bf16[256,512]{1,0:T(8,128)(2,1)S(1)} %collective-permute-done.16.refs_2_, ...), custom_call_target="tpu_custom_call" | custom-call | tf_op jit(solution)/shard_map/pallas_call | solution.py:455
  (31 shorter events, 6.7 us)
Async XLA Ops:
  0.6 27.2 %copy-start.2 = (bf16[512,512]{1,0:T(8,128)(2,1)S(1)}, bf16[512,512]{1,0:T(8,128)(2,1)}, u32[]{:S(2)}) copy-start(bf16[512,512]{1,0:T(8,128)(2,1)} %w_two_ref.1) | copy-start | bytes 1572868
  4.2 23.6 %copy-start = (bf16[512,512]{1,0:T(8,128)(2,1)S(1)}, bf16[512,512]{1,0:T(8,128)(2,1)}, u32[]{:S(2)}) copy-start(bf16[512,512]{1,0:T(8,128)(2,1)} %w_one_ref.3) | copy-start | bytes 1572868
  4.2 23.6 %copy-start.1 = (bf16[128,512]{1,0:T(8,128)(2,1)S(1)}, bf16[128,512]{1,0:T(8,128)(2,1)}, u32[]{:S(2)}) copy-start(bf16[128,512]{1,0:T(8,128)(2,1)} %feat_ref.1) | copy-start | bytes 393220
  4.2 23.6 %all-to-all-start = ((bf16[16,32,512]{2,1,0:T(8,128)(2,1)}), bf16[16,32,512]{2,1,0:T(8,128)(2,1)S(1)}, u32[]{:S(2)}, u32[]{:S(2)}) async-start(bf16[16,32,512]{2,1,0:T(8,128)(2,1)} %get-tuple-element.62), calls=%async_computation | async-start | bytes 1048576 | tf_op jit(solution)/shard_map/all_to_all | solution.py:376
  12.7 5.7 %collective-permute-start = (bf16[64,512]{1,0:T(8,128)(2,1)S(1)}, bf16[64,512]{1,0:T(8,128)(2,1)S(1)}, u32[]{:S(2)}, u32[]{:S(2)}) collective-permute-start(bf16[64,512]{1,0:T(8,128)(2,1)S(1)} %get-tuple-element.63), channel_id=1, source_target_pairs={{0,2},{2,4},{4,6},{6,8},{8,10},{10,12},{12,14},{14,16},{16,18},{18... | collective-permute-start | bytes 196616 | tf_op jit(solution)/shard_map/ppermute | solution.py:374
  16.5 6.8 %collective-permute-start.1 = (bf16[64,512]{1,0:T(8,128)(2,1)S(1)}, bf16[64,512]{1,0:T(8,128)(2,1)S(1)}, u32[]{:S(2)}, u32[]{:S(2)}) collective-permute-start(bf16[64,512]{1,0:T(8,128)(2,1)S(1)} %get-tuple-element.64), channel_id=1, source_target_pairs={{2,0},{4,2},{6,4},{8,6},{10,8},{12,10},{14,12},{16,14},{18,16},{20... | collective-permute-start | bytes 196616 | tf_op jit(solution)/shard_map/ppermute | solution.py:375
  29.0 9.5 %collective-permute-start.2 = (bf16[256,512]{1,0:T(8,128)(2,1)S(1)}, bf16[256,512]{1,0:T(8,128)(2,1)S(1)}, u32[]{:S(2)}, u32[]{:S(2)}) collective-permute-start(bf16[256,512]{1,0:T(8,128)(2,1)S(1)} %get-tuple-element.68), channel_id=1, source_target_pairs={{0,2},{2,0},{4,6},{6,4},{8,10},{10,8},{12,14},{14,12},{16,18},{18,... | collective-permute-start | bytes 786440 | tf_op jit(solution)/shard_map/ppermute | solution.py:337
  29.6 10.0 %collective-permute-start.3 = (bf16[256,512]{1,0:T(8,128)(2,1)S(1)}, bf16[256,512]{1,0:T(8,128)(2,1)S(1)}, u32[]{:S(2)}, u32[]{:S(2)}) collective-permute-start(bf16[256,512]{1,0:T(8,128)(2,1)S(1)} %get-tuple-element.69), channel_id=1, source_target_pairs={{0,4},{2,6},{4,0},{6,2},{8,12},{10,14},{12,8},{14,10},{16,20},{18,... | collective-permute-start | bytes 786440 | tf_op jit(solution)/shard_map/ppermute | solution.py:337
  30.9 12.0 %collective-permute-start.4 = (bf16[256,512]{1,0:T(8,128)(2,1)S(1)}, bf16[256,512]{1,0:T(8,128)(2,1)S(1)}, u32[]{:S(2)}, u32[]{:S(2)}) collective-permute-start(bf16[256,512]{1,0:T(8,128)(2,1)S(1)} %get-tuple-element.70), channel_id=1, source_target_pairs={{0,6},{2,4},{4,2},{6,0},{8,14},{10,12},{12,10},{14,8},{16,22},{18,... | collective-permute-start | bytes 786440 | tf_op jit(solution)/shard_map/ppermute | solution.py:337
  33.1 5.4 %collective-permute-start.5 = (bf16[160,512]{1,0:T(8,128)(2,1)S(1)}, bf16[160,512]{1,0:T(8,128)(2,1)S(1)}, u32[]{:S(2)}, u32[]{:S(2)}) collective-permute-start(bf16[160,512]{1,0:T(8,128)(2,1)S(1)} %get-tuple-element.71), channel_id=1, source_target_pairs={{0,8},{2,10},{4,12},{6,14},{8,0},{10,2},{12,4},{14,6},{16,24},{18,... | collective-permute-start | bytes 491528 | tf_op jit(solution)/shard_map/ppermute | solution.py:405
  43.1 9.4 %collective-permute-start.9 = (bf16[192,512]{1,0:T(8,128)(2,1)S(1)}, bf16[192,512]{1,0:T(8,128)(2,1)S(1)}, u32[]{:S(2)}, u32[]{:S(2)}) collective-permute-start(bf16[192,512]{1,0:T(8,128)(2,1)S(1)} %get-tuple-element.89), channel_id=1, source_target_pairs={{0,2},{2,0},{4,6},{6,4},{8,10},{10,8},{12,14},{14,12},{16,18},{18,... | collective-permute-start | bytes 589832 | tf_op jit(solution)/shard_map/ppermute | solution.py:405
  43.2 7.3 %collective-permute-start.6 = (bf16[64,512]{1,0:T(8,128)(2,1)S(1)}, bf16[64,512]{1,0:T(8,128)(2,1)S(1)}, u32[]{:S(2)}, u32[]{:S(2)}) collective-permute-start(bf16[64,512]{1,0:T(8,128)(2,1)S(1)} %get-tuple-element.86), channel_id=1, source_target_pairs={{0,8},{2,10},{4,12},{6,14},{8,16},{10,18},{12,20},{14,22},{16,24},... | collective-permute-start | bytes 196616 | tf_op jit(solution)/shard_map/ppermute | solution.py:340
  46.7 5.3 %collective-permute-start.7 = (bf16[64,512]{1,0:T(8,128)(2,1)S(1)}, bf16[64,512]{1,0:T(8,128)(2,1)S(1)}, u32[]{:S(2)}, u32[]{:S(2)}) collective-permute-start(bf16[64,512]{1,0:T(8,128)(2,1)S(1)} %get-tuple-element.87), channel_id=1, source_target_pairs={{0,16},{2,18},{4,20},{6,22},{8,24},{10,26},{12,28},{14,30},{16,0},... | collective-permute-start | bytes 196616 | tf_op jit(solution)/shard_map/ppermute | solution.py:340
  47.5 5.0 %collective-permute-start.8 = (bf16[64,512]{1,0:T(8,128)(2,1)S(1)}, bf16[64,512]{1,0:T(8,128)(2,1)S(1)}, u32[]{:S(2)}, u32[]{:S(2)}) collective-permute-start(bf16[64,512]{1,0:T(8,128)(2,1)S(1)} %get-tuple-element.88), channel_id=1, source_target_pairs={{0,24},{2,26},{4,28},{6,30},{8,0},{10,2},{12,4},{14,6},{16,8},{18,... | collective-permute-start | bytes 196616 | tf_op jit(solution)/shard_map/ppermute | solution.py:340
  52.6 10.4 %collective-permute-start.13 = (bf16[160,512]{1,0:T(8,128)(2,1)S(1)}, bf16[160,512]{1,0:T(8,128)(2,1)S(1)}, u32[]{:S(2)}, u32[]{:S(2)}) collective-permute-start(bf16[160,512]{1,0:T(8,128)(2,1)S(1)} %get-tuple-element.100), channel_id=1, source_target_pairs={{0,4},{2,6},{4,0},{6,2},{8,12},{10,14},{12,8},{14,10},{16,20},{18,... | collective-permute-start | bytes 491528 | tf_op jit(solution)/shard_map/ppermute | solution.py:405
  52.8 6.1 %collective-permute-start.12 = (bf16[64,512]{1,0:T(8,128)(2,1)S(1)}, bf16[64,512]{1,0:T(8,128)(2,1)S(1)}, u32[]{:S(2)}, u32[]{:S(2)}) collective-permute-start(bf16[64,512]{1,0:T(8,128)(2,1)S(1)} %shard_map.108), channel_id=1, source_target_pairs={{0,24},{2,26},{4,28},{6,30},{8,0},{10,2},{12,4},{14,6},{16,8},{18,... | collective-permute-start | bytes 196616 | tf_op jit(solution)/shard_map/ppermute | solution.py:340
  57.0 5.2 %collective-permute-start.11 = (bf16[64,512]{1,0:T(8,128)(2,1)S(1)}, bf16[64,512]{1,0:T(8,128)(2,1)S(1)}, u32[]{:S(2)}, u32[]{:S(2)}) collective-permute-start(bf16[64,512]{1,0:T(8,128)(2,1)S(1)} %shard_map.108), channel_id=1, source_target_pairs={{0,16},{2,18},{4,20},{6,22},{8,24},{10,26},{12,28},{14,30},{16,0},... | collective-permute-start | bytes 196616 | tf_op jit(solution)/shard_map/ppermute | solution.py:340
  57.0 6.1 %collective-permute-start.10 = (bf16[64,512]{1,0:T(8,128)(2,1)S(1)}, bf16[64,512]{1,0:T(8,128)(2,1)S(1)}, u32[]{:S(2)}, u32[]{:S(2)}) collective-permute-start(bf16[64,512]{1,0:T(8,128)(2,1)S(1)} %shard_map.108), channel_id=1, source_target_pairs={{0,8},{2,10},{4,12},{6,14},{8,16},{10,18},{12,20},{14,22},{16,24},... | collective-permute-start | bytes 196616 | tf_op jit(solution)/shard_map/ppermute | solution.py:340
  63.1 11.4 %collective-permute-start.17 = (bf16[256,512]{1,0:T(8,128)(2,1)S(1)}, bf16[256,512]{1,0:T(8,128)(2,1)S(1)}, u32[]{:S(2)}, u32[]{:S(2)}) collective-permute-start(bf16[256,512]{1,0:T(8,128)(2,1)S(1)} %pad_maximum_fusion.refs_0_), channel_id=1, source_target_pairs={{0,6},{2,4},{4,2},{6,0},{8,14},{10,12},{12,10},{14,8},{16,22},{18,... | collective-permute-start | bytes 786440 | tf_op jit(solution)/shard_map/ppermute | solution.py:337
  64.7 9.8 %collective-permute-start.16 = (bf16[256,512]{1,0:T(8,128)(2,1)S(1)}, bf16[256,512]{1,0:T(8,128)(2,1)S(1)}, u32[]{:S(2)}, u32[]{:S(2)}) collective-permute-start(bf16[256,512]{1,0:T(8,128)(2,1)S(1)} %pad_maximum_fusion.refs_0_), channel_id=1, source_target_pairs={{0,4},{2,6},{4,0},{6,2},{8,12},{10,14},{12,8},{14,10},{16,20},{18,... | collective-permute-start | bytes 786440 | tf_op jit(solution)/shard_map/ppermute | solution.py:337
  66.1 8.5 %collective-permute-start.15 = (bf16[256,512]{1,0:T(8,128)(2,1)S(1)}, bf16[256,512]{1,0:T(8,128)(2,1)S(1)}, u32[]{:S(2)}, u32[]{:S(2)}) collective-permute-start(bf16[256,512]{1,0:T(8,128)(2,1)S(1)} %pad_maximum_fusion.refs_0_), channel_id=1, source_target_pairs={{0,2},{2,0},{4,6},{6,4},{8,10},{10,8},{12,14},{14,12},{16,18},{18,... | collective-permute-start | bytes 786440 | tf_op jit(solution)/shard_map/ppermute | solution.py:337
  66.7 7.0 %collective-permute-start.14 = (bf16[160,512]{1,0:T(8,128)(2,1)S(1)}, bf16[160,512]{1,0:T(8,128)(2,1)S(1)}, u32[]{:S(2)}, u32[]{:S(2)}) collective-permute-start(bf16[160,512]{1,0:T(8,128)(2,1)S(1)} %get-tuple-element.110), channel_id=1, source_target_pairs={{0,16},{2,18},{4,20},{6,22},{8,24},{10,26},{12,28},{14,30},{16,0},... | collective-permute-start | bytes 491528 | tf_op jit(solution)/shard_map/ppermute | solution.py:405

commit v5 on v4

--- a/solution.py
+++ b/solution.py
@@ -57,7 +57,7 @@
 
 def prepare_kernel(
     count, nbr_hbm, wgt_hbm, tab_hbm, cnt_hbm, feat_hbm, up_hbm,
-    mat_ref, own_ref, send_ref, fwd_ref, bwd_ref,
+    mat_ref, own_ref, send_ref, near_ref, next_ref,
     nbr_ref, wgt_ref, tab_ref, cnt_ref, feat_ref, up_ref, sems, rows_scr, at_scr,
 ):
     inputs = (
@@ -135,10 +135,12 @@
     features = feat_ref[...]
     own_ref[...] = nn(adj_mat[0:ROWS], scaled)
     rims = nn(adj_mat[HALO_COL : HALO_COL + 2 * HALO], scaled).astype(BF16)
-    fwd_ref[0:HALO, :] = features[ROWS - HALO : ROWS]
-    fwd_ref[HALO : 2 * HALO, :] = rims[HALO : 2 * HALO]
-    bwd_ref[0:HALO, :] = features[0:HALO]
-    bwd_ref[HALO : 2 * HALO, :] = rims[0:HALO]
+    even = device % 2 == 0
+    low, high = features[0:HALO], features[ROWS - HALO : ROWS]
+    near_ref[0:HALO, :] = jnp.where(even, high, low)
+    near_ref[HALO:, :] = jnp.where(even, rims[HALO:], rims[0:HALO])
+    next_ref[0:HALO, :] = jnp.where(even, low, high)
+    next_ref[HALO:, :] = jnp.where(even, rims[0:HALO], rims[HALO:])
     rows_out = nn(pick.astype(BF16), features).astype(BF16)
     send_ref[:, 0:SLOT, :] = rows_out.reshape(count, SLOT, D)
     terms = nn(adj_mat[FAR_COL:], scaled).astype(BF16)
@@ -150,19 +152,20 @@
 
 
 def layer_kernel(
-    count, mat_ref, feat_ref, own_ref, recv_ref, left_ref, right_ref, w_one_ref, w_two_ref,
+    count, mat_ref, feat_ref, own_ref, recv_ref, near_ref, next_ref, w_one_ref, w_two_ref,
     *refs,
 ):
-    plane, piece = PLANE, 2 * D // count
-    groups = count // plane
-    part_refs = refs[:plane]
-    d_pre_ref, rim_scr, u_scr, hidden_scr, agg_scr = refs[plane:]
-    device = lax.axis_index("node")
-    group, place = device // plane, device % plane
+    part_refs = refs[:PLANE]
+    d_pre_ref, rim_scr, u_scr, hidden_scr, agg_scr = refs[PLANE:]
+    device = lax.axis_index("node")
+    place, side = device % PLANE, device // PLANE % 2
+    even = device % 2 == 0
+    left = jnp.where(even, next_ref[...], near_ref[...])
+    right = jnp.where(even, near_ref[...], next_ref[...])
     far = count * SLOT
     total = row_total(mat_ref, far)
-    rim_scr[0:HALO, :] = left_ref[0:HALO, :]
-    rim_scr[HALO : 2 * HALO, :] = right_ref[0:HALO, :]
+    rim_scr[0:HALO, :] = left[0:HALO]
+    rim_scr[HALO : 2 * HALO, :] = right[0:HALO]
     rim_scr[2 * HALO :, :] = jnp.zeros((ROWS - 2 * HALO, D), BF16)
     sums = nn(mat_ref[:, 0:ROWS], feat_ref[...])
     sums = sums + nn(mat_ref[:, HALO_COL:FAR_COL], rim_scr[...])
@@ -174,8 +177,8 @@
     u_scr[...] = own_ref[...] + nn(
         mat_ref[:, FAR_COL + far :], recv_ref[:, SLOT : 2 * SLOT, :].reshape(far, D)
     )
-    u_scr[0:HALO, :] += left_ref[HALO : 2 * HALO, :].astype(F32)
-    u_scr[ROWS - HALO : ROWS, :] += right_ref[HALO : 2 * HALO, :].astype(F32)
+    u_scr[0:HALO, :] += left[HALO:].astype(F32)
+    u_scr[ROWS - HALO : ROWS, :] += right[HALO:].astype(F32)
     u = u_scr[...].astype(BF16)
     back = nt(u, w_two_ref[...])
     pre = nn(agg, w_one_ref[...])
@@ -187,16 +190,12 @@
     )
     d_pre = (back * slope).astype(BF16)
     d_pre_ref[...] = d_pre
-    wide = D // plane
-    for v in range(plane):
+    wide = D // PLANE
+    for v in range(PLANE):
         cols = pl.ds(pl.multiple_of((place ^ v) * wide, wide), wide)
-        for half, (left, right) in enumerate(((hidden_scr, u), (agg_scr, d_pre))):
-            part = tn(left[:, cols], right).astype(part_refs[v].dtype)
-            for j in range(groups // 2):
-                to = lax.rem(half * (groups // 2) + j + groups - group, groups)
-                part_refs[v][pl.ds(pl.multiple_of(to * piece, piece), piece), :] = part[
-                    j * piece : (j + 1) * piece
-                ]
+        for half, (first, second) in enumerate(((hidden_scr, u), (agg_scr, d_pre))):
+            rows = pl.ds(pl.multiple_of((side ^ half) * wide, wide), wide)
+            part_refs[v][rows, :] = tn(first[:, cols], second).astype(part_refs[v].dtype)
 
 
 def hop_bits(count):
@@ -290,58 +289,51 @@
     out_ref[...] = sum_scr[...].astype(BF16)
 
 
-def plane_sum_kernel(piece, *refs):
-    part_refs, out_refs = refs[:PLANE], refs[PLANE:]
-    for k, out in enumerate(out_refs):
-        rows = slice(k * piece, (k + 1) * piece)
-        total = part_refs[0][rows, :].astype(F32)
-        for ref in part_refs[1:]:
-            total = total + ref[rows, :].astype(F32)
-        out[...] = total.astype(out.dtype)
-
-
-def group_sum_kernel(scale, *refs):
-    total = refs[0][...]
-    for ref in refs[1:-1]:
-        total = total + ref[...].astype(F32)
-    refs[-1][...] = (total * scale).astype(BF16)
-
-
-def gather_kernel(count, *refs):
-    piece, groups, wide = 2 * D // count, count // PLANE, D // PLANE
-    device = lax.axis_index("node")
-    group, place = device // PLANE, device % PLANE
-    outs = refs[PLANE:]
-    per = groups // 2
-    for v in range(PLANE):
-        row = (place ^ v) * wide
-        for half in range(2):
-            for j in range(per):
-                at = lax.rem(group + 2 * groups - (half * per + j), groups)
-                rows = refs[v][pl.ds(pl.multiple_of(at * piece, piece), piece), :]
-                outs[half][pl.ds(pl.multiple_of(row + j * piece, piece), piece), :] = rows
+def sum_refs(refs, rows=slice(None)):
+    total = refs[0][rows, :].astype(F32)
+    for ref in refs[1:]:
+        total = total + ref[rows, :].astype(F32)
+    return total
+
+
+def plane_sum_kernel(*refs):
+    part_refs, (keep_ref, give_ref) = refs[:PLANE], refs[PLANE:]
+    wide = D // PLANE
+    keep_ref[...] = sum_refs(part_refs, slice(0, wide))
+    give_ref[...] = sum_refs(part_refs, slice(wide, 2 * wide)).astype(BF16)
+
+
+def pair_sum_kernel(scale, one_ref, two_ref, out_ref):
+    total = one_ref[...].astype(F32) + two_ref[...].astype(F32)
+    out_ref[...] = (total * scale).astype(BF16)
+
+
+def gather_kernel(*refs):
+    chunk_refs, out_refs = refs[:PLANE], refs[PLANE:]
+    wide = D // PLANE
+    device = lax.axis_index("node")
+    place, side = device % PLANE, device // PLANE % 2
+    for v, ref in enumerate(chunk_refs):
+        row = pl.ds(pl.multiple_of((place ^ v) * wide, wide), wide)
+        for half, out_ref in enumerate(out_refs):
+            at = pl.ds(pl.multiple_of((side ^ half) * wide, wide), wide)
+            out_ref[row, :] = ref[at, :]
 
 
 def shards(
     features, upstream, weight_one, weight_two, neighbours, edge_weight, fetch_block, fetch_count
 ):
     count = lax.axis_size("node")
-    groups = count // PLANE
-    piece = 2 * D // count
     far = count * SLOT
     chain = FAR_COL + far
-    up = [(i, i + 1) for i in range(count - 1)]
-    down = [(i + 1, i) for i in range(count - 1)]
-
-    def in_plane(value, v):
-        return lax.ppermute(value, "node", [(i, i ^ v) for i in range(count)])
-
-    def across(value, k):
-        return lax.ppermute(
-            value, "node", [(i, (i + k * PLANE) % count) for i in range(count)]
-        )
-
-    matrix, own, send, to_right, to_left = call(
+    wide = D // PLANE
+    onward = [(i, i + 1) for i in range(1, count - 1, 2)]
+    onward = onward + [(target, source) for source, target in onward]
+
+    def swap(value, flip):
+        return lax.ppermute(value, "node", [(i, i ^ flip) for i in range(count)])
+
+    matrix, own, send, near, onto = call(
         functools.partial(prepare_kernel, count),
         (
             struct((ROWS, chain + far), BF16),
@@ -371,8 +363,8 @@
             )
         )
     )
-    from_left = lax.ppermute(to_right, "node", up)
-    from_right = lax.ppermute(to_left, "node", down)
+    near = swap(near, 1)
+    onto = lax.ppermute(onto, "node", onward)
     received = lax.all_to_all(send, "node", split_axis=0, concat_axis=0, tiled=True)
 
     *parts, d_pre = call(
@@ -388,8 +380,8 @@
             pltpu.VMEM((ROWS, D), BF16),
             pltpu.VMEM((ROWS, D), BF16),
         ),
-    )(matrix, features, own, received, from_left, from_right, weight_one, weight_two)
-    plane_parts = [parts[0]] + [in_plane(parts[v], v) for v in range(1, PLANE)]
+    )(matrix, features, own, received, near, onto, weight_one, weight_two)
+    parts = [parts[0]] + [swap(parts[v], v) for v in range(1, PLANE)]
 
     bits = hop_bits(count)
     carried = (
@@ -400,9 +392,6 @@
 
     def message(bit):
         return struct((hop_rows(count, bit), D), BF16)
-
-    def swap(value, bit):
-        return lax.ppermute(value, "node", [(i, i ^ (1 << bit)) for i in range(count)])
 
     def next_hop(at, got, held):
         *held, out = call(
@@ -415,34 +404,34 @@
         functools.partial(back_kernel, count, bits[0]),
         (struct((ROWS, D), F32), *carried, message(bits[0])),
     )(matrix, d_pre, weight_one)
-    plane_parts, got = lax.optimization_barrier((plane_parts, swap(out, bits[0])))
-
-    sums = call(
-        functools.partial(plane_sum_kernel, piece),
-        (struct((piece, D), F32), *[struct((piece, D), BF16)] * (groups - 1)),
-    )(*plane_parts)
+    parts, got = lax.optimization_barrier((parts, swap(out, 1 << bits[0])))
+
+    keep, give = call(plane_sum_kernel, (struct((wide, D), F32), struct((wide, D), BF16)))(*parts)
     out, held = next_hop(1, got, held)
-    sums, out = lax.optimization_barrier((sums, out))
-    shared = [sums[0]] + [across(sums[k], k) for k in range(1, groups)]
-    shared, got = lax.optimization_barrier((shared, swap(out, bits[1])))
+    give, out = lax.optimization_barrier((give, out))
+    other, got = lax.optimization_barrier((swap(give, PLANE), swap(out, 1 << bits[1])))
+
+    pair = functools.partial(pair_sum_kernel, 1.0)
+    total = call(pair, struct((wide, D), BF16))(keep, other)
+    out, held = next_hop(2, got, held)
+    for bit in bits[3:-1]:
+        total = call(pair, struct((wide, D), BF16))(total, swap(total, 1 << bit))
+    total, out = lax.optimization_barrier((total, out))
+    other, got = lax.optimization_barrier((swap(total, 1 << bits[-1]), swap(out, 1 << bits[2])))
 
     total = call(
-        functools.partial(group_sum_kernel, 1.0 / math.sqrt(ROWS * count)),
-        struct((piece, D), BF16),
-    )(*shared)
-    out, held = next_hop(2, got, held)
+        functools.partial(pair_sum_kernel, 1.0 / math.sqrt(ROWS * count)),
+        struct((wide, D), BF16),
+    )(total, other)
+    out, held = next_hop(3, got, held)
     total, out = lax.optimization_barrier((total, out))
-    pieces = [total] + [across(total, k) for k in range(1, groups)]
-    pieces, got = lax.optimization_barrier((pieces, swap(out, bits[2])))
-
-    chunk = jnp.concatenate(pieces, axis=0)
-    out, held = next_hop(3, got, held)
-    chunk, out = lax.optimization_barrier((chunk, out))
-    chunks = [chunk] + [in_plane(chunk, v) for v in range(1, PLANE)]
-    got = swap(out, bits[3])
+    other, got = lax.optimization_barrier((swap(total, PLANE), swap(out, 1 << bits[3])))
+
+    chunk = jnp.concatenate([total, other], axis=0)
+    chunks = [chunk] + [swap(chunk, v) for v in range(1, PLANE)]
     for at in range(4, len(bits)):
         out, held = next_hop(at, got, held)
-        got = swap(out, bits[at])
+        got = swap(out, 1 << bits[at])
     d_features = call(
         functools.partial(features_kernel, count, bits[-1]),
         struct((ROWS, D), BF16),
@@ -452,10 +441,7 @@
             pltpu.VMEM((count, SLOT, D), BF16),
         ),
     )(matrix, own, got, *held)
-    grad_two, grad_one = call(
-        functools.partial(gather_kernel, count),
-        (struct((D, D), BF16), struct((D, D), BF16)),
-    )(*chunks)
+    grad_two, grad_one = call(gather_kernel, (struct((D, D), BF16), struct((D, D), BF16)))(*chunks)
     return d_features, grad_one, grad_two
 
 

time: 75.9 us -> 79.9 us (1.053)
  waiting for transfers between devices: 31.9 us -> 44.2 us
  starting transfers between devices: 35.4 us -> 27.1 us
    ppermute x18 -> x15, starting transfers between devices: 27 us -> 18.6 us  [the longest x14 18 us: swap(): return lax.ppermute(value, 'node', [(i, i ^ flip) for i in range(count)])]
    ppermute x18 -> x15, waiting for transfers between devices: 27.4 us -> 34.5 us  [the longest x14 34.5 us: swap(): return lax.ppermute(value, 'node', [(i, i ^ flip) for i in range(count)])]
    all_to_all x1, waiting for transfers between devices: 4.53 us -> 9.63 us  [shards(): lax.all_to_all(send, 'node', split_axis=0, concat_axis=0, tiled=True)]
  transfers between devices with their start and end apart: 19 -> 16, of which waited for: 12 -> 11; matrix products, arithmetic and copies ran while one was open for 0% -> 0% of each run, Pallas kernels for 2% -> 2%
where the time goes in v5:
time: 79.9 us; the launch traced here: 79.6 us
  waiting for transfers between devices  44.2 us (55%)
  starting transfers between devices  27.1 us (34%)
  Pallas kernels  7.52 us (9%)
  between operations  0.8 us (1%)
    ppermute x14, waiting for transfers between devices, swap(): return lax.ppermute(value, 'node', [(i, i ^ flip) for i in range(count)])  34.5 us
    ppermute x14, starting transfers between devices, swap(): return lax.ppermute(value, 'node', [(i, i ^ flip) for i in range(count)])  18 us
    all_to_all x1, waiting for transfers between devices, shards(): lax.all_to_all(send, 'node', split_axis=0, concat_axis=0, tiled=True)  9.63 us
    all_to_all x1, starting transfers between devices, shards(): lax.all_to_all(send, 'node', split_axis=0, concat_axis=0, tiled=True)  8.46 us
    pallas_call x1, Pallas kernels, shards(): call(functools.partial(prepare_kernel, count), (struct((ROWS, chain + far...  3.54 us
  transfers between devices with their start and end apart: 16, of which 11 were waited for; matrix products, arithmetic and copies ran while one was open for 0% of the time, Pallas kernels for 2%

profile of v5, /device:TPU:0, one launch (start us, length us, event | category | flops | bytes accessed | tf_op | source)
XLA Modules:
  0.0 79.6 jit_solution(16717435021014473863)
XLA Ops:
  0.6 3.5 %shard_map.103 = (bf16[128,768]{1,0:T(8,128)(2,1)S(1)}, f32[128,512]{1,0:T(8,128)S(1)}, bf16[16,32,512]{2,1,0:T(8,128)(2,1)}, bf16[64,512]{1,0:T(8,128)(2,1)S(1)}, bf16[64,512]{1,0:T(8,128)(2,1)S(1)}) custom-call(s32[32,128]{1,0:T(8,128)} %bitcast.4, s32[32,128]{1,0:T(8,128)} %bitcast.5, s32[2,256]{1,0:T(2,128)} %bitcast.6, s32[1,256]{1,0:T(1,128)} %bitcast.7, ...), custom_call_target="tpu_custom_call" | custom-call | tf_op jit(solution)/shard_map/pallas_call | solution.py:336
  4.2 8.5 %all-to-all-start = ((bf16[16,32,512]{2,1,0:T(8,128)(2,1)}), bf16[16,32,512]{2,1,0:T(8,128)(2,1)S(1)}, u32[]{:S(2)}, u32[]{:S(2)}) async-start(bf16[16,32,512]{2,1,0:T(8,128)(2,1)} %get-tuple-element.53), calls=%async_computation | async-start | bytes 1048576 | tf_op jit(solution)/shard_map/all_to_all | solution.py:368
  12.7 1.9 %collective-permute-start = (bf16[64,512]{1,0:T(8,128)(2,1)S(1)}, bf16[64,512]{1,0:T(8,128)(2,1)S(1)}, u32[]{:S(2)}, u32[]{:S(2)}) collective-permute-start(bf16[64,512]{1,0:T(8,128)(2,1)S(1)} %get-tuple-element.54), channel_id=1, source_target_pairs={{0,2},{2,0},{4,6},{6,4},{8,10},{10,8},{12,14},{14,12},{16,18},{18,... | collective-permute-start | bytes 196616 | tf_op jit(solution)/shard_map/ppermute | solution.py:334
  15.3 2.9 %collective-permute-done.near_ref = bf16[64,512]{1,0:T(8,128)(2,1)S(1)} collective-permute-done((bf16[64,512]{1,0:T(8,128)(2,1)S(1)}, bf16[64,512]{1,0:T(8,128)(2,1)S(1)}, u32[]{:S(2)}, u32[]{:S(2)}) %collective-permute-start) | collective-permute-done | bytes 65568 | tf_op jit(solution)/shard_map/ppermute | solution.py:334
  18.2 9.6 %all-to-all-done.recv_ref = bf16[16,32,512]{2,1,0:T(8,128)(2,1)S(1)} async-done(((bf16[16,32,512]{2,1,0:T(8,128)(2,1)}), bf16[16,32,512]{2,1,0:T(8,128)(2,1)S(1)}, u32[]{:S(2)}, u32[]{:S(2)}) %all-to-all-start) | async-done | bytes 524320 | tf_op jit(solution)/shard_map/all_to_all | solution.py:368
  27.8 1.2 %shard_map.104 = (f32[256,512]{1,0:T(8,128)S(1)}, bf16[256,512]{1,0:T(8,128)(2,1)S(1)}, bf16[256,512]{1,0:T(8,128)(2,1)S(1)}, bf16[256,512]{1,0:T(8,128)(2,1)S(1)}, bf16[128,512]{1,0:T(8,128)(2,1)S(1)}) custom-call(bf16[128,768]{1,0:T(8,128)(2,1)S(1)} %get-tuple-element.51.mat_ref, bf16[128,512]{1,0:T(8,128)(2,1)S(1)} %copy-done.1, ...), custom_call_target="tpu_custom_call" | custom-call | tf_op jit(solution)/shard_map/pallas_call | solution.py:370
  29.7 1.3 %collective-permute-start.3 = (bf16[256,512]{1,0:T(8,128)(2,1)S(1)}, bf16[256,512]{1,0:T(8,128)(2,1)S(1)}, u32[]{:S(2)}, u32[]{:S(2)}) collective-permute-start(bf16[256,512]{1,0:T(8,128)(2,1)S(1)} %get-tuple-element.60), channel_id=1, source_target_pairs={{0,4},{2,6},{4,0},{6,2},{8,12},{10,14},{12,8},{14,10},{16,20},{18,... | collective-permute-start | bytes 786440 | tf_op jit(solution)/shard_map/ppermute | solution.py:334
  30.9 1.7 %collective-permute-start.4 = (bf16[256,512]{1,0:T(8,128)(2,1)S(1)}, bf16[256,512]{1,0:T(8,128)(2,1)S(1)}, u32[]{:S(2)}, u32[]{:S(2)}) collective-permute-start(bf16[256,512]{1,0:T(8,128)(2,1)S(1)} %get-tuple-element.61), channel_id=1, source_target_pairs={{0,6},{2,4},{4,2},{6,0},{8,14},{10,12},{12,10},{14,8},{16,22},{18,... | collective-permute-start | bytes 786440 | tf_op jit(solution)/shard_map/ppermute | solution.py:334
  33.2 1.3 %collective-permute-start.5 = (bf16[160,512]{1,0:T(8,128)(2,1)S(1)}, bf16[160,512]{1,0:T(8,128)(2,1)S(1)}, u32[]{:S(2)}, u32[]{:S(2)}) collective-permute-start(bf16[160,512]{1,0:T(8,128)(2,1)S(1)} %get-tuple-element.62), channel_id=1, source_target_pairs={{0,8},{2,10},{4,12},{6,14},{8,0},{10,2},{12,4},{14,6},{16,24},{18,... | collective-permute-start | bytes 491528 | tf_op jit(solution)/shard_map/ppermute | solution.py:334
  34.5 4.1 %collective-permute-done.5.got_ref = bf16[160,512]{1,0:T(8,128)(2,1)S(1)} collective-permute-done((bf16[160,512]{1,0:T(8,128)(2,1)S(1)}, bf16[160,512]{1,0:T(8,128)(2,1)S(1)}, u32[]{:S(2)}, u32[]{:S(2)}) %collective-permute-start.5) | collective-permute-done | bytes 163872 | tf_op jit(solution)/shard_map/ppermute | solution.py:334
  38.6 0.9 %collective-permute-done.3.refs_2_ = bf16[256,512]{1,0:T(8,128)(2,1)S(1)} collective-permute-done((bf16[256,512]{1,0:T(8,128)(2,1)S(1)}, bf16[256,512]{1,0:T(8,128)(2,1)S(1)}, u32[]{:S(2)}, u32[]{:S(2)}) %collective-permute-start.3) | collective-permute-done | bytes 262176 | tf_op jit(solution)/shard_map/ppermute | solution.py:334
  39.5 3.7 %collective-permute-done.4.refs_3_ = bf16[256,512]{1,0:T(8,128)(2,1)S(1)} collective-permute-done((bf16[256,512]{1,0:T(8,128)(2,1)S(1)}, bf16[256,512]{1,0:T(8,128)(2,1)S(1)}, u32[]{:S(2)}, u32[]{:S(2)}) %collective-permute-start.4) | collective-permute-done | bytes 262176 | tf_op jit(solution)/shard_map/ppermute | solution.py:334
  43.4 3.3 %collective-permute-start.6 = (bf16[128,512]{1,0:T(8,128)(2,1)S(1)}, bf16[128,512]{1,0:T(8,128)(2,1)S(1)}, u32[]{:S(2)}, u32[]{:S(2)}) collective-permute-start(bf16[128,512]{1,0:T(8,128)(2,1)S(1)} %get-tuple-element.74), channel_id=1, source_target_pairs={{0,8},{2,10},{4,12},{6,14},{8,0},{10,2},{12,4},{14,6},{16,24},{18,... | collective-permute-start | bytes 393224 | tf_op jit(solution)/shard_map/ppermute | solution.py:334
  46.7 2.9 %collective-permute-done.6.two_ref = bf16[128,512]{1,0:T(8,128)(2,1)S(1)} collective-permute-done((bf16[128,512]{1,0:T(8,128)(2,1)S(1)}, bf16[128,512]{1,0:T(8,128)(2,1)S(1)}, u32[]{:S(2)}, u32[]{:S(2)}) %collective-permute-start.6) | collective-permute-done | bytes 131104 | tf_op jit(solution)/shard_map/ppermute | solution.py:334
  49.8 4.1 %collective-permute-start.8 = (bf16[128,512]{1,0:T(8,128)(2,1)S(1)}, bf16[128,512]{1,0:T(8,128)(2,1)S(1)}, u32[]{:S(2)}, u32[]{:S(2)}) collective-permute-start(bf16[128,512]{1,0:T(8,128)(2,1)S(1)} %shard_map.108.one_ref), channel_id=1, source_target_pairs={{0,16},{2,18},{4,20},{6,22},{8,24},{10,26},{12,28},{14,30},{16,0},... | collective-permute-start | bytes 393224 | tf_op jit(solution)/shard_map/ppermute | solution.py:334
  53.9 7.0 %collective-permute-done.8.two_ref = bf16[128,512]{1,0:T(8,128)(2,1)S(1)} collective-permute-done((bf16[128,512]{1,0:T(8,128)(2,1)S(1)}, bf16[128,512]{1,0:T(8,128)(2,1)S(1)}, u32[]{:S(2)}, u32[]{:S(2)}) %collective-permute-start.8) | collective-permute-done | bytes 131104 | tf_op jit(solution)/shard_map/ppermute | solution.py:334
  61.1 6.7 %collective-permute-done.10 = bf16[128,512]{1,0:T(8,128)(2,1)S(1)} collective-permute-done((bf16[128,512]{1,0:T(8,128)(2,1)S(1)}, bf16[128,512]{1,0:T(8,128)(2,1)S(1)}, u32[]{:S(2)}, u32[]{:S(2)}) %collective-permute-start.10) | collective-permute-done | bytes 131104 | tf_op jit(solution)/shard_map/ppermute | solution.py:334
  67.9 2.8 %collective-permute-start.13 = (bf16[256,512]{1,0:T(8,128)(2,1)S(1)}, bf16[256,512]{1,0:T(8,128)(2,1)S(1)}, u32[]{:S(2)}, u32[]{:S(2)}) collective-permute-start(bf16[256,512]{1,0:T(8,128)(2,1)S(1)} %constant_dynamic-update-slice_fusion.refs_0_), channel_id=1, source_target_pairs={{0,4},{2,6},{4,0},{6,2},{8,12},{10,14},{12,8},{14,10},{16,20},{18,... | collective-permute-start | bytes 786440 | tf_op jit(solution)/shard_map/ppermute | solution.py:334
  70.7 0.7 collective-permute-start.12
  71.4 0.9 %shard_map.112 = bf16[128,512]{1,0:T(8,128)(2,1)} custom-call(bf16[128,768]{1,0:T(8,128)(2,1)S(1)} %get-tuple-element.51.mat_ref, f32[128,512]{1,0:T(8,128)S(1)} %get-tuple-element.57.own_ref, bf16[160,512]{1,0:T(8,128)(2,1)S(1)} %collective-permute-done.11.got_ref, bf16[16,16,512]{2,1,0:T(8,128)(2,1)S(1)} %get-tuple-element.93.was_ref, ...), custom_call_target="tpu_custom_call" | custom-call | tf_op jit(solution)/shard_map/pallas_call | solution.py:435
  72.3 3.0 %collective-permute-done.14.refs_3_ = bf16[256,512]{1,0:T(8,128)(2,1)S(1)} collective-permute-done((bf16[256,512]{1,0:T(8,128)(2,1)S(1)}, bf16[256,512]{1,0:T(8,128)(2,1)S(1)}, u32[]{:S(2)}, u32[]{:S(2)}) %collective-permute-start.14) | collective-permute-done | bytes 262176 | tf_op jit(solution)/shard_map/ppermute | solution.py:334
  75.3 2.6 %collective-permute-done.13.refs_2_ = bf16[256,512]{1,0:T(8,128)(2,1)S(1)} collective-permute-done((bf16[256,512]{1,0:T(8,128)(2,1)S(1)}, bf16[256,512]{1,0:T(8,128)(2,1)S(1)}, u32[]{:S(2)}, u32[]{:S(2)}) %collective-permute-start.13) | collective-permute-done | bytes 262176 | tf_op jit(solution)/shard_map/ppermute | solution.py:334
  77.9 0.7 collective-permute-done.12.refs_1_
  78.6 1.0 %shard_map.113 = (bf16[512,512]{1,0:T(8,128)(2,1)}, bf16[512,512]{1,0:T(8,128)(2,1)}) custom-call(bf16[256,512]{1,0:T(8,128)(2,1)S(1)} %constant_dynamic-update-slice_fusion.refs_0_, bf16[256,512]{1,0:T(8,128)(2,1)S(1)} %collective-permute-done.12.refs_1_, bf16[256,512]{1,0:T(8,128)(2,1)S(1)} %collective-permute-done.13.refs_2_, ...), custom_call_target="tpu_custom_call" | custom-call | tf_op jit(solution)/shard_map/pallas_call | solution.py:444
  (27 shorter events, 2.5 us)
Async XLA Ops:
  0.6 27.2 %copy-start.2 = (bf16[512,512]{1,0:T(8,128)(2,1)S(1)}, bf16[512,512]{1,0:T(8,128)(2,1)}, u32[]{:S(2)}) copy-start(bf16[512,512]{1,0:T(8,128)(2,1)} %w_two_ref.1) | copy-start | bytes 1572868
  4.2 23.6 %copy-start = (bf16[512,512]{1,0:T(8,128)(2,1)S(1)}, bf16[512,512]{1,0:T(8,128)(2,1)}, u32[]{:S(2)}) copy-start(bf16[512,512]{1,0:T(8,128)(2,1)} %w_one_ref.3) | copy-start | bytes 1572868
  4.2 23.6 %copy-start.1 = (bf16[128,512]{1,0:T(8,128)(2,1)S(1)}, bf16[128,512]{1,0:T(8,128)(2,1)}, u32[]{:S(2)}) copy-start(bf16[128,512]{1,0:T(8,128)(2,1)} %feat_ref.1) | copy-start | bytes 393220
  4.2 23.6 %all-to-all-start = ((bf16[16,32,512]{2,1,0:T(8,128)(2,1)}), bf16[16,32,512]{2,1,0:T(8,128)(2,1)S(1)}, u32[]{:S(2)}, u32[]{:S(2)}) async-start(bf16[16,32,512]{2,1,0:T(8,128)(2,1)} %get-tuple-element.53), calls=%async_computation | async-start | bytes 1048576 | tf_op jit(solution)/shard_map/all_to_all | solution.py:368
  12.7 5.5 %collective-permute-start = (bf16[64,512]{1,0:T(8,128)(2,1)S(1)}, bf16[64,512]{1,0:T(8,128)(2,1)S(1)}, u32[]{:S(2)}, u32[]{:S(2)}) collective-permute-start(bf16[64,512]{1,0:T(8,128)(2,1)S(1)} %get-tuple-element.54), channel_id=1, source_target_pairs={{0,2},{2,0},{4,6},{6,4},{8,10},{10,8},{12,14},{14,12},{16,18},{18,... | collective-permute-start | bytes 196616 | tf_op jit(solution)/shard_map/ppermute | solution.py:334
  14.6 3.6 %collective-permute-start.1 = (bf16[64,512]{1,0:T(8,128)(2,1)S(1)}, bf16[64,512]{1,0:T(8,128)(2,1)S(1)}, u32[]{:S(2)}, u32[]{:S(2)}) collective-permute-start(bf16[64,512]{1,0:T(8,128)(2,1)S(1)} %get-tuple-element.55), channel_id=1, source_target_pairs={{2,4},{6,8},{10,12},{14,16},{18,20},{22,24},{26,28},{4,2},{8,6},{1... | collective-permute-start | bytes 196616 | tf_op jit(solution)/shard_map/ppermute | solution.py:367
  29.0 9.5 %collective-permute-start.2 = (bf16[256,512]{1,0:T(8,128)(2,1)S(1)}, bf16[256,512]{1,0:T(8,128)(2,1)S(1)}, u32[]{:S(2)}, u32[]{:S(2)}) collective-permute-start(bf16[256,512]{1,0:T(8,128)(2,1)S(1)} %get-tuple-element.59), channel_id=1, source_target_pairs={{0,2},{2,0},{4,6},{6,4},{8,10},{10,8},{12,14},{14,12},{16,18},{18,... | collective-permute-start | bytes 786440 | tf_op jit(solution)/shard_map/ppermute | solution.py:334
  29.7 9.8 %collective-permute-start.3 = (bf16[256,512]{1,0:T(8,128)(2,1)S(1)}, bf16[256,512]{1,0:T(8,128)(2,1)S(1)}, u32[]{:S(2)}, u32[]{:S(2)}) collective-permute-start(bf16[256,512]{1,0:T(8,128)(2,1)S(1)} %get-tuple-element.60), channel_id=1, source_target_pairs={{0,4},{2,6},{4,0},{6,2},{8,12},{10,14},{12,8},{14,10},{16,20},{18,... | collective-permute-start | bytes 786440 | tf_op jit(solution)/shard_map/ppermute | solution.py:334
  30.9 12.3 %collective-permute-start.4 = (bf16[256,512]{1,0:T(8,128)(2,1)S(1)}, bf16[256,512]{1,0:T(8,128)(2,1)S(1)}, u32[]{:S(2)}, u32[]{:S(2)}) collective-permute-start(bf16[256,512]{1,0:T(8,128)(2,1)S(1)} %get-tuple-element.61), channel_id=1, source_target_pairs={{0,6},{2,4},{4,2},{6,0},{8,14},{10,12},{12,10},{14,8},{16,22},{18,... | collective-permute-start | bytes 786440 | tf_op jit(solution)/shard_map/ppermute | solution.py:334
  33.2 5.4 %collective-permute-start.5 = (bf16[160,512]{1,0:T(8,128)(2,1)S(1)}, bf16[160,512]{1,0:T(8,128)(2,1)S(1)}, u32[]{:S(2)}, u32[]{:S(2)}) collective-permute-start(bf16[160,512]{1,0:T(8,128)(2,1)S(1)} %get-tuple-element.62), channel_id=1, source_target_pairs={{0,8},{2,10},{4,12},{6,14},{8,0},{10,2},{12,4},{14,6},{16,24},{18,... | collective-permute-start | bytes 491528 | tf_op jit(solution)/shard_map/ppermute | solution.py:334
  43.4 6.3 %collective-permute-start.7 = (bf16[192,512]{1,0:T(8,128)(2,1)S(1)}, bf16[192,512]{1,0:T(8,128)(2,1)S(1)}, u32[]{:S(2)}, u32[]{:S(2)}) collective-permute-start(bf16[192,512]{1,0:T(8,128)(2,1)S(1)} %get-tuple-element.75), channel_id=1, source_target_pairs={{0,2},{2,0},{4,6},{6,4},{8,10},{10,8},{12,14},{14,12},{16,18},{18,... | collective-permute-start | bytes 589832 | tf_op jit(solution)/shard_map/ppermute | solution.py:334
  43.4 6.2 %collective-permute-start.6 = (bf16[128,512]{1,0:T(8,128)(2,1)S(1)}, bf16[128,512]{1,0:T(8,128)(2,1)S(1)}, u32[]{:S(2)}, u32[]{:S(2)}) collective-permute-start(bf16[128,512]{1,0:T(8,128)(2,1)S(1)} %get-tuple-element.74), channel_id=1, source_target_pairs={{0,8},{2,10},{4,12},{6,14},{8,0},{10,2},{12,4},{14,6},{16,24},{18,... | collective-permute-start | bytes 393224 | tf_op jit(solution)/shard_map/ppermute | solution.py:334
  49.7 11.1 %collective-permute-start.9 = (bf16[160,512]{1,0:T(8,128)(2,1)S(1)}, bf16[160,512]{1,0:T(8,128)(2,1)S(1)}, u32[]{:S(2)}, u32[]{:S(2)}) collective-permute-start(bf16[160,512]{1,0:T(8,128)(2,1)S(1)} %get-tuple-element.83), channel_id=1, source_target_pairs={{0,4},{2,6},{4,0},{6,2},{8,12},{10,14},{12,8},{14,10},{16,20},{18,... | collective-permute-start | bytes 491528 | tf_op jit(solution)/shard_map/ppermute | solution.py:334
  49.8 11.0 %collective-permute-start.8 = (bf16[128,512]{1,0:T(8,128)(2,1)S(1)}, bf16[128,512]{1,0:T(8,128)(2,1)S(1)}, u32[]{:S(2)}, u32[]{:S(2)}) collective-permute-start(bf16[128,512]{1,0:T(8,128)(2,1)S(1)} %shard_map.108.one_ref), channel_id=1, source_target_pairs={{0,16},{2,18},{4,20},{6,22},{8,24},{10,26},{12,28},{14,30},{16,0},... | collective-permute-start | bytes 393224 | tf_op jit(solution)/shard_map/ppermute | solution.py:334
  60.9 6.9 %collective-permute-start.11 = (bf16[160,512]{1,0:T(8,128)(2,1)S(1)}, bf16[160,512]{1,0:T(8,128)(2,1)S(1)}, u32[]{:S(2)}, u32[]{:S(2)}) collective-permute-start(bf16[160,512]{1,0:T(8,128)(2,1)S(1)} %get-tuple-element.91), channel_id=1, source_target_pairs={{0,16},{2,18},{4,20},{6,22},{8,24},{10,26},{12,28},{14,30},{16,0},... | collective-permute-start | bytes 491528 | tf_op jit(solution)/shard_map/ppermute | solution.py:334
  61.0 6.8 %collective-permute-start.10 = (bf16[128,512]{1,0:T(8,128)(2,1)S(1)}, bf16[128,512]{1,0:T(8,128)(2,1)S(1)}, u32[]{:S(2)}, u32[]{:S(2)}) collective-permute-start(bf16[128,512]{1,0:T(8,128)(2,1)S(1)} %shard_map.110), channel_id=1, source_target_pairs={{0,8},{2,10},{4,12},{6,14},{8,0},{10,2},{12,4},{14,6},{16,24},{18,... | collective-permute-start | bytes 393224 | tf_op jit(solution)/shard_map/ppermute | solution.py:334
  67.8 7.4 %collective-permute-start.14 = (bf16[256,512]{1,0:T(8,128)(2,1)S(1)}, bf16[256,512]{1,0:T(8,128)(2,1)S(1)}, u32[]{:S(2)}, u32[]{:S(2)}) collective-permute-start(bf16[256,512]{1,0:T(8,128)(2,1)S(1)} %constant_dynamic-update-slice_fusion.refs_0_), channel_id=1, source_target_pairs={{0,6},{2,4},{4,2},{6,0},{8,14},{10,12},{12,10},{14,8},{16,22},{18,... | collective-permute-start | bytes 786440 | tf_op jit(solution)/shard_map/ppermute | solution.py:334
  67.9 10.0 %collective-permute-start.13 = (bf16[256,512]{1,0:T(8,128)(2,1)S(1)}, bf16[256,512]{1,0:T(8,128)(2,1)S(1)}, u32[]{:S(2)}, u32[]{:S(2)}) collective-permute-start(bf16[256,512]{1,0:T(8,128)(2,1)S(1)} %constant_dynamic-update-slice_fusion.refs_0_), channel_id=1, source_target_pairs={{0,4},{2,6},{4,0},{6,2},{8,12},{10,14},{12,8},{14,10},{16,20},{18,... | collective-permute-start | bytes 786440 | tf_op jit(solution)/shard_map/ppermute | solution.py:334
  70.7 7.9 %collective-permute-start.12 = (bf16[256,512]{1,0:T(8,128)(2,1)S(1)}, bf16[256,512]{1,0:T(8,128)(2,1)S(1)}, u32[]{:S(2)}, u32[]{:S(2)}) collective-permute-start(bf16[256,512]{1,0:T(8,128)(2,1)S(1)} %constant_dynamic-update-slice_fusion.refs_0_), channel_id=1, source_target_pairs={{0,2},{2,0},{4,6},{6,4},{8,10},{10,8},{12,14},{14,12},{16,18},{18,... | collective-permute-start | bytes 786440 | tf_op jit(solution)/shard_map/ppermute | solution.py:334

commit v6 on v5

--- a/solution.py
+++ b/solution.py
@@ -199,18 +199,17 @@
 
 
 def hop_bits(count):
-    bits = [b for b in range(count.bit_length() - 1)]
-    return [bits[2], bits[0], bits[1]] + bits[3:]
+    return list(range(count.bit_length() - 2, 2, -1)) + [0, 1, 2]
 
 
 def hop_rows(count, bit):
     return count // 2 * SLOT + HALO * (2 if bit == 0 else 1)
 
 
-def right_moves(device, bit):
-    if bit == 2:
-        return device % 4 == 3
-    return device % (1 << bit) == 0
+def moves(device, bit):
+    low = device % (1 << bit)
+    ones = (1 << bit) - 1
+    return (low == 0, low == ones) if bit > 2 else (low == ones, low == 0)
 
 
 def pack_hop(count, bit, held_ref, left, right, out_ref):
@@ -223,7 +222,7 @@
         out_ref[size : size + HALO, :] = left
         out_ref[size + HALO :, :] = right
     else:
-        out_ref[size:, :] = jnp.where(right_moves(device, bit), right, left)
+        out_ref[size:, :] = jnp.where(moves(device, bit)[1], right, left)
 
 
 def unpack_hop(count, bit, got_ref, held_ref, left, right):
@@ -235,11 +234,8 @@
     if bit == 0:
         return got_ref[size : size + HALO, :], got_ref[size + HALO :, :]
     got = got_ref[size:, :]
-    if bit == 2:
-        moves = device % 4 == 0
-    else:
-        moves = device % (1 << bit) == (1 << bit) - 1
-    return jnp.where(moves, got, left), jnp.where(right_moves(device, bit), got, right)
+    left_moves, right_moves = moves(device, bit)
+    return jnp.where(left_moves, got, left), jnp.where(right_moves, got, right)
 
 
 def back_kernel(
@@ -404,34 +400,33 @@
         functools.partial(back_kernel, count, bits[0]),
         (struct((ROWS, D), F32), *carried, message(bits[0])),
     )(matrix, d_pre, weight_one)
-    parts, got = lax.optimization_barrier((parts, swap(out, 1 << bits[0])))
+    got = swap(out, 1 << bits[0])
+    for at in range(1, len(bits) - 3):
+        out, held = next_hop(at, got, held)
+        got = swap(out, 1 << bits[at])
+    parts, got = lax.optimization_barrier((parts, got))
 
     keep, give = call(plane_sum_kernel, (struct((wide, D), F32), struct((wide, D), BF16)))(*parts)
-    out, held = next_hop(1, got, held)
-    give, out = lax.optimization_barrier((give, out))
-    other, got = lax.optimization_barrier((swap(give, PLANE), swap(out, 1 << bits[1])))
+    out, held = next_hop(len(bits) - 3, got, held)
+    other, got = lax.optimization_barrier((swap(give, PLANE), swap(out, 1)))
 
     pair = functools.partial(pair_sum_kernel, 1.0)
     total = call(pair, struct((wide, D), BF16))(keep, other)
-    out, held = next_hop(2, got, held)
-    for bit in bits[3:-1]:
+    out, held = next_hop(len(bits) - 2, got, held)
+    for bit in range(3, len(bits) - 1):
         total = call(pair, struct((wide, D), BF16))(total, swap(total, 1 << bit))
-    total, out = lax.optimization_barrier((total, out))
-    other, got = lax.optimization_barrier((swap(total, 1 << bits[-1]), swap(out, 1 << bits[2])))
+    other, got = lax.optimization_barrier((swap(total, count // 2), swap(out, 2)))
 
     total = call(
         functools.partial(pair_sum_kernel, 1.0 / math.sqrt(ROWS * count)),
         struct((wide, D), BF16),
     )(total, other)
-    out, held = next_hop(3, got, held)
-    total, out = lax.optimization_barrier((total, out))
-    other, got = lax.optimization_barrier((swap(total, PLANE), swap(out, 1 << bits[3])))
+    other = swap(total, PLANE)
 
     chunk = jnp.concatenate([total, other], axis=0)
     chunks = [chunk] + [swap(chunk, v) for v in range(1, PLANE)]
-    for at in range(4, len(bits)):
-        out, held = next_hop(at, got, held)
-        got = swap(out, 1 << bits[at])
+    out, held = next_hop(len(bits) - 1, got, held)
+    got = swap(out, PLANE)
     d_features = call(
         functools.partial(features_kernel, count, bits[-1]),
         struct((ROWS, D), BF16),

time: 79.9 us -> 75.4 us (0.944)
  waiting for transfers between devices: 44.2 us -> 36.8 us
  starting transfers between devices: 27.1 us -> 30 us
    ppermute x14, waiting for transfers between devices: 34.5 us -> 27.2 us  [swap(): return lax.ppermute(value, 'node', [(i, i ^ flip) for i in range(count)])]
    ppermute x14, starting transfers between devices: 18 us -> 20.9 us  [swap(): return lax.ppermute(value, 'node', [(i, i ^ flip) for i in range(count)])]
  transfers between devices with their start and end apart: 16 -> 16, of which waited for: 11 -> 9; matrix products, arithmetic and copies ran while one was open for 0% -> 0% of each run, Pallas kernels for 2% -> 2%
where the time goes in v6:
time: 75.4 us; the launch traced here: 75.1 us
  waiting for transfers between devices  36.8 us (49%)
  starting transfers between devices  30 us (40%)
  Pallas kernels  7.52 us (10%)
  between operations  0.78 us (1%)
    ppermute x14, waiting for transfers between devices, swap(): return lax.ppermute(value, 'node', [(i, i ^ flip) for i in range(count)])  27.2 us
    ppermute x14, starting transfers between devices, swap(): return lax.ppermute(value, 'node', [(i, i ^ flip) for i in range(count)])  20.9 us
    all_to_all x1, waiting for transfers between devices, shards(): lax.all_to_all(send, 'node', split_axis=0, concat_axis=0, tiled=True)  9.63 us
    all_to_all x1, starting transfers between devices, shards(): lax.all_to_all(send, 'node', split_axis=0, concat_axis=0, tiled=True)  8.46 us
    pallas_call x1, Pallas kernels, shards(): call(functools.partial(prepare_kernel, count), (struct((ROWS, chain + far...  3.54 us
  transfers between devices with their start and end apart: 16, of which 9 were waited for; matrix products, arithmetic and copies ran while one was open for 0% of the time, Pallas kernels for 2%

profile of v6, /device:TPU:0, one launch (start us, length us, event | category | flops | bytes accessed | tf_op | source)
XLA Modules:
  0.0 75.1 jit_solution(15608096557006756218)
XLA Ops:
  0.6 3.5 %shard_map.103 = (bf16[128,768]{1,0:T(8,128)(2,1)S(1)}, f32[128,512]{1,0:T(8,128)S(1)}, bf16[16,32,512]{2,1,0:T(8,128)(2,1)}, bf16[64,512]{1,0:T(8,128)(2,1)S(1)}, bf16[64,512]{1,0:T(8,128)(2,1)S(1)}) custom-call(s32[32,128]{1,0:T(8,128)} %bitcast.4, s32[32,128]{1,0:T(8,128)} %bitcast.5, s32[2,256]{1,0:T(2,128)} %bitcast.6, s32[1,256]{1,0:T(1,128)} %bitcast.7, ...), custom_call_target="tpu_custom_call" | custom-call | tf_op jit(solution)/shard_map/pallas_call | solution.py:332
  4.2 8.5 %all-to-all-start = ((bf16[16,32,512]{2,1,0:T(8,128)(2,1)}), bf16[16,32,512]{2,1,0:T(8,128)(2,1)S(1)}, u32[]{:S(2)}, u32[]{:S(2)}) async-start(bf16[16,32,512]{2,1,0:T(8,128)(2,1)} %get-tuple-element.45), calls=%async_computation | async-start | bytes 1048576 | tf_op jit(solution)/shard_map/all_to_all | solution.py:364
  12.7 1.9 %collective-permute-start = (bf16[64,512]{1,0:T(8,128)(2,1)S(1)}, bf16[64,512]{1,0:T(8,128)(2,1)S(1)}, u32[]{:S(2)}, u32[]{:S(2)}) collective-permute-start(bf16[64,512]{1,0:T(8,128)(2,1)S(1)} %get-tuple-element.46), channel_id=1, source_target_pairs={{0,2},{2,0},{4,6},{6,4},{8,10},{10,8},{12,14},{14,12},{16,18},{18,... | collective-permute-start | bytes 196616 | tf_op jit(solution)/shard_map/ppermute | solution.py:330
  14.6 0.7 collective-permute-start.1
  15.3 2.9 %collective-permute-done.near_ref = bf16[64,512]{1,0:T(8,128)(2,1)S(1)} collective-permute-done((bf16[64,512]{1,0:T(8,128)(2,1)S(1)}, bf16[64,512]{1,0:T(8,128)(2,1)S(1)}, u32[]{:S(2)}, u32[]{:S(2)}) %collective-permute-start) | collective-permute-done | bytes 65568 | tf_op jit(solution)/shard_map/ppermute | solution.py:330
  18.2 9.6 %all-to-all-done.recv_ref = bf16[16,32,512]{2,1,0:T(8,128)(2,1)S(1)} async-done(((bf16[16,32,512]{2,1,0:T(8,128)(2,1)}), bf16[16,32,512]{2,1,0:T(8,128)(2,1)S(1)}, u32[]{:S(2)}, u32[]{:S(2)}) %all-to-all-start) | async-done | bytes 524320 | tf_op jit(solution)/shard_map/all_to_all | solution.py:364
  27.8 1.2 %shard_map.104 = (f32[256,512]{1,0:T(8,128)S(1)}, bf16[256,512]{1,0:T(8,128)(2,1)S(1)}, bf16[256,512]{1,0:T(8,128)(2,1)S(1)}, bf16[256,512]{1,0:T(8,128)(2,1)S(1)}, bf16[128,512]{1,0:T(8,128)(2,1)S(1)}) custom-call(bf16[128,768]{1,0:T(8,128)(2,1)S(1)} %get-tuple-element.43.mat_ref, bf16[128,512]{1,0:T(8,128)(2,1)S(1)} %copy-done.1, ...), custom_call_target="tpu_custom_call" | custom-call | tf_op jit(solution)/shard_map/pallas_call | solution.py:366
  29.0 0.6 collective-permute-start.2
  29.7 1.3 %collective-permute-start.3 = (bf16[256,512]{1,0:T(8,128)(2,1)S(1)}, bf16[256,512]{1,0:T(8,128)(2,1)S(1)}, u32[]{:S(2)}, u32[]{:S(2)}) collective-permute-start(bf16[256,512]{1,0:T(8,128)(2,1)S(1)} %get-tuple-element.52), channel_id=1, source_target_pairs={{0,4},{2,6},{4,0},{6,2},{8,12},{10,14},{12,8},{14,10},{16,20},{18,... | collective-permute-start | bytes 786440 | tf_op jit(solution)/shard_map/ppermute | solution.py:330
  30.9 1.7 %collective-permute-start.4 = (bf16[256,512]{1,0:T(8,128)(2,1)S(1)}, bf16[256,512]{1,0:T(8,128)(2,1)S(1)}, u32[]{:S(2)}, u32[]{:S(2)}) collective-permute-start(bf16[256,512]{1,0:T(8,128)(2,1)S(1)} %get-tuple-element.53), channel_id=1, source_target_pairs={{0,6},{2,4},{4,2},{6,0},{8,14},{10,12},{12,10},{14,8},{16,22},{18,... | collective-permute-start | bytes 786440 | tf_op jit(solution)/shard_map/ppermute | solution.py:330
  33.2 3.1 %collective-permute-start.5 = (bf16[160,512]{1,0:T(8,128)(2,1)S(1)}, bf16[160,512]{1,0:T(8,128)(2,1)S(1)}, u32[]{:S(2)}, u32[]{:S(2)}) collective-permute-start(bf16[160,512]{1,0:T(8,128)(2,1)S(1)} %get-tuple-element.54), channel_id=1, source_target_pairs={{0,16},{2,18},{4,20},{6,22},{8,24},{10,26},{12,28},{14,30},{16,0},... | collective-permute-start | bytes 491528 | tf_op jit(solution)/shard_map/ppermute | solution.py:330
  36.3 5.8 %collective-permute-done.5.got_ref = bf16[160,512]{1,0:T(8,128)(2,1)S(1)} collective-permute-done((bf16[160,512]{1,0:T(8,128)(2,1)S(1)}, bf16[160,512]{1,0:T(8,128)(2,1)S(1)}, u32[]{:S(2)}, u32[]{:S(2)}) %collective-permute-start.5) | collective-permute-done | bytes 163872 | tf_op jit(solution)/shard_map/ppermute | solution.py:330
  42.1 1.3 %collective-permute-start.7 = (bf16[192,512]{1,0:T(8,128)(2,1)S(1)}, bf16[192,512]{1,0:T(8,128)(2,1)S(1)}, u32[]{:S(2)}, u32[]{:S(2)}) collective-permute-start(bf16[192,512]{1,0:T(8,128)(2,1)S(1)} %get-tuple-element.65), channel_id=1, source_target_pairs={{0,2},{2,0},{4,6},{6,4},{8,10},{10,8},{12,14},{14,12},{16,18},{18,... | collective-permute-start | bytes 589832 | tf_op jit(solution)/shard_map/ppermute | solution.py:330
  43.5 3.4 %collective-permute-start.6 = (bf16[128,512]{1,0:T(8,128)(2,1)S(1)}, bf16[128,512]{1,0:T(8,128)(2,1)S(1)}, u32[]{:S(2)}, u32[]{:S(2)}) collective-permute-start(bf16[128,512]{1,0:T(8,128)(2,1)S(1)} %get-tuple-element.60), channel_id=1, source_target_pairs={{0,8},{2,10},{4,12},{6,14},{8,0},{10,2},{12,4},{14,6},{16,24},{18,... | collective-permute-start | bytes 393224 | tf_op jit(solution)/shard_map/ppermute | solution.py:330
  46.9 2.9 %collective-permute-done.6.two_ref = bf16[128,512]{1,0:T(8,128)(2,1)S(1)} collective-permute-done((bf16[128,512]{1,0:T(8,128)(2,1)S(1)}, bf16[128,512]{1,0:T(8,128)(2,1)S(1)}, u32[]{:S(2)}, u32[]{:S(2)}) %collective-permute-start.6) | collective-permute-done | bytes 131104 | tf_op jit(solution)/shard_map/ppermute | solution.py:330
  50.0 3.9 %collective-permute-start.8 = (bf16[128,512]{1,0:T(8,128)(2,1)S(1)}, bf16[128,512]{1,0:T(8,128)(2,1)S(1)}, u32[]{:S(2)}, u32[]{:S(2)}) collective-permute-start(bf16[128,512]{1,0:T(8,128)(2,1)S(1)} %shard_map.108.one_ref), channel_id=1, source_target_pairs={{0,16},{2,18},{4,20},{6,22},{8,24},{10,26},{12,28},{14,30},{16,0},... | collective-permute-start | bytes 393224 | tf_op jit(solution)/shard_map/ppermute | solution.py:330
  53.9 4.5 %collective-permute-done.8.two_ref = bf16[128,512]{1,0:T(8,128)(2,1)S(1)} collective-permute-done((bf16[128,512]{1,0:T(8,128)(2,1)S(1)}, bf16[128,512]{1,0:T(8,128)(2,1)S(1)}, u32[]{:S(2)}, u32[]{:S(2)}) %collective-permute-start.8) | collective-permute-done | bytes 131104 | tf_op jit(solution)/shard_map/ppermute | solution.py:330
  58.5 5.0 %collective-permute-done.11 = bf16[128,512]{1,0:T(8,128)(2,1)S(1)} collective-permute-done((bf16[128,512]{1,0:T(8,128)(2,1)S(1)}, bf16[128,512]{1,0:T(8,128)(2,1)S(1)}, u32[]{:S(2)}, u32[]{:S(2)}) %collective-permute-start.11) | collective-permute-done | bytes 131104 | tf_op jit(solution)/shard_map/ppermute | solution.py:330
  63.5 2.7 %collective-permute-start.13 = (bf16[256,512]{1,0:T(8,128)(2,1)S(1)}, bf16[256,512]{1,0:T(8,128)(2,1)S(1)}, u32[]{:S(2)}, u32[]{:S(2)}) collective-permute-start(bf16[256,512]{1,0:T(8,128)(2,1)S(1)} %pad_maximum_fusion.refs_0_), channel_id=1, source_target_pairs={{0,4},{2,6},{4,0},{6,2},{8,12},{10,14},{12,8},{14,10},{16,20},{18,... | collective-permute-start | bytes 786440 | tf_op jit(solution)/shard_map/ppermute | solution.py:330
  66.3 0.7 collective-permute-start.12
  67.1 5.3 %collective-permute-done.10.got_ref = bf16[160,512]{1,0:T(8,128)(2,1)S(1)} collective-permute-done((bf16[160,512]{1,0:T(8,128)(2,1)S(1)}, bf16[160,512]{1,0:T(8,128)(2,1)S(1)}, u32[]{:S(2)}, u32[]{:S(2)}) %collective-permute-start.10) | collective-permute-done | bytes 163872 | tf_op jit(solution)/shard_map/ppermute | solution.py:330
  72.4 0.9 %shard_map.111 = bf16[128,512]{1,0:T(8,128)(2,1)} custom-call(bf16[128,768]{1,0:T(8,128)(2,1)S(1)} %get-tuple-element.43.mat_ref, f32[128,512]{1,0:T(8,128)S(1)} %get-tuple-element.49.own_ref, bf16[160,512]{1,0:T(8,128)(2,1)S(1)} %collective-permute-done.10.got_ref, bf16[16,16,512]{2,1,0:T(8,128)(2,1)S(1)} %get-tuple-element.77.was_ref, ...), custom_call_target="tpu_custom_call" | custom-call | tf_op jit(solution)/shard_map/pallas_call | solution.py:430
  73.4 0.7 collective-permute-done.12.refs_1_
  74.1 1.0 %shard_map.113 = (bf16[512,512]{1,0:T(8,128)(2,1)}, bf16[512,512]{1,0:T(8,128)(2,1)}) custom-call(bf16[256,512]{1,0:T(8,128)(2,1)S(1)} %pad_maximum_fusion.refs_0_, bf16[256,512]{1,0:T(8,128)(2,1)S(1)} %collective-permute-done.12.refs_1_, bf16[256,512]{1,0:T(8,128)(2,1)S(1)} %collective-permute-done.13.refs_2_, ...), custom_call_target="tpu_custom_call" | custom-call | tf_op jit(solution)/shard_map/pallas_call | solution.py:439
  (26 shorter events, 1.3 us)
Async XLA Ops:
  0.6 27.2 %copy-start.2 = (bf16[512,512]{1,0:T(8,128)(2,1)S(1)}, bf16[512,512]{1,0:T(8,128)(2,1)}, u32[]{:S(2)}) copy-start(bf16[512,512]{1,0:T(8,128)(2,1)} %w_two_ref.1) | copy-start | bytes 1572868
  4.2 23.6 %copy-start = (bf16[512,512]{1,0:T(8,128)(2,1)S(1)}, bf16[512,512]{1,0:T(8,128)(2,1)}, u32[]{:S(2)}) copy-start(bf16[512,512]{1,0:T(8,128)(2,1)} %w_one_ref.3) | copy-start | bytes 1572868
  4.2 23.6 %copy-start.1 = (bf16[128,512]{1,0:T(8,128)(2,1)S(1)}, bf16[128,512]{1,0:T(8,128)(2,1)}, u32[]{:S(2)}) copy-start(bf16[128,512]{1,0:T(8,128)(2,1)} %feat_ref.1) | copy-start | bytes 393220
  4.2 23.6 %all-to-all-start = ((bf16[16,32,512]{2,1,0:T(8,128)(2,1)}), bf16[16,32,512]{2,1,0:T(8,128)(2,1)S(1)}, u32[]{:S(2)}, u32[]{:S(2)}) async-start(bf16[16,32,512]{2,1,0:T(8,128)(2,1)} %get-tuple-element.45), calls=%async_computation | async-start | bytes 1048576 | tf_op jit(solution)/shard_map/all_to_all | solution.py:364
  12.7 5.5 %collective-permute-start = (bf16[64,512]{1,0:T(8,128)(2,1)S(1)}, bf16[64,512]{1,0:T(8,128)(2,1)S(1)}, u32[]{:S(2)}, u32[]{:S(2)}) collective-permute-start(bf16[64,512]{1,0:T(8,128)(2,1)S(1)} %get-tuple-element.46), channel_id=1, source_target_pairs={{0,2},{2,0},{4,6},{6,4},{8,10},{10,8},{12,14},{14,12},{16,18},{18,... | collective-permute-start | bytes 196616 | tf_op jit(solution)/shard_map/ppermute | solution.py:330
  14.6 3.6 %collective-permute-start.1 = (bf16[64,512]{1,0:T(8,128)(2,1)S(1)}, bf16[64,512]{1,0:T(8,128)(2,1)S(1)}, u32[]{:S(2)}, u32[]{:S(2)}) collective-permute-start(bf16[64,512]{1,0:T(8,128)(2,1)S(1)} %get-tuple-element.47), channel_id=1, source_target_pairs={{2,4},{6,8},{10,12},{14,16},{18,20},{22,24},{26,28},{4,2},{8,6},{1... | collective-permute-start | bytes 196616 | tf_op jit(solution)/shard_map/ppermute | solution.py:363
  29.0 13.0 %collective-permute-start.2 = (bf16[256,512]{1,0:T(8,128)(2,1)S(1)}, bf16[256,512]{1,0:T(8,128)(2,1)S(1)}, u32[]{:S(2)}, u32[]{:S(2)}) collective-permute-start(bf16[256,512]{1,0:T(8,128)(2,1)S(1)} %get-tuple-element.51), channel_id=1, source_target_pairs={{0,2},{2,0},{4,6},{6,4},{8,10},{10,8},{12,14},{14,12},{16,18},{18,... | collective-permute-start | bytes 786440 | tf_op jit(solution)/shard_map/ppermute | solution.py:330
  29.7 12.4 %collective-permute-start.3 = (bf16[256,512]{1,0:T(8,128)(2,1)S(1)}, bf16[256,512]{1,0:T(8,128)(2,1)S(1)}, u32[]{:S(2)}, u32[]{:S(2)}) collective-permute-start(bf16[256,512]{1,0:T(8,128)(2,1)S(1)} %get-tuple-element.52), channel_id=1, source_target_pairs={{0,4},{2,6},{4,0},{6,2},{8,12},{10,14},{12,8},{14,10},{16,20},{18,... | collective-permute-start | bytes 786440 | tf_op jit(solution)/shard_map/ppermute | solution.py:330
  30.9 11.1 %collective-permute-start.4 = (bf16[256,512]{1,0:T(8,128)(2,1)S(1)}, bf16[256,512]{1,0:T(8,128)(2,1)S(1)}, u32[]{:S(2)}, u32[]{:S(2)}) collective-permute-start(bf16[256,512]{1,0:T(8,128)(2,1)S(1)} %get-tuple-element.53), channel_id=1, source_target_pairs={{0,6},{2,4},{4,2},{6,0},{8,14},{10,12},{12,10},{14,8},{16,22},{18,... | collective-permute-start | bytes 786440 | tf_op jit(solution)/shard_map/ppermute | solution.py:330
  33.2 8.9 %collective-permute-start.5 = (bf16[160,512]{1,0:T(8,128)(2,1)S(1)}, bf16[160,512]{1,0:T(8,128)(2,1)S(1)}, u32[]{:S(2)}, u32[]{:S(2)}) collective-permute-start(bf16[160,512]{1,0:T(8,128)(2,1)S(1)} %get-tuple-element.54), channel_id=1, source_target_pairs={{0,16},{2,18},{4,20},{6,22},{8,24},{10,26},{12,28},{14,30},{16,0},... | collective-permute-start | bytes 491528 | tf_op jit(solution)/shard_map/ppermute | solution.py:330
  42.1 7.7 %collective-permute-start.7 = (bf16[192,512]{1,0:T(8,128)(2,1)S(1)}, bf16[192,512]{1,0:T(8,128)(2,1)S(1)}, u32[]{:S(2)}, u32[]{:S(2)}) collective-permute-start(bf16[192,512]{1,0:T(8,128)(2,1)S(1)} %get-tuple-element.65), channel_id=1, source_target_pairs={{0,2},{2,0},{4,6},{6,4},{8,10},{10,8},{12,14},{14,12},{16,18},{18,... | collective-permute-start | bytes 589832 | tf_op jit(solution)/shard_map/ppermute | solution.py:330
  43.5 6.3 %collective-permute-start.6 = (bf16[128,512]{1,0:T(8,128)(2,1)S(1)}, bf16[128,512]{1,0:T(8,128)(2,1)S(1)}, u32[]{:S(2)}, u32[]{:S(2)}) collective-permute-start(bf16[128,512]{1,0:T(8,128)(2,1)S(1)} %get-tuple-element.60), channel_id=1, source_target_pairs={{0,8},{2,10},{4,12},{6,14},{8,0},{10,2},{12,4},{14,6},{16,24},{18,... | collective-permute-start | bytes 393224 | tf_op jit(solution)/shard_map/ppermute | solution.py:330
  49.9 8.5 %collective-permute-start.9 = (bf16[160,512]{1,0:T(8,128)(2,1)S(1)}, bf16[160,512]{1,0:T(8,128)(2,1)S(1)}, u32[]{:S(2)}, u32[]{:S(2)}) collective-permute-start(bf16[160,512]{1,0:T(8,128)(2,1)S(1)} %get-tuple-element.71), channel_id=1, source_target_pairs={{0,4},{2,6},{4,0},{6,2},{8,12},{10,14},{12,8},{14,10},{16,20},{18,... | collective-permute-start | bytes 491528 | tf_op jit(solution)/shard_map/ppermute | solution.py:330
  50.0 8.4 %collective-permute-start.8 = (bf16[128,512]{1,0:T(8,128)(2,1)S(1)}, bf16[128,512]{1,0:T(8,128)(2,1)S(1)}, u32[]{:S(2)}, u32[]{:S(2)}) collective-permute-start(bf16[128,512]{1,0:T(8,128)(2,1)S(1)} %shard_map.108.one_ref), channel_id=1, source_target_pairs={{0,16},{2,18},{4,20},{6,22},{8,24},{10,26},{12,28},{14,30},{16,0},... | collective-permute-start | bytes 393224 | tf_op jit(solution)/shard_map/ppermute | solution.py:330
  58.4 5.0 %collective-permute-start.11 = (bf16[128,512]{1,0:T(8,128)(2,1)S(1)}, bf16[128,512]{1,0:T(8,128)(2,1)S(1)}, u32[]{:S(2)}, u32[]{:S(2)}) collective-permute-start(bf16[128,512]{1,0:T(8,128)(2,1)S(1)} %shard_map.112), channel_id=1, source_target_pairs={{0,8},{2,10},{4,12},{6,14},{8,0},{10,2},{12,4},{14,6},{16,24},{18,... | collective-permute-start | bytes 393224 | tf_op jit(solution)/shard_map/ppermute | solution.py:330
  63.5 9.8 %collective-permute-start.14 = (bf16[256,512]{1,0:T(8,128)(2,1)S(1)}, bf16[256,512]{1,0:T(8,128)(2,1)S(1)}, u32[]{:S(2)}, u32[]{:S(2)}) collective-permute-start(bf16[256,512]{1,0:T(8,128)(2,1)S(1)} %pad_maximum_fusion.refs_0_), channel_id=1, source_target_pairs={{0,6},{2,4},{4,2},{6,0},{8,14},{10,12},{12,10},{14,8},{16,22},{18,... | collective-permute-start | bytes 786440 | tf_op jit(solution)/shard_map/ppermute | solution.py:330
  63.5 9.9 %collective-permute-start.13 = (bf16[256,512]{1,0:T(8,128)(2,1)S(1)}, bf16[256,512]{1,0:T(8,128)(2,1)S(1)}, u32[]{:S(2)}, u32[]{:S(2)}) collective-permute-start(bf16[256,512]{1,0:T(8,128)(2,1)S(1)} %pad_maximum_fusion.refs_0_), channel_id=1, source_target_pairs={{0,4},{2,6},{4,0},{6,2},{8,12},{10,14},{12,8},{14,10},{16,20},{18,... | collective-permute-start | bytes 786440 | tf_op jit(solution)/shard_map/ppermute | solution.py:330
  66.3 7.8 %collective-permute-start.12 = (bf16[256,512]{1,0:T(8,128)(2,1)S(1)}, bf16[256,512]{1,0:T(8,128)(2,1)S(1)}, u32[]{:S(2)}, u32[]{:S(2)}) collective-permute-start(bf16[256,512]{1,0:T(8,128)(2,1)S(1)} %pad_maximum_fusion.refs_0_), channel_id=1, source_target_pairs={{0,2},{2,0},{4,6},{6,4},{8,10},{10,8},{12,14},{14,12},{16,18},{18,... | collective-permute-start | bytes 786440 | tf_op jit(solution)/shard_map/ppermute | solution.py:330
  67.0 5.4 %collective-permute-start.10 = (bf16[160,512]{1,0:T(8,128)(2,1)S(1)}, bf16[160,512]{1,0:T(8,128)(2,1)S(1)}, u32[]{:S(2)}, u32[]{:S(2)}) collective-permute-start(bf16[160,512]{1,0:T(8,128)(2,1)S(1)} %get-tuple-element.76), channel_id=1, source_target_pairs={{0,8},{2,10},{4,12},{6,14},{8,0},{10,2},{12,4},{14,6},{16,24},{18,... | collective-permute-start | bytes 491528 | tf_op jit(solution)/shard_map/ppermute | solution.py:330

commit v7 on v6

--- a/solution.py
+++ b/solution.py
@@ -19,6 +19,7 @@
 HALO_COL = ROWS
 FAR_COL = 2 * ROWS
 PLANE = 4
+WIDE = D // PLANE
 
 F32 = jnp.float32
 BF16 = jnp.bfloat16
@@ -57,12 +58,13 @@
 
 def prepare_kernel(
     count, nbr_hbm, wgt_hbm, tab_hbm, cnt_hbm, feat_hbm, up_hbm,
-    mat_ref, own_ref, send_ref, near_ref, next_ref,
+    mat_ref, pick_ref, total_ref, own_ref, send_hbm, near_ref, next_ref,
     nbr_ref, wgt_ref, tab_ref, cnt_ref, feat_ref, up_ref, sems, rows_scr, at_scr,
+    rows_out, terms_out, out_sems,
 ):
     inputs = (
-        (tab_hbm, tab_ref), (cnt_hbm, cnt_ref), (nbr_hbm, nbr_ref),
-        (wgt_hbm, wgt_ref), (up_hbm, up_ref), (feat_hbm, feat_ref),
+        (tab_hbm, tab_ref), (cnt_hbm, cnt_ref), (feat_hbm, feat_ref),
+        (nbr_hbm, nbr_ref), (wgt_hbm, wgt_ref), (up_hbm, up_ref),
     )
     copies = [
         pltpu.make_async_copy(src, dst, sems.at[i]) for i, (src, dst) in enumerate(inputs)
@@ -81,6 +83,7 @@
     step = min(pairs, 256)
     listed = jnp.zeros((far, 8), F32)
     asked = jnp.zeros((far, 8), F32)
+    asked_wide = jnp.zeros((8, far), F32)
     peer_wide = iota((far, step), 0) // SLOT
     for at in range(0, pairs, step):
         pair = iota((far, step), 1) + at
@@ -89,6 +92,7 @@
         theirs = jnp.where(pair == peer_wide * count + device, 1.0, 0.0).astype(BF16)
         listed = listed + nt(mine, rows)
         asked = asked + nt(theirs, rows)
+        asked_wide = asked_wide + nt(rows, theirs)
     listed = listed.astype(jnp.int32)
     asked = asked.astype(jnp.int32)
     col = iota((far, 1), 0)
@@ -99,9 +103,20 @@
     in_band = (node >= first - HALO) & (node < first + ROWS + HALO)
     far_node = jnp.where((slot < listed[:, 2:3]) & jnp.logical_not(in_band), node, -1)
     asked_row = jnp.where(slot == 0, asked[:, 0:1], asked[:, 1:2]) * BLK + inner
-
+    pick = jnp.where(asked_row == iota((far, ROWS), 1), 1.0, 0.0).astype(BF16)
+    wide_col = iota((1, far), 1)
+    asked_wide = asked_wide.astype(jnp.int32)
+    wide_row = jnp.where(wide_col // BLK % CAP == 0, asked_wide[0:1], asked_wide[1:2]) * BLK
+    wide_row = wide_row + wide_col % BLK
+    pick_ref[...] = jnp.where(wide_row == iota((ROWS, far), 0), 1.0, 0.0).astype(BF16)
     copies[2].wait()
+    features = feat_ref[...]
+    rows_out[...] = nn(pick, features).astype(BF16).reshape(count, SLOT, D)
+    rows_copy = pltpu.make_async_copy(rows_out, send_hbm.at[:, 0:SLOT, :], out_sems.at[0])
+    rows_copy.start()
+
     copies[3].wait()
+    copies[4].wait()
     weight = wgt_ref[...].astype(F32)
     neighbour = nbr_ref[...]
 
@@ -122,17 +137,17 @@
         at_scr[FAR_COL + at : FAR_COL + at + ROWS, :] = counted(nodes, jnp.zeros(square, F32))
 
     adj_mat = at_scr[...]
-    matrix = adj_mat.T
+    total = jnp.broadcast_to(jnp.sum(adj_mat, axis=0, keepdims=True), square).T
+    total_ref[...] = total
     adj_mat = adj_mat.astype(BF16)
-    total = jnp.sum(matrix, axis=1, keepdims=True)
-    mat_ref[:, 0 : FAR_COL + far] = matrix.astype(BF16)
-    pick = jnp.where(asked_row == iota((far, ROWS), 1), 1.0, 0.0)
-    mat_ref[:, FAR_COL + far :] = pick.T.astype(BF16)
-
-    copies[4].wait()
-    scaled = (up_ref[...].astype(F32) / total).astype(BF16)
+    mat_ref[...] = adj_mat
     copies[5].wait()
-    features = feat_ref[...]
+    scaled = (up_ref[...].astype(F32) / total[:, 0:1]).astype(BF16)
+    terms_out[...] = nn(adj_mat[FAR_COL:], scaled).astype(BF16).reshape(count, SLOT, D)
+    terms_copy = pltpu.make_async_copy(
+        terms_out, send_hbm.at[:, SLOT : 2 * SLOT, :], out_sems.at[1]
+    )
+    terms_copy.start()
     own_ref[...] = nn(adj_mat[0:ROWS], scaled)
     rims = nn(adj_mat[HALO_COL : HALO_COL + 2 * HALO], scaled).astype(BF16)
     even = device % 2 == 0
@@ -141,61 +156,54 @@
     near_ref[HALO:, :] = jnp.where(even, rims[HALO:], rims[0:HALO])
     next_ref[0:HALO, :] = jnp.where(even, low, high)
     next_ref[HALO:, :] = jnp.where(even, rims[0:HALO], rims[HALO:])
-    rows_out = nn(pick.astype(BF16), features).astype(BF16)
-    send_ref[:, 0:SLOT, :] = rows_out.reshape(count, SLOT, D)
-    terms = nn(adj_mat[FAR_COL:], scaled).astype(BF16)
-    send_ref[:, SLOT : 2 * SLOT, :] = terms.reshape(count, SLOT, D)
-
-
-def row_total(mat_ref, far):
-    return jnp.sum(mat_ref[:, 0 : FAR_COL + far].astype(F32), axis=1, keepdims=True)
+    rows_copy.wait()
+    terms_copy.wait()
 
 
 def layer_kernel(
-    count, mat_ref, feat_ref, own_ref, recv_ref, near_ref, next_ref, w_one_ref, w_two_ref,
+    count, mat_ref, pick_ref, total_ref, feat_ref, own_ref, recv_ref, near_ref, next_ref,
+    w_one_ref, w_two_ref,
     *refs,
 ):
-    part_refs = refs[:PLANE]
-    d_pre_ref, rim_scr, u_scr, hidden_scr, agg_scr = refs[PLANE:]
+    part_refs = refs[:PLANE], refs[PLANE : 2 * PLANE]
+    d_pre_ref, rim_scr, u_scr, first_scr, second_scr = refs[2 * PLANE :]
     device = lax.axis_index("node")
     place, side = device % PLANE, device // PLANE % 2
     even = device % 2 == 0
     left = jnp.where(even, next_ref[...], near_ref[...])
     right = jnp.where(even, near_ref[...], next_ref[...])
     far = count * SLOT
-    total = row_total(mat_ref, far)
     rim_scr[0:HALO, :] = left[0:HALO]
     rim_scr[HALO : 2 * HALO, :] = right[0:HALO]
     rim_scr[2 * HALO :, :] = jnp.zeros((ROWS - 2 * HALO, D), BF16)
-    sums = nn(mat_ref[:, 0:ROWS], feat_ref[...])
-    sums = sums + nn(mat_ref[:, HALO_COL:FAR_COL], rim_scr[...])
-    sums = sums + nn(
-        mat_ref[:, FAR_COL : FAR_COL + far], recv_ref[:, 0:SLOT, :].reshape(far, D)
-    )
-    agg = (sums / total).astype(BF16)
-    agg_scr[...] = agg
+    sums = tn(mat_ref[0:ROWS, :], feat_ref[...])
+    sums = sums + tn(mat_ref[HALO_COL:FAR_COL, :], rim_scr[...])
+    sums = sums + tn(mat_ref[FAR_COL:, :], recv_ref[:, 0:SLOT, :].reshape(far, D))
+    agg = (sums / total_ref[:, 0:1]).astype(BF16)
+    first_scr[1] = agg
     u_scr[...] = own_ref[...] + nn(
-        mat_ref[:, FAR_COL + far :], recv_ref[:, SLOT : 2 * SLOT, :].reshape(far, D)
+        pick_ref[...], recv_ref[:, SLOT : 2 * SLOT, :].reshape(far, D)
     )
     u_scr[0:HALO, :] += left[HALO:].astype(F32)
     u_scr[ROWS - HALO : ROWS, :] += right[HALO:].astype(F32)
     u = u_scr[...].astype(BF16)
+    second_scr[0] = u
     back = nt(u, w_two_ref[...])
     pre = nn(agg, w_one_ref[...])
     square = pre * pre
     bend = jnp.tanh(0.7978845608 * pre * (1.0 + 0.044715 * square))
-    hidden_scr[...] = (0.5 * pre * (1.0 + bend)).astype(BF16)
+    first_scr[0] = (0.5 * pre * (1.0 + bend)).astype(BF16)
     slope = 0.5 * (1.0 + bend) + 0.5 * pre * (1.0 - bend * bend) * (
         0.7978845608 * (1.0 + 3.0 * 0.044715 * square)
     )
     d_pre = (back * slope).astype(BF16)
     d_pre_ref[...] = d_pre
-    wide = D // PLANE
-    for v in range(PLANE):
-        cols = pl.ds(pl.multiple_of((place ^ v) * wide, wide), wide)
-        for half, (first, second) in enumerate(((hidden_scr, u), (agg_scr, d_pre))):
-            rows = pl.ds(pl.multiple_of((side ^ half) * wide, wide), wide)
-            part_refs[v][rows, :] = tn(first[:, cols], second).astype(part_refs[v].dtype)
+    second_scr[1] = d_pre
+    for half, half_refs in enumerate(part_refs):
+        for v, ref in enumerate(half_refs):
+            cols = pl.ds(pl.multiple_of((place ^ v) * WIDE, WIDE), WIDE)
+            part = tn(first_scr[side ^ half, :, cols], second_scr[side ^ half])
+            ref[...] = part.astype(ref.dtype)
 
 
 def hop_bits(count):
@@ -239,19 +247,19 @@
 
 
 def back_kernel(
-    count, bit, mat_ref, d_pre_ref, w_one_ref, own_ref, held_ref, left_ref, right_ref, out_ref
-):
-    device = lax.axis_index("node")
-    far = count * SLOT
-    q = (nt(d_pre_ref[...], w_one_ref[...]) / row_total(mat_ref, far)).astype(BF16)
-    rims = tn(mat_ref[:, HALO_COL:FAR_COL], q).astype(BF16)
+    count, bit, mat_ref, total_ref, d_pre_ref, w_one_ref,
+    own_ref, held_ref, left_ref, right_ref, out_ref,
+):
+    device = lax.axis_index("node")
+    q = (nt(d_pre_ref[...], w_one_ref[...]) / total_ref[:, 0:1]).astype(BF16)
+    rims = nn(mat_ref[HALO_COL : HALO_COL + 2 * HALO, :], q).astype(BF16)
     left_ref[...] = rims[0:HALO]
     right_ref[...] = rims[HALO : 2 * HALO]
-    terms = tn(mat_ref[:, FAR_COL : FAR_COL + far], q).astype(BF16).reshape(count, SLOT, D)
+    terms = nn(mat_ref[FAR_COL:, :], q).astype(BF16).reshape(count, SLOT, D)
     for peer in range(count):
         held_ref[device ^ peer] = terms[peer]
     pack_hop(count, bit, held_ref, rims[0:HALO], rims[HALO : 2 * HALO], out_ref)
-    own_ref[...] = tn(mat_ref[:, 0:ROWS], q)
+    own_ref[...] = nn(mat_ref[0:ROWS, :], q)
 
 
 def hop_kernel(
@@ -268,7 +276,7 @@
 
 
 def features_kernel(
-    count, last, mat_ref, own_ref, got_ref, was_ref, was_left_ref, was_right_ref,
+    count, last, pick_ref, own_ref, got_ref, was_ref, was_left_ref, was_right_ref,
     out_ref, sum_scr, held_scr, block_scr,
 ):
     device = lax.axis_index("node")
@@ -279,24 +287,17 @@
     )
     for r in range(count):
         block_scr[device ^ r] = held_scr[r]
-    sum_scr[...] = own_ref[...] + nn(mat_ref[:, FAR_COL + far :], block_scr[...].reshape(far, D))
+    sum_scr[...] = own_ref[...] + nn(pick_ref[...], block_scr[...].reshape(far, D))
     sum_scr[0:HALO, :] += right.astype(F32)
     sum_scr[ROWS - HALO : ROWS, :] += left.astype(F32)
     out_ref[...] = sum_scr[...].astype(BF16)
 
 
-def sum_refs(refs, rows=slice(None)):
-    total = refs[0][rows, :].astype(F32)
-    for ref in refs[1:]:
-        total = total + ref[rows, :].astype(F32)
-    return total
-
-
-def plane_sum_kernel(*refs):
-    part_refs, (keep_ref, give_ref) = refs[:PLANE], refs[PLANE:]
-    wide = D // PLANE
-    keep_ref[...] = sum_refs(part_refs, slice(0, wide))
-    give_ref[...] = sum_refs(part_refs, slice(wide, 2 * wide)).astype(BF16)
+def sum_kernel(*refs):
+    total = refs[0][...].astype(F32)
+    for ref in refs[1:-1]:
+        total = total + ref[...].astype(F32)
+    refs[-1][...] = total.astype(BF16)
 
 
 def pair_sum_kernel(scale, one_ref, two_ref, out_ref):
@@ -305,15 +306,23 @@
 
 
 def gather_kernel(*refs):
-    chunk_refs, out_refs = refs[:PLANE], refs[PLANE:]
-    wide = D // PLANE
+    chunk_refs, out_refs, sems = refs[: 2 * PLANE], refs[2 * PLANE : 2 * PLANE + 2], refs[-1]
     device = lax.axis_index("node")
     place, side = device % PLANE, device // PLANE % 2
-    for v, ref in enumerate(chunk_refs):
-        row = pl.ds(pl.multiple_of((place ^ v) * wide, wide), wide)
-        for half, out_ref in enumerate(out_refs):
-            at = pl.ds(pl.multiple_of((side ^ half) * wide, wide), wide)
-            out_ref[row, :] = ref[at, :]
+    for low in range(2):
+
+        @pl.when(side == low)
+        def _():
+            copies = []
+            for at, ref in enumerate(chunk_refs):
+                row = pl.multiple_of((place ^ (at % PLANE)) * WIDE, WIDE)
+                out_ref = out_refs[low ^ (at // PLANE)]
+                copies.append(
+                    pltpu.make_async_copy(ref, out_ref.at[pl.ds(row, WIDE), :], sems.at[at])
+                )
+                copies[-1].start()
+            for copy in copies:
+                copy.wait()
 
 
 def shards(
@@ -322,17 +331,19 @@
     count = lax.axis_size("node")
     far = count * SLOT
     chain = FAR_COL + far
-    wide = D // PLANE
     onward = [(i, i + 1) for i in range(1, count - 1, 2)]
     onward = onward + [(target, source) for source, target in onward]
 
     def swap(value, flip):
         return lax.ppermute(value, "node", [(i, i ^ flip) for i in range(count)])
 
-    matrix, own, send, near, onto = call(
+    vmem, hbm = (pl.BlockSpec(memory_space=space) for space in (pltpu.VMEM, pltpu.HBM))
+    matrix, pick, total, own, send, near, onto = call(
         functools.partial(prepare_kernel, count),
         (
-            struct((ROWS, chain + far), BF16),
+            struct((chain, ROWS), BF16),
+            struct((ROWS, far), BF16),
+            struct((ROWS, ROWS), F32),
             struct((ROWS, D), F32),
             struct((count, 2 * SLOT, D), BF16),
             struct((2 * HALO, D), BF16),
@@ -348,8 +359,12 @@
             pltpu.SemaphoreType.DMA((6,)),
             pltpu.VMEM((8, count * count), F32),
             pltpu.VMEM((chain, ROWS), F32),
+            pltpu.VMEM((count, SLOT, D), BF16),
+            pltpu.VMEM((count, SLOT, D), BF16),
+            pltpu.SemaphoreType.DMA((2,)),
         ),
-        in_specs=[pl.BlockSpec(memory_space=pltpu.HBM)] * 6,
+        in_specs=[hbm] * 6,
+        out_specs=(vmem, vmem, vmem, vmem, hbm, vmem, vmem),
     )(
         *(
             pltpu.with_memory_space_constraint(value, pltpu.HBM)
@@ -363,21 +378,20 @@
     onto = lax.ppermute(onto, "node", onward)
     received = lax.all_to_all(send, "node", split_axis=0, concat_axis=0, tiled=True)
 
+    piece, sent = struct((WIDE, D), F32), struct((WIDE, D), BF16)
     *parts, d_pre = call(
         functools.partial(layer_kernel, count),
-        (
-            struct((2 * D // PLANE, D), F32),
-            *[struct((2 * D // PLANE, D), BF16)] * (PLANE - 1),
-            struct((ROWS, D), BF16),
-        ),
+        (*([piece] + [sent] * (PLANE - 1)) * 2, struct((ROWS, D), BF16)),
         (
             pltpu.VMEM((ROWS, D), BF16),
             pltpu.VMEM((ROWS, D), F32),
-            pltpu.VMEM((ROWS, D), BF16),
-            pltpu.VMEM((ROWS, D), BF16),
+            pltpu.VMEM((2, ROWS, D), BF16),
+            pltpu.VMEM((2, ROWS, D), BF16),
         ),
-    )(matrix, features, own, received, near, onto, weight_one, weight_two)
-    parts = [parts[0]] + [swap(parts[v], v) for v in range(1, PLANE)]
+    )(matrix, pick, total, features, own, received, near, onto, weight_one, weight_two)
+    kept, given = parts[:PLANE], parts[PLANE:]
+    given = [given[0]] + [swap(given[v], v) for v in range(1, PLANE)]
+    kept = [kept[0]] + [swap(kept[v], v) for v in range(1, PLANE)]
 
     bits = hop_bits(count)
     carried = (
@@ -399,34 +413,23 @@
     own, *held, out = call(
         functools.partial(back_kernel, count, bits[0]),
         (struct((ROWS, D), F32), *carried, message(bits[0])),
-    )(matrix, d_pre, weight_one)
+    )(matrix, total, d_pre, weight_one)
     got = swap(out, 1 << bits[0])
-    for at in range(1, len(bits) - 3):
+    for at in range(1, len(bits)):
         out, held = next_hop(at, got, held)
         got = swap(out, 1 << bits[at])
-    parts, got = lax.optimization_barrier((parts, got))
-
-    keep, give = call(plane_sum_kernel, (struct((wide, D), F32), struct((wide, D), BF16)))(*parts)
-    out, held = next_hop(len(bits) - 3, got, held)
-    other, got = lax.optimization_barrier((swap(give, PLANE), swap(out, 1)))
-
-    pair = functools.partial(pair_sum_kernel, 1.0)
-    total = call(pair, struct((wide, D), BF16))(keep, other)
-    out, held = next_hop(len(bits) - 2, got, held)
+    total = call(sum_kernel, sent)(*kept, swap(call(sum_kernel, sent)(*given), PLANE))
     for bit in range(3, len(bits) - 1):
-        total = call(pair, struct((wide, D), BF16))(total, swap(total, 1 << bit))
-    other, got = lax.optimization_barrier((swap(total, count // 2), swap(out, 2)))
-
+        total = call(functools.partial(pair_sum_kernel, 1.0), sent)(
+            total, swap(total, 1 << bit)
+        )
+    other = swap(total, count // 2)
     total = call(
-        functools.partial(pair_sum_kernel, 1.0 / math.sqrt(ROWS * count)),
-        struct((wide, D), BF16),
+        functools.partial(pair_sum_kernel, 1.0 / math.sqrt(ROWS * count)), sent
     )(total, other)
-    other = swap(total, PLANE)
-
-    chunk = jnp.concatenate([total, other], axis=0)
-    chunks = [chunk] + [swap(chunk, v) for v in range(1, PLANE)]
-    out, held = next_hop(len(bits) - 1, got, held)
-    got = swap(out, PLANE)
+    far_total = swap(total, PLANE)
+    chunks = [total] + [swap(total, v) for v in range(1, PLANE)]
+    chunks = chunks + [far_total] + [swap(far_total, v) for v in range(1, PLANE)]
     d_features = call(
         functools.partial(features_kernel, count, bits[-1]),
         struct((ROWS, D), BF16),
@@ -435,8 +438,15 @@
             pltpu.VMEM((count, SLOT, D), BF16),
             pltpu.VMEM((count, SLOT, D), BF16),
         ),
-    )(matrix, own, got, *held)
-    grad_two, grad_one = call(gather_kernel, (struct((D, D), BF16), struct((D, D), BF16)))(*chunks)
+    )(pick, own, got, *held)
+    anywhere = pl.BlockSpec(memory_space=pl.ANY)
+    grad_two, grad_one = call(
+        gather_kernel,
+        (struct((D, D), BF16), struct((D, D), BF16)),
+        (pltpu.SemaphoreType.DMA((2 * PLANE,)),),
+        in_specs=[anywhere] * (2 * PLANE),
+        out_specs=(anywhere, anywhere),
+    )(*chunks)
     return d_features, grad_one, grad_two
 
 

time: 75.4 us -> 71.7 us (0.951)
  waiting for transfers between devices: 36.8 us -> 25.9 us
  starting transfers between devices: 30 us -> 37.4 us
    ppermute x14 -> x20, waiting for transfers between devices: 27.2 us -> 16.3 us  [swap(): return lax.ppermute(value, 'node', [(i, i ^ flip) for i in range(count)])]
    ppermute x14 -> x20, starting transfers between devices: 20.9 us -> 28.3 us  [swap(): return lax.ppermute(value, 'node', [(i, i ^ flip) for i in range(count)])]
  transfers between devices with their start and end apart: 16 -> 22, of which waited for: 9 -> 11; matrix products, arithmetic and copies ran while one was open for 0% -> 0% of each run, Pallas kernels for 2% -> 2%
where the time goes in v7:
time: 71.7 us; the launch traced here: 71.5 us
  starting transfers between devices  37.4 us (52%)
  waiting for transfers between devices  25.9 us (36%)
  Pallas kernels  7.35 us (10%)
  between operations  0.76 us (1%)
    ppermute x20, starting transfers between devices, swap(): return lax.ppermute(value, 'node', [(i, i ^ flip) for i in range(count)])  28.3 us
    ppermute x20, waiting for transfers between devices, swap(): return lax.ppermute(value, 'node', [(i, i ^ flip) for i in range(count)])  16.3 us
    all_to_all x1, waiting for transfers between devices, shards(): lax.all_to_all(send, 'node', split_axis=0, concat_axis=0, tiled=True)  9.62 us
    all_to_all x1, starting transfers between devices, shards(): lax.all_to_all(send, 'node', split_axis=0, concat_axis=0, tiled=True)  8.46 us
    pallas_call x1, Pallas kernels, shards(): call(functools.partial(prepare_kernel, count), (struct((chain, ROWS), BF1...  3.36 us
  transfers between devices with their start and end apart: 22, of which 11 were waited for; matrix products, arithmetic and copies ran while one was open for 0% of the time, Pallas kernels for 2%

profile of v7, /device:TPU:0, one launch (start us, length us, event | category | flops | bytes accessed | tf_op | source)
XLA Modules:
  0.0 71.5 jit_solution(6481506798961567474)
XLA Ops:
  0.6 3.4 %shard_map.103 = (bf16[512,128]{1,0:T(8,128)(2,1)S(1)}, bf16[128,256]{1,0:T(8,128)(2,1)S(1)}, f32[128,128]{1,0:T(8,128)S(1)}, f32[128,512]{1,0:T(8,128)S(1)}, bf...) custom-call(s32[32,128]{1,0:T(8,128)} %bitcast.4, s32[32,128]{1,0:T(8,128)} %bitcast.5, ...), custom_call_target="tpu_custom_call" | custom-call | tf_op jit(solution)/shard_map/pallas_call | solution.py:341
  4.0 8.5 %all-to-all-start = ((bf16[16,32,512]{2,1,0:T(8,128)(2,1)}), bf16[16,32,512]{2,1,0:T(8,128)(2,1)S(1)}, u32[]{:S(2)}, u32[]{:S(2)}) async-start(bf16[16,32,512]{2,1,0:T(8,128)(2,1)} %get-tuple-element.42), calls=%async_computation | async-start | bytes 1048576 | tf_op jit(solution)/shard_map/all_to_all | solution.py:379
  12.5 1.9 %collective-permute-start = (bf16[64,512]{1,0:T(8,128)(2,1)S(1)}, bf16[64,512]{1,0:T(8,128)(2,1)S(1)}, u32[]{:S(2)}, u32[]{:S(2)}) collective-permute-start(bf16[64,512]{1,0:T(8,128)(2,1)S(1)} %get-tuple-element.43), channel_id=1, source_target_pairs={{0,2},{2,0},{4,6},{6,4},{8,10},{10,8},{12,14},{14,12},{16,18},{18,... | collective-permute-start | bytes 196616 | tf_op jit(solution)/shard_map/ppermute | solution.py:338
  15.1 2.9 %collective-permute-done.near_ref = bf16[64,512]{1,0:T(8,128)(2,1)S(1)} collective-permute-done((bf16[64,512]{1,0:T(8,128)(2,1)S(1)}, bf16[64,512]{1,0:T(8,128)(2,1)S(1)}, u32[]{:S(2)}, u32[]{:S(2)}) %collective-permute-start) | collective-permute-done | bytes 65568 | tf_op jit(solution)/shard_map/ppermute | solution.py:338
  18.0 9.6 %all-to-all-done.recv_ref = bf16[16,32,512]{2,1,0:T(8,128)(2,1)S(1)} async-done(((bf16[16,32,512]{2,1,0:T(8,128)(2,1)}), bf16[16,32,512]{2,1,0:T(8,128)(2,1)S(1)}, u32[]{:S(2)}, u32[]{:S(2)}) %all-to-all-start) | async-done | bytes 524320 | tf_op jit(solution)/shard_map/all_to_all | solution.py:379
  27.6 1.2 %shard_map.104 = (f32[128,512]{1,0:T(8,128)S(1)}, bf16[128,512]{1,0:T(8,128)(2,1)S(1)}, bf16[128,512]{1,0:T(8,128)(2,1)S(1)}, bf16[128,512]{1,0:T(8,128)(2,1)S(1...) custom-call(bf16[512,128]{1,0:T(8,128)(2,1)S(1)} %get-tuple-element., ...), custom_call_target="tpu_custom_call" | custom-call | tf_op jit(solution)/shard_map/pallas_call | solution.py:382
  29.5 3.1 %collective-permute-start.2 = (bf16[160,512]{1,0:T(8,128)(2,1)S(1)}, bf16[160,512]{1,0:T(8,128)(2,1)S(1)}, u32[]{:S(2)}, u32[]{:S(2)}) collective-permute-start(bf16[160,512]{1,0:T(8,128)(2,1)S(1)} %get-tuple-element.47), channel_id=1, source_target_pairs={{0,16},{2,18},{4,20},{6,22},{8,24},{10,26},{12,28},{14,30},{16,0},... | collective-permute-start | bytes 491528 | tf_op jit(solution)/shard_map/ppermute | solution.py:338
  32.6 3.5 %collective-permute-start.11 = (bf16[128,512]{1,0:T(8,128)(2,1)S(1)}, bf16[128,512]{1,0:T(8,128)(2,1)S(1)}, u32[]{:S(2)}, u32[]{:S(2)}) collective-permute-start(bf16[128,512]{1,0:T(8,128)(2,1)S(1)} %get-tuple-element.70), channel_id=1, source_target_pairs={{0,6},{2,4},{4,2},{6,0},{8,14},{10,12},{12,10},{14,8},{16,22},{18,... | collective-permute-start | bytes 393224 | tf_op jit(solution)/shard_map/ppermute | solution.py:338
  36.1 2.9 %collective-permute-done.9.refs_1_ = bf16[128,512]{1,0:T(8,128)(2,1)S(1)} collective-permute-done((bf16[128,512]{1,0:T(8,128)(2,1)S(1)}, bf16[128,512]{1,0:T(8,128)(2,1)S(1)}, u32[]{:S(2)}, u32[]{:S(2)}) %collective-permute-start.9) | collective-permute-done | bytes 131104 | tf_op jit(solution)/shard_map/ppermute | solution.py:338
  39.0 1.6 %collective-permute-done.10.refs_2_ = bf16[128,512]{1,0:T(8,128)(2,1)S(1)} collective-permute-done((bf16[128,512]{1,0:T(8,128)(2,1)S(1)}, bf16[128,512]{1,0:T(8,128)(2,1)S(1)}, u32[]{:S(2)}, u32[]{:S(2)}) %collective-permute-start.10) | collective-permute-done | bytes 131104 | tf_op jit(solution)/shard_map/ppermute | solution.py:338
  40.6 1.3 %collective-permute-start.8 = (bf16[128,512]{1,0:T(8,128)(2,1)S(1)}, bf16[128,512]{1,0:T(8,128)(2,1)S(1)}, u32[]{:S(2)}, u32[]{:S(2)}) collective-permute-start(bf16[128,512]{1,0:T(8,128)(2,1)S(1)} %get-tuple-element.66), channel_id=1, source_target_pairs={{0,6},{2,4},{4,2},{6,0},{8,14},{10,12},{12,10},{14,8},{16,22},{18,... | collective-permute-start | bytes 393224 | tf_op jit(solution)/shard_map/ppermute | solution.py:338
  41.9 2.0 %collective-permute-start.12 = (bf16[128,512]{1,0:T(8,128)(2,1)S(1)}, bf16[128,512]{1,0:T(8,128)(2,1)S(1)}, u32[]{:S(2)}, u32[]{:S(2)}) collective-permute-start(bf16[128,512]{1,0:T(8,128)(2,1)S(1)} %shard_map.110), channel_id=1, source_target_pairs={{0,8},{2,10},{4,12},{6,14},{8,0},{10,2},{12,4},{14,6},{16,24},{18,... | collective-permute-start | bytes 393224 | tf_op jit(solution)/shard_map/ppermute | solution.py:338
  44.6 2.1 %collective-permute-done.8.refs_3_ = bf16[128,512]{1,0:T(8,128)(2,1)S(1)} collective-permute-done((bf16[128,512]{1,0:T(8,128)(2,1)S(1)}, bf16[128,512]{1,0:T(8,128)(2,1)S(1)}, u32[]{:S(2)}, u32[]{:S(2)}) %collective-permute-start.8) | collective-permute-done | bytes 131104 | tf_op jit(solution)/shard_map/ppermute | solution.py:338
  47.1 2.6 %collective-permute-start.13 = (bf16[128,512]{1,0:T(8,128)(2,1)S(1)}, bf16[128,512]{1,0:T(8,128)(2,1)S(1)}, u32[]{:S(2)}, u32[]{:S(2)}) collective-permute-start(bf16[128,512]{1,0:T(8,128)(2,1)S(1)} %shard_map.111.one_ref), channel_id=1, source_target_pairs={{0,16},{2,18},{4,20},{6,22},{8,24},{10,26},{12,28},{14,30},{16,0},... | collective-permute-start | bytes 393224 | tf_op jit(solution)/shard_map/ppermute | solution.py:338
  50.0 1.3 %collective-permute-start.4 = (bf16[160,512]{1,0:T(8,128)(2,1)S(1)}, bf16[160,512]{1,0:T(8,128)(2,1)S(1)}, u32[]{:S(2)}, u32[]{:S(2)}) collective-permute-start(bf16[160,512]{1,0:T(8,128)(2,1)S(1)} %get-tuple-element.55), channel_id=1, source_target_pairs={{0,4},{2,6},{4,0},{6,2},{8,12},{10,14},{12,8},{14,10},{16,20},{18,... | collective-permute-start | bytes 491528 | tf_op jit(solution)/shard_map/ppermute | solution.py:338
  51.3 1.9 %collective-permute-done.13.two_ref = bf16[128,512]{1,0:T(8,128)(2,1)S(1)} collective-permute-done((bf16[128,512]{1,0:T(8,128)(2,1)S(1)}, bf16[128,512]{1,0:T(8,128)(2,1)S(1)}, u32[]{:S(2)}, u32[]{:S(2)}) %collective-permute-start.13) | collective-permute-done | bytes 131104 | tf_op jit(solution)/shard_map/ppermute | solution.py:338
  53.2 2.6 %collective-permute-start.17 = (bf16[128,512]{1,0:T(8,128)(2,1)S(1)}, bf16[128,512]{1,0:T(8,128)(2,1)S(1)}, u32[]{:S(2)}, u32[]{:S(2)}) collective-permute-start(bf16[128,512]{1,0:T(8,128)(2,1)S(1)} %shard_map.112.refs_0_), channel_id=1, source_target_pairs={{0,8},{2,10},{4,12},{6,14},{8,0},{10,2},{12,4},{14,6},{16,24},{18,... | collective-permute-start | bytes 393224 | tf_op jit(solution)/shard_map/ppermute | solution.py:338
  56.8 1.4 %collective-permute-start.15 = (bf16[128,512]{1,0:T(8,128)(2,1)S(1)}, bf16[128,512]{1,0:T(8,128)(2,1)S(1)}, u32[]{:S(2)}, u32[]{:S(2)}) collective-permute-start(bf16[128,512]{1,0:T(8,128)(2,1)S(1)} %shard_map.112.refs_0_), channel_id=1, source_target_pairs={{0,4},{2,6},{4,0},{6,2},{8,12},{10,14},{12,8},{14,10},{16,20},{18,... | collective-permute-start | bytes 393224 | tf_op jit(solution)/shard_map/ppermute | solution.py:338
  58.2 2.3 %collective-permute-start.5 = (bf16[160,512]{1,0:T(8,128)(2,1)S(1)}, bf16[160,512]{1,0:T(8,128)(2,1)S(1)}, u32[]{:S(2)}, u32[]{:S(2)}) collective-permute-start(bf16[160,512]{1,0:T(8,128)(2,1)S(1)} %get-tuple-element.59), channel_id=1, source_target_pairs={{0,8},{2,10},{4,12},{6,14},{8,0},{10,2},{12,4},{14,6},{16,24},{18,... | collective-permute-start | bytes 491528 | tf_op jit(solution)/shard_map/ppermute | solution.py:338
  60.5 1.8 %collective-permute-start.14 = (bf16[128,512]{1,0:T(8,128)(2,1)S(1)}, bf16[128,512]{1,0:T(8,128)(2,1)S(1)}, u32[]{:S(2)}, u32[]{:S(2)}) collective-permute-start(bf16[128,512]{1,0:T(8,128)(2,1)S(1)} %shard_map.112.refs_0_), channel_id=1, source_target_pairs={{0,2},{2,0},{4,6},{6,4},{8,10},{10,8},{12,14},{14,12},{16,18},{18,... | collective-permute-start | bytes 393224 | tf_op jit(solution)/shard_map/ppermute | solution.py:338
  62.3 1.2 %collective-permute-start.20 = (bf16[128,512]{1,0:T(8,128)(2,1)S(1)}, bf16[128,512]{1,0:T(8,128)(2,1)S(1)}, u32[]{:S(2)}, u32[]{:S(2)}) collective-permute-start(bf16[128,512]{1,0:T(8,128)(2,1)S(1)} %collective-permute-done.17.refs_4_), channel_id=1, source_target_pairs={{0,6},{2,4},{4,2},{6,0},{8,14},{10,12},{12,10},{14,8},{16,22},{18,... | collective-permute-start | bytes 393224 | tf_op jit(solution)/shard_map/ppermute | solution.py:338
  64.3 1.5 %collective-permute-start.18 = (bf16[128,512]{1,0:T(8,128)(2,1)S(1)}, bf16[128,512]{1,0:T(8,128)(2,1)S(1)}, u32[]{:S(2)}, u32[]{:S(2)}) collective-permute-start(bf16[128,512]{1,0:T(8,128)(2,1)S(1)} %collective-permute-done.17.refs_4_), channel_id=1, source_target_pairs={{0,2},{2,0},{4,6},{6,4},{8,10},{10,8},{12,14},{14,12},{16,18},{18,... | collective-permute-start | bytes 393224 | tf_op jit(solution)/shard_map/ppermute | solution.py:338
  65.8 2.5 %collective-permute-done.20.refs_7_ = bf16[128,512]{1,0:T(8,128)(2,1)S(1)} collective-permute-done((bf16[128,512]{1,0:T(8,128)(2,1)S(1)}, bf16[128,512]{1,0:T(8,128)(2,1)S(1)}, u32[]{:S(2)}, u32[]{:S(2)}) %collective-permute-start.20) | collective-permute-done | bytes 131104 | tf_op jit(solution)/shard_map/ppermute | solution.py:338
  68.2 1.3 %collective-permute-done.19.refs_6_ = bf16[128,512]{1,0:T(8,128)(2,1)S(1)} collective-permute-done((bf16[128,512]{1,0:T(8,128)(2,1)S(1)}, bf16[128,512]{1,0:T(8,128)(2,1)S(1)}, u32[]{:S(2)}, u32[]{:S(2)}) %collective-permute-start.19) | collective-permute-done | bytes 131104 | tf_op jit(solution)/shard_map/ppermute | solution.py:338
  (37 shorter events, 6.3 us)
Async XLA Ops:
  0.6 27.0 %copy-start.2 = (bf16[512,512]{1,0:T(8,128)(2,1)S(1)}, bf16[512,512]{1,0:T(8,128)(2,1)}, u32[]{:S(2)}) copy-start(bf16[512,512]{1,0:T(8,128)(2,1)} %w_two_ref.1) | copy-start | bytes 1572868
  4.0 23.6 %copy-start = (bf16[512,512]{1,0:T(8,128)(2,1)S(1)}, bf16[512,512]{1,0:T(8,128)(2,1)}, u32[]{:S(2)}) copy-start(bf16[512,512]{1,0:T(8,128)(2,1)} %w_one_ref.3) | copy-start | bytes 1572868
  4.0 23.6 %all-to-all-start = ((bf16[16,32,512]{2,1,0:T(8,128)(2,1)}), bf16[16,32,512]{2,1,0:T(8,128)(2,1)S(1)}, u32[]{:S(2)}, u32[]{:S(2)}) async-start(bf16[16,32,512]{2,1,0:T(8,128)(2,1)} %get-tuple-element.42), calls=%async_computation | async-start | bytes 1048576 | tf_op jit(solution)/shard_map/all_to_all | solution.py:379
  12.5 5.5 %collective-permute-start = (bf16[64,512]{1,0:T(8,128)(2,1)S(1)}, bf16[64,512]{1,0:T(8,128)(2,1)S(1)}, u32[]{:S(2)}, u32[]{:S(2)}) collective-permute-start(bf16[64,512]{1,0:T(8,128)(2,1)S(1)} %get-tuple-element.43), channel_id=1, source_target_pairs={{0,2},{2,0},{4,6},{6,4},{8,10},{10,8},{12,14},{14,12},{16,18},{18,... | collective-permute-start | bytes 196616 | tf_op jit(solution)/shard_map/ppermute | solution.py:338
  14.4 3.6 %collective-permute-start.1 = (bf16[64,512]{1,0:T(8,128)(2,1)S(1)}, bf16[64,512]{1,0:T(8,128)(2,1)S(1)}, u32[]{:S(2)}, u32[]{:S(2)}) collective-permute-start(bf16[64,512]{1,0:T(8,128)(2,1)S(1)} %get-tuple-element.44), channel_id=1, source_target_pairs={{2,4},{6,8},{10,12},{14,16},{18,20},{22,24},{26,28},{4,2},{8,6},{1... | collective-permute-start | bytes 196616 | tf_op jit(solution)/shard_map/ppermute | solution.py:378
  29.5 14.5 %collective-permute-start.2 = (bf16[160,512]{1,0:T(8,128)(2,1)S(1)}, bf16[160,512]{1,0:T(8,128)(2,1)S(1)}, u32[]{:S(2)}, u32[]{:S(2)}) collective-permute-start(bf16[160,512]{1,0:T(8,128)(2,1)S(1)} %get-tuple-element.47), channel_id=1, source_target_pairs={{0,16},{2,18},{4,20},{6,22},{8,24},{10,26},{12,28},{14,30},{16,0},... | collective-permute-start | bytes 491528 | tf_op jit(solution)/shard_map/ppermute | solution.py:338
  32.6 6.4 %collective-permute-start.9 = (bf16[128,512]{1,0:T(8,128)(2,1)S(1)}, bf16[128,512]{1,0:T(8,128)(2,1)S(1)}, u32[]{:S(2)}, u32[]{:S(2)}) collective-permute-start(bf16[128,512]{1,0:T(8,128)(2,1)S(1)} %get-tuple-element.68), channel_id=1, source_target_pairs={{0,2},{2,0},{4,6},{6,4},{8,10},{10,8},{12,14},{14,12},{16,18},{18,... | collective-permute-start | bytes 393224 | tf_op jit(solution)/shard_map/ppermute | solution.py:338
  32.6 8.0 %collective-permute-start.10 = (bf16[128,512]{1,0:T(8,128)(2,1)S(1)}, bf16[128,512]{1,0:T(8,128)(2,1)S(1)}, u32[]{:S(2)}, u32[]{:S(2)}) collective-permute-start(bf16[128,512]{1,0:T(8,128)(2,1)S(1)} %get-tuple-element.69), channel_id=1, source_target_pairs={{0,4},{2,6},{4,0},{6,2},{8,12},{10,14},{12,8},{14,10},{16,20},{18,... | collective-permute-start | bytes 393224 | tf_op jit(solution)/shard_map/ppermute | solution.py:338
  32.6 9.3 %collective-permute-start.11 = (bf16[128,512]{1,0:T(8,128)(2,1)S(1)}, bf16[128,512]{1,0:T(8,128)(2,1)S(1)}, u32[]{:S(2)}, u32[]{:S(2)}) collective-permute-start(bf16[128,512]{1,0:T(8,128)(2,1)S(1)} %get-tuple-element.70), channel_id=1, source_target_pairs={{0,6},{2,4},{4,2},{6,0},{8,14},{10,12},{12,10},{14,8},{16,22},{18,... | collective-permute-start | bytes 393224 | tf_op jit(solution)/shard_map/ppermute | solution.py:338
  36.0 8.6 %collective-permute-start.6 = (bf16[128,512]{1,0:T(8,128)(2,1)S(1)}, bf16[128,512]{1,0:T(8,128)(2,1)S(1)}, u32[]{:S(2)}, u32[]{:S(2)}) collective-permute-start(bf16[128,512]{1,0:T(8,128)(2,1)S(1)} %get-tuple-element.64), channel_id=1, source_target_pairs={{0,2},{2,0},{4,6},{6,4},{8,10},{10,8},{12,14},{14,12},{16,18},{18,... | collective-permute-start | bytes 393224 | tf_op jit(solution)/shard_map/ppermute | solution.py:338
  39.0 5.6 %collective-permute-start.7 = (bf16[128,512]{1,0:T(8,128)(2,1)S(1)}, bf16[128,512]{1,0:T(8,128)(2,1)S(1)}, u32[]{:S(2)}, u32[]{:S(2)}) collective-permute-start(bf16[128,512]{1,0:T(8,128)(2,1)S(1)} %get-tuple-element.65), channel_id=1, source_target_pairs={{0,4},{2,6},{4,0},{6,2},{8,12},{10,14},{12,8},{14,10},{16,20},{18,... | collective-permute-start | bytes 393224 | tf_op jit(solution)/shard_map/ppermute | solution.py:338
  40.6 6.1 %collective-permute-start.8 = (bf16[128,512]{1,0:T(8,128)(2,1)S(1)}, bf16[128,512]{1,0:T(8,128)(2,1)S(1)}, u32[]{:S(2)}, u32[]{:S(2)}) collective-permute-start(bf16[128,512]{1,0:T(8,128)(2,1)S(1)} %get-tuple-element.66), channel_id=1, source_target_pairs={{0,6},{2,4},{4,2},{6,0},{8,14},{10,12},{12,10},{14,8},{16,22},{18,... | collective-permute-start | bytes 393224 | tf_op jit(solution)/shard_map/ppermute | solution.py:338
  41.9 5.1 %collective-permute-start.12 = (bf16[128,512]{1,0:T(8,128)(2,1)S(1)}, bf16[128,512]{1,0:T(8,128)(2,1)S(1)}, u32[]{:S(2)}, u32[]{:S(2)}) collective-permute-start(bf16[128,512]{1,0:T(8,128)(2,1)S(1)} %shard_map.110), channel_id=1, source_target_pairs={{0,8},{2,10},{4,12},{6,14},{8,0},{10,2},{12,4},{14,6},{16,24},{18,... | collective-permute-start | bytes 393224 | tf_op jit(solution)/shard_map/ppermute | solution.py:338
  44.0 5.9 %collective-permute-start.3 = (bf16[192,512]{1,0:T(8,128)(2,1)S(1)}, bf16[192,512]{1,0:T(8,128)(2,1)S(1)}, u32[]{:S(2)}, u32[]{:S(2)}) collective-permute-start(bf16[192,512]{1,0:T(8,128)(2,1)S(1)} %get-tuple-element.51), channel_id=1, source_target_pairs={{0,2},{2,0},{4,6},{6,4},{8,10},{10,8},{12,14},{14,12},{16,18},{18,... | collective-permute-start | bytes 589832 | tf_op jit(solution)/shard_map/ppermute | solution.py:338
  47.1 6.0 %collective-permute-start.13 = (bf16[128,512]{1,0:T(8,128)(2,1)S(1)}, bf16[128,512]{1,0:T(8,128)(2,1)S(1)}, u32[]{:S(2)}, u32[]{:S(2)}) collective-permute-start(bf16[128,512]{1,0:T(8,128)(2,1)S(1)} %shard_map.111.one_ref), channel_id=1, source_target_pairs={{0,16},{2,18},{4,20},{6,22},{8,24},{10,26},{12,28},{14,30},{16,0},... | collective-permute-start | bytes 393224 | tf_op jit(solution)/shard_map/ppermute | solution.py:338
  50.0 8.2 %collective-permute-start.4 = (bf16[160,512]{1,0:T(8,128)(2,1)S(1)}, bf16[160,512]{1,0:T(8,128)(2,1)S(1)}, u32[]{:S(2)}, u32[]{:S(2)}) collective-permute-start(bf16[160,512]{1,0:T(8,128)(2,1)S(1)} %get-tuple-element.55), channel_id=1, source_target_pairs={{0,4},{2,6},{4,0},{6,2},{8,12},{10,14},{12,8},{14,10},{16,20},{18,... | collective-permute-start | bytes 491528 | tf_op jit(solution)/shard_map/ppermute | solution.py:338
  53.2 9.1 %collective-permute-start.17 = (bf16[128,512]{1,0:T(8,128)(2,1)S(1)}, bf16[128,512]{1,0:T(8,128)(2,1)S(1)}, u32[]{:S(2)}, u32[]{:S(2)}) collective-permute-start(bf16[128,512]{1,0:T(8,128)(2,1)S(1)} %shard_map.112.refs_0_), channel_id=1, source_target_pairs={{0,8},{2,10},{4,12},{6,14},{8,0},{10,2},{12,4},{14,6},{16,24},{18,... | collective-permute-start | bytes 393224 | tf_op jit(solution)/shard_map/ppermute | solution.py:338
  55.8 7.7 %collective-permute-start.16 = (bf16[128,512]{1,0:T(8,128)(2,1)S(1)}, bf16[128,512]{1,0:T(8,128)(2,1)S(1)}, u32[]{:S(2)}, u32[]{:S(2)}) collective-permute-start(bf16[128,512]{1,0:T(8,128)(2,1)S(1)} %shard_map.112.refs_0_), channel_id=1, source_target_pairs={{0,6},{2,4},{4,2},{6,0},{8,14},{10,12},{12,10},{14,8},{16,22},{18,... | collective-permute-start | bytes 393224 | tf_op jit(solution)/shard_map/ppermute | solution.py:338
  56.8 7.5 %collective-permute-start.15 = (bf16[128,512]{1,0:T(8,128)(2,1)S(1)}, bf16[128,512]{1,0:T(8,128)(2,1)S(1)}, u32[]{:S(2)}, u32[]{:S(2)}) collective-permute-start(bf16[128,512]{1,0:T(8,128)(2,1)S(1)} %shard_map.112.refs_0_), channel_id=1, source_target_pairs={{0,4},{2,6},{4,0},{6,2},{8,12},{10,14},{12,8},{14,10},{16,20},{18,... | collective-permute-start | bytes 393224 | tf_op jit(solution)/shard_map/ppermute | solution.py:338
  58.2 12.4 %collective-permute-start.5 = (bf16[160,512]{1,0:T(8,128)(2,1)S(1)}, bf16[160,512]{1,0:T(8,128)(2,1)S(1)}, u32[]{:S(2)}, u32[]{:S(2)}) collective-permute-start(bf16[160,512]{1,0:T(8,128)(2,1)S(1)} %get-tuple-element.59), channel_id=1, source_target_pairs={{0,8},{2,10},{4,12},{6,14},{8,0},{10,2},{12,4},{14,6},{16,24},{18,... | collective-permute-start | bytes 491528 | tf_op jit(solution)/shard_map/ppermute | solution.py:338
  60.5 5.3 %collective-permute-start.14 = (bf16[128,512]{1,0:T(8,128)(2,1)S(1)}, bf16[128,512]{1,0:T(8,128)(2,1)S(1)}, u32[]{:S(2)}, u32[]{:S(2)}) collective-permute-start(bf16[128,512]{1,0:T(8,128)(2,1)S(1)} %shard_map.112.refs_0_), channel_id=1, source_target_pairs={{0,2},{2,0},{4,6},{6,4},{8,10},{10,8},{12,14},{14,12},{16,18},{18,... | collective-permute-start | bytes 393224 | tf_op jit(solution)/shard_map/ppermute | solution.py:338
  62.3 6.0 %collective-permute-start.20 = (bf16[128,512]{1,0:T(8,128)(2,1)S(1)}, bf16[128,512]{1,0:T(8,128)(2,1)S(1)}, u32[]{:S(2)}, u32[]{:S(2)}) collective-permute-start(bf16[128,512]{1,0:T(8,128)(2,1)S(1)} %collective-permute-done.17.refs_4_), channel_id=1, source_target_pairs={{0,6},{2,4},{4,2},{6,0},{8,14},{10,12},{12,10},{14,8},{16,22},{18,... | collective-permute-start | bytes 393224 | tf_op jit(solution)/shard_map/ppermute | solution.py:338
  63.5 6.0 %collective-permute-start.19 = (bf16[128,512]{1,0:T(8,128)(2,1)S(1)}, bf16[128,512]{1,0:T(8,128)(2,1)S(1)}, u32[]{:S(2)}, u32[]{:S(2)}) collective-permute-start(bf16[128,512]{1,0:T(8,128)(2,1)S(1)} %collective-permute-done.17.refs_4_), channel_id=1, source_target_pairs={{0,4},{2,6},{4,0},{6,2},{8,12},{10,14},{12,8},{14,10},{16,20},{18,... | collective-permute-start | bytes 393224 | tf_op jit(solution)/shard_map/ppermute | solution.py:338
  64.3 5.3 %collective-permute-start.18 = (bf16[128,512]{1,0:T(8,128)(2,1)S(1)}, bf16[128,512]{1,0:T(8,128)(2,1)S(1)}, u32[]{:S(2)}, u32[]{:S(2)}) collective-permute-start(bf16[128,512]{1,0:T(8,128)(2,1)S(1)} %collective-permute-done.17.refs_4_), channel_id=1, source_target_pairs={{0,2},{2,0},{4,6},{6,4},{8,10},{10,8},{12,14},{14,12},{16,18},{18,... | collective-permute-start | bytes 393224 | tf_op jit(solution)/shard_map/ppermute | solution.py:338
  (1 other events, 23.6 us)

commit v8 on v7

--- a/solution.py
+++ b/solution.py
@@ -42,7 +42,11 @@
     return lax.broadcasted_iota(jnp.int32, shape, dim)
 
 
-def call(kernel, out_shape, scratch=(), **specs):
+def call(kernel, out_shape, scratch=(), work=0, **specs):
+    if work:
+        specs["cost_estimate"] = pl.CostEstimate(
+            flops=work, transcendentals=0, bytes_accessed=work // 64
+        )
     return pl.pallas_call(
         kernel,
         out_shape=out_shape,
@@ -418,7 +422,7 @@
     for at in range(1, len(bits)):
         out, held = next_hop(at, got, held)
         got = swap(out, 1 << bits[at])
-    total = call(sum_kernel, sent)(*kept, swap(call(sum_kernel, sent)(*given), PLANE))
+    total = call(sum_kernel, sent)(*kept, swap(call(sum_kernel, sent, work=1073741824)(*given), PLANE))
     for bit in range(3, len(bits) - 1):
         total = call(functools.partial(pair_sum_kernel, 1.0), sent)(
             total, swap(total, 1 << bit)

time: 71.7 us -> 69.5 us (0.969)
  waiting for transfers between devices: 25.9 us -> 20.9 us
  starting transfers between devices: 37.4 us -> 40.2 us
    ppermute x20, waiting for transfers between devices: 16.3 us -> 11.2 us  [swap(): return lax.ppermute(value, 'node', [(i, i ^ flip) for i in range(count)])]
    ppermute x20, starting transfers between devices: 28.3 us -> 31.1 us  [swap(): return lax.ppermute(value, 'node', [(i, i ^ flip) for i in range(count)])]
  transfers between devices with their start and end apart: 22 -> 22, of which waited for: 11 -> 10; matrix products, arithmetic and copies ran while one was open for 0% -> 0% of each run, Pallas kernels for 2% -> 3%
where the time goes in v8:
time: 69.5 us; the launch traced here: 69.2 us
  starting transfers between devices  40.2 us (58%)
  waiting for transfers between devices  20.9 us (30%)
  Pallas kernels  7.35 us (11%)
  between operations  0.76 us (1%)
    ppermute x20, starting transfers between devices, swap(): return lax.ppermute(value, 'node', [(i, i ^ flip) for i in range(count)])  31.1 us
    ppermute x20, waiting for transfers between devices, swap(): return lax.ppermute(value, 'node', [(i, i ^ flip) for i in range(count)])  11.2 us
    all_to_all x1, waiting for transfers between devices, shards(): lax.all_to_all(send, 'node', split_axis=0, concat_axis=0, tiled=True)  9.62 us
    all_to_all x1, starting transfers between devices, shards(): lax.all_to_all(send, 'node', split_axis=0, concat_axis=0, tiled=True)  8.46 us
    pallas_call x1, Pallas kernels, shards(): call(functools.partial(prepare_kernel, count), (struct((chain, ROWS), BF1...  3.36 us
  transfers between devices with their start and end apart: 22, of which 10 were waited for; matrix products, arithmetic and copies ran while one was open for 0% of the time, Pallas kernels for 3%

profile of v8, /device:TPU:0, one launch (start us, length us, event | category | flops | bytes accessed | tf_op | source)
XLA Modules:
  0.0 69.2 jit_solution(9538886563733430739)
XLA Ops:
  0.6 3.4 %shard_map.103 = (bf16[512,128]{1,0:T(8,128)(2,1)S(1)}, bf16[128,256]{1,0:T(8,128)(2,1)S(1)}, f32[128,128]{1,0:T(8,128)S(1)}, f32[128,512]{1,0:T(8,128)S(1)}, bf...) custom-call(s32[32,128]{1,0:T(8,128)} %bitcast.4, s32[32,128]{1,0:T(8,128)} %bitcast.5, ...), custom_call_target="tpu_custom_call" | custom-call | tf_op jit(solution)/shard_map/pallas_call | solution.py:345
  4.0 8.5 %all-to-all-start = ((bf16[16,32,512]{2,1,0:T(8,128)(2,1)}), bf16[16,32,512]{2,1,0:T(8,128)(2,1)S(1)}, u32[]{:S(2)}, u32[]{:S(2)}) async-start(bf16[16,32,512]{2,1,0:T(8,128)(2,1)} %get-tuple-element.42), calls=%async_computation | async-start | bytes 1048576 | tf_op jit(solution)/shard_map/all_to_all | solution.py:383
  12.5 1.9 %collective-permute-start = (bf16[64,512]{1,0:T(8,128)(2,1)S(1)}, bf16[64,512]{1,0:T(8,128)(2,1)S(1)}, u32[]{:S(2)}, u32[]{:S(2)}) collective-permute-start(bf16[64,512]{1,0:T(8,128)(2,1)S(1)} %get-tuple-element.43), channel_id=1, source_target_pairs={{0,2},{2,0},{4,6},{6,4},{8,10},{10,8},{12,14},{14,12},{16,18},{18,... | collective-permute-start | bytes 196616 | tf_op jit(solution)/shard_map/ppermute | solution.py:342
  15.1 2.9 %collective-permute-done.near_ref = bf16[64,512]{1,0:T(8,128)(2,1)S(1)} collective-permute-done((bf16[64,512]{1,0:T(8,128)(2,1)S(1)}, bf16[64,512]{1,0:T(8,128)(2,1)S(1)}, u32[]{:S(2)}, u32[]{:S(2)}) %collective-permute-start) | collective-permute-done | bytes 65568 | tf_op jit(solution)/shard_map/ppermute | solution.py:342
  18.0 9.6 %all-to-all-done.recv_ref = bf16[16,32,512]{2,1,0:T(8,128)(2,1)S(1)} async-done(((bf16[16,32,512]{2,1,0:T(8,128)(2,1)}), bf16[16,32,512]{2,1,0:T(8,128)(2,1)S(1)}, u32[]{:S(2)}, u32[]{:S(2)}) %all-to-all-start) | async-done | bytes 524320 | tf_op jit(solution)/shard_map/all_to_all | solution.py:383
  27.6 1.2 %shard_map.104 = (f32[128,512]{1,0:T(8,128)S(1)}, bf16[128,512]{1,0:T(8,128)(2,1)S(1)}, bf16[128,512]{1,0:T(8,128)(2,1)S(1)}, bf16[128,512]{1,0:T(8,128)(2,1)S(1...) custom-call(bf16[512,128]{1,0:T(8,128)(2,1)S(1)} %get-tuple-element., ...), custom_call_target="tpu_custom_call" | custom-call | tf_op jit(solution)/shard_map/pallas_call | solution.py:386
  29.5 1.3 %collective-permute-start.10 = (bf16[128,512]{1,0:T(8,128)(2,1)S(1)}, bf16[128,512]{1,0:T(8,128)(2,1)S(1)}, u32[]{:S(2)}, u32[]{:S(2)}) collective-permute-start(bf16[128,512]{1,0:T(8,128)(2,1)S(1)} %get-tuple-element.69), channel_id=1, source_target_pairs={{0,4},{2,6},{4,0},{6,2},{8,12},{10,14},{12,8},{14,10},{16,20},{18,... | collective-permute-start | bytes 393224 | tf_op jit(solution)/shard_map/ppermute | solution.py:342
  30.8 1.7 %collective-permute-start.11 = (bf16[128,512]{1,0:T(8,128)(2,1)S(1)}, bf16[128,512]{1,0:T(8,128)(2,1)S(1)}, u32[]{:S(2)}, u32[]{:S(2)}) collective-permute-start(bf16[128,512]{1,0:T(8,128)(2,1)S(1)} %get-tuple-element.70), channel_id=1, source_target_pairs={{0,6},{2,4},{4,2},{6,0},{8,14},{10,12},{12,10},{14,8},{16,22},{18,... | collective-permute-start | bytes 393224 | tf_op jit(solution)/shard_map/ppermute | solution.py:342
  33.0 3.1 %collective-permute-start.2 = (bf16[160,512]{1,0:T(8,128)(2,1)S(1)}, bf16[160,512]{1,0:T(8,128)(2,1)S(1)}, u32[]{:S(2)}, u32[]{:S(2)}) collective-permute-start(bf16[160,512]{1,0:T(8,128)(2,1)S(1)} %get-tuple-element.47), channel_id=1, source_target_pairs={{0,16},{2,18},{4,20},{6,22},{8,24},{10,26},{12,28},{14,30},{16,0},... | collective-permute-start | bytes 491528 | tf_op jit(solution)/shard_map/ppermute | solution.py:342
  36.7 2.9 %collective-permute-start.8 = (bf16[128,512]{1,0:T(8,128)(2,1)S(1)}, bf16[128,512]{1,0:T(8,128)(2,1)S(1)}, u32[]{:S(2)}, u32[]{:S(2)}) collective-permute-start(bf16[128,512]{1,0:T(8,128)(2,1)S(1)} %get-tuple-element.66), channel_id=1, source_target_pairs={{0,6},{2,4},{4,2},{6,0},{8,14},{10,12},{12,10},{14,8},{16,22},{18,... | collective-permute-start | bytes 393224 | tf_op jit(solution)/shard_map/ppermute | solution.py:342
  40.7 1.3 %collective-permute-done.2.got_ref = bf16[160,512]{1,0:T(8,128)(2,1)S(1)} collective-permute-done((bf16[160,512]{1,0:T(8,128)(2,1)S(1)}, bf16[160,512]{1,0:T(8,128)(2,1)S(1)}, u32[]{:S(2)}, u32[]{:S(2)}) %collective-permute-start.2) | collective-permute-done | bytes 163872 | tf_op jit(solution)/shard_map/ppermute | solution.py:342
  42.1 1.3 %collective-permute-start.3 = (bf16[192,512]{1,0:T(8,128)(2,1)S(1)}, bf16[192,512]{1,0:T(8,128)(2,1)S(1)}, u32[]{:S(2)}, u32[]{:S(2)}) collective-permute-start(bf16[192,512]{1,0:T(8,128)(2,1)S(1)} %get-tuple-element.51), channel_id=1, source_target_pairs={{0,2},{2,0},{4,6},{6,4},{8,10},{10,8},{12,14},{14,12},{16,18},{18,... | collective-permute-start | bytes 589832 | tf_op jit(solution)/shard_map/ppermute | solution.py:342
  43.3 1.4 %collective-permute-done.12.refs_4_ = bf16[128,512]{1,0:T(8,128)(2,1)S(1)} collective-permute-done((bf16[128,512]{1,0:T(8,128)(2,1)S(1)}, bf16[128,512]{1,0:T(8,128)(2,1)S(1)}, u32[]{:S(2)}, u32[]{:S(2)}) %collective-permute-start.12) | collective-permute-done | bytes 131104 | tf_op jit(solution)/shard_map/ppermute | solution.py:342
  44.8 3.0 %collective-permute-start.13 = (bf16[128,512]{1,0:T(8,128)(2,1)S(1)}, bf16[128,512]{1,0:T(8,128)(2,1)S(1)}, u32[]{:S(2)}, u32[]{:S(2)}) collective-permute-start(bf16[128,512]{1,0:T(8,128)(2,1)S(1)} %shard_map.111.one_ref), channel_id=1, source_target_pairs={{0,16},{2,18},{4,20},{6,22},{8,24},{10,26},{12,28},{14,30},{16,0},... | collective-permute-start | bytes 393224 | tf_op jit(solution)/shard_map/ppermute | solution.py:342
  48.0 2.6 %collective-permute-start.4 = (bf16[160,512]{1,0:T(8,128)(2,1)S(1)}, bf16[160,512]{1,0:T(8,128)(2,1)S(1)}, u32[]{:S(2)}, u32[]{:S(2)}) collective-permute-start(bf16[160,512]{1,0:T(8,128)(2,1)S(1)} %get-tuple-element.55), channel_id=1, source_target_pairs={{0,4},{2,6},{4,0},{6,2},{8,12},{10,14},{12,8},{14,10},{16,20},{18,... | collective-permute-start | bytes 491528 | tf_op jit(solution)/shard_map/ppermute | solution.py:342
  50.6 1.2 %collective-permute-done.13.two_ref = bf16[128,512]{1,0:T(8,128)(2,1)S(1)} collective-permute-done((bf16[128,512]{1,0:T(8,128)(2,1)S(1)}, bf16[128,512]{1,0:T(8,128)(2,1)S(1)}, u32[]{:S(2)}, u32[]{:S(2)}) %collective-permute-start.13) | collective-permute-done | bytes 131104 | tf_op jit(solution)/shard_map/ppermute | solution.py:342
  51.8 1.3 %collective-permute-start.17 = (bf16[128,512]{1,0:T(8,128)(2,1)S(1)}, bf16[128,512]{1,0:T(8,128)(2,1)S(1)}, u32[]{:S(2)}, u32[]{:S(2)}) collective-permute-start(bf16[128,512]{1,0:T(8,128)(2,1)S(1)} %shard_map.112.refs_0_), channel_id=1, source_target_pairs={{0,8},{2,10},{4,12},{6,14},{8,0},{10,2},{12,4},{14,6},{16,24},{18,... | collective-permute-start | bytes 393224 | tf_op jit(solution)/shard_map/ppermute | solution.py:342
  53.9 3.5 %collective-permute-start.15 = (bf16[128,512]{1,0:T(8,128)(2,1)S(1)}, bf16[128,512]{1,0:T(8,128)(2,1)S(1)}, u32[]{:S(2)}, u32[]{:S(2)}) collective-permute-start(bf16[128,512]{1,0:T(8,128)(2,1)S(1)} %shard_map.112.refs_0_), channel_id=1, source_target_pairs={{0,4},{2,6},{4,0},{6,2},{8,12},{10,14},{12,8},{14,10},{16,20},{18,... | collective-permute-start | bytes 393224 | tf_op jit(solution)/shard_map/ppermute | solution.py:342
  58.2 1.6 %collective-permute-start.20 = (bf16[128,512]{1,0:T(8,128)(2,1)S(1)}, bf16[128,512]{1,0:T(8,128)(2,1)S(1)}, u32[]{:S(2)}, u32[]{:S(2)}) collective-permute-start(bf16[128,512]{1,0:T(8,128)(2,1)S(1)} %collective-permute-done.17.refs_4_), channel_id=1, source_target_pairs={{0,6},{2,4},{4,2},{6,0},{8,14},{10,12},{12,10},{14,8},{16,22},{18,... | collective-permute-start | bytes 393224 | tf_op jit(solution)/shard_map/ppermute | solution.py:342
  59.8 2.1 %collective-permute-start.19 = (bf16[128,512]{1,0:T(8,128)(2,1)S(1)}, bf16[128,512]{1,0:T(8,128)(2,1)S(1)}, u32[]{:S(2)}, u32[]{:S(2)}) collective-permute-start(bf16[128,512]{1,0:T(8,128)(2,1)S(1)} %collective-permute-done.17.refs_4_), channel_id=1, source_target_pairs={{0,4},{2,6},{4,0},{6,2},{8,12},{10,14},{12,8},{14,10},{16,20},{18,... | collective-permute-start | bytes 393224 | tf_op jit(solution)/shard_map/ppermute | solution.py:342
  62.3 1.3 %collective-permute-start.18 = (bf16[128,512]{1,0:T(8,128)(2,1)S(1)}, bf16[128,512]{1,0:T(8,128)(2,1)S(1)}, u32[]{:S(2)}, u32[]{:S(2)}) collective-permute-start(bf16[128,512]{1,0:T(8,128)(2,1)S(1)} %collective-permute-done.17.refs_4_), channel_id=1, source_target_pairs={{0,2},{2,0},{4,6},{6,4},{8,10},{10,8},{12,14},{14,12},{16,18},{18,... | collective-permute-start | bytes 393224 | tf_op jit(solution)/shard_map/ppermute | solution.py:342
  64.2 1.3 %collective-permute-done.19.refs_6_ = bf16[128,512]{1,0:T(8,128)(2,1)S(1)} collective-permute-done((bf16[128,512]{1,0:T(8,128)(2,1)S(1)}, bf16[128,512]{1,0:T(8,128)(2,1)S(1)}, u32[]{:S(2)}, u32[]{:S(2)}) %collective-permute-start.19) | collective-permute-done | bytes 131104 | tf_op jit(solution)/shard_map/ppermute | solution.py:342
  65.5 1.8 %collective-permute-done.18.refs_5_ = bf16[128,512]{1,0:T(8,128)(2,1)S(1)} collective-permute-done((bf16[128,512]{1,0:T(8,128)(2,1)S(1)}, bf16[128,512]{1,0:T(8,128)(2,1)S(1)}, u32[]{:S(2)}, u32[]{:S(2)}) %collective-permute-start.18) | collective-permute-done | bytes 131104 | tf_op jit(solution)/shard_map/ppermute | solution.py:342
  67.3 1.0 %shard_map.113 = (bf16[512,512]{1,0:T(8,128)(2,1)}, bf16[512,512]{1,0:T(8,128)(2,1)}) custom-call(bf16[128,512]{1,0:T(8,128)(2,1)S(1)} %shard_map.112.refs_0_, bf16[128,512]{1,0:T(8,128)(2,1)S(1)} %collective-permute-done.14.refs_1_, bf16[128,512]{1,0:T(8,128)(2,1)S(1)} %collective-permute-done.15.refs_2_, ...), custom_call_target="tpu_custom_call" | custom-call | tf_op jit(solution)/shard_map/pallas_call | solution.py:447
  (37 shorter events, 7.4 us)
Async XLA Ops:
  0.6 27.0 %copy-start.2 = (bf16[512,512]{1,0:T(8,128)(2,1)S(1)}, bf16[512,512]{1,0:T(8,128)(2,1)}, u32[]{:S(2)}) copy-start(bf16[512,512]{1,0:T(8,128)(2,1)} %w_two_ref.1) | copy-start | bytes 1572868
  4.0 23.6 %copy-start = (bf16[512,512]{1,0:T(8,128)(2,1)S(1)}, bf16[512,512]{1,0:T(8,128)(2,1)}, u32[]{:S(2)}) copy-start(bf16[512,512]{1,0:T(8,128)(2,1)} %w_one_ref.3) | copy-start | bytes 1572868
  4.0 23.6 %all-to-all-start = ((bf16[16,32,512]{2,1,0:T(8,128)(2,1)}), bf16[16,32,512]{2,1,0:T(8,128)(2,1)S(1)}, u32[]{:S(2)}, u32[]{:S(2)}) async-start(bf16[16,32,512]{2,1,0:T(8,128)(2,1)} %get-tuple-element.42), calls=%async_computation | async-start | bytes 1048576 | tf_op jit(solution)/shard_map/all_to_all | solution.py:383
  12.5 5.5 %collective-permute-start = (bf16[64,512]{1,0:T(8,128)(2,1)S(1)}, bf16[64,512]{1,0:T(8,128)(2,1)S(1)}, u32[]{:S(2)}, u32[]{:S(2)}) collective-permute-start(bf16[64,512]{1,0:T(8,128)(2,1)S(1)} %get-tuple-element.43), channel_id=1, source_target_pairs={{0,2},{2,0},{4,6},{6,4},{8,10},{10,8},{12,14},{14,12},{16,18},{18,... | collective-permute-start | bytes 196616 | tf_op jit(solution)/shard_map/ppermute | solution.py:342
  14.4 3.6 %collective-permute-start.1 = (bf16[64,512]{1,0:T(8,128)(2,1)S(1)}, bf16[64,512]{1,0:T(8,128)(2,1)S(1)}, u32[]{:S(2)}, u32[]{:S(2)}) collective-permute-start(bf16[64,512]{1,0:T(8,128)(2,1)S(1)} %get-tuple-element.44), channel_id=1, source_target_pairs={{2,4},{6,8},{10,12},{14,16},{18,20},{22,24},{26,28},{4,2},{8,6},{1... | collective-permute-start | bytes 196616 | tf_op jit(solution)/shard_map/ppermute | solution.py:382
  28.9 7.3 %collective-permute-start.9 = (bf16[128,512]{1,0:T(8,128)(2,1)S(1)}, bf16[128,512]{1,0:T(8,128)(2,1)S(1)}, u32[]{:S(2)}, u32[]{:S(2)}) collective-permute-start(bf16[128,512]{1,0:T(8,128)(2,1)S(1)} %get-tuple-element.68), channel_id=1, source_target_pairs={{0,2},{2,0},{4,6},{6,4},{8,10},{10,8},{12,14},{14,12},{16,18},{18,... | collective-permute-start | bytes 393224 | tf_op jit(solution)/shard_map/ppermute | solution.py:342
  29.5 7.2 %collective-permute-start.10 = (bf16[128,512]{1,0:T(8,128)(2,1)S(1)}, bf16[128,512]{1,0:T(8,128)(2,1)S(1)}, u32[]{:S(2)}, u32[]{:S(2)}) collective-permute-start(bf16[128,512]{1,0:T(8,128)(2,1)S(1)} %get-tuple-element.69), channel_id=1, source_target_pairs={{0,4},{2,6},{4,0},{6,2},{8,12},{10,14},{12,8},{14,10},{16,20},{18,... | collective-permute-start | bytes 393224 | tf_op jit(solution)/shard_map/ppermute | solution.py:342
  30.8 8.8 %collective-permute-start.11 = (bf16[128,512]{1,0:T(8,128)(2,1)S(1)}, bf16[128,512]{1,0:T(8,128)(2,1)S(1)}, u32[]{:S(2)}, u32[]{:S(2)}) collective-permute-start(bf16[128,512]{1,0:T(8,128)(2,1)S(1)} %get-tuple-element.70), channel_id=1, source_target_pairs={{0,6},{2,4},{4,2},{6,0},{8,14},{10,12},{12,10},{14,8},{16,22},{18,... | collective-permute-start | bytes 393224 | tf_op jit(solution)/shard_map/ppermute | solution.py:342
  33.0 9.0 %collective-permute-start.2 = (bf16[160,512]{1,0:T(8,128)(2,1)S(1)}, bf16[160,512]{1,0:T(8,128)(2,1)S(1)}, u32[]{:S(2)}, u32[]{:S(2)}) collective-permute-start(bf16[160,512]{1,0:T(8,128)(2,1)S(1)} %get-tuple-element.47), channel_id=1, source_target_pairs={{0,16},{2,18},{4,20},{6,22},{8,24},{10,26},{12,28},{14,30},{16,0},... | collective-permute-start | bytes 491528 | tf_op jit(solution)/shard_map/ppermute | solution.py:342
  36.1 7.2 %collective-permute-start.6 = (bf16[128,512]{1,0:T(8,128)(2,1)S(1)}, bf16[128,512]{1,0:T(8,128)(2,1)S(1)}, u32[]{:S(2)}, u32[]{:S(2)}) collective-permute-start(bf16[128,512]{1,0:T(8,128)(2,1)S(1)} %get-tuple-element.64), channel_id=1, source_target_pairs={{0,2},{2,0},{4,6},{6,4},{8,10},{10,8},{12,14},{14,12},{16,18},{18,... | collective-permute-start | bytes 393224 | tf_op jit(solution)/shard_map/ppermute | solution.py:342
  36.2 7.1 %collective-permute-start.7 = (bf16[128,512]{1,0:T(8,128)(2,1)S(1)}, bf16[128,512]{1,0:T(8,128)(2,1)S(1)}, u32[]{:S(2)}, u32[]{:S(2)}) collective-permute-start(bf16[128,512]{1,0:T(8,128)(2,1)S(1)} %get-tuple-element.65), channel_id=1, source_target_pairs={{0,4},{2,6},{4,0},{6,2},{8,12},{10,14},{12,8},{14,10},{16,20},{18,... | collective-permute-start | bytes 393224 | tf_op jit(solution)/shard_map/ppermute | solution.py:342
  36.7 6.6 %collective-permute-start.8 = (bf16[128,512]{1,0:T(8,128)(2,1)S(1)}, bf16[128,512]{1,0:T(8,128)(2,1)S(1)}, u32[]{:S(2)}, u32[]{:S(2)}) collective-permute-start(bf16[128,512]{1,0:T(8,128)(2,1)S(1)} %get-tuple-element.66), channel_id=1, source_target_pairs={{0,6},{2,4},{4,2},{6,0},{8,14},{10,12},{12,10},{14,8},{16,22},{18,... | collective-permute-start | bytes 393224 | tf_op jit(solution)/shard_map/ppermute | solution.py:342
  39.7 5.0 %collective-permute-start.12 = (bf16[128,512]{1,0:T(8,128)(2,1)S(1)}, bf16[128,512]{1,0:T(8,128)(2,1)S(1)}, u32[]{:S(2)}, u32[]{:S(2)}) collective-permute-start(bf16[128,512]{1,0:T(8,128)(2,1)S(1)} %shard_map.110), channel_id=1, source_target_pairs={{0,8},{2,10},{4,12},{6,14},{8,0},{10,2},{12,4},{14,6},{16,24},{18,... | collective-permute-start | bytes 393224 | tf_op jit(solution)/shard_map/ppermute | solution.py:342
  42.1 5.9 %collective-permute-start.3 = (bf16[192,512]{1,0:T(8,128)(2,1)S(1)}, bf16[192,512]{1,0:T(8,128)(2,1)S(1)}, u32[]{:S(2)}, u32[]{:S(2)}) collective-permute-start(bf16[192,512]{1,0:T(8,128)(2,1)S(1)} %get-tuple-element.51), channel_id=1, source_target_pairs={{0,2},{2,0},{4,6},{6,4},{8,10},{10,8},{12,14},{14,12},{16,18},{18,... | collective-permute-start | bytes 589832 | tf_op jit(solution)/shard_map/ppermute | solution.py:342
  44.8 7.0 %collective-permute-start.13 = (bf16[128,512]{1,0:T(8,128)(2,1)S(1)}, bf16[128,512]{1,0:T(8,128)(2,1)S(1)}, u32[]{:S(2)}, u32[]{:S(2)}) collective-permute-start(bf16[128,512]{1,0:T(8,128)(2,1)S(1)} %shard_map.111.one_ref), channel_id=1, source_target_pairs={{0,16},{2,18},{4,20},{6,22},{8,24},{10,26},{12,28},{14,30},{16,0},... | collective-permute-start | bytes 393224 | tf_op jit(solution)/shard_map/ppermute | solution.py:342
  48.0 9.4 %collective-permute-start.4 = (bf16[160,512]{1,0:T(8,128)(2,1)S(1)}, bf16[160,512]{1,0:T(8,128)(2,1)S(1)}, u32[]{:S(2)}, u32[]{:S(2)}) collective-permute-start(bf16[160,512]{1,0:T(8,128)(2,1)S(1)} %get-tuple-element.55), channel_id=1, source_target_pairs={{0,4},{2,6},{4,0},{6,2},{8,12},{10,14},{12,8},{14,10},{16,20},{18,... | collective-permute-start | bytes 491528 | tf_op jit(solution)/shard_map/ppermute | solution.py:342
  51.8 6.3 %collective-permute-start.17 = (bf16[128,512]{1,0:T(8,128)(2,1)S(1)}, bf16[128,512]{1,0:T(8,128)(2,1)S(1)}, u32[]{:S(2)}, u32[]{:S(2)}) collective-permute-start(bf16[128,512]{1,0:T(8,128)(2,1)S(1)} %shard_map.112.refs_0_), channel_id=1, source_target_pairs={{0,8},{2,10},{4,12},{6,14},{8,0},{10,2},{12,4},{14,6},{16,24},{18,... | collective-permute-start | bytes 393224 | tf_op jit(solution)/shard_map/ppermute | solution.py:342
  53.1 6.6 %collective-permute-start.16 = (bf16[128,512]{1,0:T(8,128)(2,1)S(1)}, bf16[128,512]{1,0:T(8,128)(2,1)S(1)}, u32[]{:S(2)}, u32[]{:S(2)}) collective-permute-start(bf16[128,512]{1,0:T(8,128)(2,1)S(1)} %shard_map.112.refs_0_), channel_id=1, source_target_pairs={{0,6},{2,4},{4,2},{6,0},{8,14},{10,12},{12,10},{14,8},{16,22},{18,... | collective-permute-start | bytes 393224 | tf_op jit(solution)/shard_map/ppermute | solution.py:342
  53.9 8.4 %collective-permute-start.15 = (bf16[128,512]{1,0:T(8,128)(2,1)S(1)}, bf16[128,512]{1,0:T(8,128)(2,1)S(1)}, u32[]{:S(2)}, u32[]{:S(2)}) collective-permute-start(bf16[128,512]{1,0:T(8,128)(2,1)S(1)} %shard_map.112.refs_0_), channel_id=1, source_target_pairs={{0,4},{2,6},{4,0},{6,2},{8,12},{10,14},{12,8},{14,10},{16,20},{18,... | collective-permute-start | bytes 393224 | tf_op jit(solution)/shard_map/ppermute | solution.py:342
  57.5 10.8 %collective-permute-start.5 = (bf16[160,512]{1,0:T(8,128)(2,1)S(1)}, bf16[160,512]{1,0:T(8,128)(2,1)S(1)}, u32[]{:S(2)}, u32[]{:S(2)}) collective-permute-start(bf16[160,512]{1,0:T(8,128)(2,1)S(1)} %get-tuple-element.59), channel_id=1, source_target_pairs={{0,8},{2,10},{4,12},{6,14},{8,0},{10,2},{12,4},{14,6},{16,24},{18,... | collective-permute-start | bytes 491528 | tf_op jit(solution)/shard_map/ppermute | solution.py:342
  57.6 6.0 %collective-permute-start.14 = (bf16[128,512]{1,0:T(8,128)(2,1)S(1)}, bf16[128,512]{1,0:T(8,128)(2,1)S(1)}, u32[]{:S(2)}, u32[]{:S(2)}) collective-permute-start(bf16[128,512]{1,0:T(8,128)(2,1)S(1)} %shard_map.112.refs_0_), channel_id=1, source_target_pairs={{0,2},{2,0},{4,6},{6,4},{8,10},{10,8},{12,14},{14,12},{16,18},{18,... | collective-permute-start | bytes 393224 | tf_op jit(solution)/shard_map/ppermute | solution.py:342
  58.2 6.0 %collective-permute-start.20 = (bf16[128,512]{1,0:T(8,128)(2,1)S(1)}, bf16[128,512]{1,0:T(8,128)(2,1)S(1)}, u32[]{:S(2)}, u32[]{:S(2)}) collective-permute-start(bf16[128,512]{1,0:T(8,128)(2,1)S(1)} %collective-permute-done.17.refs_4_), channel_id=1, source_target_pairs={{0,6},{2,4},{4,2},{6,0},{8,14},{10,12},{12,10},{14,8},{16,22},{18,... | collective-permute-start | bytes 393224 | tf_op jit(solution)/shard_map/ppermute | solution.py:342
  59.8 5.7 %collective-permute-start.19 = (bf16[128,512]{1,0:T(8,128)(2,1)S(1)}, bf16[128,512]{1,0:T(8,128)(2,1)S(1)}, u32[]{:S(2)}, u32[]{:S(2)}) collective-permute-start(bf16[128,512]{1,0:T(8,128)(2,1)S(1)} %collective-permute-done.17.refs_4_), channel_id=1, source_target_pairs={{0,4},{2,6},{4,0},{6,2},{8,12},{10,14},{12,8},{14,10},{16,20},{18,... | collective-permute-start | bytes 393224 | tf_op jit(solution)/shard_map/ppermute | solution.py:342
  62.3 5.0 %collective-permute-start.18 = (bf16[128,512]{1,0:T(8,128)(2,1)S(1)}, bf16[128,512]{1,0:T(8,128)(2,1)S(1)}, u32[]{:S(2)}, u32[]{:S(2)}) collective-permute-start(bf16[128,512]{1,0:T(8,128)(2,1)S(1)} %collective-permute-done.17.refs_4_), channel_id=1, source_target_pairs={{0,2},{2,0},{4,6},{6,4},{8,10},{10,8},{12,14},{14,12},{16,18},{18,... | collective-permute-start | bytes 393224 | tf_op jit(solution)/shard_map/ppermute | solution.py:342
  (1 other events, 23.6 us)

commit v9 on v8

--- a/solution.py
+++ b/solution.py
@@ -309,23 +309,31 @@
     out_ref[...] = (total * scale).astype(BF16)
 
 
-def gather_kernel(*refs):
-    chunk_refs, out_refs, sems = refs[: 2 * PLANE], refs[2 * PLANE : 2 * PLANE + 2], refs[-1]
+def last_kernel(count, last, *refs):
+    chunk_refs, refs = refs[: 2 * PLANE], refs[2 * PLANE :]
+    in_refs, (out_ref, two_ref, one_ref, *scratch, sems) = refs[:6], refs[6:]
     device = lax.axis_index("node")
     place, side = device % PLANE, device // PLANE % 2
+
+    def copies(low):
+        for at, ref in enumerate(chunk_refs):
+            row = pl.multiple_of((place ^ (at % PLANE)) * WIDE, WIDE)
+            grad_ref = (two_ref, one_ref)[low ^ (at // PLANE)]
+            yield pltpu.make_async_copy(ref, grad_ref.at[pl.ds(row, WIDE), :], sems.at[at])
+
     for low in range(2):
 
         @pl.when(side == low)
         def _():
-            copies = []
-            for at, ref in enumerate(chunk_refs):
-                row = pl.multiple_of((place ^ (at % PLANE)) * WIDE, WIDE)
-                out_ref = out_refs[low ^ (at // PLANE)]
-                copies.append(
-                    pltpu.make_async_copy(ref, out_ref.at[pl.ds(row, WIDE), :], sems.at[at])
-                )
-                copies[-1].start()
-            for copy in copies:
+            for copy in copies(low):
+                copy.start()
+
+    features_kernel(count, last, *in_refs, out_ref, *scratch)
+    for low in range(2):
+
+        @pl.when(side == low)
+        def _():
+            for copy in copies(low):
                 copy.wait()
 
 
@@ -422,7 +430,7 @@
     for at in range(1, len(bits)):
         out, held = next_hop(at, got, held)
         got = swap(out, 1 << bits[at])
-    total = call(sum_kernel, sent)(*kept, swap(call(sum_kernel, sent, work=1073741824)(*given), PLANE))
+    total = call(sum_kernel, sent, work=268435456)(*kept, swap(call(sum_kernel, sent, work=1073741824)(*given), PLANE))
     for bit in range(3, len(bits) - 1):
         total = call(functools.partial(pair_sum_kernel, 1.0), sent)(
             total, swap(total, 1 << bit)
@@ -434,23 +442,19 @@
     far_total = swap(total, PLANE)
     chunks = [total] + [swap(total, v) for v in range(1, PLANE)]
     chunks = chunks + [far_total] + [swap(far_total, v) for v in range(1, PLANE)]
-    d_features = call(
-        functools.partial(features_kernel, count, bits[-1]),
-        struct((ROWS, D), BF16),
+    anywhere = pl.BlockSpec(memory_space=pl.ANY)
+    d_features, grad_two, grad_one = call(
+        functools.partial(last_kernel, count, bits[-1]),
+        (struct((ROWS, D), BF16), struct((D, D), BF16), struct((D, D), BF16)),
         (
             pltpu.VMEM((ROWS, D), F32),
             pltpu.VMEM((count, SLOT, D), BF16),
             pltpu.VMEM((count, SLOT, D), BF16),
+            pltpu.SemaphoreType.DMA((2 * PLANE,)),
         ),
-    )(pick, own, got, *held)
-    anywhere = pl.BlockSpec(memory_space=pl.ANY)
-    grad_two, grad_one = call(
-        gather_kernel,
-        (struct((D, D), BF16), struct((D, D), BF16)),
-        (pltpu.SemaphoreType.DMA((2 * PLANE,)),),
-        in_specs=[anywhere] * (2 * PLANE),
-        out_specs=(anywhere, anywhere),
-    )(*chunks)
+        in_specs=[anywhere] * (2 * PLANE) + [vmem] * 6,
+        out_specs=(vmem, anywhere, anywhere),
+    )(*chunks, pick, own, got, *held)
     return d_features, grad_one, grad_two
 
 

time: 69.5 us -> 69.3 us (level)
    pallas_call x3 -> x2, Pallas kernels: 1.98 us -> 1.8 us  [the longest x1 1.72 us: shards(): call(functools.partial(last_kernel, count, bits[-1]), (struct((ROWS, D),...]
  transfers between devices with their start and end apart: 22 -> 22, of which waited for: 10 -> 10; matrix products, arithmetic and copies ran while one was open for 0% -> 0% of each run, Pallas kernels for 3% -> 1%
where the time goes in v9:
time: 69.3 us; the launch traced here: 69 us
  starting transfers between devices  40.2 us (58%)
  waiting for transfers between devices  20.9 us (30%)
  Pallas kernels  7.17 us (10%)
  between operations  0.74 us (1%)
    ppermute x20, starting transfers between devices, swap(): return lax.ppermute(value, 'node', [(i, i ^ flip) for i in range(count)])  31.1 us
    ppermute x20, waiting for transfers between devices, swap(): return lax.ppermute(value, 'node', [(i, i ^ flip) for i in range(count)])  11.2 us
    all_to_all x1, waiting for transfers between devices, shards(): lax.all_to_all(send, 'node', split_axis=0, concat_axis=0, tiled=True)  9.62 us
    all_to_all x1, starting transfers between devices, shards(): lax.all_to_all(send, 'node', split_axis=0, concat_axis=0, tiled=True)  8.46 us
    pallas_call x1, Pallas kernels, shards(): call(functools.partial(prepare_kernel, count), (struct((chain, ROWS), BF1...  3.36 us
    pallas_call x1, Pallas kernels, shards(): call(functools.partial(last_kernel, count, bits[-1]), (struct((ROWS, D),...  1.72 us
  transfers between devices with their start and end apart: 22, of which 10 were waited for; matrix products, arithmetic and copies ran while one was open for 0% of the time, Pallas kernels for 1%

profile of v9, /device:TPU:0, one launch (start us, length us, event | category | flops | bytes accessed | tf_op | source)
XLA Modules:
  0.0 69.0 jit_solution(4698434833120630575)
XLA Ops:
  0.6 3.4 %shard_map.103 = (bf16[512,128]{1,0:T(8,128)(2,1)S(1)}, bf16[128,256]{1,0:T(8,128)(2,1)S(1)}, f32[128,128]{1,0:T(8,128)S(1)}, f32[128,512]{1,0:T(8,128)S(1)}, bf...) custom-call(s32[32,128]{1,0:T(8,128)} %bitcast.4, s32[32,128]{1,0:T(8,128)} %bitcast.5, ...), custom_call_target="tpu_custom_call" | custom-call | tf_op jit(solution)/shard_map/pallas_call | solution.py:353
  4.0 8.5 %all-to-all-start = ((bf16[16,32,512]{2,1,0:T(8,128)(2,1)}), bf16[16,32,512]{2,1,0:T(8,128)(2,1)S(1)}, u32[]{:S(2)}, u32[]{:S(2)}) async-start(bf16[16,32,512]{2,1,0:T(8,128)(2,1)} %get-tuple-element.43), calls=%async_computation | async-start | bytes 1048576 | tf_op jit(solution)/shard_map/all_to_all | solution.py:391
  12.5 1.9 %collective-permute-start = (bf16[64,512]{1,0:T(8,128)(2,1)S(1)}, bf16[64,512]{1,0:T(8,128)(2,1)S(1)}, u32[]{:S(2)}, u32[]{:S(2)}) collective-permute-start(bf16[64,512]{1,0:T(8,128)(2,1)S(1)} %get-tuple-element.44), channel_id=1, source_target_pairs={{0,2},{2,0},{4,6},{6,4},{8,10},{10,8},{12,14},{14,12},{16,18},{18,... | collective-permute-start | bytes 196616 | tf_op jit(solution)/shard_map/ppermute | solution.py:350
  15.1 2.9 %collective-permute-done.near_ref = bf16[64,512]{1,0:T(8,128)(2,1)S(1)} collective-permute-done((bf16[64,512]{1,0:T(8,128)(2,1)S(1)}, bf16[64,512]{1,0:T(8,128)(2,1)S(1)}, u32[]{:S(2)}, u32[]{:S(2)}) %collective-permute-start) | collective-permute-done | bytes 65568 | tf_op jit(solution)/shard_map/ppermute | solution.py:350
  18.0 9.6 %all-to-all-done.recv_ref = bf16[16,32,512]{2,1,0:T(8,128)(2,1)S(1)} async-done(((bf16[16,32,512]{2,1,0:T(8,128)(2,1)}), bf16[16,32,512]{2,1,0:T(8,128)(2,1)S(1)}, u32[]{:S(2)}, u32[]{:S(2)}) %all-to-all-start) | async-done | bytes 524320 | tf_op jit(solution)/shard_map/all_to_all | solution.py:391
  27.6 1.2 %shard_map.104 = (f32[128,512]{1,0:T(8,128)S(1)}, bf16[128,512]{1,0:T(8,128)(2,1)S(1)}, bf16[128,512]{1,0:T(8,128)(2,1)S(1)}, bf16[128,512]{1,0:T(8,128)(2,1)S(1...) custom-call(bf16[512,128]{1,0:T(8,128)(2,1)S(1)} %get-tuple-element., ...), custom_call_target="tpu_custom_call" | custom-call | tf_op jit(solution)/shard_map/pallas_call | solution.py:394
  29.5 1.3 %collective-permute-start.6 = (bf16[128,512]{1,0:T(8,128)(2,1)S(1)}, bf16[128,512]{1,0:T(8,128)(2,1)S(1)}, u32[]{:S(2)}, u32[]{:S(2)}) collective-permute-start(bf16[128,512]{1,0:T(8,128)(2,1)S(1)} %get-tuple-element.52), channel_id=1, source_target_pairs={{0,4},{2,6},{4,0},{6,2},{8,12},{10,14},{12,8},{14,10},{16,20},{18,... | collective-permute-start | bytes 393224 | tf_op jit(solution)/shard_map/ppermute | solution.py:350
  30.8 1.7 %collective-permute-start.7 = (bf16[128,512]{1,0:T(8,128)(2,1)S(1)}, bf16[128,512]{1,0:T(8,128)(2,1)S(1)}, u32[]{:S(2)}, u32[]{:S(2)}) collective-permute-start(bf16[128,512]{1,0:T(8,128)(2,1)S(1)} %get-tuple-element.53), channel_id=1, source_target_pairs={{0,6},{2,4},{4,2},{6,0},{8,14},{10,12},{12,10},{14,8},{16,22},{18,... | collective-permute-start | bytes 393224 | tf_op jit(solution)/shard_map/ppermute | solution.py:350
  33.0 3.1 %collective-permute-start.17 = (bf16[160,512]{1,0:T(8,128)(2,1)S(1)}, bf16[160,512]{1,0:T(8,128)(2,1)S(1)}, u32[]{:S(2)}, u32[]{:S(2)}) collective-permute-start(bf16[160,512]{1,0:T(8,128)(2,1)S(1)} %get-tuple-element.56), channel_id=1, source_target_pairs={{0,16},{2,18},{4,20},{6,22},{8,24},{10,26},{12,28},{14,30},{16,0},... | collective-permute-start | bytes 491528 | tf_op jit(solution)/shard_map/ppermute | solution.py:350
  36.7 2.9 %collective-permute-start.4 = (bf16[128,512]{1,0:T(8,128)(2,1)S(1)}, bf16[128,512]{1,0:T(8,128)(2,1)S(1)}, u32[]{:S(2)}, u32[]{:S(2)}) collective-permute-start(bf16[128,512]{1,0:T(8,128)(2,1)S(1)} %get-tuple-element.49), channel_id=1, source_target_pairs={{0,6},{2,4},{4,2},{6,0},{8,14},{10,12},{12,10},{14,8},{16,22},{18,... | collective-permute-start | bytes 393224 | tf_op jit(solution)/shard_map/ppermute | solution.py:350
  40.7 1.3 %collective-permute-done.17.got_ref = bf16[160,512]{1,0:T(8,128)(2,1)S(1)} collective-permute-done((bf16[160,512]{1,0:T(8,128)(2,1)S(1)}, bf16[160,512]{1,0:T(8,128)(2,1)S(1)}, u32[]{:S(2)}, u32[]{:S(2)}) %collective-permute-start.17) | collective-permute-done | bytes 163872 | tf_op jit(solution)/shard_map/ppermute | solution.py:350
  42.1 1.3 %collective-permute-start.18 = (bf16[192,512]{1,0:T(8,128)(2,1)S(1)}, bf16[192,512]{1,0:T(8,128)(2,1)S(1)}, u32[]{:S(2)}, u32[]{:S(2)}) collective-permute-start(bf16[192,512]{1,0:T(8,128)(2,1)S(1)} %get-tuple-element.60), channel_id=1, source_target_pairs={{0,2},{2,0},{4,6},{6,4},{8,10},{10,8},{12,14},{14,12},{16,18},{18,... | collective-permute-start | bytes 589832 | tf_op jit(solution)/shard_map/ppermute | solution.py:350
  43.3 1.4 %collective-permute-done.8.refs_4_ = bf16[128,512]{1,0:T(8,128)(2,1)S(1)} collective-permute-done((bf16[128,512]{1,0:T(8,128)(2,1)S(1)}, bf16[128,512]{1,0:T(8,128)(2,1)S(1)}, u32[]{:S(2)}, u32[]{:S(2)}) %collective-permute-start.8) | collective-permute-done | bytes 131104 | tf_op jit(solution)/shard_map/ppermute | solution.py:350
  44.8 3.0 %collective-permute-start.9 = (bf16[128,512]{1,0:T(8,128)(2,1)S(1)}, bf16[128,512]{1,0:T(8,128)(2,1)S(1)}, u32[]{:S(2)}, u32[]{:S(2)}) collective-permute-start(bf16[128,512]{1,0:T(8,128)(2,1)S(1)} %shard_map.106.one_ref), channel_id=1, source_target_pairs={{0,16},{2,18},{4,20},{6,22},{8,24},{10,26},{12,28},{14,30},{16,0},... | collective-permute-start | bytes 393224 | tf_op jit(solution)/shard_map/ppermute | solution.py:350
  48.0 2.6 %collective-permute-start.19 = (bf16[160,512]{1,0:T(8,128)(2,1)S(1)}, bf16[160,512]{1,0:T(8,128)(2,1)S(1)}, u32[]{:S(2)}, u32[]{:S(2)}) collective-permute-start(bf16[160,512]{1,0:T(8,128)(2,1)S(1)} %get-tuple-element.64), channel_id=1, source_target_pairs={{0,4},{2,6},{4,0},{6,2},{8,12},{10,14},{12,8},{14,10},{16,20},{18,... | collective-permute-start | bytes 491528 | tf_op jit(solution)/shard_map/ppermute | solution.py:350
  50.6 1.2 %collective-permute-done.9.two_ref = bf16[128,512]{1,0:T(8,128)(2,1)S(1)} collective-permute-done((bf16[128,512]{1,0:T(8,128)(2,1)S(1)}, bf16[128,512]{1,0:T(8,128)(2,1)S(1)}, u32[]{:S(2)}, u32[]{:S(2)}) %collective-permute-start.9) | collective-permute-done | bytes 131104 | tf_op jit(solution)/shard_map/ppermute | solution.py:350
  51.8 1.3 %collective-permute-start.13 = (bf16[128,512]{1,0:T(8,128)(2,1)S(1)}, bf16[128,512]{1,0:T(8,128)(2,1)S(1)}, u32[]{:S(2)}, u32[]{:S(2)}) collective-permute-start(bf16[128,512]{1,0:T(8,128)(2,1)S(1)} %shard_map.107.refs_0_), channel_id=1, source_target_pairs={{0,8},{2,10},{4,12},{6,14},{8,0},{10,2},{12,4},{14,6},{16,24},{18,... | collective-permute-start | bytes 393224 | tf_op jit(solution)/shard_map/ppermute | solution.py:350
  53.9 3.5 %collective-permute-start.11 = (bf16[128,512]{1,0:T(8,128)(2,1)S(1)}, bf16[128,512]{1,0:T(8,128)(2,1)S(1)}, u32[]{:S(2)}, u32[]{:S(2)}) collective-permute-start(bf16[128,512]{1,0:T(8,128)(2,1)S(1)} %shard_map.107.refs_0_), channel_id=1, source_target_pairs={{0,4},{2,6},{4,0},{6,2},{8,12},{10,14},{12,8},{14,10},{16,20},{18,... | collective-permute-start | bytes 393224 | tf_op jit(solution)/shard_map/ppermute | solution.py:350
  58.2 1.6 %collective-permute-start.16 = (bf16[128,512]{1,0:T(8,128)(2,1)S(1)}, bf16[128,512]{1,0:T(8,128)(2,1)S(1)}, u32[]{:S(2)}, u32[]{:S(2)}) collective-permute-start(bf16[128,512]{1,0:T(8,128)(2,1)S(1)} %collective-permute-done.13.refs_4_), channel_id=1, source_target_pairs={{0,6},{2,4},{4,2},{6,0},{8,14},{10,12},{12,10},{14,8},{16,22},{18,... | collective-permute-start | bytes 393224 | tf_op jit(solution)/shard_map/ppermute | solution.py:350
  59.8 2.1 %collective-permute-start.15 = (bf16[128,512]{1,0:T(8,128)(2,1)S(1)}, bf16[128,512]{1,0:T(8,128)(2,1)S(1)}, u32[]{:S(2)}, u32[]{:S(2)}) collective-permute-start(bf16[128,512]{1,0:T(8,128)(2,1)S(1)} %collective-permute-done.13.refs_4_), channel_id=1, source_target_pairs={{0,4},{2,6},{4,0},{6,2},{8,12},{10,14},{12,8},{14,10},{16,20},{18,... | collective-permute-start | bytes 393224 | tf_op jit(solution)/shard_map/ppermute | solution.py:350
  62.3 1.3 %collective-permute-start.14 = (bf16[128,512]{1,0:T(8,128)(2,1)S(1)}, bf16[128,512]{1,0:T(8,128)(2,1)S(1)}, u32[]{:S(2)}, u32[]{:S(2)}) collective-permute-start(bf16[128,512]{1,0:T(8,128)(2,1)S(1)} %collective-permute-done.13.refs_4_), channel_id=1, source_target_pairs={{0,2},{2,0},{4,6},{6,4},{8,10},{10,8},{12,14},{14,12},{16,18},{18,... | collective-permute-start | bytes 393224 | tf_op jit(solution)/shard_map/ppermute | solution.py:350
  64.2 1.3 %collective-permute-done.15.refs_6_ = bf16[128,512]{1,0:T(8,128)(2,1)S(1)} collective-permute-done((bf16[128,512]{1,0:T(8,128)(2,1)S(1)}, bf16[128,512]{1,0:T(8,128)(2,1)S(1)}, u32[]{:S(2)}, u32[]{:S(2)}) %collective-permute-start.15) | collective-permute-done | bytes 131104 | tf_op jit(solution)/shard_map/ppermute | solution.py:350
  65.5 1.8 %collective-permute-done.14.refs_5_ = bf16[128,512]{1,0:T(8,128)(2,1)S(1)} collective-permute-done((bf16[128,512]{1,0:T(8,128)(2,1)S(1)}, bf16[128,512]{1,0:T(8,128)(2,1)S(1)}, u32[]{:S(2)}, u32[]{:S(2)}) %collective-permute-start.14) | collective-permute-done | bytes 131104 | tf_op jit(solution)/shard_map/ppermute | solution.py:350
  67.3 1.7 %shard_map.112 = (bf16[128,512]{1,0:T(8,128)(2,1)}, bf16[512,512]{1,0:T(8,128)(2,1)}, bf16[512,512]{1,0:T(8,128)(2,1)}) custom-call(bf16[128,512]{1,0:T(8,128)(2,1)S(1)} %shard_map.107.refs_0_, bf16[128,512]{1,0:T(8,128)(2,1)S(1)} %collective-permute-done.10.refs_1_, bf16[128,512]{1,0:T(8,128)(2,1)S(1)} %collective-permute-done.11.refs_2_, ...), custom_call_target="tpu_custom_call" | custom-call | tf_op jit(solution)/shard_map/pallas_call | solution.py:446
  (36 shorter events, 6.5 us)
Async XLA Ops:
  0.6 27.0 %copy-start.2 = (bf16[512,512]{1,0:T(8,128)(2,1)S(1)}, bf16[512,512]{1,0:T(8,128)(2,1)}, u32[]{:S(2)}) copy-start(bf16[512,512]{1,0:T(8,128)(2,1)} %w_two_ref.1) | copy-start | bytes 1572868
  4.0 23.6 %copy-start = (bf16[512,512]{1,0:T(8,128)(2,1)S(1)}, bf16[512,512]{1,0:T(8,128)(2,1)}, u32[]{:S(2)}) copy-start(bf16[512,512]{1,0:T(8,128)(2,1)} %w_one_ref.3) | copy-start | bytes 1572868
  4.0 23.6 %all-to-all-start = ((bf16[16,32,512]{2,1,0:T(8,128)(2,1)}), bf16[16,32,512]{2,1,0:T(8,128)(2,1)S(1)}, u32[]{:S(2)}, u32[]{:S(2)}) async-start(bf16[16,32,512]{2,1,0:T(8,128)(2,1)} %get-tuple-element.43), calls=%async_computation | async-start | bytes 1048576 | tf_op jit(solution)/shard_map/all_to_all | solution.py:391
  12.5 5.5 %collective-permute-start = (bf16[64,512]{1,0:T(8,128)(2,1)S(1)}, bf16[64,512]{1,0:T(8,128)(2,1)S(1)}, u32[]{:S(2)}, u32[]{:S(2)}) collective-permute-start(bf16[64,512]{1,0:T(8,128)(2,1)S(1)} %get-tuple-element.44), channel_id=1, source_target_pairs={{0,2},{2,0},{4,6},{6,4},{8,10},{10,8},{12,14},{14,12},{16,18},{18,... | collective-permute-start | bytes 196616 | tf_op jit(solution)/shard_map/ppermute | solution.py:350
  14.4 3.6 %collective-permute-start.1 = (bf16[64,512]{1,0:T(8,128)(2,1)S(1)}, bf16[64,512]{1,0:T(8,128)(2,1)S(1)}, u32[]{:S(2)}, u32[]{:S(2)}) collective-permute-start(bf16[64,512]{1,0:T(8,128)(2,1)S(1)} %get-tuple-element.45), channel_id=1, source_target_pairs={{2,4},{6,8},{10,12},{14,16},{18,20},{22,24},{26,28},{4,2},{8,6},{1... | collective-permute-start | bytes 196616 | tf_op jit(solution)/shard_map/ppermute | solution.py:390
  28.9 7.3 %collective-permute-start.5 = (bf16[128,512]{1,0:T(8,128)(2,1)S(1)}, bf16[128,512]{1,0:T(8,128)(2,1)S(1)}, u32[]{:S(2)}, u32[]{:S(2)}) collective-permute-start(bf16[128,512]{1,0:T(8,128)(2,1)S(1)} %get-tuple-element.51), channel_id=1, source_target_pairs={{0,2},{2,0},{4,6},{6,4},{8,10},{10,8},{12,14},{14,12},{16,18},{18,... | collective-permute-start | bytes 393224 | tf_op jit(solution)/shard_map/ppermute | solution.py:350
  29.5 7.2 %collective-permute-start.6 = (bf16[128,512]{1,0:T(8,128)(2,1)S(1)}, bf16[128,512]{1,0:T(8,128)(2,1)S(1)}, u32[]{:S(2)}, u32[]{:S(2)}) collective-permute-start(bf16[128,512]{1,0:T(8,128)(2,1)S(1)} %get-tuple-element.52), channel_id=1, source_target_pairs={{0,4},{2,6},{4,0},{6,2},{8,12},{10,14},{12,8},{14,10},{16,20},{18,... | collective-permute-start | bytes 393224 | tf_op jit(solution)/shard_map/ppermute | solution.py:350
  30.8 8.8 %collective-permute-start.7 = (bf16[128,512]{1,0:T(8,128)(2,1)S(1)}, bf16[128,512]{1,0:T(8,128)(2,1)S(1)}, u32[]{:S(2)}, u32[]{:S(2)}) collective-permute-start(bf16[128,512]{1,0:T(8,128)(2,1)S(1)} %get-tuple-element.53), channel_id=1, source_target_pairs={{0,6},{2,4},{4,2},{6,0},{8,14},{10,12},{12,10},{14,8},{16,22},{18,... | collective-permute-start | bytes 393224 | tf_op jit(solution)/shard_map/ppermute | solution.py:350
  33.0 9.0 %collective-permute-start.17 = (bf16[160,512]{1,0:T(8,128)(2,1)S(1)}, bf16[160,512]{1,0:T(8,128)(2,1)S(1)}, u32[]{:S(2)}, u32[]{:S(2)}) collective-permute-start(bf16[160,512]{1,0:T(8,128)(2,1)S(1)} %get-tuple-element.56), channel_id=1, source_target_pairs={{0,16},{2,18},{4,20},{6,22},{8,24},{10,26},{12,28},{14,30},{16,0},... | collective-permute-start | bytes 491528 | tf_op jit(solution)/shard_map/ppermute | solution.py:350
  36.1 7.2 %collective-permute-start.2 = (bf16[128,512]{1,0:T(8,128)(2,1)S(1)}, bf16[128,512]{1,0:T(8,128)(2,1)S(1)}, u32[]{:S(2)}, u32[]{:S(2)}) collective-permute-start(bf16[128,512]{1,0:T(8,128)(2,1)S(1)} %get-tuple-element.47), channel_id=1, source_target_pairs={{0,2},{2,0},{4,6},{6,4},{8,10},{10,8},{12,14},{14,12},{16,18},{18,... | collective-permute-start | bytes 393224 | tf_op jit(solution)/shard_map/ppermute | solution.py:350
  36.2 7.1 %collective-permute-start.3 = (bf16[128,512]{1,0:T(8,128)(2,1)S(1)}, bf16[128,512]{1,0:T(8,128)(2,1)S(1)}, u32[]{:S(2)}, u32[]{:S(2)}) collective-permute-start(bf16[128,512]{1,0:T(8,128)(2,1)S(1)} %get-tuple-element.48), channel_id=1, source_target_pairs={{0,4},{2,6},{4,0},{6,2},{8,12},{10,14},{12,8},{14,10},{16,20},{18,... | collective-permute-start | bytes 393224 | tf_op jit(solution)/shard_map/ppermute | solution.py:350
  36.7 6.6 %collective-permute-start.4 = (bf16[128,512]{1,0:T(8,128)(2,1)S(1)}, bf16[128,512]{1,0:T(8,128)(2,1)S(1)}, u32[]{:S(2)}, u32[]{:S(2)}) collective-permute-start(bf16[128,512]{1,0:T(8,128)(2,1)S(1)} %get-tuple-element.49), channel_id=1, source_target_pairs={{0,6},{2,4},{4,2},{6,0},{8,14},{10,12},{12,10},{14,8},{16,22},{18,... | collective-permute-start | bytes 393224 | tf_op jit(solution)/shard_map/ppermute | solution.py:350
  39.7 5.0 %collective-permute-start.8 = (bf16[128,512]{1,0:T(8,128)(2,1)S(1)}, bf16[128,512]{1,0:T(8,128)(2,1)S(1)}, u32[]{:S(2)}, u32[]{:S(2)}) collective-permute-start(bf16[128,512]{1,0:T(8,128)(2,1)S(1)} %shard_map.105), channel_id=1, source_target_pairs={{0,8},{2,10},{4,12},{6,14},{8,0},{10,2},{12,4},{14,6},{16,24},{18,... | collective-permute-start | bytes 393224 | tf_op jit(solution)/shard_map/ppermute | solution.py:350
  42.1 5.9 %collective-permute-start.18 = (bf16[192,512]{1,0:T(8,128)(2,1)S(1)}, bf16[192,512]{1,0:T(8,128)(2,1)S(1)}, u32[]{:S(2)}, u32[]{:S(2)}) collective-permute-start(bf16[192,512]{1,0:T(8,128)(2,1)S(1)} %get-tuple-element.60), channel_id=1, source_target_pairs={{0,2},{2,0},{4,6},{6,4},{8,10},{10,8},{12,14},{14,12},{16,18},{18,... | collective-permute-start | bytes 589832 | tf_op jit(solution)/shard_map/ppermute | solution.py:350
  44.8 7.0 %collective-permute-start.9 = (bf16[128,512]{1,0:T(8,128)(2,1)S(1)}, bf16[128,512]{1,0:T(8,128)(2,1)S(1)}, u32[]{:S(2)}, u32[]{:S(2)}) collective-permute-start(bf16[128,512]{1,0:T(8,128)(2,1)S(1)} %shard_map.106.one_ref), channel_id=1, source_target_pairs={{0,16},{2,18},{4,20},{6,22},{8,24},{10,26},{12,28},{14,30},{16,0},... | collective-permute-start | bytes 393224 | tf_op jit(solution)/shard_map/ppermute | solution.py:350
  48.0 9.4 %collective-permute-start.19 = (bf16[160,512]{1,0:T(8,128)(2,1)S(1)}, bf16[160,512]{1,0:T(8,128)(2,1)S(1)}, u32[]{:S(2)}, u32[]{:S(2)}) collective-permute-start(bf16[160,512]{1,0:T(8,128)(2,1)S(1)} %get-tuple-element.64), channel_id=1, source_target_pairs={{0,4},{2,6},{4,0},{6,2},{8,12},{10,14},{12,8},{14,10},{16,20},{18,... | collective-permute-start | bytes 491528 | tf_op jit(solution)/shard_map/ppermute | solution.py:350
  51.8 6.3 %collective-permute-start.13 = (bf16[128,512]{1,0:T(8,128)(2,1)S(1)}, bf16[128,512]{1,0:T(8,128)(2,1)S(1)}, u32[]{:S(2)}, u32[]{:S(2)}) collective-permute-start(bf16[128,512]{1,0:T(8,128)(2,1)S(1)} %shard_map.107.refs_0_), channel_id=1, source_target_pairs={{0,8},{2,10},{4,12},{6,14},{8,0},{10,2},{12,4},{14,6},{16,24},{18,... | collective-permute-start | bytes 393224 | tf_op jit(solution)/shard_map/ppermute | solution.py:350
  53.1 6.6 %collective-permute-start.12 = (bf16[128,512]{1,0:T(8,128)(2,1)S(1)}, bf16[128,512]{1,0:T(8,128)(2,1)S(1)}, u32[]{:S(2)}, u32[]{:S(2)}) collective-permute-start(bf16[128,512]{1,0:T(8,128)(2,1)S(1)} %shard_map.107.refs_0_), channel_id=1, source_target_pairs={{0,6},{2,4},{4,2},{6,0},{8,14},{10,12},{12,10},{14,8},{16,22},{18,... | collective-permute-start | bytes 393224 | tf_op jit(solution)/shard_map/ppermute | solution.py:350
  53.9 8.4 %collective-permute-start.11 = (bf16[128,512]{1,0:T(8,128)(2,1)S(1)}, bf16[128,512]{1,0:T(8,128)(2,1)S(1)}, u32[]{:S(2)}, u32[]{:S(2)}) collective-permute-start(bf16[128,512]{1,0:T(8,128)(2,1)S(1)} %shard_map.107.refs_0_), channel_id=1, source_target_pairs={{0,4},{2,6},{4,0},{6,2},{8,12},{10,14},{12,8},{14,10},{16,20},{18,... | collective-permute-start | bytes 393224 | tf_op jit(solution)/shard_map/ppermute | solution.py:350
  57.5 9.8 %collective-permute-start.20 = (bf16[160,512]{1,0:T(8,128)(2,1)S(1)}, bf16[160,512]{1,0:T(8,128)(2,1)S(1)}, u32[]{:S(2)}, u32[]{:S(2)}) collective-permute-start(bf16[160,512]{1,0:T(8,128)(2,1)S(1)} %get-tuple-element.68), channel_id=1, source_target_pairs={{0,8},{2,10},{4,12},{6,14},{8,0},{10,2},{12,4},{14,6},{16,24},{18,... | collective-permute-start | bytes 491528 | tf_op jit(solution)/shard_map/ppermute | solution.py:350
  57.6 6.0 %collective-permute-start.10 = (bf16[128,512]{1,0:T(8,128)(2,1)S(1)}, bf16[128,512]{1,0:T(8,128)(2,1)S(1)}, u32[]{:S(2)}, u32[]{:S(2)}) collective-permute-start(bf16[128,512]{1,0:T(8,128)(2,1)S(1)} %shard_map.107.refs_0_), channel_id=1, source_target_pairs={{0,2},{2,0},{4,6},{6,4},{8,10},{10,8},{12,14},{14,12},{16,18},{18,... | collective-permute-start | bytes 393224 | tf_op jit(solution)/shard_map/ppermute | solution.py:350
  58.2 6.0 %collective-permute-start.16 = (bf16[128,512]{1,0:T(8,128)(2,1)S(1)}, bf16[128,512]{1,0:T(8,128)(2,1)S(1)}, u32[]{:S(2)}, u32[]{:S(2)}) collective-permute-start(bf16[128,512]{1,0:T(8,128)(2,1)S(1)} %collective-permute-done.13.refs_4_), channel_id=1, source_target_pairs={{0,6},{2,4},{4,2},{6,0},{8,14},{10,12},{12,10},{14,8},{16,22},{18,... | collective-permute-start | bytes 393224 | tf_op jit(solution)/shard_map/ppermute | solution.py:350
  59.8 5.7 %collective-permute-start.15 = (bf16[128,512]{1,0:T(8,128)(2,1)S(1)}, bf16[128,512]{1,0:T(8,128)(2,1)S(1)}, u32[]{:S(2)}, u32[]{:S(2)}) collective-permute-start(bf16[128,512]{1,0:T(8,128)(2,1)S(1)} %collective-permute-done.13.refs_4_), channel_id=1, source_target_pairs={{0,4},{2,6},{4,0},{6,2},{8,12},{10,14},{12,8},{14,10},{16,20},{18,... | collective-permute-start | bytes 393224 | tf_op jit(solution)/shard_map/ppermute | solution.py:350
  62.3 5.0 %collective-permute-start.14 = (bf16[128,512]{1,0:T(8,128)(2,1)S(1)}, bf16[128,512]{1,0:T(8,128)(2,1)S(1)}, u32[]{:S(2)}, u32[]{:S(2)}) collective-permute-start(bf16[128,512]{1,0:T(8,128)(2,1)S(1)} %collective-permute-done.13.refs_4_), channel_id=1, source_target_pairs={{0,2},{2,0},{4,6},{6,4},{8,10},{10,8},{12,14},{14,12},{16,18},{18,... | collective-permute-start | bytes 393224 | tf_op jit(solution)/shard_map/ppermute | solution.py:350
  (1 other events, 23.6 us)

commit v10 on v9

--- a/solution.py
+++ b/solution.py
@@ -427,7 +427,7 @@
         (struct((ROWS, D), F32), *carried, message(bits[0])),
     )(matrix, total, d_pre, weight_one)
     got = swap(out, 1 << bits[0])
-    for at in range(1, len(bits)):
+    for at in range(1, len(bits) - 1):
         out, held = next_hop(at, got, held)
         got = swap(out, 1 << bits[at])
     total = call(sum_kernel, sent, work=268435456)(*kept, swap(call(sum_kernel, sent, work=1073741824)(*given), PLANE))
@@ -440,6 +440,9 @@
         functools.partial(pair_sum_kernel, 1.0 / math.sqrt(ROWS * count)), sent
     )(total, other)
     far_total = swap(total, PLANE)
+    far_total, got = lax.optimization_barrier((far_total, got))
+    out, held = next_hop(len(bits) - 1, got, held)
+    got = swap(out, 1 << bits[-1])
     chunks = [total] + [swap(total, v) for v in range(1, PLANE)]
     chunks = chunks + [far_total] + [swap(far_total, v) for v in range(1, PLANE)]
     anywhere = pl.BlockSpec(memory_space=pl.ANY)

time: 69.3 us -> 70.7 us (1.020)
  waiting for transfers between devices: 20.9 us -> 21.7 us
    ppermute x20, waiting for transfers between devices: 11.2 us -> 12.1 us  [swap(): return lax.ppermute(value, 'node', [(i, i ^ flip) for i in range(count)])]
  transfers between devices with their start and end apart: 22 -> 22, of which waited for: 10 -> 11; matrix products, arithmetic and copies ran while one was open for 0% -> 0% of each run, Pallas kernels for 1% -> 1%
where the time goes in v10:
time: 70.7 us; the launch traced here: 70.5 us
  starting transfers between devices  40.8 us (58%)
  waiting for transfers between devices  21.7 us (31%)
  Pallas kernels  7.17 us (10%)
  between operations  0.74 us (1%)
    ppermute x20, starting transfers between devices, swap(): return lax.ppermute(value, 'node', [(i, i ^ flip) for i in range(count)])  31.7 us
    ppermute x20, waiting for transfers between devices, swap(): return lax.ppermute(value, 'node', [(i, i ^ flip) for i in range(count)])  12.1 us
    all_to_all x1, waiting for transfers between devices, shards(): lax.all_to_all(send, 'node', split_axis=0, concat_axis=0, tiled=True)  9.62 us
    all_to_all x1, starting transfers between devices, shards(): lax.all_to_all(send, 'node', split_axis=0, concat_axis=0, tiled=True)  8.46 us
    pallas_call x1, Pallas kernels, shards(): call(functools.partial(prepare_kernel, count), (struct((chain, ROWS), BF1...  3.36 us
    pallas_call x1, Pallas kernels, shards(): call(functools.partial(last_kernel, count, bits[-1]), (struct((ROWS, D),...  1.72 us
  transfers between devices with their start and end apart: 22, of which 11 were waited for; matrix products, arithmetic and copies ran while one was open for 0% of the time, Pallas kernels for 1%

profile of v10, /device:TPU:0, one launch (start us, length us, event | category | flops | bytes accessed | tf_op | source)
XLA Modules:
  0.0 70.5 jit_solution(14596795642881494213)
XLA Ops:
  0.6 3.4 %shard_map.103 = (bf16[512,128]{1,0:T(8,128)(2,1)S(1)}, bf16[128,256]{1,0:T(8,128)(2,1)S(1)}, f32[128,128]{1,0:T(8,128)S(1)}, f32[128,512]{1,0:T(8,128)S(1)}, bf...) custom-call(s32[32,128]{1,0:T(8,128)} %bitcast.4, s32[32,128]{1,0:T(8,128)} %bitcast.5, ...), custom_call_target="tpu_custom_call" | custom-call | tf_op jit(solution)/shard_map/pallas_call | solution.py:353
  4.0 8.5 %all-to-all-start = ((bf16[16,32,512]{2,1,0:T(8,128)(2,1)}), bf16[16,32,512]{2,1,0:T(8,128)(2,1)S(1)}, u32[]{:S(2)}, u32[]{:S(2)}) async-start(bf16[16,32,512]{2,1,0:T(8,128)(2,1)} %get-tuple-element.45), calls=%async_computation | async-start | bytes 1048576 | tf_op jit(solution)/shard_map/all_to_all | solution.py:391
  12.5 1.9 %collective-permute-start = (bf16[64,512]{1,0:T(8,128)(2,1)S(1)}, bf16[64,512]{1,0:T(8,128)(2,1)S(1)}, u32[]{:S(2)}, u32[]{:S(2)}) collective-permute-start(bf16[64,512]{1,0:T(8,128)(2,1)S(1)} %get-tuple-element.46), channel_id=1, source_target_pairs={{0,2},{2,0},{4,6},{6,4},{8,10},{10,8},{12,14},{14,12},{16,18},{18,... | collective-permute-start | bytes 196616 | tf_op jit(solution)/shard_map/ppermute | solution.py:350
  15.1 2.9 %collective-permute-done.near_ref = bf16[64,512]{1,0:T(8,128)(2,1)S(1)} collective-permute-done((bf16[64,512]{1,0:T(8,128)(2,1)S(1)}, bf16[64,512]{1,0:T(8,128)(2,1)S(1)}, u32[]{:S(2)}, u32[]{:S(2)}) %collective-permute-start) | collective-permute-done | bytes 65568 | tf_op jit(solution)/shard_map/ppermute | solution.py:350
  18.0 9.6 %all-to-all-done.recv_ref = bf16[16,32,512]{2,1,0:T(8,128)(2,1)S(1)} async-done(((bf16[16,32,512]{2,1,0:T(8,128)(2,1)}), bf16[16,32,512]{2,1,0:T(8,128)(2,1)S(1)}, u32[]{:S(2)}, u32[]{:S(2)}) %all-to-all-start) | async-done | bytes 524320 | tf_op jit(solution)/shard_map/all_to_all | solution.py:391
  27.6 1.2 %shard_map.104 = (f32[128,512]{1,0:T(8,128)S(1)}, bf16[128,512]{1,0:T(8,128)(2,1)S(1)}, bf16[128,512]{1,0:T(8,128)(2,1)S(1)}, bf16[128,512]{1,0:T(8,128)(2,1)S(1...) custom-call(bf16[512,128]{1,0:T(8,128)(2,1)S(1)} %get-tuple-element., ...), custom_call_target="tpu_custom_call" | custom-call | tf_op jit(solution)/shard_map/pallas_call | solution.py:394
  29.5 1.3 %collective-permute-start.6 = (bf16[128,512]{1,0:T(8,128)(2,1)S(1)}, bf16[128,512]{1,0:T(8,128)(2,1)S(1)}, u32[]{:S(2)}, u32[]{:S(2)}) collective-permute-start(bf16[128,512]{1,0:T(8,128)(2,1)S(1)} %get-tuple-element.54), channel_id=1, source_target_pairs={{0,4},{2,6},{4,0},{6,2},{8,12},{10,14},{12,8},{14,10},{16,20},{18,... | collective-permute-start | bytes 393224 | tf_op jit(solution)/shard_map/ppermute | solution.py:350
  30.8 1.7 %collective-permute-start.7 = (bf16[128,512]{1,0:T(8,128)(2,1)S(1)}, bf16[128,512]{1,0:T(8,128)(2,1)S(1)}, u32[]{:S(2)}, u32[]{:S(2)}) collective-permute-start(bf16[128,512]{1,0:T(8,128)(2,1)S(1)} %get-tuple-element.55), channel_id=1, source_target_pairs={{0,6},{2,4},{4,2},{6,0},{8,14},{10,12},{12,10},{14,8},{16,22},{18,... | collective-permute-start | bytes 393224 | tf_op jit(solution)/shard_map/ppermute | solution.py:350
  33.0 3.1 %collective-permute-start.14 = (bf16[160,512]{1,0:T(8,128)(2,1)S(1)}, bf16[160,512]{1,0:T(8,128)(2,1)S(1)}, u32[]{:S(2)}, u32[]{:S(2)}) collective-permute-start(bf16[160,512]{1,0:T(8,128)(2,1)S(1)} %get-tuple-element.57), channel_id=1, source_target_pairs={{0,16},{2,18},{4,20},{6,22},{8,24},{10,26},{12,28},{14,30},{16,0},... | collective-permute-start | bytes 491528 | tf_op jit(solution)/shard_map/ppermute | solution.py:350
  36.7 2.9 %collective-permute-start.4 = (bf16[128,512]{1,0:T(8,128)(2,1)S(1)}, bf16[128,512]{1,0:T(8,128)(2,1)S(1)}, u32[]{:S(2)}, u32[]{:S(2)}) collective-permute-start(bf16[128,512]{1,0:T(8,128)(2,1)S(1)} %get-tuple-element.51), channel_id=1, source_target_pairs={{0,6},{2,4},{4,2},{6,0},{8,14},{10,12},{12,10},{14,8},{16,22},{18,... | collective-permute-start | bytes 393224 | tf_op jit(solution)/shard_map/ppermute | solution.py:350
  40.7 1.3 %collective-permute-done.14.got_ref = bf16[160,512]{1,0:T(8,128)(2,1)S(1)} collective-permute-done((bf16[160,512]{1,0:T(8,128)(2,1)S(1)}, bf16[160,512]{1,0:T(8,128)(2,1)S(1)}, u32[]{:S(2)}, u32[]{:S(2)}) %collective-permute-start.14) | collective-permute-done | bytes 163872 | tf_op jit(solution)/shard_map/ppermute | solution.py:350
  42.1 1.3 %collective-permute-start.15 = (bf16[192,512]{1,0:T(8,128)(2,1)S(1)}, bf16[192,512]{1,0:T(8,128)(2,1)S(1)}, u32[]{:S(2)}, u32[]{:S(2)}) collective-permute-start(bf16[192,512]{1,0:T(8,128)(2,1)S(1)} %get-tuple-element.61), channel_id=1, source_target_pairs={{0,2},{2,0},{4,6},{6,4},{8,10},{10,8},{12,14},{14,12},{16,18},{18,... | collective-permute-start | bytes 589832 | tf_op jit(solution)/shard_map/ppermute | solution.py:350
  43.3 1.4 %collective-permute-done.8.refs_4_ = bf16[128,512]{1,0:T(8,128)(2,1)S(1)} collective-permute-done((bf16[128,512]{1,0:T(8,128)(2,1)S(1)}, bf16[128,512]{1,0:T(8,128)(2,1)S(1)}, u32[]{:S(2)}, u32[]{:S(2)}) %collective-permute-start.8) | collective-permute-done | bytes 131104 | tf_op jit(solution)/shard_map/ppermute | solution.py:350
  44.8 3.0 %collective-permute-start.9 = (bf16[128,512]{1,0:T(8,128)(2,1)S(1)}, bf16[128,512]{1,0:T(8,128)(2,1)S(1)}, u32[]{:S(2)}, u32[]{:S(2)}) collective-permute-start(bf16[128,512]{1,0:T(8,128)(2,1)S(1)} %shard_map.106.one_ref), channel_id=1, source_target_pairs={{0,16},{2,18},{4,20},{6,22},{8,24},{10,26},{12,28},{14,30},{16,0},... | collective-permute-start | bytes 393224 | tf_op jit(solution)/shard_map/ppermute | solution.py:350
  48.0 2.6 %collective-permute-start.16 = (bf16[160,512]{1,0:T(8,128)(2,1)S(1)}, bf16[160,512]{1,0:T(8,128)(2,1)S(1)}, u32[]{:S(2)}, u32[]{:S(2)}) collective-permute-start(bf16[160,512]{1,0:T(8,128)(2,1)S(1)} %get-tuple-element.65), channel_id=1, source_target_pairs={{0,4},{2,6},{4,0},{6,2},{8,12},{10,14},{12,8},{14,10},{16,20},{18,... | collective-permute-start | bytes 491528 | tf_op jit(solution)/shard_map/ppermute | solution.py:350
  50.6 1.2 %collective-permute-done.9.two_ref = bf16[128,512]{1,0:T(8,128)(2,1)S(1)} collective-permute-done((bf16[128,512]{1,0:T(8,128)(2,1)S(1)}, bf16[128,512]{1,0:T(8,128)(2,1)S(1)}, u32[]{:S(2)}, u32[]{:S(2)}) %collective-permute-start.9) | collective-permute-done | bytes 131104 | tf_op jit(solution)/shard_map/ppermute | solution.py:350
  51.8 1.3 %collective-permute-start.13 = (bf16[128,512]{1,0:T(8,128)(2,1)S(1)}, bf16[128,512]{1,0:T(8,128)(2,1)S(1)}, u32[]{:S(2)}, u32[]{:S(2)}) collective-permute-start(bf16[128,512]{1,0:T(8,128)(2,1)S(1)} %shard_map.107.refs_0_), channel_id=1, source_target_pairs={{0,8},{2,10},{4,12},{6,14},{8,0},{10,2},{12,4},{14,6},{16,24},{18,... | collective-permute-start | bytes 393224 | tf_op jit(solution)/shard_map/ppermute | solution.py:350
  53.9 3.5 %collective-permute-start.11 = (bf16[128,512]{1,0:T(8,128)(2,1)S(1)}, bf16[128,512]{1,0:T(8,128)(2,1)S(1)}, u32[]{:S(2)}, u32[]{:S(2)}) collective-permute-start(bf16[128,512]{1,0:T(8,128)(2,1)S(1)} %shard_map.107.refs_0_), channel_id=1, source_target_pairs={{0,4},{2,6},{4,0},{6,2},{8,12},{10,14},{12,8},{14,10},{16,20},{18,... | collective-permute-start | bytes 393224 | tf_op jit(solution)/shard_map/ppermute | solution.py:350
  58.0 1.6 %collective-permute-start.20 = (bf16[160,512]{1,0:T(8,128)(2,1)S(1)}, bf16[160,512]{1,0:T(8,128)(2,1)S(1)}, u32[]{:S(2)}, u32[]{:S(2)}) collective-permute-start(bf16[160,512]{1,0:T(8,128)(2,1)S(1)} %get-tuple-element.72), channel_id=1, source_target_pairs={{0,8},{2,10},{4,12},{6,14},{8,0},{10,2},{12,4},{14,6},{16,24},{18,... | collective-permute-start | bytes 491528 | tf_op jit(solution)/shard_map/ppermute | solution.py:350
  59.6 1.5 %collective-permute-start.10 = (bf16[128,512]{1,0:T(8,128)(2,1)S(1)}, bf16[128,512]{1,0:T(8,128)(2,1)S(1)}, u32[]{:S(2)}, u32[]{:S(2)}) collective-permute-start(bf16[128,512]{1,0:T(8,128)(2,1)S(1)} %shard_map.107.refs_0_), channel_id=1, source_target_pairs={{0,2},{2,0},{4,6},{6,4},{8,10},{10,8},{12,14},{14,12},{16,18},{18,... | collective-permute-start | bytes 393224 | tf_op jit(solution)/shard_map/ppermute | solution.py:350
  63.8 1.2 %collective-permute-start.17 = (bf16[128,512]{1,0:T(8,128)(2,1)S(1)}, bf16[128,512]{1,0:T(8,128)(2,1)S(1)}, u32[]{:S(2)}, u32[]{:S(2)}) collective-permute-start(bf16[128,512]{1,0:T(8,128)(2,1)S(1)} %collective-permute-done.13.refs_4_), channel_id=1, source_target_pairs={{0,2},{2,0},{4,6},{6,4},{8,10},{10,8},{12,14},{14,12},{16,18},{18,... | collective-permute-start | bytes 393224 | tf_op jit(solution)/shard_map/ppermute | solution.py:350
  65.0 2.1 %collective-permute-done.19.refs_7_ = bf16[128,512]{1,0:T(8,128)(2,1)S(1)} collective-permute-done((bf16[128,512]{1,0:T(8,128)(2,1)S(1)}, bf16[128,512]{1,0:T(8,128)(2,1)S(1)}, u32[]{:S(2)}, u32[]{:S(2)}) %collective-permute-start.19) | collective-permute-done | bytes 131104 | tf_op jit(solution)/shard_map/ppermute | solution.py:350
  67.1 1.3 %collective-permute-done.18.refs_6_ = bf16[128,512]{1,0:T(8,128)(2,1)S(1)} collective-permute-done((bf16[128,512]{1,0:T(8,128)(2,1)S(1)}, bf16[128,512]{1,0:T(8,128)(2,1)S(1)}, u32[]{:S(2)}, u32[]{:S(2)}) %collective-permute-start.18) | collective-permute-done | bytes 131104 | tf_op jit(solution)/shard_map/ppermute | solution.py:350
  68.8 1.7 %shard_map.112 = (bf16[128,512]{1,0:T(8,128)(2,1)}, bf16[512,512]{1,0:T(8,128)(2,1)}, bf16[512,512]{1,0:T(8,128)(2,1)}) custom-call(bf16[128,512]{1,0:T(8,128)(2,1)S(1)} %shard_map.107.refs_0_, bf16[128,512]{1,0:T(8,128)(2,1)S(1)} %collective-permute-done.10.refs_1_, bf16[128,512]{1,0:T(8,128)(2,1)S(1)} %collective-permute-done.11.refs_2_, ...), custom_call_target="tpu_custom_call" | custom-call | tf_op jit(solution)/shard_map/pallas_call | solution.py:449
  (36 shorter events, 8.4 us)
Async XLA Ops:
  0.6 27.0 %copy-start.2 = (bf16[512,512]{1,0:T(8,128)(2,1)S(1)}, bf16[512,512]{1,0:T(8,128)(2,1)}, u32[]{:S(2)}) copy-start(bf16[512,512]{1,0:T(8,128)(2,1)} %w_two_ref.1) | copy-start | bytes 1572868
  4.0 23.6 %copy-start = (bf16[512,512]{1,0:T(8,128)(2,1)S(1)}, bf16[512,512]{1,0:T(8,128)(2,1)}, u32[]{:S(2)}) copy-start(bf16[512,512]{1,0:T(8,128)(2,1)} %w_one_ref.3) | copy-start | bytes 1572868
  4.0 23.6 %all-to-all-start = ((bf16[16,32,512]{2,1,0:T(8,128)(2,1)}), bf16[16,32,512]{2,1,0:T(8,128)(2,1)S(1)}, u32[]{:S(2)}, u32[]{:S(2)}) async-start(bf16[16,32,512]{2,1,0:T(8,128)(2,1)} %get-tuple-element.45), calls=%async_computation | async-start | bytes 1048576 | tf_op jit(solution)/shard_map/all_to_all | solution.py:391
  12.5 5.5 %collective-permute-start = (bf16[64,512]{1,0:T(8,128)(2,1)S(1)}, bf16[64,512]{1,0:T(8,128)(2,1)S(1)}, u32[]{:S(2)}, u32[]{:S(2)}) collective-permute-start(bf16[64,512]{1,0:T(8,128)(2,1)S(1)} %get-tuple-element.46), channel_id=1, source_target_pairs={{0,2},{2,0},{4,6},{6,4},{8,10},{10,8},{12,14},{14,12},{16,18},{18,... | collective-permute-start | bytes 196616 | tf_op jit(solution)/shard_map/ppermute | solution.py:350
  14.4 3.6 %collective-permute-start.1 = (bf16[64,512]{1,0:T(8,128)(2,1)S(1)}, bf16[64,512]{1,0:T(8,128)(2,1)S(1)}, u32[]{:S(2)}, u32[]{:S(2)}) collective-permute-start(bf16[64,512]{1,0:T(8,128)(2,1)S(1)} %get-tuple-element.47), channel_id=1, source_target_pairs={{2,4},{6,8},{10,12},{14,16},{18,20},{22,24},{26,28},{4,2},{8,6},{1... | collective-permute-start | bytes 196616 | tf_op jit(solution)/shard_map/ppermute | solution.py:390
  28.9 7.3 %collective-permute-start.5 = (bf16[128,512]{1,0:T(8,128)(2,1)S(1)}, bf16[128,512]{1,0:T(8,128)(2,1)S(1)}, u32[]{:S(2)}, u32[]{:S(2)}) collective-permute-start(bf16[128,512]{1,0:T(8,128)(2,1)S(1)} %get-tuple-element.53), channel_id=1, source_target_pairs={{0,2},{2,0},{4,6},{6,4},{8,10},{10,8},{12,14},{14,12},{16,18},{18,... | collective-permute-start | bytes 393224 | tf_op jit(solution)/shard_map/ppermute | solution.py:350
  29.5 7.2 %collective-permute-start.6 = (bf16[128,512]{1,0:T(8,128)(2,1)S(1)}, bf16[128,512]{1,0:T(8,128)(2,1)S(1)}, u32[]{:S(2)}, u32[]{:S(2)}) collective-permute-start(bf16[128,512]{1,0:T(8,128)(2,1)S(1)} %get-tuple-element.54), channel_id=1, source_target_pairs={{0,4},{2,6},{4,0},{6,2},{8,12},{10,14},{12,8},{14,10},{16,20},{18,... | collective-permute-start | bytes 393224 | tf_op jit(solution)/shard_map/ppermute | solution.py:350
  30.8 8.8 %collective-permute-start.7 = (bf16[128,512]{1,0:T(8,128)(2,1)S(1)}, bf16[128,512]{1,0:T(8,128)(2,1)S(1)}, u32[]{:S(2)}, u32[]{:S(2)}) collective-permute-start(bf16[128,512]{1,0:T(8,128)(2,1)S(1)} %get-tuple-element.55), channel_id=1, source_target_pairs={{0,6},{2,4},{4,2},{6,0},{8,14},{10,12},{12,10},{14,8},{16,22},{18,... | collective-permute-start | bytes 393224 | tf_op jit(solution)/shard_map/ppermute | solution.py:350
  33.0 9.0 %collective-permute-start.14 = (bf16[160,512]{1,0:T(8,128)(2,1)S(1)}, bf16[160,512]{1,0:T(8,128)(2,1)S(1)}, u32[]{:S(2)}, u32[]{:S(2)}) collective-permute-start(bf16[160,512]{1,0:T(8,128)(2,1)S(1)} %get-tuple-element.57), channel_id=1, source_target_pairs={{0,16},{2,18},{4,20},{6,22},{8,24},{10,26},{12,28},{14,30},{16,0},... | collective-permute-start | bytes 491528 | tf_op jit(solution)/shard_map/ppermute | solution.py:350
  36.1 7.2 %collective-permute-start.2 = (bf16[128,512]{1,0:T(8,128)(2,1)S(1)}, bf16[128,512]{1,0:T(8,128)(2,1)S(1)}, u32[]{:S(2)}, u32[]{:S(2)}) collective-permute-start(bf16[128,512]{1,0:T(8,128)(2,1)S(1)} %get-tuple-element.49), channel_id=1, source_target_pairs={{0,2},{2,0},{4,6},{6,4},{8,10},{10,8},{12,14},{14,12},{16,18},{18,... | collective-permute-start | bytes 393224 | tf_op jit(solution)/shard_map/ppermute | solution.py:350
  36.2 7.1 %collective-permute-start.3 = (bf16[128,512]{1,0:T(8,128)(2,1)S(1)}, bf16[128,512]{1,0:T(8,128)(2,1)S(1)}, u32[]{:S(2)}, u32[]{:S(2)}) collective-permute-start(bf16[128,512]{1,0:T(8,128)(2,1)S(1)} %get-tuple-element.50), channel_id=1, source_target_pairs={{0,4},{2,6},{4,0},{6,2},{8,12},{10,14},{12,8},{14,10},{16,20},{18,... | collective-permute-start | bytes 393224 | tf_op jit(solution)/shard_map/ppermute | solution.py:350
  36.7 6.6 %collective-permute-start.4 = (bf16[128,512]{1,0:T(8,128)(2,1)S(1)}, bf16[128,512]{1,0:T(8,128)(2,1)S(1)}, u32[]{:S(2)}, u32[]{:S(2)}) collective-permute-start(bf16[128,512]{1,0:T(8,128)(2,1)S(1)} %get-tuple-element.51), channel_id=1, source_target_pairs={{0,6},{2,4},{4,2},{6,0},{8,14},{10,12},{12,10},{14,8},{16,22},{18,... | collective-permute-start | bytes 393224 | tf_op jit(solution)/shard_map/ppermute | solution.py:350
  39.7 5.0 %collective-permute-start.8 = (bf16[128,512]{1,0:T(8,128)(2,1)S(1)}, bf16[128,512]{1,0:T(8,128)(2,1)S(1)}, u32[]{:S(2)}, u32[]{:S(2)}) collective-permute-start(bf16[128,512]{1,0:T(8,128)(2,1)S(1)} %shard_map.105), channel_id=1, source_target_pairs={{0,8},{2,10},{4,12},{6,14},{8,0},{10,2},{12,4},{14,6},{16,24},{18,... | collective-permute-start | bytes 393224 | tf_op jit(solution)/shard_map/ppermute | solution.py:350
  42.1 5.9 %collective-permute-start.15 = (bf16[192,512]{1,0:T(8,128)(2,1)S(1)}, bf16[192,512]{1,0:T(8,128)(2,1)S(1)}, u32[]{:S(2)}, u32[]{:S(2)}) collective-permute-start(bf16[192,512]{1,0:T(8,128)(2,1)S(1)} %get-tuple-element.61), channel_id=1, source_target_pairs={{0,2},{2,0},{4,6},{6,4},{8,10},{10,8},{12,14},{14,12},{16,18},{18,... | collective-permute-start | bytes 589832 | tf_op jit(solution)/shard_map/ppermute | solution.py:350
  44.8 7.0 %collective-permute-start.9 = (bf16[128,512]{1,0:T(8,128)(2,1)S(1)}, bf16[128,512]{1,0:T(8,128)(2,1)S(1)}, u32[]{:S(2)}, u32[]{:S(2)}) collective-permute-start(bf16[128,512]{1,0:T(8,128)(2,1)S(1)} %shard_map.106.one_ref), channel_id=1, source_target_pairs={{0,16},{2,18},{4,20},{6,22},{8,24},{10,26},{12,28},{14,30},{16,0},... | collective-permute-start | bytes 393224 | tf_op jit(solution)/shard_map/ppermute | solution.py:350
  48.0 9.9 %collective-permute-start.16 = (bf16[160,512]{1,0:T(8,128)(2,1)S(1)}, bf16[160,512]{1,0:T(8,128)(2,1)S(1)}, u32[]{:S(2)}, u32[]{:S(2)}) collective-permute-start(bf16[160,512]{1,0:T(8,128)(2,1)S(1)} %get-tuple-element.65), channel_id=1, source_target_pairs={{0,4},{2,6},{4,0},{6,2},{8,12},{10,14},{12,8},{14,10},{16,20},{18,... | collective-permute-start | bytes 491528 | tf_op jit(solution)/shard_map/ppermute | solution.py:350
  51.8 6.1 %collective-permute-start.13 = (bf16[128,512]{1,0:T(8,128)(2,1)S(1)}, bf16[128,512]{1,0:T(8,128)(2,1)S(1)}, u32[]{:S(2)}, u32[]{:S(2)}) collective-permute-start(bf16[128,512]{1,0:T(8,128)(2,1)S(1)} %shard_map.107.refs_0_), channel_id=1, source_target_pairs={{0,8},{2,10},{4,12},{6,14},{8,0},{10,2},{12,4},{14,6},{16,24},{18,... | collective-permute-start | bytes 393224 | tf_op jit(solution)/shard_map/ppermute | solution.py:350
  53.1 9.1 %collective-permute-start.12 = (bf16[128,512]{1,0:T(8,128)(2,1)S(1)}, bf16[128,512]{1,0:T(8,128)(2,1)S(1)}, u32[]{:S(2)}, u32[]{:S(2)}) collective-permute-start(bf16[128,512]{1,0:T(8,128)(2,1)S(1)} %shard_map.107.refs_0_), channel_id=1, source_target_pairs={{0,6},{2,4},{4,2},{6,0},{8,14},{10,12},{12,10},{14,8},{16,22},{18,... | collective-permute-start | bytes 393224 | tf_op jit(solution)/shard_map/ppermute | solution.py:350
  53.9 9.8 %collective-permute-start.11 = (bf16[128,512]{1,0:T(8,128)(2,1)S(1)}, bf16[128,512]{1,0:T(8,128)(2,1)S(1)}, u32[]{:S(2)}, u32[]{:S(2)}) collective-permute-start(bf16[128,512]{1,0:T(8,128)(2,1)S(1)} %shard_map.107.refs_0_), channel_id=1, source_target_pairs={{0,4},{2,6},{4,0},{6,2},{8,12},{10,14},{12,8},{14,10},{16,20},{18,... | collective-permute-start | bytes 393224 | tf_op jit(solution)/shard_map/ppermute | solution.py:350
  58.0 10.7 %collective-permute-start.20 = (bf16[160,512]{1,0:T(8,128)(2,1)S(1)}, bf16[160,512]{1,0:T(8,128)(2,1)S(1)}, u32[]{:S(2)}, u32[]{:S(2)}) collective-permute-start(bf16[160,512]{1,0:T(8,128)(2,1)S(1)} %get-tuple-element.72), channel_id=1, source_target_pairs={{0,8},{2,10},{4,12},{6,14},{8,0},{10,2},{12,4},{14,6},{16,24},{18,... | collective-permute-start | bytes 491528 | tf_op jit(solution)/shard_map/ppermute | solution.py:350
  59.6 5.4 %collective-permute-start.10 = (bf16[128,512]{1,0:T(8,128)(2,1)S(1)}, bf16[128,512]{1,0:T(8,128)(2,1)S(1)}, u32[]{:S(2)}, u32[]{:S(2)}) collective-permute-start(bf16[128,512]{1,0:T(8,128)(2,1)S(1)} %shard_map.107.refs_0_), channel_id=1, source_target_pairs={{0,2},{2,0},{4,6},{6,4},{8,10},{10,8},{12,14},{14,12},{16,18},{18,... | collective-permute-start | bytes 393224 | tf_op jit(solution)/shard_map/ppermute | solution.py:350
  61.1 6.0 %collective-permute-start.19 = (bf16[128,512]{1,0:T(8,128)(2,1)S(1)}, bf16[128,512]{1,0:T(8,128)(2,1)S(1)}, u32[]{:S(2)}, u32[]{:S(2)}) collective-permute-start(bf16[128,512]{1,0:T(8,128)(2,1)S(1)} %collective-permute-done.13.refs_4_), channel_id=1, source_target_pairs={{0,6},{2,4},{4,2},{6,0},{8,14},{10,12},{12,10},{14,8},{16,22},{18,... | collective-permute-start | bytes 393224 | tf_op jit(solution)/shard_map/ppermute | solution.py:350
  62.3 6.1 %collective-permute-start.18 = (bf16[128,512]{1,0:T(8,128)(2,1)S(1)}, bf16[128,512]{1,0:T(8,128)(2,1)S(1)}, u32[]{:S(2)}, u32[]{:S(2)}) collective-permute-start(bf16[128,512]{1,0:T(8,128)(2,1)S(1)} %collective-permute-done.13.refs_4_), channel_id=1, source_target_pairs={{0,4},{2,6},{4,0},{6,2},{8,12},{10,14},{12,8},{14,10},{16,20},{18,... | collective-permute-start | bytes 393224 | tf_op jit(solution)/shard_map/ppermute | solution.py:350
  63.8 5.0 %collective-permute-start.17 = (bf16[128,512]{1,0:T(8,128)(2,1)S(1)}, bf16[128,512]{1,0:T(8,128)(2,1)S(1)}, u32[]{:S(2)}, u32[]{:S(2)}) collective-permute-start(bf16[128,512]{1,0:T(8,128)(2,1)S(1)} %collective-permute-done.13.refs_4_), channel_id=1, source_target_pairs={{0,2},{2,0},{4,6},{6,4},{8,10},{10,8},{12,14},{14,12},{16,18},{18,... | collective-permute-start | bytes 393224 | tf_op jit(solution)/shard_map/ppermute | solution.py:350
  (1 other events, 23.6 us)
